TPU v7x, 32 devices: a whole 2x2x4 slice. The times are simulated.
32 devices in a mesh: wide: 16 (over z, x, core), blk: 2 (over y).
Axes of the slice: x: 2, y: 2, z: 4, core: 2. Of those that a mesh axis runs over, the one named last changes fastest.
Arguments:
- tokens: bfloat16 [16, 2048, 1280], P('wide', 'blk'), may hold values from -6 to 6
- cell_start: int32 [16, 2048], P('wide', 'blk'), may hold values from 0 to 2047, as said below
- norm1_gain: float32 [1280], replicated, may hold values from 0.1 to 1.9
- norm1_bias: float32 [1280], replicated, may hold values from -3 to 3
- w_qkv: bfloat16 [1280, 3840], replicated, may hold values from -0.15625 to 0.15625
- bias_q: float32 [1280], replicated, may hold values from -3 to 3
- bias_v: float32 [1280], replicated, may hold values from -3 to 3
- w_out: bfloat16 [1280, 1280], replicated, may hold values from -0.625 to 0.625
- bias_out: float32 [1280], replicated, may hold values from -3 to 3
- norm2_gain: float32 [1280], replicated, may hold values from 0.1 to 1.9
- norm2_bias: float32 [1280], replicated, may hold values from -3 to 3
- w_in: bfloat16 [1280, 5120], replicated, may hold values from -0.15625 to 0.15625
- bias_in: float32 [5120], replicated, may hold values from -3 to 3
- w_back: bfloat16 [5120, 1280], replicated, may hold values from -0.078125 to 0.078125
- bias_back: float32 [1280], replicated, may hold values from -3 to 3
- cotangent: bfloat16 [16, 2048, 1280], P('wide', 'blk'), may hold values from -6 to 6
Outputs:
- mixed: bfloat16 [16, 2048, 1280], P('wide', 'blk')
- grad_tokens: float32 [16, 2048, 1280], P('wide', 'blk')
- grad_norm1_gain: float32 [1280], P('wide')
- grad_norm1_bias: float32 [1280], P('wide')
- grad_w_qkv: float32 [1280, 3840], P('wide')
- grad_bias_q: float32 [1280], P('wide')
- grad_bias_v: float32 [1280], P('wide')
- grad_w_out: float32 [1280, 1280], P('wide')
- grad_bias_out: float32 [1280], P('wide')
- grad_norm2_gain: float32 [1280], P('wide')
- grad_norm2_bias: float32 [1280], P('wide')
- grad_w_in: float32 [1280, 5120], P('wide')
- grad_bias_in: float32 [5120], P('wide')
- grad_w_back: float32 [5120, 1280], P('wide')
- grad_bias_back: float32 [1280], P('wide')
Inputs may be any that keep to these rules, and one draw needn't show every extreme that they name: cell_start[r, p] is the first position of the cell holding position p of row r: it never falls along a row, equals p where a cell begins and is 0 at p = 0. In every row the last position 2047 is a cell of its own. In each aligned pair of rows one row has a cell that holds positions 511 to 1535.
All inputs are finite; a program needn't handle non-finite values.
Results may differ from a plain program's by a relative error of at most 0.02.
Values may be sent and summed in bfloat16 or wider, within the bound.
No kernel may reach another device: no remote copies, remote signals or barrier semaphores. Data moves between devices by JAX's collectives and lax.ppermute only.
A program may use at most 448 MiB of HBM per device.

v0:
```python
import jax
import jax.numpy as jnp
from jax import lax
from jax.sharding import PartitionSpec as P

HEADS = 20
HEAD_DIM = 64


NEGATIVE = -1e30


def from_behind(array, axis, by):
    count = lax.axis_size(axis)
    return lax.ppermute(array, axis, [(i, (i + by) % count) for i in range(count)])


def layer_norm(values, gain, shift):
    centred = values - jnp.mean(values, axis=-1, keepdims=True)
    spread = jnp.mean(centred * centred, axis=-1, keepdims=True)
    return centred * lax.rsqrt(spread + 1e-05) * gain + shift


def gelu_exact(values):
    return jax.nn.gelu(values, approximate=False)


def on_device(
    tokens,
    cell_start,
    norm1_gain,
    norm1_bias,
    w_qkv,
    bias_q,
    bias_v,
    w_out,
    bias_out,
    norm2_gain,
    norm2_bias,
    w_in,
    bias_in,
    w_back,
    bias_back,
    cotangent,
):
    row_count, seg_len, model_width = tokens.shape
    token_count = row_count * seg_len
    inputs = tokens.astype(jnp.float32).reshape(token_count, model_width)
    normed1, norm1_pull = jax.vjp(layer_norm, inputs, norm1_gain, norm1_bias)
    acts1 = normed1.astype(jnp.bfloat16)
    mixed_qkv = jnp.dot(acts1, w_qkv, preferred_element_type=jnp.float32)
    query = (
        (mixed_qkv[:, :model_width] + bias_q)
        .astype(jnp.bfloat16)
        .reshape(row_count, seg_len, HEADS, HEAD_DIM)
    )
    keys = (
        mixed_qkv[:, model_width : 2 * model_width]
        .astype(jnp.bfloat16)
        .reshape(row_count, seg_len, model_width)
    )
    values = (
        (mixed_qkv[:, 2 * model_width :] + bias_v)
        .astype(jnp.bfloat16)
        .reshape(row_count, seg_len, model_width)
    )
    all_cells = lax.all_gather(cell_start, "blk", axis=1, tiled=True)

    def allowed_for(offset, length):
        other = lax.dynamic_slice_in_dim(all_cells, offset, length, 1)
        return cell_start[:, :, None] == other[:, None, :]

    def heads_of(part):
        return part.reshape(row_count, part.shape[1], HEADS, HEAD_DIM)

    def scores_for(key_part, allowed):
        raw = (
            jnp.einsum(
                "rqhd,rkhd->rqhk", query, heads_of(key_part), preferred_element_type=jnp.float32
            )
            * 0.125
        )
        return jnp.where(allowed[:, :, None, :], raw, NEGATIVE)

    first_top = jnp.full((row_count, seg_len, HEADS), NEGATIVE, jnp.float32)
    first_sum = jnp.zeros((row_count, seg_len, HEADS), jnp.float32)
    initial = (first_top, first_sum)
    key_part = lax.all_gather(keys, "blk", axis=1, tiled=True)
    allowed = allowed_for(jnp.int32(0), key_part.shape[1])

    def stats_update(state):
        scores = scores_for(key_part, allowed)
        newest = jnp.maximum(state[0], jnp.max(scores, axis=-1))
        expo = jnp.where(allowed[:, :, None, :], jnp.exp(scores - newest[..., None]), 0.0)
        totals = jnp.sum(expo, axis=-1)
        return (newest, totals)

    stats = lax.cond(jnp.any(allowed), stats_update, lambda state: state, initial)
    highest, totals = (stats[0], stats[1])
    empty_acc = jnp.zeros((row_count, seg_len, HEADS, HEAD_DIM), jnp.float32)

    def weigh(scores, allowed):
        expo = jnp.where(allowed[:, :, None, :], jnp.exp(scores - highest[..., None]), 0.0)
        return (expo / totals[..., None]).astype(jnp.bfloat16)

    both_key_part = lax.all_gather(keys, "blk", axis=1, tiled=True)
    value_part = lax.all_gather(values, "blk", axis=1, tiled=True)
    both_allowed = allowed_for(jnp.int32(0), both_key_part.shape[1])

    def both_update(acc):
        scores = scores_for(both_key_part, both_allowed)
        return jnp.einsum(
            "rqhk,rkhd->rqhd",
            weigh(scores, both_allowed),
            heads_of(value_part),
            preferred_element_type=jnp.float32,
        )

    attended = lax.cond(jnp.any(both_allowed), both_update, lambda acc: acc, empty_acc)
    attended_low = attended.astype(jnp.bfloat16).reshape(token_count, model_width)
    middle = inputs + jnp.dot(attended_low, w_out, preferred_element_type=jnp.float32) + bias_out
    normed2, norm2_pull = jax.vjp(layer_norm, middle, norm2_gain, norm2_bias)
    acts2 = normed2.astype(jnp.bfloat16)
    pre = jnp.dot(acts2, w_in, preferred_element_type=jnp.float32) + bias_in
    act_full, gelu_pull = jax.vjp(gelu_exact, pre)
    act_low = act_full.astype(jnp.bfloat16)
    output = middle + jnp.dot(act_low, w_back, preferred_element_type=jnp.float32) + bias_back
    mixed = output.astype(jnp.bfloat16).reshape(tokens.shape)
    grad_out = cotangent.astype(jnp.float32).reshape(token_count, model_width)
    d_out = grad_out.astype(jnp.bfloat16)
    grad_w_back = jnp.einsum("nf,nd->fd", act_low, d_out, preferred_element_type=jnp.float32)
    grad_bias_back = jnp.sum(d_out.astype(jnp.float32), axis=0)
    d_act = jnp.einsum("nd,fd->nf", d_out, w_back, preferred_element_type=jnp.float32)
    d_pre = gelu_pull(d_act)[0].astype(jnp.bfloat16)
    grad_w_in = jnp.einsum("nd,nf->df", acts2, d_pre, preferred_element_type=jnp.float32)
    grad_bias_in = jnp.sum(d_pre.astype(jnp.float32), axis=0)
    d_norm2 = jnp.einsum("nf,df->nd", d_pre, w_in, preferred_element_type=jnp.float32)
    d_middle_norm, grad_norm2_gain, grad_norm2_bias = norm2_pull(d_norm2)
    d_middle = grad_out + d_middle_norm
    ffn_shares = (
        lax.psum_scatter(
            grad_norm2_gain.astype(jnp.bfloat16), "wide", scatter_dimension=0, tiled=True
        ).astype(jnp.float32),
        lax.psum_scatter(
            grad_norm2_bias.astype(jnp.bfloat16), "wide", scatter_dimension=0, tiled=True
        ).astype(jnp.float32),
        lax.psum_scatter(
            grad_w_in.astype(jnp.bfloat16), "wide", scatter_dimension=0, tiled=True
        ).astype(jnp.float32),
        lax.psum_scatter(
            grad_bias_in.astype(jnp.bfloat16), "wide", scatter_dimension=0, tiled=True
        ).astype(jnp.float32),
        lax.psum_scatter(
            grad_w_back.astype(jnp.bfloat16), "wide", scatter_dimension=0, tiled=True
        ).astype(jnp.float32),
        lax.psum_scatter(
            grad_bias_back.astype(jnp.bfloat16), "wide", scatter_dimension=0, tiled=True
        ).astype(jnp.float32),
    )
    ffn_done = (
        lax.psum(ffn_shares[0].astype(jnp.bfloat16), "blk").astype(jnp.float32),
        lax.psum(ffn_shares[1].astype(jnp.bfloat16), "blk").astype(jnp.float32),
        lax.psum(ffn_shares[2].astype(jnp.bfloat16), "blk").astype(jnp.float32),
        lax.psum(ffn_shares[3].astype(jnp.bfloat16), "blk").astype(jnp.float32),
        lax.psum(ffn_shares[4].astype(jnp.bfloat16), "blk").astype(jnp.float32),
        lax.psum(ffn_shares[5].astype(jnp.bfloat16), "blk").astype(jnp.float32),
    )
    d_branch = d_middle.astype(jnp.bfloat16)
    grad_w_out = jnp.einsum("nd,ne->de", attended_low, d_branch, preferred_element_type=jnp.float32)
    grad_bias_out = jnp.sum(d_branch.astype(jnp.float32), axis=0)
    d_attended = (
        jnp.einsum("ne,de->nd", d_branch, w_out, preferred_element_type=jnp.float32)
        .astype(jnp.bfloat16)
        .reshape(row_count, seg_len, HEADS, HEAD_DIM)
    )
    log_totals = highest + jnp.log(totals)
    row_delta = jnp.sum(d_attended.astype(jnp.float32) * attended, axis=-1)
    group_size = lax.axis_size("blk")
    my_index = lax.axis_index("blk")

    def visit_block(turn_index, state):
        key_part, value_part, grad_keys, grad_values, grad_query = state
        source = (my_index - turn_index) % group_size
        allowed = allowed_for(source * seg_len, seg_len)

        def visit_update(sums):
            sum_keys, sum_values, sum_query = sums
            scores = scores_for(key_part, allowed)
            probs = jnp.where(allowed[:, :, None, :], jnp.exp(scores - log_totals[..., None]), 0.0)
            d_probs = jnp.einsum(
                "rqhd,rkhd->rqhk",
                d_attended,
                heads_of(value_part),
                preferred_element_type=jnp.float32,
            )
            d_scores = (probs * (d_probs - row_delta[..., None]) * 0.125).astype(jnp.bfloat16)
            sum_query = sum_query + jnp.einsum(
                "rqhk,rkhd->rqhd", d_scores, heads_of(key_part), preferred_element_type=jnp.float32
            )
            sum_keys = sum_keys + jnp.einsum(
                "rqhk,rqhd->rkhd", d_scores, query, preferred_element_type=jnp.float32
            )
            sum_values = sum_values + jnp.einsum(
                "rqhk,rqhd->rkhd",
                probs.astype(jnp.bfloat16),
                d_attended,
                preferred_element_type=jnp.float32,
            )
            return (sum_keys, sum_values, sum_query)

        grad_keys, grad_values, grad_query = lax.cond(
            jnp.any(allowed), visit_update, lambda sums: sums, (grad_keys, grad_values, grad_query)
        )
        key_part, value_part = from_behind((key_part, value_part), "blk", 1)
        grad_keys, grad_values = (
            from_behind(grad_keys.astype(jnp.bfloat16), "blk", 1).astype(grad_keys.dtype),
            from_behind(grad_values.astype(jnp.bfloat16), "blk", 1).astype(grad_values.dtype),
        )
        return (key_part, value_part, grad_keys, grad_values, grad_query)

    zero_heads = jnp.zeros((row_count, seg_len, HEADS, HEAD_DIM), jnp.float32)
    final = lax.fori_loop(
        0, group_size, visit_block, (keys, values, zero_heads, zero_heads, zero_heads)
    )
    d_keys = final[2].astype(jnp.bfloat16).reshape(token_count, model_width)
    d_values = final[3].astype(jnp.bfloat16).reshape(token_count, model_width)
    d_query = final[4].astype(jnp.bfloat16).reshape(token_count, model_width)
    d_qkv = jnp.concatenate([d_query, d_keys, d_values], axis=1)
    grad_w_qkv = jnp.einsum("nd,ne->de", acts1, d_qkv, preferred_element_type=jnp.float32)
    grad_bias_q = jnp.sum(d_query.astype(jnp.float32), axis=0)
    grad_bias_v = jnp.sum(d_values.astype(jnp.float32), axis=0)
    d_norm1 = jnp.einsum("ne,de->nd", d_qkv, w_qkv, preferred_element_type=jnp.float32)
    d_inputs_norm, grad_norm1_gain, grad_norm1_bias = norm1_pull(d_norm1)
    grad_tokens = (d_middle + d_inputs_norm).reshape(tokens.shape)
    attn_shares = (
        lax.psum_scatter(
            grad_norm1_gain.astype(jnp.bfloat16), "wide", scatter_dimension=0, tiled=True
        ).astype(jnp.float32),
        lax.psum_scatter(
            grad_norm1_bias.astype(jnp.bfloat16), "wide", scatter_dimension=0, tiled=True
        ).astype(jnp.float32),
        lax.psum_scatter(
            grad_w_qkv.astype(jnp.bfloat16), "wide", scatter_dimension=0, tiled=True
        ).astype(jnp.float32),
        lax.psum_scatter(
            grad_bias_q.astype(jnp.bfloat16), "wide", scatter_dimension=0, tiled=True
        ).astype(jnp.float32),
        lax.psum_scatter(
            grad_bias_v.astype(jnp.bfloat16), "wide", scatter_dimension=0, tiled=True
        ).astype(jnp.float32),
        lax.psum_scatter(
            grad_w_out.astype(jnp.bfloat16), "wide", scatter_dimension=0, tiled=True
        ).astype(jnp.float32),
        lax.psum_scatter(
            grad_bias_out.astype(jnp.bfloat16), "wide", scatter_dimension=0, tiled=True
        ).astype(jnp.float32),
    )
    attn_done = (
        lax.psum(attn_shares[0].astype(jnp.bfloat16), "blk").astype(jnp.float32),
        lax.psum(attn_shares[1].astype(jnp.bfloat16), "blk").astype(jnp.float32),
        lax.psum(attn_shares[2].astype(jnp.bfloat16), "blk").astype(jnp.float32),
        lax.psum(attn_shares[3].astype(jnp.bfloat16), "blk").astype(jnp.float32),
        lax.psum(attn_shares[4].astype(jnp.bfloat16), "blk").astype(jnp.float32),
        lax.psum(attn_shares[5].astype(jnp.bfloat16), "blk").astype(jnp.float32),
        lax.psum(attn_shares[6].astype(jnp.bfloat16), "blk").astype(jnp.float32),
    )
    return (
        mixed,
        grad_tokens,
        attn_done[0],
        attn_done[1],
        attn_done[2],
        attn_done[3],
        attn_done[4],
        attn_done[5],
        attn_done[6],
        ffn_done[0],
        ffn_done[1],
        ffn_done[2],
        ffn_done[3],
        ffn_done[4],
        ffn_done[5],
    )


def solution(mesh):
    placed = (
        P("wide", "blk", None),
        P("wide", "blk"),
        P(),
        P(),
        P(),
        P(),
        P(),
        P(),
        P(),
        P(),
        P(),
        P(),
        P(),
        P(),
        P(),
        P("wide", "blk", None),
    )
    return jax.shard_map(
        on_device,
        mesh=mesh,
        in_specs=placed,
        out_specs=(
            P("wide", "blk", None),
            P("wide", "blk", None),
            P("wide"),
            P("wide"),
            P("wide", None),
            P("wide"),
            P("wide"),
            P("wide", None),
            P("wide"),
            P("wide"),
            P("wide"),
            P("wide", None),
            P("wide"),
            P("wide", None),
            P("wide"),
        ),
        check_vma=False,
    )
```

profile of v0, /device:TPU:0, one launch (start us, length us, event | category | flops | bytes accessed | tf_op | source)
XLA Modules:
  0.0 1830.3 jit_solution(12447462378810096950)
XLA Ops:
  69.2 36.3 %all-gather.5.cloned.1.call-done = bf16[2048,1280]{1,0:T(8,128)(2,1)} async-done(((bf16[1024,1280]{1,0:T(8,128)(2,1)}), bf16[2048,1280]{1,0:T(8,128)(2,1)}) %all-gather.5.cloned.1.call-update) | async-done | bytes 5242896 | tf_op jit(solution)/shard_map/all_gather | solution.py:106
  105.5 124.0 %conditional.3 = (f32[1,1024,20]{1,2,0:T(8,128)}, f32[1,1024,20]{1,2,0:T(8,128)}, f32[1,1024,20]{1,2,0:T(8,128)S(1)}) conditional(s32[]{:T(128)} %convert_element_type.222, () %tuple.58, (pred[1,1024,2048]{1,2,0:T(8,128)(4,1)}, bf16[1,2048,1280]{2,1,0:T(8,128)(2,1)}, bf16[1,1024,20,64]{1,3,2,0:T(8,128)(2,1)}) %tuple.148), branch_computations={%region_3.0_spmd, %region_4.7_spmd} | conditional | flops 5704232960 | bytes 358744096 | solution.py:98
  113.6 59.4 %fusion = (f32[1024,20]{0,1:T(8,128)S(1)}, f32[20,2048,1024]{2,1,0:T(8,128)}) fusion(pred[1024,2048]{0,1:T(8,128)(4,1)} %bitcast.262, bf16[2048,20,64]{0,2,1:T(8,128)(2,1)} %bitcast.268, bf16[1,1024,20,64]{1,3,2,0:T(8,128)(2,1)} %get-tuple-element.348), kind=kOutput, calls=%fused_computation.2 | convolution fusion | flops 5494517760 | bytes 177815552 | tf_op jit(solution)/shard_map/cond/branch_1_fun/rqhd,rkhd->rqhk/dot_general | solution.py:78
  173.6 54.9 %select_reduce_fusion = f32[1024,20]{0,1:T(8,128)} fusion(f32[20,2048,1024]{2,1,0:T(8,128)} %get-tuple-element.592, f32[1024,20]{0,1:T(8,128)S(1)} %get-tuple-element.589, pred[1024,2048]{0,1:T(8,128)(4,1)} %bitcast.263), kind=kLoop, calls=%fused_computation.1 | loop fusion | flops 209694720 | bytes 170033152 | tf_op jit(solution)/shard_map/cond/branch_1_fun/reduce_sum | solution.py:95
  230.1 80.9 %conditional.4 = (f32[1,1024,20,64]{1,3,2,0:T(8,128)}, bf16[1024,1280]{0,1:T(8,128)(2,1)}) conditional(s32[]{:T(128)} %convert_element_type.222, () %tuple.57, (pred[1,1024,2048]{1,2,0:T(8,128)(4,1)}, bf16[1,2048,1280]{2,1,0:T(8,128)(2,1)}, bf16[1,1024,20,64]{1,3,2,0:T(8,128)(2,1)}, f32[1,1024,20]{1,2,0:T(8,128)}, f32[1,1024,20]{1,2,0:T(8,128)}, ...), branch_computations={%region_7.8_spmd, %region_8.9_spmd} | conditional | flops 10990387200 | bytes 44204048 | solution.py:119
  246.3 64.8 %fusion.99 = (bf16[1,1024,20,64]{1,3,2,0:T(8,128)(2,1)}, f32[1,1024,20,64]{1,3,2,0:T(8,128)}) fusion(bf16[2048,20,64]{0,2,1:T(8,128)(2,1)} %bitcast.266, f32[1024,20]{0,1:T(8,128)} %bitcast.13, f32[1024,20]{0,1:T(8,128)} %bitcast.12, pred[1024,2048]{0,1:T(8,128)(4,1)} %bitcast.264, bf16[2048,20,64]{0,2,1:T(8,128)(2,1)} %bitcast.267, ...), kind=kOutput, calls=%fused_computation.133 | convolution fusion | flops 10990387200 | bytes 23232512 | tf_op jit(solution)/shard_map/cond/branch_1_fun/rqhk,rkhd->rqhd/dot_general | solution.py:112
  320.5 75.9 %multiply_convert_fusion = (bf16[1024,5120]{1,0:T(8,128)(2,1)}, f32[1024,5120]{1,0:T(8,128)}, f32[1024,5120]{1,0:T(8,128)}) fusion(f32[5120]{0:T(1024)S(1)} %copy-done.45, bf16[1280,5120]{1,0:T(8,128)(2,1)} %param.35, f32[1024,1280]{1,0:T(8,128)} %copy-done.10, f32[1280]{0:T(1024)S(1)} %copy-done.49, f32[1280]{0:T(1024)S(1)} %copy-done.41, ...), kind=kOutput, calls=%fused_computation.54 | convolution fusion | flops 13774356480 | bytes 70817792 | tf_op jit(solution)/shard_map/dot_general | solution.py:124
  396.5 31.3 %fusion.103 = (bf16[5120]{0:T(1024)(128)(2,1)}, bf16[1024,5120]{1,0:T(8,128)(2,1)}) fusion(f32[1024,5120]{1,0:T(8,128)} %get-tuple-element.588, bf16[5120,1280]{1,0:T(8,128)(2,1)} %param.37, bf16[1,1024,1280]{2,1,0:T(8,128)(2,1)S(1)} %copy-done.8, f32[1024,5120]{1,0:T(8,128)} %get-tuple-element.605, f32[5120]{0:T(1024)S(1)} %copy-done.45), kind=kOutput, calls=%fused_computation.135 | convolution fusion | flops 13505653760 | bytes 68188160 | tf_op jit(solution)/shard_map/nd,fd->nf/dot_general | solution.py:133
  427.7 23.3 %multiply_reduce_fusion = (bf16[1280]{0:T(1024)(128)(2,1)}, f32[1024]{0:T(1024)S(1)}, bf16[1280]{0:T(1024)(128)(2,1)}, f32[1024,1280]{1,0:T(8,128)}) fusion(f32[1024,1280]{1,0:T(8,128)} %copy-done.10, f32[1024]{0:T(1024)S(1)} %fusion.83, f32[1024]{0:T(1024)S(1)} %broadcast_multiply_fusion, f32[1280]{0:T(1024)S(1)} %copy-done.41, ...), kind=kOutput, calls=%fused_computation.96 | convolution fusion | flops 13432255488 | bytes 34101248 | tf_op jit(solution)/shard_map/nf,df->nd/dot_general | solution.py:137
  482.5 823.4 %while.24 = (s32[]{:T(128)}, bf16[1,1024,1280]{1,2,0:T(8,128)(2,1)}, bf16[1,1024,1280]{1,2,0:T(8,128)(2,1)}, f32[1,1024,20,64]{1,3,2,0:T(8,128)}, f32[1,1024,20,...) while((s32[]{:T(128)}, ...), condition=%wide.region_18.19_spmd.clone, body=%wide.region_14.18_spmd.clone.sunk | while | flops 13708296192 | bytes 560743040 | solution.py:222
  498.4 162.4 %conditional.7 = ((f32[1,1024,20,64]{1,3,2,0:T(8,128)}, f32[1,1024,20,64]{1,3,2,0:T(8,128)}, f32[1,1024,20,64]{1,3,2,0:T(8,128)})) conditional(s32[]{:T(128)} %convert_element_type.354, (f32[1,1024,20,64]{1,3,2,0:T(8,128)}, f32[1,1024,20,64]{1,3,2,0:T(8,128)}, f32[1,1024,20,64]{1,3,2,0:T(8,128)}) %tuple.117, (pred[1,1024,1024]{1,2,0:T(8,128)(4,1)}, ...), branch_computations={%region_16.16_spmd, %region_17.17_spmd} | conditional | flops 13698334720 | bytes 433832000 | solution.py:211
  498.4 31.5 %fusion.44 = f32[20,1024,1024]{2,1,0:T(8,128)} fusion(bf16[1024,20,64]{0,2,1:T(8,128)(2,1)S(1)} %bitcast.252, bf16[1,1024,20,64]{1,3,2,0:T(8,128)(2,1)} %get-tuple-element.358), kind=kOutput, calls=%fused_computation.41 | convolution fusion | flops 2684354560 | bytes 89128960 | tf_op jit(solution)/shard_map/while/body/eval_jaxpr/cond/branch_1_fun/rqhd,rkhd->rqhk/dot_general | solution.py:78
  529.9 51.0 %fusion.32 = bf16[1024,20,1024]{0,2,1:T(8,128)(2,1)} fusion(f32[20,1024,1024]{2,1,0:T(8,128)} %fusion.44, f32[1024,20]{0,1:T(8,128)S(1)} %bitcast.280, f32[1024,20]{0,1:T(8,128)S(1)} %bitcast.281, pred[1024,1024]{0,1:T(8,128)(4,1)S(1)} %bitcast.258, bf16[1024,20,64]{0,2,1:T(8,128)(2,1)} %bitcast.28, bf16[1,1024,20,64]{1,3,2,0:T(8,128)(2,1)} %get-tuple-element.361), kind=kOutput, calls=%fused_computation.31 | convolution fusion | flops 2852126720 | bytes 132284416 | tf_op jit(solution)/shard_map/while/body/eval_jaxpr/cond/branch_1_fun/rqhd,rkhd->rqhk/dot_general | solution.py:190
  623.8 37.1 %bitcast_add_fusion.1 = f32[1,1024,20,64]{1,3,2,0:T(8,128)} fusion(f32[1,1024,20,64]{1,3,2,0:T(8,128)} %get-tuple-element.363, bf16[1,1024,20,64]{1,3,2,0:T(8,128)(2,1)} %get-tuple-element.361, f32[20,1024,1024]{2,1,0:T(8,128)} %fusion.44, f32[1024,20]{0,1:T(8,128)S(1)} %bitcast.282, pred[1024,1024]{0,1:T(8,128)(4,1)} %bitcast.257), kind=kOutput, calls=%fused_computation.35 | convolution fusion | flops 2790522880 | bytes 98123776 | tf_op jit(solution)/shard_map/while/body/eval_jaxpr/cond/branch_1_fun/rqhk,rqhd->rkhd/dot_general | solution.py:203
  671.3 54.0 %collective-permute-done.2 = bf16[1,1024,20,64]{1,3,2,0:T(8,128)(2,1)} collective-permute-done((bf16[1,1024,20,64]{1,3,2,0:T(8,128)(2,1)}, bf16[1,1024,20,64]{1,3,2,0:T(8,128)(2,1)}, u32[]{:S(2)}, u32[]{:S(2)}) %collective-permute-start.2) | collective-permute-done | bytes 2621472 | tf_op jit(solution)/shard_map/while/body/eval_jaxpr/ppermute | solution.py:15
  730.1 51.4 %collective-permute-done.3 = bf16[1,1024,20,64]{1,3,2,0:T(8,128)(2,1)} collective-permute-done((bf16[1,1024,20,64]{1,3,2,0:T(8,128)(2,1)}, bf16[1,1024,20,64]{1,3,2,0:T(8,128)(2,1)}, u32[]{:S(2)}, u32[]{:S(2)}) %collective-permute-start.3) | collective-permute-done | bytes 2621472 | tf_op jit(solution)/shard_map/while/body/eval_jaxpr/ppermute | solution.py:15
  786.3 51.4 %collective-permute-done = bf16[1,1024,1280]{1,2,0:T(8,128)(2,1)} collective-permute-done((bf16[1,1024,1280]{1,2,0:T(8,128)(2,1)S(1)}, bf16[1,1024,1280]{1,2,0:T(8,128)(2,1)}, u32[]{:S(2)}, u32[]{:S(2)}) %collective-permute-start) | collective-permute-done | bytes 2621472 | tf_op jit(solution)/shard_map/while/body/eval_jaxpr/ppermute | solution.py:15
  837.7 55.3 %collective-permute-done.1 = bf16[1,1024,1280]{1,2,0:T(8,128)(2,1)} collective-permute-done((bf16[1,1024,1280]{1,2,0:T(8,128)(2,1)}, bf16[1,1024,1280]{1,2,0:T(8,128)(2,1)}, u32[]{:S(2)}, u32[]{:S(2)}) %collective-permute-start.1) | collective-permute-done | bytes 2621472 | tf_op jit(solution)/shard_map/while/body/eval_jaxpr/ppermute | solution.py:15
  912.6 161.6 %conditional.7 = ((f32[1,1024,20,64]{1,3,2,0:T(8,128)}, f32[1,1024,20,64]{1,3,2,0:T(8,128)}, f32[1,1024,20,64]{1,3,2,0:T(8,128)})) conditional(s32[]{:T(128)} %convert_element_type.354, (f32[1,1024,20,64]{1,3,2,0:T(8,128)}, f32[1,1024,20,64]{1,3,2,0:T(8,128)}, f32[1,1024,20,64]{1,3,2,0:T(8,128)}) %tuple.117, (pred[1,1024,1024]{1,2,0:T(8,128)(4,1)}, ...), branch_computations={%region_16.16_spmd, %region_17.17_spmd} | conditional | flops 13698334720 | bytes 433832000 | solution.py:211
  912.6 30.7 %fusion.44 = f32[20,1024,1024]{2,1,0:T(8,128)} fusion(bf16[1024,20,64]{0,2,1:T(8,128)(2,1)S(1)} %bitcast.252, bf16[1,1024,20,64]{1,3,2,0:T(8,128)(2,1)} %get-tuple-element.358), kind=kOutput, calls=%fused_computation.41 | convolution fusion | flops 2684354560 | bytes 89128960 | tf_op jit(solution)/shard_map/while/body/eval_jaxpr/cond/branch_1_fun/rqhd,rkhd->rqhk/dot_general | solution.py:78
  943.3 51.0 %fusion.32 = bf16[1024,20,1024]{0,2,1:T(8,128)(2,1)} fusion(f32[20,1024,1024]{2,1,0:T(8,128)} %fusion.44, f32[1024,20]{0,1:T(8,128)S(1)} %bitcast.280, f32[1024,20]{0,1:T(8,128)S(1)} %bitcast.281, pred[1024,1024]{0,1:T(8,128)(4,1)S(1)} %bitcast.258, bf16[1024,20,64]{0,2,1:T(8,128)(2,1)} %bitcast.28, bf16[1,1024,20,64]{1,3,2,0:T(8,128)(2,1)} %get-tuple-element.361), kind=kOutput, calls=%fused_computation.31 | convolution fusion | flops 2852126720 | bytes 132284416 | tf_op jit(solution)/shard_map/while/body/eval_jaxpr/cond/branch_1_fun/rqhd,rkhd->rqhk/dot_general | solution.py:190
  1037.1 37.1 %bitcast_add_fusion.1 = f32[1,1024,20,64]{1,3,2,0:T(8,128)} fusion(f32[1,1024,20,64]{1,3,2,0:T(8,128)} %get-tuple-element.363, bf16[1,1024,20,64]{1,3,2,0:T(8,128)(2,1)} %get-tuple-element.361, f32[20,1024,1024]{2,1,0:T(8,128)} %fusion.44, f32[1024,20]{0,1:T(8,128)S(1)} %bitcast.282, pred[1024,1024]{0,1:T(8,128)(4,1)} %bitcast.257), kind=kOutput, calls=%fused_computation.35 | convolution fusion | flops 2790522880 | bytes 98123776 | tf_op jit(solution)/shard_map/while/body/eval_jaxpr/cond/branch_1_fun/rqhk,rqhd->rkhd/dot_general | solution.py:203
  1084.7 54.1 %collective-permute-done.2 = bf16[1,1024,20,64]{1,3,2,0:T(8,128)(2,1)} collective-permute-done((bf16[1,1024,20,64]{1,3,2,0:T(8,128)(2,1)}, bf16[1,1024,20,64]{1,3,2,0:T(8,128)(2,1)}, u32[]{:S(2)}, u32[]{:S(2)}) %collective-permute-start.2) | collective-permute-done | bytes 2621472 | tf_op jit(solution)/shard_map/while/body/eval_jaxpr/ppermute | solution.py:15
  1143.6 51.4 %collective-permute-done.3 = bf16[1,1024,20,64]{1,3,2,0:T(8,128)(2,1)} collective-permute-done((bf16[1,1024,20,64]{1,3,2,0:T(8,128)(2,1)}, bf16[1,1024,20,64]{1,3,2,0:T(8,128)(2,1)}, u32[]{:S(2)}, u32[]{:S(2)}) %collective-permute-start.3) | collective-permute-done | bytes 2621472 | tf_op jit(solution)/shard_map/while/body/eval_jaxpr/ppermute | solution.py:15
  1199.7 51.4 %collective-permute-done = bf16[1,1024,1280]{1,2,0:T(8,128)(2,1)} collective-permute-done((bf16[1,1024,1280]{1,2,0:T(8,128)(2,1)S(1)}, bf16[1,1024,1280]{1,2,0:T(8,128)(2,1)}, u32[]{:S(2)}, u32[]{:S(2)}) %collective-permute-start) | collective-permute-done | bytes 2621472 | tf_op jit(solution)/shard_map/while/body/eval_jaxpr/ppermute | solution.py:15
  1251.2 54.4 %collective-permute-done.1 = bf16[1,1024,1280]{1,2,0:T(8,128)(2,1)} collective-permute-done((bf16[1,1024,1280]{1,2,0:T(8,128)(2,1)}, bf16[1,1024,1280]{1,2,0:T(8,128)(2,1)}, u32[]{:S(2)}, u32[]{:S(2)}) %collective-permute-start.1) | collective-permute-done | bytes 2621472 | tf_op jit(solution)/shard_map/while/body/eval_jaxpr/ppermute | solution.py:15
  1334.8 21.9 %convolution_convert_fusion = bf16[1280,5120]{1,0:T(8,128)(2,1)} fusion(bf16[1024,5120]{1,0:T(8,128)(2,1)} %get-tuple-element.609, f32[1024,1280]{1,0:T(8,128)} %copy-done.10, f32[1280]{0:T(1024)S(1)} %copy-done.50, f32[1280]{0:T(1024)S(1)} %copy-done.42, f32[1024]{0:T(1024)S(1)} %copy-done.37, f32[1024]{0:T(1024)S(1)} %copy-done.32), kind=kOutput, calls=%fused_computation.68 | convolution fusion | flops 13434880000 | bytes 28854272 | tf_op jit(solution)/shard_map/nd,nf->df/dot_general | solution.py:135
  1399.9 21.8 %fusion.75 = bf16[1,1024,1280]{2,1,0:T(8,128)(2,1)} fusion(f32[1024,1280]{1,0:T(8,128)} %copy-done.10, bf16[1024,5120]{1,0:T(8,128)(2,1)} %get-tuple-element.587, bf16[5120,1280]{1,0:T(8,128)(2,1)} %param.37, f32[1280]{0:T(1024)S(1)} %copy-done.51), kind=kOutput, calls=%fused_computation.107 | convolution fusion | flops 13425704960 | bytes 31462400 | tf_op jit(solution)/shard_map/dot_general | solution.py:127
  1421.7 27.1 %reduce-scatter.5.cloned.1.call-done = bf16[80,3840]{1,0:T(8,128)(2,1)} async-done(((bf16[1280,3840]{1,0:T(8,128)(2,1)}), bf16[80,3840]{1,0:T(8,128)(2,1)}) %reduce-scatter.5.cloned.1.call-update) | async-done | bytes 614416 | tf_op jit(solution)/shard_map/reduce_scatter | solution.py:242
  1448.8 142.6 %reduce-scatter.9.cloned.1.call-done = bf16[80,5120]{1,0:T(8,128)(2,1)} async-done(((bf16[1280,5120]{1,0:T(8,128)(2,1)}), bf16[80,5120]{1,0:T(8,128)(2,1)}) %reduce-scatter.9.cloned.1.call-update) | async-done | bytes 819216 | tf_op jit(solution)/shard_map/reduce_scatter | solution.py:147
  1591.4 141.5 %reduce-scatter.11.cloned.1.call-done = bf16[320,1280]{1,0:T(8,128)(2,1)} async-done(((bf16[5120,1280]{1,0:T(8,128)(2,1)}), bf16[320,1280]{1,0:T(8,128)(2,1)}) %reduce-scatter.11.cloned.1.call-update) | async-done | bytes 819216 | tf_op jit(solution)/shard_map/reduce_scatter | solution.py:153
  1737.3 59.8 %all-reduce.9 = (bf16[1280]{0:T(1024)(128)(2,1)S(1)}, bf16[1280]{0:T(1024)(128)(2,1)S(1)}, bf16[1280]{0:T(1024)(128)(2,1)S(1)}, bf16[1280]{0:T(1024)(128)(2,1)S(...) all-reduce(bf16[1280]{0:T(1024)(128)(2,1)S(1)} %get-tuple-element.5, ...), channel_id=4, replica_groups=mesh['wide'=16,'blk'=2] {'wide'}, use_global_device_ids=true, to_apply=%region_22.23.clone | all-reduce | flops 15360 | bytes 61440
  (229 shorter events, 388.6 us)
Async XLA Ops:
  7.2 303.9 %copy-start = (bf16[1280,1280]{1,0:T(8,128)(2,1)S(1)}, bf16[1280,1280]{1,0:T(8,128)(2,1)}, u32[]{:S(2)}) copy-start(bf16[1280,1280]{1,0:T(8,128)(2,1)} %param.31) | copy-start | bytes 9830404
  7.2 98.3 %all-gather.5.cloned.1.call-start = ((), (), s32[]{:S(2)}) async-start(), calls=%async_computation.8 | async-start | bytes 7864320 | tf_op jit(solution)/shard_map/all_gather | solution.py:106
  34.0 195.5 %all-gather.7.cloned.1.call-start = ((), (), s32[]{:S(2)}) async-start(), calls=%async_computation.9 | async-start | bytes 7864320 | tf_op jit(solution)/shard_map/all_gather | solution.py:107
  41.4 1380.4 %reduce-scatter.7.cloned.1.call-start = ((), (), s32[]{:S(2)}) async-start(), calls=%async_computation.5 | async-start | bytes 3481600 | tf_op jit(solution)/shard_map/reduce_scatter | solution.py:251
  229.5 81.6 %copy-start.46 = (f32[1280]{0:T(1024)S(1)}, f32[1280]{0:T(1024)}, u32[]{:S(2)}) copy-start(f32[1280]{0:T(1024)} %param.32) | copy-start | bytes 15364
  317.6 133.5 %copy-start.31 = (f32[1024]{0:T(1024)}, f32[1024]{0:T(1024)S(1)}, u32[]{:S(2)}) copy-start(f32[1024]{0:T(1024)S(1)} %broadcast_multiply_fusion) | copy-start | bytes 12292
  320.5 130.6 %copy-start.36 = (f32[1024]{0:T(1024)}, f32[1024]{0:T(1024)S(1)}, u32[]{:S(2)}) copy-start(f32[1024]{0:T(1024)S(1)} %fusion.83) | copy-start | bytes 12292
  320.5 76.0 %copy-start.8 = (bf16[1,1024,1280]{2,1,0:T(8,128)(2,1)S(1)}, bf16[1,1024,1280]{2,1,0:T(8,128)(2,1)}, u32[]{:S(2)}) copy-start(bf16[1,1024,1280]{2,1,0:T(8,128)(2,1)} %param.39) | copy-start | bytes 7864324
  427.7 23.3 %copy-start.30 = (f32[1024]{0:T(1024)S(1)}, f32[1024]{0:T(1024)}, u32[]{:S(2)}) copy-start(f32[1024]{0:T(1024)} %copy-done.29) | copy-start | bytes 12292
  475.0 973.8 %reduce-scatter.5.cloned.1.call-start = ((), (), s32[]{:S(2)}) async-start(), calls=%async_computation.4 | async-start | bytes 10444800 | tf_op jit(solution)/shard_map/reduce_scatter | solution.py:242
  498.4 31.5 %copy-start.7 = (pred[1,1024,1024]{1,2,0:T(8,128)(4,1)S(1)}, pred[1,1024,1024]{1,2,0:T(8,128)(4,1)}, u32[]{:S(2)}) copy-start(pred[1,1024,1024]{1,2,0:T(8,128)(4,1)} %get-tuple-element.356) | copy-start | bytes 3145732 | tf_op jit(solution)/shard_map/while/body/eval_jaxpr/cond
  665.3 60.0 %collective-permute-start.2 = (bf16[1,1024,20,64]{1,3,2,0:T(8,128)(2,1)}, bf16[1,1024,20,64]{1,3,2,0:T(8,128)(2,1)}, u32[]{:S(2)}, u32[]{:S(2)}) collective-permute-start(bf16[1,1024,20,64]{1,3,2,0:T(8,128)(2,1)} %convert_element_type.355), channel_id=1, source_target_pairs={{0,1},{1,0},{2,3},{3,2},{4,5},{5,4},{6,7},{7,6},{8,9},{9,8},{10,11... | collective-permute-start | bytes 7864328 | tf_op jit(solution)/shard_map/while/body/eval_jaxpr/ppermute | solution.py:15
  668.2 113.3 %collective-permute-start.3 = (bf16[1,1024,20,64]{1,3,2,0:T(8,128)(2,1)}, bf16[1,1024,20,64]{1,3,2,0:T(8,128)(2,1)}, u32[]{:S(2)}, u32[]{:S(2)}) collective-permute-start(bf16[1,1024,20,64]{1,3,2,0:T(8,128)(2,1)} %convert_element_type.357), channel_id=1, source_target_pairs={{0,1},{1,0},{2,3},{3,2},{4,5},{5,4},{6,7},{7,6},{8,9},{9,8},{10,11... | collective-permute-start | bytes 7864328 | tf_op jit(solution)/shard_map/while/body/eval_jaxpr/ppermute | solution.py:15
  669.3 168.4 %collective-permute-start = (bf16[1,1024,1280]{1,2,0:T(8,128)(2,1)S(1)}, bf16[1,1024,1280]{1,2,0:T(8,128)(2,1)}, u32[]{:S(2)}, u32[]{:S(2)}) collective-permute-start(bf16[1,1024,1280]{1,2,0:T(8,128)(2,1)S(1)} %copy.98), channel_id=1, source_target_pairs={{0,1},{1,0},{2,3},{3,2},{4,5},{5,4},{6,7},{7,6},{8,9},{9,8},{10,11... | collective-permute-start | bytes 7864328 | tf_op jit(solution)/shard_map/while/body/eval_jaxpr/ppermute | solution.py:15
  670.2 222.8 %collective-permute-start.1 = (bf16[1,1024,1280]{1,2,0:T(8,128)(2,1)}, bf16[1,1024,1280]{1,2,0:T(8,128)(2,1)}, u32[]{:S(2)}, u32[]{:S(2)}) collective-permute-start(bf16[1,1024,1280]{1,2,0:T(8,128)(2,1)} %copy.99), channel_id=1, source_target_pairs={{0,1},{1,0},{2,3},{3,2},{4,5},{5,4},{6,7},{7,6},{8,9},{9,8},{10,11... | collective-permute-start | bytes 7864328 | tf_op jit(solution)/shard_map/while/body/eval_jaxpr/ppermute | solution.py:15
  730.1 162.9 %copy-start.19 = (s32[1,1024]{1,0:T(1,128)S(1)}, s32[1,1024]{1,0:T(1,128)}, u32[]{:S(2)}) copy-start(s32[1,1024]{1,0:T(1,128)} %get-tuple-element.840) | copy-start | bytes 12292 | tf_op jit(solution)/shard_map/while
  912.6 30.7 %copy-start.7 = (pred[1,1024,1024]{1,2,0:T(8,128)(4,1)S(1)}, pred[1,1024,1024]{1,2,0:T(8,128)(4,1)}, u32[]{:S(2)}) copy-start(pred[1,1024,1024]{1,2,0:T(8,128)(4,1)} %get-tuple-element.356) | copy-start | bytes 3145732 | tf_op jit(solution)/shard_map/while/body/eval_jaxpr/cond
  1078.7 60.1 %collective-permute-start.2 = (bf16[1,1024,20,64]{1,3,2,0:T(8,128)(2,1)}, bf16[1,1024,20,64]{1,3,2,0:T(8,128)(2,1)}, u32[]{:S(2)}, u32[]{:S(2)}) collective-permute-start(bf16[1,1024,20,64]{1,3,2,0:T(8,128)(2,1)} %convert_element_type.355), channel_id=1, source_target_pairs={{0,1},{1,0},{2,3},{3,2},{4,5},{5,4},{6,7},{7,6},{8,9},{9,8},{10,11... | collective-permute-start | bytes 7864328 | tf_op jit(solution)/shard_map/while/body/eval_jaxpr/ppermute | solution.py:15
  1081.5 113.5 %collective-permute-start.3 = (bf16[1,1024,20,64]{1,3,2,0:T(8,128)(2,1)}, bf16[1,1024,20,64]{1,3,2,0:T(8,128)(2,1)}, u32[]{:S(2)}, u32[]{:S(2)}) collective-permute-start(bf16[1,1024,20,64]{1,3,2,0:T(8,128)(2,1)} %convert_element_type.357), channel_id=1, source_target_pairs={{0,1},{1,0},{2,3},{3,2},{4,5},{5,4},{6,7},{7,6},{8,9},{9,8},{10,11... | collective-permute-start | bytes 7864328 | tf_op jit(solution)/shard_map/while/body/eval_jaxpr/ppermute | solution.py:15
  1082.7 168.5 %collective-permute-start = (bf16[1,1024,1280]{1,2,0:T(8,128)(2,1)S(1)}, bf16[1,1024,1280]{1,2,0:T(8,128)(2,1)}, u32[]{:S(2)}, u32[]{:S(2)}) collective-permute-start(bf16[1,1024,1280]{1,2,0:T(8,128)(2,1)S(1)} %copy.98), channel_id=1, source_target_pairs={{0,1},{1,0},{2,3},{3,2},{4,5},{5,4},{6,7},{7,6},{8,9},{9,8},{10,11... | collective-permute-start | bytes 7864328 | tf_op jit(solution)/shard_map/while/body/eval_jaxpr/ppermute | solution.py:15
  1083.5 222.0 %collective-permute-start.1 = (bf16[1,1024,1280]{1,2,0:T(8,128)(2,1)}, bf16[1,1024,1280]{1,2,0:T(8,128)(2,1)}, u32[]{:S(2)}, u32[]{:S(2)}) collective-permute-start(bf16[1,1024,1280]{1,2,0:T(8,128)(2,1)} %copy.99), channel_id=1, source_target_pairs={{0,1},{1,0},{2,3},{3,2},{4,5},{5,4},{6,7},{7,6},{8,9},{9,8},{10,11... | collective-permute-start | bytes 7864328 | tf_op jit(solution)/shard_map/while/body/eval_jaxpr/ppermute | solution.py:15
  1143.6 161.9 %copy-start.19 = (s32[1,1024]{1,0:T(1,128)S(1)}, s32[1,1024]{1,0:T(1,128)}, u32[]{:S(2)}) copy-start(s32[1,1024]{1,0:T(1,128)} %get-tuple-element.840) | copy-start | bytes 12292 | tf_op jit(solution)/shard_map/while
  1334.1 257.3 %reduce-scatter.9.cloned.1.call-start = ((), (), s32[]{:S(2)}) async-start(), calls=%async_computation.6 | async-start | bytes 13926400 | tf_op jit(solution)/shard_map/reduce_scatter | solution.py:147
  1356.7 376.2 %reduce-scatter.11.cloned.1.call-start = ((), (), s32[]{:S(2)}) async-start(), calls=%async_computation.7 | async-start | bytes 13926400 | tf_op jit(solution)/shard_map/reduce_scatter | solution.py:153
  1377.2 438.9 %all-reduce.14.cloned.1.call-start = ((), (), s32[]{:S(2)}) async-start(), calls=%async_computation.10 | async-start | bytes 4915200 | tf_op jit(solution)/shard_map/psum | solution.py:261
  1381.6 18.4 %copy-start.51 = (f32[1280]{0:T(1024)S(1)}, f32[1280]{0:T(1024)}, u32[]{:S(2)}) copy-start(f32[1280]{0:T(1024)} %param.38) | copy-start | bytes 15364
  1399.9 333.0 %copy-start.28 = (f32[1024]{0:T(1024)S(1)}, f32[1024]{0:T(1024)}, u32[]{:S(2)}) copy-start(f32[1024]{0:T(1024)} %copy-done.27) | copy-start | bytes 12292
  1421.7 315.6 %copy-start.35 = (bf16[1280]{0:T(1024)(128)(2,1)S(1)}, bf16[1280]{0:T(1024)(128)(2,1)}, u32[]{:S(2)}) copy-start(bf16[1280]{0:T(1024)(128)(2,1)} %get-tuple-element.579) | copy-start | bytes 7684
  1421.7 315.6 %copy-start.38 = (bf16[5120]{0:T(1024)(128)(2,1)S(1)}, bf16[5120]{0:T(1024)(128)(2,1)}, u32[]{:S(2)}) copy-start(bf16[5120]{0:T(1024)(128)(2,1)} %get-tuple-element.608) | copy-start | bytes 30724
  1421.7 315.6 %copy-start.43 = (bf16[1280]{0:T(1024)(128)(2,1)S(1)}, bf16[1280]{0:T(1024)(128)(2,1)}, u32[]{:S(2)}) copy-start(bf16[1280]{0:T(1024)(128)(2,1)} %get-tuple-element.524) | copy-start | bytes 7684
  1421.7 315.6 %copy-start.44 = (bf16[1280]{0:T(1024)(128)(2,1)S(1)}, bf16[1280]{0:T(1024)(128)(2,1)}, u32[]{:S(2)}) copy-start(bf16[1280]{0:T(1024)(128)(2,1)} %get-tuple-element.528) | copy-start | bytes 7684
  1732.9 74.7 %copy-start.26 = (f32[1024]{0:T(1024)S(1)}, f32[1024]{0:T(1024)}, u32[]{:S(2)}) copy-start(f32[1024]{0:T(1024)} %copy-done.25) | copy-start | bytes 12292
  (39 other events, 181.3 us)
Sparse Core Ops, SparseCore 0:
  34.1 71.3 all-gather.4
  107.0 68.5 all-gather.6
  475.2 67.0 reduce-scatter.6
  1334.2 114.5 reduce-scatter.4
  1453.3 138.0 reduce-scatter.8
  1595.4 137.4 reduce-scatter.10
  1735.6 70.5 all-reduce.13
where the time goes:
time: 1840 us; the launch traced here: 1830 us
  waiting for transfers between devices  771 us (42%)
  matrix products  712 us (39%)
  other arithmetic  175 us (10%)
  local copies, waits for them, and re-layouts  73.4 us (4%)
  blocking collectives  70.3 us (4%)
    ppermute x8, waiting for transfers between devices, from_behind(): lax.ppermute(array, axis, [(i, (i + by) % count) for i in range(count)])  423 us
    reduce_scatter x1, waiting for transfers between devices, on_device(): lax.psum_scatter(grad_w_in.astype(jnp.bfloat16), 'wide', scatter_dimensio...  143 us
    reduce_scatter x1, waiting for transfers between devices, on_device(): lax.psum_scatter(grad_w_back.astype(jnp.bfloat16), 'wide', scatter_dimens...  141 us
    dot_general x3, matrix products, scores_for(): jnp.einsum('rqhd,rkhd->rqhk', query, heads_of(key_part), preferred_elemen...  122 us
    dot_general x2, matrix products, visit_update(): jnp.einsum('rqhd,rkhd->rqhk', d_attended, heads_of(value_part), preferred...  102 us
    dot_general x1, matrix products, on_device(): pre = jnp.dot(acts2, w_in, preferred_element_type=jnp.float32) + bias_in  75.9 us
    dot_general x2, matrix products, visit_update(): jnp.einsum('rqhk,rqhd->rkhd', probs.astype(jnp.bfloat16), d_attended, pre...  74.1 us
    dot_general x1, matrix products, both_update(): jnp.einsum('rqhk,rkhd->rqhd', weigh(scores, both_allowed), heads_of(value...  64.8 us
  transfers between devices with their start and end apart: 15, of which 12 were waited for; matrix products, arithmetic and copies ran while one was open for 37% of the time, Pallas kernels for 0%

commit v1 on v0

v1 whole, which is shorter than its diff:
```python
import functools
import math

import jax
import jax.numpy as jnp
from jax import lax
from jax.experimental import pallas as pl
from jax.experimental.pallas import tpu as pltpu
from jax.sharding import PartitionSpec as P

HEADS = 20
HEAD_DIM = 64
HD = HEAD_DIM
EPS = 1e-05
NEG = -1e30
LOG2E = math.log2(math.e)
C2 = LOG2E / math.sqrt(HEAD_DIM)
F32 = jnp.float32
BF = jnp.bfloat16
NN = (((1,), (0,)), ((), ()))
NT = (((1,), (1,)), ((), ()))
TN = (((0,), (0,)), ((), ()))
VMEM_LIMIT = 56 * 2**20


def dot(a, b, dims):
    return lax.dot_general(a, b, dims, preferred_element_type=F32)


def head_sumsq(x,hp16):
    W=x.shape[1]
    sq=x.astype(F32)*x.astype(F32)
    row=lax.broadcasted_iota(jnp.int32,(hp16,W),0); col=lax.broadcasted_iota(jnp.int32,(hp16,W),1)
    ones=jnp.where(row==col//HD,1.0,0.0).astype(BF)
    return lax.dot_general(ones,sq.astype(BF),NT,preferred_element_type=F32)

def fwd_kernel(flags,cq,ck,q,k,v,*rest,first,tq,tk,heads):
    if first:
        accT_o,m_o,l_o,qm,vT,bias,acc,m,l,kn=rest
    else:
        accT_i,m_i,l_i,o_o,lse_o,qm,vT,bias,acc,m,l,kn=rest
    r=pl.program_id(0); qi=pl.program_id(1)
    nk=k.shape[1]//tk
    hp16=m.shape[0]
    @pl.when(qi==0)
    def _():
        vT[...]=v[0].T
        kn[...]=jnp.broadcast_to(jnp.sqrt(jnp.max(head_sumsq(k[0],hp16),1,keepdims=True)),kn.shape)
    lane=lax.broadcasted_iota(jnp.int32,(tq,128),1)
    for hp in range(heads//2):
        qp=q[0,:,hp*128:(hp+1)*128]
        qm[2*hp]=jnp.where(lane<64,qp,0).astype(BF)
        qm[2*hp+1]=jnp.where(lane>=64,qp,0).astype(BF)
    bound=jnp.sqrt(head_sumsq(q[0],hp16))*kn[:,0:1]*(C2*1.02)
    safe=jnp.max(bound)<50.0
    if first:
        m0=bound
    else:
        m0=jnp.maximum(bound,m_i[0])
    def loop(online):
        if first:
            acc[...]=jnp.zeros_like(acc); l[...]=jnp.zeros_like(l)
            m[...]=jnp.full_like(m,NEG) if online else m0
        elif online:
            acc[...]=accT_i[0]; m[...]=m_i[0]; l[...]=l_i[0]
        else:
            al=jnp.exp2(m_i[0]-m0)
            m[...]=m0; l[...]=al*l_i[0]
            for hh in range(heads):
                hs=slice(hh*HD,(hh+1)*HD)
                acc[hs,:]=al[hh:hh+1,:]*accT_i[0,hs,:]
        def body(kt,masked):
            ks=pl.ds(pl.multiple_of(kt*tk,tk),tk)
            if online:
                @pl.loop(0,heads//2)
                def _(hp):
                    kp=k[0,ks,pl.ds(pl.multiple_of(hp*128,128),128)]
                    for j in range(2):
                        hh=2*hp+j
                        s=lax.dot_general(kp,qm[hh],NT,preferred_element_type=F32)*C2+bias[...]
                        mp=m[pl.ds(hh,1),:]
                        mn=jnp.maximum(mp,jnp.max(s,0,keepdims=True))
                        p=jnp.exp2(s-mn)
                        al=jnp.exp2(mp-mn)
                        m[pl.ds(hh,1),:]=mn
                        l[pl.ds(hh,1),:]=al*l[pl.ds(hh,1),:]+jnp.sum(p,0,keepdims=True)
                        hs=pl.ds(pl.multiple_of(hh*HD,HD),HD)
                        acc[hs,:]=al*acc[hs,:]+lax.dot_general(vT[hs,ks],p.astype(BF),NN,preferred_element_type=F32)
                return
            def score(hh):
                s=lax.dot_general(k[0,ks,(hh//2)*128:(hh//2+1)*128],qm[hh],NT,preferred_element_type=F32)*C2
                if masked: s=s+bias[...]
                return s
            s=score(0); pp=None
            for hh in range(heads+1):
                if hh+1<heads: sn=score(hh+1)
                if pp is not None:
                    hs=slice((hh-1)*HD,hh*HD)
                    acc[hs,:]+=lax.dot_general(vT[hs,ks],pp,NN,preferred_element_type=F32)
                if hh<heads:
                    p=jnp.exp2(s-m[hh:hh+1,:])
                    l[hh:hh+1,:]+=jnp.sum(p,0,keepdims=True)
                    pp=p.astype(BF)
                s=sn
        @pl.loop(0,nk)
        def _(kt):
            f=flags[r,qi,kt]
            def mask():
                ks=pl.ds(pl.multiple_of(kt*tk,tk),tk)
                bias[...]=jnp.where(ck[0,ks,0:1]==cq[0,0:1,:],0.0,NEG)
            if online:
                @pl.when(f>0)
                def _():
                    mask(); body(kt,True)
            else:
                @pl.when(f==1)
                def _():
                    mask(); body(kt,True)
                @pl.when(f==2)
                def _(): body(kt,False)
    @pl.when(safe)
    def _(): loop(False)
    @pl.when(jnp.logical_not(safe))
    def _(): loop(True)
    if first:
        accT_o[0]=acc[...]; m_o[0]=m[...]; l_o[0]=l[...]
    else:
        for hp in range(heads//2):
            parts=[]
            for hh in (2*hp,2*hp+1):
                parts.append(acc[hh*HD:(hh+1)*HD,:]/l[hh:hh+1,:])
            o_o[0,:,hp*128:(hp+1)*128]=jnp.concatenate(parts,0).T.astype(BF)
        lse_o[0]=m[...]+jnp.log2(l[...])

def attn_fwd(flags,cq,ck,q,k,v,state=None,tq=256,tk=256,heads=10):
    nr,S,W=q.shape; Sk=k.shape[1]; hp16=-(-heads//8)*8
    first=state is None
    qs=lambda r,i,*_:(r,i,0); ts=lambda r,i,*_:(r,0,i); ks=lambda r,i,*_:(r,0,0)
    stspec=[pl.BlockSpec((1,W,tq),ts),pl.BlockSpec((1,hp16,tq),ts),pl.BlockSpec((1,hp16,tq),ts)]
    ins=[pl.BlockSpec((1,1,tq),ts),pl.BlockSpec((1,Sk,128),ks),pl.BlockSpec((1,tq,W),qs),pl.BlockSpec((1,Sk,W),ks),pl.BlockSpec((1,Sk,W),ks)]
    if first:
        outs=stspec
        osh=[jax.ShapeDtypeStruct((nr,W,S),F32)]+[jax.ShapeDtypeStruct((nr,hp16,S),F32)]*2
    else:
        ins=ins+stspec
        outs=[pl.BlockSpec((1,tq,W),qs),pl.BlockSpec((1,hp16,tq),ts)]
        osh=[jax.ShapeDtypeStruct((nr,S,W),BF),jax.ShapeDtypeStruct((nr,hp16,S),F32)]
    fl=4*nr*S*Sk*W
    return pl.pallas_call(functools.partial(fwd_kernel,first=first,tq=tq,tk=tk,heads=heads),
        out_shape=osh,
        grid_spec=pltpu.PrefetchScalarGridSpec(num_scalar_prefetch=1,grid=(nr,S//tq),in_specs=ins,out_specs=outs,
          scratch_shapes=[pltpu.VMEM((heads,tq,128),BF),pltpu.VMEM((W,Sk),BF),pltpu.VMEM((tk,tq),F32),pltpu.VMEM((W,tq),F32),pltpu.VMEM((hp16,tq),F32),pltpu.VMEM((hp16,tq),F32),pltpu.VMEM((hp16,128),F32)]),
        compiler_params=pltpu.CompilerParams(dimension_semantics=("arbitrary","arbitrary"),vmem_limit_bytes=VMEM_LIMIT),
        cost_estimate=pl.CostEstimate(flops=fl*4,bytes_accessed=nr*(S*W*2+2*Sk*W*2+S*W*4),transcendentals=nr*S*Sk*heads),
        name="attn_fwd_a" if first else "attn_fwd_b",
    )(flags,cq,ck,q,k,v,*(state or ()))

def bwd_kernel(flags,cq,ck,q,k,v,do,o,lse,*rest,first,tq,tk,heads):
    if first:
        dqT_o,dk_o,dv_o,qm,dom,kT,bias,dqT,dk,dv,delta=rest
    else:
        dqT_i,dq_o,dk_o,dv_o,qm,dom,kT,bias,dqT,dk,dv,delta=rest
    r=pl.program_id(0); qi=pl.program_id(1); nq=pl.num_programs(1)
    nk=k.shape[1]//tk
    @pl.when(qi==0)
    def _():
        kT[...]=k[0].T
        dk[...]=jnp.zeros_like(dk); dv[...]=jnp.zeros_like(dv)
    lane=lax.broadcasted_iota(jnp.int32,(tq,128),1)
    for hp in range(heads//2):
        c=slice(hp*128,(hp+1)*128)
        qp=q[0,:,c]*jnp.asarray(0.125,BF); dp_=do[0,:,c]
        qm[2*hp]=jnp.where(lane<64,qp,0).astype(BF)
        qm[2*hp+1]=jnp.where(lane>=64,qp,0).astype(BF)
        dom[2*hp]=jnp.where(lane<64,dp_,0).astype(BF)
        dom[2*hp+1]=jnp.where(lane>=64,dp_,0).astype(BF)
    W=heads*HD
    prod=do[0].astype(F32)*o[0].astype(F32)
    hi=prod.astype(BF); lo=(prod-hi.astype(F32)).astype(BF)
    hp16=delta.shape[0]
    row=lax.broadcasted_iota(jnp.int32,(hp16,W),0); col=lax.broadcasted_iota(jnp.int32,(hp16,W),1)
    ones=jnp.where(row==col//HD,1.0,0.0).astype(BF)
    delta[...]=lax.dot_general(ones,hi,NT,preferred_element_type=F32)+lax.dot_general(ones,lo,NT,preferred_element_type=F32)
    if first: dqT[...]=jnp.zeros_like(dqT)
    else: dqT[...]=dqT_i[0]
    def body(kt,masked):
        ks=pl.ds(pl.multiple_of(kt*tk,tk),tk)
        def col(hh): return slice((hh//2)*128,(hh//2+1)*128)
        def score(hh):
            s=lax.dot_general(k[0,ks,col(hh)],qm[hh],NT,preferred_element_type=F32)*LOG2E
            if masked: s=s+bias[...]
            return s,lax.dot_general(v[0,ks,col(hh)],dom[hh],NT,preferred_element_type=F32)
        nxt=score(0); prev=None
        for hh in range(heads+1):
            cur=nxt
            if hh+1<heads: nxt=score(hh+1)
            if prev is not None:
                h1=hh-1; pb,dsb=prev
                hs=slice(h1*HD,(h1+1)*HD)
                dqT[hs,:]+=lax.dot_general(kT[hs,ks],dsb,NN,preferred_element_type=F32)
                dv[ks,col(h1)]+=jnp.dot(pb,dom[h1],preferred_element_type=F32)
                dk[ks,col(h1)]+=jnp.dot(dsb,qm[h1],preferred_element_type=F32)
            if hh<heads:
                s,dp=cur
                p=jnp.exp2(s-lse[0,hh:hh+1,:])
                ds=p*(dp-delta[hh:hh+1,:])
                prev=(p.astype(BF),ds.astype(BF))
    @pl.loop(0,nk)
    def _(kt):
        f=flags[r,qi,kt]
        @pl.when(f==1)
        def _():
            ks=pl.ds(pl.multiple_of(kt*tk,tk),tk)
            bias[...]=jnp.where(ck[0,ks,0:1]==cq[0,0:1,:],0.0,NEG)
            body(kt,True)
        @pl.when(f==2)
        def _(): body(kt,False)
    if first: dqT_o[0]=dqT[...]
    else: dq_o[0]=(dqT[...]*0.125).T.astype(BF)
    @pl.when(qi==nq-1)
    def _():
        dk_o[0]=dk[...].astype(BF); dv_o[0]=dv[...].astype(BF)

def attn_bwd(flags,cq,ck,q,k,v,do,o,lse,dqT=None,tq=256,tk=256,heads=10):
    nr,S,W=q.shape; Sk=k.shape[1]; hp16=lse.shape[1]
    first=dqT is None
    qs=lambda r,i,*_:(r,i,0); ts=lambda r,i,*_:(r,0,i); ks=lambda r,i,*_:(r,0,0)
    ins=[pl.BlockSpec((1,1,tq),ts),pl.BlockSpec((1,Sk,128),ks),pl.BlockSpec((1,tq,W),qs),pl.BlockSpec((1,Sk,W),ks),pl.BlockSpec((1,Sk,W),ks),
         pl.BlockSpec((1,tq,W),qs),pl.BlockSpec((1,tq,W),qs),pl.BlockSpec((1,hp16,tq),ts)]
    dko=[pl.BlockSpec((1,Sk,W),ks)]*2; dksh=[jax.ShapeDtypeStruct((nr,Sk,W),BF)]*2
    if first:
        outs=[pl.BlockSpec((1,W,tq),ts)]+dko; osh=[jax.ShapeDtypeStruct((nr,W,S),F32)]+dksh
        extra=()
    else:
        ins=ins+[pl.BlockSpec((1,W,tq),ts)]
        outs=[pl.BlockSpec((1,tq,W),qs)]+dko; osh=[jax.ShapeDtypeStruct((nr,S,W),BF)]+dksh
        extra=(dqT,)
    fl=10*nr*S*Sk*W
    return pl.pallas_call(functools.partial(bwd_kernel,first=first,tq=tq,tk=tk,heads=heads),
        out_shape=osh,
        grid_spec=pltpu.PrefetchScalarGridSpec(num_scalar_prefetch=1,grid=(nr,S//tq),in_specs=ins,out_specs=outs,
          scratch_shapes=[pltpu.VMEM((heads,tq,128),BF),pltpu.VMEM((heads,tq,128),BF),pltpu.VMEM((W,Sk),BF),pltpu.VMEM((tk,tq),F32),pltpu.VMEM((W,tq),F32),
             pltpu.VMEM((Sk,W),F32),pltpu.VMEM((Sk,W),F32),pltpu.VMEM((hp16,tq),F32)]),
        compiler_params=pltpu.CompilerParams(dimension_semantics=("arbitrary","arbitrary"),vmem_limit_bytes=VMEM_LIMIT),
        cost_estimate=pl.CostEstimate(flops=fl*4,bytes_accessed=nr*(3*S*W*2+4*Sk*W*2+S*W*4),transcendentals=nr*S*Sk*heads),
        name="attn_bwd_a" if first else "attn_bwd_b",
    )(flags,cq,ck,q,k,v,do,o,lse,*extra)


def ffn_kernel(core, acts, w, b, d_act, act_o, theirs_o, mine_o, sum_o):
    del core
    step = pl.program_id(0)
    half = pl.num_programs(0) // 2
    rows = acts.shape[0]
    chunk = min(256, rows)
    count = rows // chunk

    def product(i):
        return dot(acts[i * chunk : (i + 1) * chunk, :], w[...], NN) + b[...]

    pre = product(0)
    total = None
    for i in range(count):
        following = product(i + 1) if i + 1 < count else None
        at = slice(i * chunk, (i + 1) * chunk)
        cdf = 0.5 + 0.5 * lax.erf(pre * math.sqrt(0.5))
        pdf = jnp.exp(-0.5 * pre * pre) * (1.0 / math.sqrt(2.0 * math.pi))
        act_o[at, :] = (pre * cdf).astype(BF)
        d_pre = (d_act[at, :].astype(F32) * (cdf + pre * pdf)).astype(BF)

        @pl.when(step < half)
        def _():
            theirs_o[at, :] = d_pre

        @pl.when(step >= half)
        def _():
            mine_o[at, :] = d_pre

        part = jnp.sum(d_pre.astype(F32), axis=0, keepdims=True)
        total = part if total is None else total + part
        pre = following
    sum_o[...] = total


def ffn_call(core, acts, w, b, d_act):
    rows, width = acts.shape
    ff = w.shape[1]
    tile = 512
    half = ff // 2 // tile

    def place(i, core):
        return jnp.where(i < half, 1 - core[0], core[0]) * half + lax.rem(i, half)

    col = lambda i, core: (0, place(i, core))
    return pl.pallas_call(
        ffn_kernel,
        out_shape=[
            jax.ShapeDtypeStruct((rows, ff), BF),
            jax.ShapeDtypeStruct((rows, ff // 2), BF),
            jax.ShapeDtypeStruct((rows, ff // 2), BF),
            jax.ShapeDtypeStruct((1, ff), F32),
        ],
        grid_spec=pltpu.PrefetchScalarGridSpec(
            num_scalar_prefetch=1,
            grid=(2 * half,),
            in_specs=[
                pl.BlockSpec((rows, width), lambda i, core: (0, 0)),
                pl.BlockSpec((width, tile), col),
                pl.BlockSpec((1, tile), col),
                pl.BlockSpec((rows, tile), col),
            ],
            out_specs=[
                pl.BlockSpec((rows, tile), col),
                pl.BlockSpec((rows, tile), lambda i, core: (0, jnp.minimum(i, half - 1))),
                pl.BlockSpec((rows, tile), lambda i, core: (0, jnp.maximum(i - half, 0))),
                pl.BlockSpec((1, tile), col),
            ],
        ),
        compiler_params=pltpu.CompilerParams(vmem_limit_bytes=VMEM_LIMIT),
        cost_estimate=pl.CostEstimate(
            flops=2 * rows * width * ff,
            bytes_accessed=2 * (rows * width + width * ff + 3 * rows * ff),
            transcendentals=2 * rows * ff,
        ),
        name="ffn",
    )(core, acts, w, b, d_act)


def grad_kernel(where, *refs, groups, first, second):
    ins = refs[: sum(2 * len(g) for g in groups)]
    outs = refs[len(ins) : len(ins) + first]
    acc = refs[-1]
    height = acc.shape[0] // len(groups)
    at = 0
    for index, group in enumerate(groups):
        total = None
        for _ in group:
            part = dot(ins[at][...], ins[at + 1][...], TN)
            total = part if total is None else total + part
            at += 2
        acc[index * height : (index + 1) * height, :] = total
    rows = acc.shape[0] // (first * second)
    for one in range(first):
        for two in range(second):
            block = lax.bitwise_xor(two * first + one, where[0])
            outs[one][two] = acc[pl.ds(pl.multiple_of(block * rows, 16), rows), :].astype(BF)


def grad_call(where, groups, first, second, tile, name):
    width = groups[0][0][3]
    ins, flat, flops, moved = [], [], 0, 0
    height = sum(g[0][0].shape[1] for g in groups)
    for group in groups:
        for a, b, offset, n in group:
            ins.append(pl.BlockSpec(a.shape, lambda i, where: (0, 0)))
            if offset is None:
                ins.append(pl.BlockSpec((b.shape[0], tile), lambda i, where: (0, i)))
            else:
                ins.append(
                    pl.BlockSpec(
                        (b.shape[0], tile),
                        lambda i, where, offset=offset: (0, where[offset] * (width // tile) + i),
                    )
                )
            flat += [a, b]
            flops += 2 * a.shape[0] * a.shape[1] * n
            moved += 2 * a.shape[0] * (a.shape[1] + n)
    rows = height // (first * second)
    return pl.pallas_call(
        functools.partial(
            grad_kernel,
            groups=[[None] * len(g) for g in groups],
            first=first,
            second=second,
        ),
        out_shape=[jax.ShapeDtypeStruct((second, rows, width), BF)] * first,
        grid_spec=pltpu.PrefetchScalarGridSpec(
            num_scalar_prefetch=1,
            grid=(width // tile,),
            in_specs=ins,
            out_specs=[pl.BlockSpec((second, rows, tile), lambda i, where: (0, 0, i))] * first,
            scratch_shapes=[pltpu.VMEM((height, tile), F32)],
        ),
        compiler_params=pltpu.CompilerParams(vmem_limit_bytes=VMEM_LIMIT),
        cost_estimate=pl.CostEstimate(
            flops=flops, bytes_accessed=moved + 2 * height * width, transcendentals=0
        ),
        name=name,
    )(where, *flat)


def back_kernel(where, a1, b1, a2, b2, out):
    del where
    out[0] = (dot(a1[...], b1[...], TN) + dot(a2[...], b2[...], TN)).astype(BF)


def back_call(where, own, mate, one, first, second, name):
    (a1, b1), (a2, b2) = own, mate
    tokens, ff = a1.shape
    rows = ff // (first * second)
    width = b2.shape[1]
    if rows % 128:
        total = dot(a1, lax.dynamic_slice_in_dim(b1, where[1] * width, width, 1), TN) + dot(a2, b2, TN)
        total = total.astype(BF).reshape(first * second, rows, width)
        return jnp.stack([total[lax.bitwise_xor(two * first + one, where[0])] for two in range(second)])

    def block(i, where):
        return (0, lax.bitwise_xor(i * first + one, where[0]))

    return pl.pallas_call(
        back_kernel,
        out_shape=jax.ShapeDtypeStruct((second, rows, width), BF),
        grid_spec=pltpu.PrefetchScalarGridSpec(
            num_scalar_prefetch=1,
            grid=(second,),
            in_specs=[
                pl.BlockSpec((tokens, rows), block),
                pl.BlockSpec((tokens, width), lambda i, where: (0, where[1])),
                pl.BlockSpec((tokens, rows), block),
                pl.BlockSpec((tokens, width), lambda i, where: (0, 0)),
            ],
            out_specs=pl.BlockSpec((1, rows, width), lambda i, where: (i, 0, 0)),
        ),
        compiler_params=pltpu.CompilerParams(vmem_limit_bytes=VMEM_LIMIT),
        cost_estimate=pl.CostEstimate(
            flops=4 * tokens * second * rows * width,
            bytes_accessed=2 * (2 * tokens * (second * rows + width) + second * rows * width),
            transcendentals=0,
        ),
        name=name,
    )(where, a1, b1, a2, b2)


def tile_flags(queries, keys, tq, tk):
    q_first, q_last = queries[:, ::tq], queries[:, tq - 1 :: tq]
    k_first, k_last = keys[:, ::tk], keys[:, tk - 1 :: tk]
    meet = (q_first[:, :, None] <= k_last[:, None, :]) & (k_first[:, None, :] <= q_last[:, :, None])
    whole = (
        (q_first == q_last)[:, :, None]
        & (k_first == k_last)[:, None, :]
        & (q_first[:, :, None] == k_first[:, None, :])
    )
    return jnp.where(whole, 2, jnp.where(meet, 1, 0)).astype(jnp.int32)


def layer_norm_parts(values):
    centred = values - jnp.mean(values, axis=-1, keepdims=True)
    rstd = lax.rsqrt(jnp.mean(centred * centred, axis=-1, keepdims=True) + EPS)
    return centred * rstd, rstd


def layer_norm_back(d_norm, gain, xhat, rstd):
    e = d_norm * gain
    return rstd * (
        e - jnp.mean(e, axis=-1, keepdims=True) - xhat * jnp.mean(e * xhat, axis=-1, keepdims=True)
    )


def on_device(
    tokens,
    cell_start,
    norm1_gain,
    norm1_bias,
    w_qkv,
    bias_q,
    bias_v,
    w_out,
    bias_out,
    norm2_gain,
    norm2_bias,
    w_in,
    bias_in,
    w_back,
    bias_back,
    cotangent,
):
    rows, seg, width = tokens.shape
    count = rows * seg
    ff = w_in.shape[1]
    half = width // 2
    wide = lax.axis_size("wide")
    group = lax.axis_size("blk")
    place = lax.axis_index("wide")
    core = place % 2
    chips = wide // 2
    first = 2 if chips <= 8 else 4
    second = chips // first
    heads = HEADS // 2
    tq, tk = min(512, seg), min(256, seg)
    where = jnp.stack([place // 2, core]).astype(jnp.int32)
    where_out = jnp.stack([lax.bitwise_xor(place // 2, core * (chips // 2)), core]).astype(jnp.int32)

    def across(array, by):
        return lax.ppermute(array, "wide", [(i, i ^ by) for i in range(wide)])

    def to_mate(array):
        return across(array, 1)

    def from_ahead(array, by):
        return lax.ppermute(array, "blk", [((i + by) % group, i) for i in range(group)])

    def to_ahead(array, by):
        return lax.ppermute(array, "blk", [(i, (i + by) % group) for i in range(group)])

    def cut(array, start, size, axis):
        return lax.dynamic_slice_in_dim(array, start, size, axis)

    inputs = tokens.astype(F32).reshape(count, width)
    xhat1, rstd1 = layer_norm_parts(inputs)
    acts = (xhat1 * norm1_gain + norm1_bias).astype(BF)
    far_acts = [from_ahead(acts, by) for by in range(1, group)]
    acts_sets = [acts, to_mate(acts)]
    cells = [cell_start, to_mate(cell_start)]
    far_cells = [jnp.concatenate([from_ahead(c, by) for by in range(1, group)], axis=1) for c in cells]

    w_q = cut(w_qkv, core * half, half, 1)
    w_k = cut(w_qkv, width + core * half, half, 1)
    w_v = cut(w_qkv, 2 * width + core * half, half, 1)
    b_q = cut(bias_q, core * half, half, 0)
    b_v = cut(bias_v, core * half, half, 0)

    def by_row(array):
        return array.reshape(rows, -1, half)

    def columns(array):
        return jnp.broadcast_to(array[:, :, None], array.shape + (128,))

    queries = [by_row((dot(a, w_q, NN) + b_q).astype(BF)) for a in acts_sets]
    keys = [by_row(dot(a, w_k, NN).astype(BF)) for a in acts_sets]
    values = [by_row((dot(a, w_v, NN) + b_v).astype(BF)) for a in acts_sets]
    near_flags = [tile_flags(c, c, tq, tk) for c in cells]
    far_flags = [tile_flags(c, f, tq, tk) for c, f in zip(cells, far_cells)]
    cell_rows = [c[:, None, :] for c in cells]
    near_columns = [columns(c) for c in cells]
    far_columns = [columns(c) for c in far_cells]
    states = [
        attn_fwd(near_flags[s], cell_rows[s], near_columns[s], queries[s], keys[s], values[s], None, tq, tk, heads)
        for s in range(2)
    ]
    d_out = cotangent.reshape(count, width)
    d_act = dot(d_out, w_back, NT).astype(BF)

    far_sets = [far_acts, [to_mate(a) for a in far_acts]]

    def joined(parts):
        return parts[0] if len(parts) == 1 else jnp.concatenate(parts, axis=1)

    far_keys = [joined([by_row(dot(a, w_k, NN).astype(BF)) for a in f]) for f in far_sets]
    far_values = [joined([by_row((dot(a, w_v, NN) + b_v).astype(BF)) for a in f]) for f in far_sets]
    attended = [None, None]
    stats = [None, None]
    for s in (1, 0):
        attended[s], stats[s] = attn_fwd(
            far_flags[s], cell_rows[s], far_columns[s], queries[s], far_keys[s], far_values[s], states[s], tq, tk, heads
        )
    flat = [a.reshape(count, half) for a in attended]
    own_rest = to_mate(flat[1])
    mate_rest = to_mate(flat[0])
    w_out_own = cut(w_out, core * half, half, 0)
    w_out_mate = cut(w_out, (1 - core) * half, half, 0)
    middle = inputs + (dot(flat[0], w_out_own, NN) + dot(own_rest, w_out_mate, NN)) + bias_out

    xhat2, rstd2 = layer_norm_parts(middle)
    acts2 = (xhat2 * norm2_gain + norm2_bias).astype(BF)
    acts2_mate = to_mate(acts2)
    act, d_pre_theirs, d_pre_mine, d_pre_sum = ffn_call(
        where[1:], acts2, w_in, bias_in.reshape(1, ff), d_act
    )
    d_pre_mate = to_mate(d_pre_theirs)
    act_mate = to_mate(act)
    d_out_mate = to_mate(cut(d_out, (1 - core) * half, half, 1))
    w_in_mine = cut(w_in, core * (ff // 2), ff // 2, 1)
    w_in_theirs = cut(w_in, (1 - core) * (ff // 2), ff // 2, 1)
    d_norm2 = dot(d_pre_theirs, w_in_theirs, NT) + dot(d_pre_mine, w_in_mine, NT)
    grad_out = d_out.astype(F32)
    d_middle = grad_out + layer_norm_back(d_norm2, norm2_gain, xhat2, rstd2)
    d_z = d_middle.astype(BF)
    d_att_mate = to_mate(dot(d_z, w_out_mate, NT).astype(BF))
    d_att = [by_row(dot(d_z, w_out_own, NT).astype(BF)), by_row(d_att_mate)]
    d_z_mate = to_mate(cut(d_z, (1 - core) * half, half, 1))

    mixed = (middle + dot(act, w_back, NN) + bias_back).astype(BF).reshape(tokens.shape)

    def scatter(parts):
        received = [across(parts[one], 2 * one) for one in range(1, first)]
        sums = []
        for two in range(second):
            total = parts[0][two].astype(F32)
            for part in received:
                total = total + part[two].astype(F32)
            sums.append(total.astype(BF))
        total = sums[0].astype(F32)
        for two in range(1, second):
            total = total + across(sums[two], 2 * first * two).astype(F32)
        total = total.astype(BF)
        if group == 2:
            return total.astype(F32) + from_ahead(total, 1).astype(F32)
        return lax.psum(total, "blk").astype(F32)

    def finish(total):
        split = total.astype(BF).reshape(2, -1, total.shape[-1])
        theirs = lax.dynamic_index_in_dim(split, 1 - core, 0, keepdims=False)
        mine = lax.dynamic_index_in_dim(split, core, 0, keepdims=False)
        other = to_mate(theirs)
        low, high = jnp.where(core == 0, mine, other), jnp.where(core == 0, other, mine)
        return low.astype(F32), high.astype(F32)

    grad_in = grad_call(
        where, [[(acts2, d_pre_mine, None, ff // 2), (acts2_mate, d_pre_mate, None, ff // 2)]], first, second, 512, "grad_in"
    )
    grad_back = [
        back_call(where, (act, d_out), (act_mate, d_out_mate), one, first, second, "grad_back")
        for one in list(range(1, first)) + [0]
    ]
    grad_back = [grad_back[-1]] + grad_back[:-1]
    grad_w_in = jnp.concatenate(finish(scatter(grad_in)), axis=1)
    grad_w_back = jnp.concatenate(finish(scatter(grad_back)), axis=1)
    grad_o = grad_call(
        where_out,
        [
            [(flat[0], d_z, 1, half), (flat[1], d_z_mate, None, half)],
            [(own_rest, d_z, 1, half), (mate_rest, d_z_mate, None, half)],
        ],
        first,
        second,
        half,
        "grad_out",
    )
    grad_w_out = jnp.concatenate(finish(scatter(grad_o)), axis=1)

    def vectors(parts):
        packed = jnp.concatenate([p.reshape(wide, -1) for p in parts], axis=1)
        total = packed
        digits = [(1, 2), (2, first), (2 * first, second)]
        for stride, size in reversed(digits):
            total = total.reshape(-1, size, stride, packed.shape[1])
            mine = (place // stride) % size
            kept = lax.dynamic_index_in_dim(total, mine, 1, keepdims=False)
            for by in range(1, size):
                send = lax.dynamic_index_in_dim(total, mine ^ by, 1, keepdims=False)
                kept = kept + across(send, by * stride)
            total = kept.reshape(stride, packed.shape[1])
        total = total.reshape(-1)
        if group == 2:
            total = total + from_ahead(total, 1)
        else:
            total = lax.psum(total, "blk")
        out, at = [], 0
        for p in parts:
            size = p.size // wide
            out.append(total[at : at + size])
            at += size
        return out

    early = vectors(
        [
            jnp.sum(d_z.astype(F32), axis=0),
            jnp.sum(d_norm2 * xhat2, axis=0),
            jnp.sum(d_norm2, axis=0),
            d_pre_sum,
            jnp.sum(grad_out, axis=0),
        ]
    )

    far_back = [
        attn_bwd(
            far_flags[s], cell_rows[s], far_columns[s], queries[s], far_keys[s], far_values[s],
            d_att[s], attended[s], stats[s], None, tq, tk, heads,
        )
        for s in range(2)
    ]

    def far_norm(s, by):
        at = slice(by * seg, (by + 1) * seg)
        d_k = far_back[s][1][:, at].reshape(count, half)
        d_v = far_back[s][2][:, at].reshape(count, half)
        return d_k, d_v, dot(d_k, w_k, NT) + dot(d_v, w_v, NT)

    far_grads = [[far_norm(s, by) for by in range(group - 1)] for s in range(2)]
    d_norm1_far = None
    for by in range(group - 1):
        part = far_grads[0][by][2] + to_mate(far_grads[1][by][2].astype(BF)).astype(F32)
        part = to_ahead(part.astype(BF), by + 1).astype(F32)
        d_norm1_far = part if d_norm1_far is None else d_norm1_far + part
    near_back = [
        attn_bwd(
            near_flags[s], cell_rows[s], near_columns[s], queries[s], keys[s], values[s],
            d_att[s], attended[s], stats[s], far_back[s][0], tq, tk, heads,
        )
        for s in range(2)
    ]
    d_q = [b[0].reshape(count, half) for b in near_back]
    d_k = [b[1].reshape(count, half) for b in near_back]
    d_v = [b[2].reshape(count, half) for b in near_back]

    def grad_far(column, near, name):
        pairs = [(acts_sets[s], near[s], None, half) for s in range(2)]
        for s in range(2):
            for by in range(group - 1):
                pairs.append((far_sets[s][by], far_grads[s][by][column], None, half))
        return grad_call(where, [pairs], first, second, half, name)

    grad_k = finish(scatter(grad_far(0, d_k, "grad_k")))
    grad_v = finish(scatter(grad_far(1, d_v, "grad_v")))
    grad_q = finish(
        scatter(grad_call(where, [[(acts_sets[s], d_q[s], None, half) for s in range(2)]], first, second, half, "grad_q"))
    )
    grad_w_qkv = jnp.concatenate(grad_q + grad_k + grad_v, axis=1)

    near_norm = [dot(d_q[s], w_q, NT) + dot(d_k[s], w_k, NT) + dot(d_v[s], w_v, NT) for s in range(2)]
    d_norm1 = near_norm[0] + to_mate(near_norm[1].astype(BF)).astype(F32) + d_norm1_far
    grad_tokens = (d_middle + layer_norm_back(d_norm1, norm1_gain, xhat1, rstd1)).reshape(tokens.shape)

    def widened(array):
        return lax.dynamic_update_slice_in_dim(jnp.zeros((width,), F32), array, core * half, 0)

    def column_sum(arrays):
        return sum(jnp.sum(a.astype(F32), axis=0) for a in arrays)

    late = vectors(
        [
            jnp.sum(d_norm1 * xhat1, axis=0),
            jnp.sum(d_norm1, axis=0),
            widened(column_sum(d_q)),
            widened(column_sum(d_v + [g[1] for f in far_grads for g in f])),
        ]
    )
    return (
        mixed,
        grad_tokens,
        late[0],
        late[1],
        grad_w_qkv,
        late[2],
        late[3],
        grad_w_out,
        early[0],
        early[1],
        early[2],
        grad_w_in,
        early[3],
        grad_w_back,
        early[4],
    )


def solution(mesh):
    spread = P("wide", "blk", None)
    placed = (spread, P("wide", "blk")) + (P(),) * 13 + (spread,)
    matrix, vector = P("wide", None), P("wide")
    return jax.shard_map(
        on_device,
        mesh=mesh,
        in_specs=placed,
        out_specs=(
            spread, spread, vector, vector, matrix, vector, vector, matrix, vector, vector, vector,
            matrix, vector, matrix, vector,
        ),
        check_vma=False,
    )
```

time: 1840 us -> 995 us (0.54)
  waiting for transfers between devices: 771 us -> 247 us
  matrix products: 712 us -> 190 us
  Pallas kernels: 0 us -> 307 us
  starting transfers between devices: 8.39 us -> 144 us
  other arithmetic: 175 us -> 67.2 us
  blocking collectives: 70.3 us -> 0 us
  local copies, waits for them, and re-layouts: 73.4 us -> 20.3 us
    dot_general x24 -> x28, matrix products: 712 us -> 190 us  [dot(): return lax.dot_general(a, b, dims, preferred_element_type=F32)]
    reduce_scatter x4 -> x0, waiting for transfers between devices: 311 us -> none  [the longest x1 143 us: on_device(): lax.psum_scatter(grad_w_in.astype(jnp.bfloat16), 'wide', scatter_dimensio...]
    pallas_call x0 -> x16, Pallas kernels: none -> 307 us  [the longest x4 108 us: attn_bwd(): pl.pallas_call(functools.partial(bwd_kernel, first=first, tq=tq, tk=tk, h...]
    ppermute x8 -> x65, waiting for transfers between devices: 423 us -> 247 us  [the longest x53 170 us: across(): return lax.ppermute(array, 'wide', [(i, i ^ by) for i in range(wide)])]
    ppermute x8 -> x65, starting transfers between devices: 8.1 us -> 144 us  [the longest x53 127 us: across(): return lax.ppermute(array, 'wide', [(i, i ^ by) for i in range(wide)])]
    unnamed x1 -> x0, blocking collectives: 59.8 us -> none
    reduce_sum x10 -> x11, other arithmetic: 84.1 us -> 25.8 us  [the longest x1 10.7 us: on_device(): jnp.sum(d_norm1 * xhat1, axis=0)]
    all_gather x2 -> x0, waiting for transfers between devices: 36.3 us -> none  [the longest x1 36.3 us: on_device(): both_key_part = lax.all_gather(keys, 'blk', axis=1, tiled=True)]
  transfers between devices with their start and end apart: 15 -> 65, of which waited for: 12 -> 23; matrix products, arithmetic and copies ran while one was open for 37% -> 26% of each run, Pallas kernels for 0% -> 30%
where the time goes in v1:
time: 995 us; the launch traced here: 978 us
  Pallas kernels  307 us (31%)
  waiting for transfers between devices  247 us (25%)
  matrix products  190 us (19%)
  starting transfers between devices  144 us (14%)
  other arithmetic  67.2 us (7%)
  local copies, waits for them, and re-layouts  20.3 us (2%)
    dot_general x28, matrix products, dot(): return lax.dot_general(a, b, dims, preferred_element_type=F32)  190 us
    ppermute x53, waiting for transfers between devices, across(): return lax.ppermute(array, 'wide', [(i, i ^ by) for i in range(wide)])  170 us
    ppermute x53, starting transfers between devices, across(): return lax.ppermute(array, 'wide', [(i, i ^ by) for i in range(wide)])  127 us
    pallas_call x4, Pallas kernels, attn_bwd(): pl.pallas_call(functools.partial(bwd_kernel, first=first, tq=tq, tk=tk, h...  108 us
    pallas_call x5, Pallas kernels, grad_call(): pl.pallas_call(functools.partial(grad_kernel, groups=[[None] * len(g) for...  72.4 us
    pallas_call x4, Pallas kernels, attn_fwd(): pl.pallas_call(functools.partial(fwd_kernel, first=first, tq=tq, tk=tk, h...  62.1 us
    ppermute x11, waiting for transfers between devices, from_ahead(): lax.ppermute(array, 'blk', [((i + by) % group, i) for i in range(group)])  47.7 us
    pallas_call x1, Pallas kernels, ffn_call(): pl.pallas_call(ffn_kernel, out_shape=[jax.ShapeDtypeStruct((rows, ff), BF...  37.4 us
  transfers between devices with their start and end apart: 65, of which 23 were waited for; matrix products, arithmetic and copies ran while one was open for 26% of the time, Pallas kernels for 30%

profile of v1, /device:TPU:0, one launch (start us, length us, event | category | flops | bytes accessed | tf_op | source)
XLA Modules:
  0.0 977.8 jit_solution(12881347031680780526)
XLA Ops:
  27.4 21.2 %convolution_convert_fusion.d_act = bf16[1024,5120]{1,0:T(8,128)(2,1)} fusion(bf16[5120,1280]{1,0:T(8,128)(2,1)} %param.29, bf16[1,1024,1280]{2,1,0:T(8,128)(2,1)S(1)} %copy-done.8), kind=kOutput, calls=%fused_computation | convolution fusion | flops 13427015680 | bytes 26214400 | tf_op jit(solution)/shard_map/dot_general | solution.py:27
  54.4 13.2 %collective-permute-done = s32[1,1024]{1,0:T(1,128)S(1)} collective-permute-done((s32[1,1024]{1,0:T(1,128)S(1)}, s32[1,1024]{1,0:T(1,128)S(1)}, u32[]{:S(2)}, u32[]{:S(2)}) %collective-permute-start) | collective-permute-done | bytes 4128 | tf_op jit(solution)/shard_map/ppermute | solution.py:500
  69.5 17.8 %attn_fwd_a.2 = (f32[1,640,1024]{2,1,0:T(8,128)}, f32[1,16,1024]{2,1,0:T(8,128)}, f32[1,16,1024]{2,1,0:T(8,128)}) custom-call(s32[1,2,4]{2,1,0:T(2,128)} %get-tuple-element.140.flags, s32[1,1,1024]{2,1,0:T(1,128)} %bitcast.350, s32[1,1024,128]{2,1,0:T(8,128)} %broadcast_in_dim.48.ck, bf16[1,1024,640]{2,1,0:T(8,128)(2,1)} %fusion.37.q, ...), custom_call_target="tpu_custom_call" | custom-call | flops 10737418240 | bytes 6553600 | tf_op jit(solution)/shard_map/attn_fwd_a/pallas_call | solution.py:149
  115.8 18.2 %attn_fwd_a.3 = (f32[1,640,1024]{2,1,0:T(8,128)}, f32[1,16,1024]{2,1,0:T(8,128)}, f32[1,16,1024]{2,1,0:T(8,128)}) custom-call(s32[1,2,4]{2,1,0:T(2,128)} %get-tuple-element.138.flags, s32[1,1,1024]{2,1,0:T(1,128)} %bitcast.356, s32[1,1024,128]{2,1,0:T(8,128)} %broadcast_in_dim.53.ck, bf16[1,1024,640]{2,1,0:T(8,128)(2,1)} %fusion.40.q, ...), custom_call_target="tpu_custom_call" | custom-call | flops 10737418240 | bytes 6553600 | tf_op jit(solution)/shard_map/attn_fwd_a/pallas_call | solution.py:149
  163.3 17.2 %attn_fwd_b.2 = (bf16[1,1024,640]{2,1,0:T(8,128)(2,1)}, f32[1,16,1024]{2,1,0:T(8,128)}) custom-call(s32[1,2,4]{2,1,0:T(2,128)} %get-tuple-element.141.flags, s32[1,1,1024]{2,1,0:T(1,128)} %bitcast.351, s32[1,1024,128]{2,1,0:T(8,128)} %broadcast_in_dim.46.ck, bf16[1,1024,640]{2,1,0:T(8,128)(2,1)} %fusion.37.q, bf16[1,1024,640]{2,1,0:T(8,128)(2,1)} %fusion.43.k, ...), custom_call_target="tpu_custom_call" | custom-call | flops 10737418240 | bytes 6553600 | tf_op jit(solution)/shard_map/attn_fwd_b/pallas_call | solution.py:149
  191.9 37.4 %ffn.1 = (bf16[1024,5120]{1,0:T(8,128)(2,1)}, bf16[1024,2560]{1,0:T(8,128)(2,1)}, bf16[1024,2560]{1,0:T(8,128)(2,1)}, f32[1,5120]{1,0:T(1,128)}) custom-call(s32[1]{0:T(128)} %bitcast.37.core, bf16[1024,1280]{1,0:T(8,128)(2,1)} %add_convert_fusion.4.acts.refs_0_, bf16[1280,5120]{1,0:T(8,128)(2,1)} %w.1, f32[1,5120]{1,0:T(1,128)} %bitcast.378, ...), custom_call_target="tpu_custom_call" | custom-call | flops 13421772800 | bytes 47185920 | tf_op jit(solution)/shard_map/ffn/pallas_call | solution.py:295
  229.3 12.4 %fusion = f32[1024,1280]{1,0:T(8,128)} fusion(bf16[1024,2560]{1,0:T(8,128)(2,1)} %get-tuple-element.61.refs_1_, bf16[1280,5120]{1,0:T(8,128)(2,1)} %w.1, s32[]{:T(128)S(6)} %select_n.251), kind=kOutput, calls=%fused_computation.1 | convolution fusion | flops 6710886400 | bytes 17039364 | tf_op jit(solution)/shard_map/dot_general | solution.py:27
  241.8 14.4 %multiply_reduce_fusion = (f32[1280]{0:T(1024)S(1)}, f32[1024]{0:T(1024)S(1)}, f32[1024]{0:T(1024)S(1)}, f32[1280]{0:T(1024)S(1)}, f32[1024,1280]{1,0:T(8,128)}) fusion(f32[1024,1280]{1,0:T(8,128)S(1)} %bitcast.318, f32[1024]{0:T(1024)S(1)} %add_rsqrt_fusion, f32[1024]{0:T(1024)S(1)} %broadcast_multiply_fusion.4, f32[1280]{0:T(1024)S(1)} %copy-done.33, ...), kind=kOutput, calls=%fused_computation.27 | convolution fusion | flops 6723989504 | bytes 27556868 | tf_op jit(solution)/shard_map/dot_general | solution.py:27
  277.9 29.2 %attn_bwd_a.2 = (f32[1,640,1024]{2,1,0:T(8,128)}, bf16[1,1024,640]{2,1,0:T(8,128)(2,1)}, bf16[1,1024,640]{2,1,0:T(8,128)(2,1)}) custom-call(s32[1,2,4]{2,1,0:T(2,128)} %get-tuple-element.141.flags, s32[1,1,1024]{2,1,0:T(1,128)} %bitcast.352, s32[1,1024,128]{2,1,0:T(8,128)} %broadcast_in_dim.46.ck, bf16[1,1024,640]{2,1,0:T(8,128)(2,1)} %fusion.37.q, ...), custom_call_target="tpu_custom_call" | custom-call | flops 26843545600 | bytes 11796480 | tf_op jit(solution)/shard_map/attn_bwd_a/pallas_call | solution.py:239
  307.1 33.3 %attn_bwd_b.2 = (bf16[1,1024,640]{2,1,0:T(8,128)(2,1)}, bf16[1,1024,640]{2,1,0:T(8,128)(2,1)}, bf16[1,1024,640]{2,1,0:T(8,128)(2,1)}) custom-call(s32[1,2,4]{2,1,0:T(2,128)} %get-tuple-element.140.flags, s32[1,1,1024]{2,1,0:T(1,128)} %bitcast.353, s32[1,1024,128]{2,1,0:T(8,128)} %broadcast_in_dim.48.ck, bf16[1,1024,640]{2,1,0:T(8,128)(2,1)} %fusion.37.q, ...), custom_call_target="tpu_custom_call" | custom-call | flops 26843545600 | bytes 11796480 | tf_op jit(solution)/shard_map/attn_bwd_b/pallas_call | solution.py:239
  365.5 17.3 %fusion.25 = bf16[1,1024,1280]{2,1,0:T(8,128)(2,1)} fusion(f32[1024,1280]{1,0:T(8,128)S(1)} %bitcast.320, bf16[1024,5120]{1,0:T(8,128)(2,1)} %get-tuple-element.59.a1, bf16[5120,1280]{1,0:T(8,128)(2,1)S(1)} %bitcast.375, f32[1280]{0:T(1024)S(1)} %copy-done.45), kind=kOutput, calls=%fused_computation.41 | convolution fusion | flops 13425704960 | bytes 31462400 | tf_op jit(solution)/shard_map/dot_general | solution.py:27
  384.6 11.9 %collective-permute-start.46 = (f32[1,2,640]{2,1,0:T(2,128)S(1)}, f32[1,2,640]{2,1,0:T(2,128)S(1)}, u32[]{:S(2)}, u32[]{:S(2)}) collective-permute-start(f32[1,2,640]{2,1,0:T(2,128)S(1)} %fusion.156), channel_id=1, source_target_pairs={{0,4},{2,6},{4,0},{6,2},{8,12},{10,14},{12,8},{14,10},{16,20},{18,... | collective-permute-start | bytes 15368 | tf_op jit(solution)/shard_map/ppermute | solution.py:494
  404.9 12.6 %attn_bwd_a.3 = (f32[1,640,1024]{2,1,0:T(8,128)}, bf16[1,1024,640]{2,1,0:T(8,128)(2,1)}, bf16[1,1024,640]{2,1,0:T(8,128)(2,1)}) custom-call(s32[1,2,4]{2,1,0:T(2,128)} %get-tuple-element.139.flags, s32[1,1,1024]{2,1,0:T(1,128)} %bitcast.358, s32[1,1024,128]{2,1,0:T(8,128)} %broadcast_in_dim.51.ck, bf16[1,1024,640]{2,1,0:T(8,128)(2,1)} %fusion.40.q, ...), custom_call_target="tpu_custom_call" | custom-call | flops 26843545600 | bytes 11796480 | tf_op jit(solution)/shard_map/attn_bwd_a/pallas_call | solution.py:239
  417.5 33.2 %attn_bwd_b.3 = (bf16[1,1024,640]{2,1,0:T(8,128)(2,1)}, bf16[1,1024,640]{2,1,0:T(8,128)(2,1)}, bf16[1,1024,640]{2,1,0:T(8,128)(2,1)}) custom-call(s32[1,2,4]{2,1,0:T(2,128)} %get-tuple-element.138.flags, s32[1,1,1024]{2,1,0:T(1,128)} %bitcast.359, s32[1,1024,128]{2,1,0:T(8,128)} %broadcast_in_dim.53.ck, bf16[1,1024,640]{2,1,0:T(8,128)(2,1)} %fusion.40.q, ...), custom_call_target="tpu_custom_call" | custom-call | flops 26843545600 | bytes 11796480 | tf_op jit(solution)/shard_map/attn_bwd_b/pallas_call | solution.py:239
  459.7 10.5 %grad_out.1 = (bf16[4,160,640]{2,1,0:T(8,128)(2,1)}, bf16[4,160,640]{2,1,0:T(8,128)(2,1)}) custom-call(s32[2]{0:T(128)} %pad_add_fusion.1.where, bf16[1024,640]{1,0:T(8,128)(2,1)} %bitcast.331, bf16[1024,1280]{1,0:T(8,128)(2,1)} %copy-done.6, bf16[1024,640]{1,0:T(8,128)(2,1)} %bitcast.329, bf16[1024,640]{1,0:T(8,128)(2,1)} %copy-done.12, ...), custom_call_target="tpu_custom_call" | custom-call | flops 3355443200 | bytes 12124160 | tf_op jit(solution)/shard_map/grad_out/pallas_call | solution.py:369
  470.2 24.9 %collective-permute-start.37 = (bf16[4,160,640]{2,1,0:T(8,128)(2,1)}, bf16[4,160,640]{2,1,0:T(8,128)(2,1)}, u32[]{:S(2)}, u32[]{:S(2)}) collective-permute-start(bf16[4,160,640]{2,1,0:T(8,128)(2,1)} %get-tuple-element.83), channel_id=1, source_target_pairs={{0,4},{2,6},{4,0},{6,2},{8,12},{10,14},{12,8},{14,10},{16,20},{18,... | collective-permute-start | bytes 2457608 | tf_op jit(solution)/shard_map/ppermute | solution.py:494
  495.6 15.9 %grad_v.1 = (bf16[4,160,640]{2,1,0:T(8,128)(2,1)}, bf16[4,160,640]{2,1,0:T(8,128)(2,1)}) custom-call(s32[2]{0:T(128)} %pad_add_fusion.where, bf16[1024,1280]{1,0:T(8,128)(2,1)} %fusion.13.refs_0_, bf16[1024,640]{1,0:T(8,128)(2,1)} %bitcast.334, bf16[1024,1280]{1,0:T(8,128)(2,1)} %collective-permute-done.4.refs_2_, bf16[1024,640]{1,0:T(8,128)(2,1)} %bitcast.323, ...), custom_call_target="tpu_custom_call" | custom-call | flops 6710886400 | bytes 17367040 | tf_op jit(solution)/shard_map/grad_v/pallas_call | solution.py:369
  517.6 15.8 %grad_k.1 = (bf16[4,160,640]{2,1,0:T(8,128)(2,1)}, bf16[4,160,640]{2,1,0:T(8,128)(2,1)}) custom-call(s32[2]{0:T(128)} %pad_add_fusion.where, bf16[1024,1280]{1,0:T(8,128)(2,1)} %fusion.13.refs_0_, bf16[1024,640]{1,0:T(8,128)(2,1)} %bitcast.380, bf16[1024,1280]{1,0:T(8,128)(2,1)} %collective-permute-done.4.refs_2_, bf16[1024,640]{1,0:T(8,128)(2,1)} %bitcast.382, ...), custom_call_target="tpu_custom_call" | custom-call | flops 6710886400 | bytes 17367040 | tf_op jit(solution)/shard_map/grad_k/pallas_call | solution.py:369
  598.2 11.9 %collective-permute-done.31 = bf16[160,640]{1,0:T(8,128)(2,1)S(1)} collective-permute-done((bf16[160,640]{1,0:T(8,128)(2,1)S(1)}, bf16[160,640]{1,0:T(8,128)(2,1)S(1)}, u32[]{:S(2)}, u32[]{:S(2)}) %collective-permute-start.31) | collective-permute-done | bytes 204832 | tf_op jit(solution)/shard_map/ppermute | solution.py:494
  618.6 10.1 %collective-permute-done.25 = bf16[160,640]{1,0:T(8,128)(2,1)S(1)} collective-permute-done((bf16[160,640]{1,0:T(8,128)(2,1)S(1)}, bf16[160,640]{1,0:T(8,128)(2,1)S(1)}, u32[]{:S(2)}, u32[]{:S(2)}) %collective-permute-start.25) | collective-permute-done | bytes 204832 | tf_op jit(solution)/shard_map/ppermute | solution.py:494
  689.3 20.6 %grad_in.1 = (bf16[4,160,2560]{2,1,0:T(8,128)(2,1)}, bf16[4,160,2560]{2,1,0:T(8,128)(2,1)}) custom-call(s32[2]{0:T(128)} %pad_add_fusion.where, bf16[1024,1280]{1,0:T(8,128)(2,1)} %add_convert_fusion.4.acts.refs_0_, bf16[1024,2560]{1,0:T(8,128)(2,1)} %get-tuple-element.61.refs_1_, bf16[1024,1280]{1,0:T(8,128)(2,1)} %copy-done.43, bf16[1024,2560]{1,0:T(8,128)(2,1)} %copy-done.41), custom_call_target="tpu_custom_call" | custom-call | flops 13421772800 | bytes 22282240 | tf_op jit(solution)/shard_map/grad_in/pallas_call | solution.py:369
  712.0 29.6 %collective-permute-done.10 = bf16[1024,1280]{1,0:T(8,128)(2,1)} collective-permute-done((bf16[1024,1280]{1,0:T(8,128)(2,1)}, bf16[1024,1280]{1,0:T(8,128)(2,1)}, u32[]{:S(2)}, u32[]{:S(2)}) %collective-permute-start.10) | collective-permute-done | bytes 2621472 | tf_op jit(solution)/shard_map/ppermute | solution.py:503
  741.6 10.7 %fusion.19 = (f32[1280]{0:T(1024)S(1)}, f32[1024]{0:T(1024)S(1)}, f32[1024]{0:T(1024)S(1)}, f32[1280]{0:T(1024)S(1)}, f32[1024,1280]{1,0:T(8,128)}) fusion(bf16[1,1024,1280]{2,1,0:T(8,128)(2,1)S(1)} %copy-done.4, f32[1024]{0:T(1024)S(1)} %copy-done.32, f32[1024]{0:T(1024)S(1)} %copy-done.28, f32[1280]{0:T(1024)S(1)} %copy-done.30, ...), kind=kLoop, calls=%fused_computation.24 | loop fusion | flops 20966912 | bytes 28867584 | tf_op jit(solution)/shard_map/reduce_sum | solution.py:722
  765.6 18.2 %collective-permute-done.14 = f32[1,2,320]{2,1,0:T(2,128)S(1)} collective-permute-done((f32[1,2,320]{2,1,0:T(2,128)S(1)}, f32[1,2,320]{2,1,0:T(2,128)S(1)}, u32[]{:S(2)}, u32[]{:S(2)}) %collective-permute-start.14) | collective-permute-done | bytes 2592 | tf_op jit(solution)/shard_map/ppermute | solution.py:494
  785.7 13.4 %grad_back.3 = bf16[4,640,640]{2,1,0:T(8,128)(2,1)} custom-call(s32[2]{0:T(128)} %pad_add_fusion.where, bf16[1024,5120]{1,0:T(8,128)(2,1)} %get-tuple-element.59.a1, bf16[1024,1280]{1,0:T(8,128)(2,1)} %bitcast.321, bf16[1024,5120]{1,0:T(8,128)(2,1)} %collective-permute-done.57.a2, bf16[1024,640]{1,0:T(8,128)(2,1)} %collective-permute-done.58.b2), custom_call_target="tpu_custom_call" | custom-call | flops 6710886400 | bytes 16384000 | tf_op jit(solution)/shard_map/grad_back/pallas_call | solution.py:410
  815.8 26.0 %collective-permute-done.52 = bf16[160,2560]{1,0:T(8,128)(2,1)S(1)} collective-permute-done((bf16[160,2560]{1,0:T(8,128)(2,1)S(1)}, bf16[160,2560]{1,0:T(8,128)(2,1)S(1)}, u32[]{:S(2)}, u32[]{:S(2)}) %collective-permute-start.52) | collective-permute-done | bytes 819232 | tf_op jit(solution)/shard_map/ppermute | solution.py:494
  841.8 22.1 %collective-permute-done.53 = bf16[160,2560]{1,0:T(8,128)(2,1)S(1)} collective-permute-done((bf16[160,2560]{1,0:T(8,128)(2,1)S(1)}, bf16[160,2560]{1,0:T(8,128)(2,1)S(1)}, u32[]{:S(2)}, u32[]{:S(2)}) %collective-permute-start.53) | collective-permute-done | bytes 819232 | tf_op jit(solution)/shard_map/ppermute | solution.py:494
  867.6 13.5 %grad_back.2 = bf16[4,640,640]{2,1,0:T(8,128)(2,1)} custom-call(s32[2]{0:T(128)} %pad_add_fusion.where, bf16[1024,5120]{1,0:T(8,128)(2,1)} %get-tuple-element.59.a1, bf16[1024,1280]{1,0:T(8,128)(2,1)} %bitcast.322, bf16[1024,5120]{1,0:T(8,128)(2,1)} %collective-permute-done.57.a2, bf16[1024,640]{1,0:T(8,128)(2,1)} %collective-permute-done.58.b2), custom_call_target="tpu_custom_call" | custom-call | flops 6710886400 | bytes 16384000 | tf_op jit(solution)/shard_map/grad_back/pallas_call | solution.py:410
  884.0 16.5 %collective-permute-start.60 = (bf16[640,640]{1,0:T(8,128)(2,1)S(1)}, bf16[640,640]{1,0:T(8,128)(2,1)S(1)}, u32[]{:S(2)}, u32[]{:S(2)}) collective-permute-start(bf16[640,640]{1,0:T(8,128)(2,1)S(1)} %get-tuple-element.99), channel_id=1, source_target_pairs={{0,8},{2,10},{4,12},{6,14},{8,0},{10,2},{12,4},{14,6},{16,24},{18,... | collective-permute-start | bytes 2457608 | tf_op jit(solution)/shard_map/ppermute | solution.py:494
  903.3 29.8 %collective-permute-done.60 = bf16[640,640]{1,0:T(8,128)(2,1)S(1)} collective-permute-done((bf16[640,640]{1,0:T(8,128)(2,1)S(1)}, bf16[640,640]{1,0:T(8,128)(2,1)S(1)}, u32[]{:S(2)}, u32[]{:S(2)}) %collective-permute-start.60) | collective-permute-done | bytes 819232 | tf_op jit(solution)/shard_map/ppermute | solution.py:494
  933.1 24.7 %collective-permute-done.61 = bf16[640,640]{1,0:T(8,128)(2,1)S(1)} collective-permute-done((bf16[640,640]{1,0:T(8,128)(2,1)S(1)}, bf16[640,640]{1,0:T(8,128)(2,1)S(1)}, u32[]{:S(2)}, u32[]{:S(2)}) %collective-permute-start.61) | collective-permute-done | bytes 819232 | tf_op jit(solution)/shard_map/ppermute | solution.py:494
  960.7 13.1 %collective-permute-done.63 = bf16[640,640]{1,0:T(8,128)(2,1)S(1)} collective-permute-done((bf16[640,640]{1,0:T(8,128)(2,1)S(1)}, bf16[640,640]{1,0:T(8,128)(2,1)S(1)}, u32[]{:S(2)}, u32[]{:S(2)}) %collective-permute-start.63) | collective-permute-done | bytes 819232 | tf_op jit(solution)/shard_map/ppermute | solution.py:500
  (395 shorter events, 359.1 us)
Async XLA Ops:
  6.7 87.3 %collective-permute-start.4 = (bf16[1024,1280]{1,0:T(8,128)(2,1)}, bf16[1024,1280]{1,0:T(8,128)(2,1)}, u32[]{:S(2)}, u32[]{:S(2)}) collective-permute-start(bf16[1024,1280]{1,0:T(8,128)(2,1)} %fusion.13.refs_0_), channel_id=1, source_target_pairs={{0,2},{2,0},{4,6},{6,4},{8,10},{10,8},{12,14},{14,12},{16,18},{18,... | collective-permute-start | bytes 7864328 | tf_op jit(solution)/shard_map/ppermute | solution.py:494
  7.2 81.0 %collective-permute-start.1 = (bf16[1024,1280]{1,0:T(8,128)(2,1)}, bf16[1024,1280]{1,0:T(8,128)(2,1)}, u32[]{:S(2)}, u32[]{:S(2)}) collective-permute-start(bf16[1024,1280]{1,0:T(8,128)(2,1)} %fusion.13.refs_0_), channel_id=1, source_target_pairs={{1,0},{0,1},{3,2},{2,3},{5,4},{4,5},{7,6},{6,7},{9,8},{8,9},{11,10... | collective-permute-start | bytes 7864328 | tf_op jit(solution)/shard_map/ppermute | solution.py:500
  9.8 42.4 %collective-permute-start.2 = (s32[1,1024]{1,0:T(1,128)S(1)}, s32[1,1024]{1,0:T(1,128)S(1)}, u32[]{:S(2)}, u32[]{:S(2)}) collective-permute-start(s32[1,1024]{1,0:T(1,128)S(1)} %copy-done.37), channel_id=1, source_target_pairs={{0,2},{2,0},{4,6},{6,4},{8,10},{10,8},{12,14},{14,12},{16,18},{18,... | collective-permute-start | bytes 12296 | tf_op jit(solution)/shard_map/ppermute | solution.py:494
  9.9 57.7 %collective-permute-start = (s32[1,1024]{1,0:T(1,128)S(1)}, s32[1,1024]{1,0:T(1,128)S(1)}, u32[]{:S(2)}, u32[]{:S(2)}) collective-permute-start(s32[1,1024]{1,0:T(1,128)S(1)} %copy-done.37), channel_id=1, source_target_pairs={{1,0},{0,1},{3,2},{2,3},{5,4},{4,5},{7,6},{6,7},{9,8},{8,9},{11,10... | collective-permute-start | bytes 12296 | tf_op jit(solution)/shard_map/ppermute | solution.py:500
  52.4 34.9 %collective-permute-start.3 = (s32[1,1024]{1,0:T(1,128)S(1)}, s32[1,1024]{1,0:T(1,128)S(1)}, u32[]{:S(2)}, u32[]{:S(2)}) collective-permute-start(s32[1,1024]{1,0:T(1,128)S(1)} %collective-permute-done.2), channel_id=1, source_target_pairs={{1,0},{0,1},{3,2},{2,3},{5,4},{4,5},{7,6},{6,7},{9,8},{8,9},{11,10... | collective-permute-start | bytes 12296 | tf_op jit(solution)/shard_map/ppermute | solution.py:500
  88.2 45.7 %collective-permute-start.5 = (bf16[1024,1280]{1,0:T(8,128)(2,1)}, bf16[1024,1280]{1,0:T(8,128)(2,1)S(1)}, u32[]{:S(2)}, u32[]{:S(2)}) collective-permute-start(bf16[1024,1280]{1,0:T(8,128)(2,1)} %collective-permute-done.1.refs_4_), channel_id=1, source_target_pairs={{0,2},{2,0},{4,6},{6,4},{8,10},{10,8},{12,14},{14,12},{16,18},{18,... | collective-permute-start | bytes 7864328 | tf_op jit(solution)/shard_map/ppermute | solution.py:494
  180.5 278.1 %collective-permute-start.36 = (bf16[1024,640]{1,0:T(8,128)(2,1)}, bf16[1024,640]{1,0:T(8,128)(2,1)}, u32[]{:S(2)}, u32[]{:S(2)}) collective-permute-start(bf16[1024,640]{1,0:T(8,128)(2,1)} %bitcast.330), channel_id=1, source_target_pairs={{0,2},{2,0},{4,6},{6,4},{8,10},{10,8},{12,14},{14,12},{16,18},{18,... | collective-permute-start | bytes 3932168 | tf_op jit(solution)/shard_map/ppermute | solution.py:494
  268.7 517.0 %collective-permute-start.57 = (bf16[1024,5120]{1,0:T(8,128)(2,1)}, bf16[1024,5120]{1,0:T(8,128)(2,1)}, u32[]{:S(2)}, u32[]{:S(2)}) collective-permute-start(bf16[1024,5120]{1,0:T(8,128)(2,1)} %get-tuple-element.59.a1), channel_id=1, source_target_pairs={{0,2},{2,0},{4,6},{6,4},{8,10},{10,8},{12,14},{14,12},{16,18},{18,... | collective-permute-start | bytes 31457288 | tf_op jit(solution)/shard_map/ppermute | solution.py:494
  271.0 113.1 %collective-permute-start.43 = (f32[1,4,640]{2,1,0:T(4,128)S(1)}, f32[1,4,640]{2,1,0:T(4,128)S(1)}, u32[]{:S(2)}, u32[]{:S(2)}) collective-permute-start(f32[1,4,640]{2,1,0:T(4,128)S(1)} %get-tuple-element.124), channel_id=1, source_target_pairs={{0,8},{2,10},{4,12},{6,14},{8,0},{10,2},{12,4},{14,6},{16,24},{18,... | collective-permute-start | bytes 30728 | tf_op jit(solution)/shard_map/ppermute | solution.py:494
  275.5 108.6 %collective-permute-start.44 = (f32[1,4,640]{2,1,0:T(4,128)S(1)}, f32[1,4,640]{2,1,0:T(4,128)S(1)}, u32[]{:S(2)}, u32[]{:S(2)}) collective-permute-start(f32[1,4,640]{2,1,0:T(4,128)S(1)} %get-tuple-element.126), channel_id=1, source_target_pairs={{0,16},{2,18},{4,20},{6,22},{8,24},{10,26},{12,28},{14,30},{16,0},... | collective-permute-start | bytes 30728 | tf_op jit(solution)/shard_map/ppermute | solution.py:494
  275.5 109.1 %collective-permute-start.45 = (f32[1,4,640]{2,1,0:T(4,128)S(1)}, f32[1,4,640]{2,1,0:T(4,128)S(1)}, u32[]{:S(2)}, u32[]{:S(2)}) collective-permute-start(f32[1,4,640]{2,1,0:T(4,128)S(1)} %get-tuple-element.125), channel_id=1, source_target_pairs={{0,24},{2,26},{4,28},{6,30},{8,16},{10,18},{12,20},{14,22},{16,8},... | collective-permute-start | bytes 30728 | tf_op jit(solution)/shard_map/ppermute | solution.py:494
  384.0 74.6 %collective-permute-start.35 = (bf16[1024,640]{1,0:T(8,128)(2,1)}, bf16[1024,640]{1,0:T(8,128)(2,1)S(1)}, u32[]{:S(2)}, u32[]{:S(2)}) collective-permute-start(bf16[1024,640]{1,0:T(8,128)(2,1)} %constant_dynamic-slice_fusion.4), channel_id=1, source_target_pairs={{0,2},{2,0},{4,6},{6,4},{8,10},{10,8},{12,14},{14,12},{16,18},{18,... | collective-permute-start | bytes 3932168 | tf_op jit(solution)/shard_map/ppermute | solution.py:494
  470.2 90.0 %collective-permute-start.37 = (bf16[4,160,640]{2,1,0:T(8,128)(2,1)}, bf16[4,160,640]{2,1,0:T(8,128)(2,1)}, u32[]{:S(2)}, u32[]{:S(2)}) collective-permute-start(bf16[4,160,640]{2,1,0:T(8,128)(2,1)} %get-tuple-element.83), channel_id=1, source_target_pairs={{0,4},{2,6},{4,0},{6,2},{8,12},{10,14},{12,8},{14,10},{16,20},{18,... | collective-permute-start | bytes 2457608 | tf_op jit(solution)/shard_map/ppermute | solution.py:494
  511.5 50.3 %collective-permute-start.29 = (bf16[4,160,640]{2,1,0:T(8,128)(2,1)}, bf16[4,160,640]{2,1,0:T(8,128)(2,1)}, u32[]{:S(2)}, u32[]{:S(2)}) collective-permute-start(bf16[4,160,640]{2,1,0:T(8,128)(2,1)} %get-tuple-element.81), channel_id=1, source_target_pairs={{0,4},{2,6},{4,0},{6,2},{8,12},{10,14},{12,8},{14,10},{16,20},{18,... | collective-permute-start | bytes 2457608 | tf_op jit(solution)/shard_map/ppermute | solution.py:494
  533.4 38.2 %collective-permute-start.23 = (bf16[4,160,640]{2,1,0:T(8,128)(2,1)}, bf16[4,160,640]{2,1,0:T(8,128)(2,1)}, u32[]{:S(2)}, u32[]{:S(2)}) collective-permute-start(bf16[4,160,640]{2,1,0:T(8,128)(2,1)} %get-tuple-element.79), channel_id=1, source_target_pairs={{0,4},{2,6},{4,0},{6,2},{8,12},{10,14},{12,8},{14,10},{16,20},{18,... | collective-permute-start | bytes 2457608 | tf_op jit(solution)/shard_map/ppermute | solution.py:494
  560.3 125.3 %collective-permute-start.50 = (bf16[1024,2560]{1,0:T(8,128)(2,1)S(1)}, bf16[1024,2560]{1,0:T(8,128)(2,1)S(1)}, u32[]{:S(2)}, u32[]{:S(2)}) collective-permute-start(bf16[1024,2560]{1,0:T(8,128)(2,1)S(1)} %bitcast.377), channel_id=1, source_target_pairs={{0,2},{2,0},{4,6},{6,4},{8,10},{10,8},{12,14},{14,12},{16,18},{18,... | collective-permute-start | bytes 15728648 | tf_op jit(solution)/shard_map/ppermute | solution.py:494
  589.9 85.0 %collective-permute-start.9 = (bf16[1024,1280]{1,0:T(8,128)(2,1)S(1)}, bf16[1024,1280]{1,0:T(8,128)(2,1)S(1)}, u32[]{:S(2)}, u32[]{:S(2)}) collective-permute-start(bf16[1024,1280]{1,0:T(8,128)(2,1)S(1)} %add_convert_fusion.1), channel_id=1, source_target_pairs={{0,2},{2,0},{4,6},{6,4},{8,10},{10,8},{12,14},{14,12},{16,18},{18,... | collective-permute-start | bytes 7864328 | tf_op jit(solution)/shard_map/ppermute | solution.py:494
  647.3 38.1 %collective-permute-start.49 = (bf16[1024,1280]{1,0:T(8,128)(2,1)S(1)}, bf16[1024,1280]{1,0:T(8,128)(2,1)S(1)}, u32[]{:S(2)}, u32[]{:S(2)}) collective-permute-start(bf16[1024,1280]{1,0:T(8,128)(2,1)S(1)} %copy-done.14), channel_id=1, source_target_pairs={{0,2},{2,0},{4,6},{6,4},{8,10},{10,8},{12,14},{14,12},{16,18},{18,... | collective-permute-start | bytes 7864328 | tf_op jit(solution)/shard_map/ppermute | solution.py:494
  682.1 59.5 %collective-permute-start.10 = (bf16[1024,1280]{1,0:T(8,128)(2,1)}, bf16[1024,1280]{1,0:T(8,128)(2,1)}, u32[]{:S(2)}, u32[]{:S(2)}) collective-permute-start(bf16[1024,1280]{1,0:T(8,128)(2,1)} %add_convert_fusion), channel_id=1, source_target_pairs={{0,1},{1,0},{2,3},{3,2},{4,5},{5,4},{6,7},{7,6},{8,9},{9,8},{10,11... | collective-permute-start | bytes 7864328 | tf_op jit(solution)/shard_map/ppermute | solution.py:503
  685.4 100.3 %collective-permute-start.58 = (bf16[1024,640]{1,0:T(8,128)(2,1)}, bf16[1024,640]{1,0:T(8,128)(2,1)}, u32[]{:S(2)}, u32[]{:S(2)}) collective-permute-start(bf16[1024,640]{1,0:T(8,128)(2,1)} %dynamic-slice_bitcast_fusion), channel_id=1, source_target_pairs={{0,2},{2,0},{4,6},{6,4},{8,10},{10,8},{12,14},{14,12},{16,18},{18,... | collective-permute-start | bytes 3932168 | tf_op jit(solution)/shard_map/ppermute | solution.py:494
  689.3 67.2 %collective-permute-start.34 = (bf16[80,640]{1,0:T(8,128)(2,1)S(1)}, bf16[80,640]{1,0:T(8,128)(2,1)S(1)}, u32[]{:S(2)}, u32[]{:S(2)}) collective-permute-start(bf16[80,640]{1,0:T(8,128)(2,1)S(1)} %dynamic-slice_bitcast_fusion.4), channel_id=1, source_target_pairs={{0,2},{2,0},{4,6},{6,4},{8,10},{10,8},{12,14},{14,12},{16,18},{18,... | collective-permute-start | bytes 307208 | tf_op jit(solution)/shard_map/ppermute | solution.py:494
  709.9 91.0 %collective-permute-start.51 = (bf16[4,160,2560]{2,1,0:T(8,128)(2,1)}, bf16[4,160,2560]{2,1,0:T(8,128)(2,1)}, u32[]{:S(2)}, u32[]{:S(2)}) collective-permute-start(bf16[4,160,2560]{2,1,0:T(8,128)(2,1)} %get-tuple-element.86), channel_id=1, source_target_pairs={{0,4},{2,6},{4,0},{6,2},{8,12},{10,14},{12,8},{14,10},{16,20},{18,... | collective-permute-start | bytes 9830408 | tf_op jit(solution)/shard_map/ppermute | solution.py:494
  785.1 30.7 %collective-permute-start.16 = (f32[320]{0:T(512)S(1)}, f32[320]{0:T(512)S(1)}, u32[]{:S(2)}, u32[]{:S(2)}) collective-permute-start(f32[320]{0:T(512)S(1)} %fusion.163), channel_id=1, source_target_pairs={{1,0},{0,1},{3,2},{2,3},{5,4},{4,5},{7,6},{6,7},{9,8},{8,9},{11,10... | collective-permute-start | bytes 3848 | tf_op jit(solution)/shard_map/ppermute | solution.py:500
  799.1 81.9 %collective-permute-start.59 = (bf16[4,640,640]{2,1,0:T(8,128)(2,1)}, bf16[4,640,640]{2,1,0:T(8,128)(2,1)}, u32[]{:S(2)}, u32[]{:S(2)}) collective-permute-start(bf16[4,640,640]{2,1,0:T(8,128)(2,1)} %grad_back.3), channel_id=1, source_target_pairs={{0,4},{2,6},{4,0},{6,2},{8,12},{10,14},{12,8},{14,10},{16,20},{18,... | collective-permute-start | bytes 9830408 | tf_op jit(solution)/shard_map/ppermute | solution.py:494
  803.1 38.6 %collective-permute-start.52 = (bf16[160,2560]{1,0:T(8,128)(2,1)S(1)}, bf16[160,2560]{1,0:T(8,128)(2,1)S(1)}, u32[]{:S(2)}, u32[]{:S(2)}) collective-permute-start(bf16[160,2560]{1,0:T(8,128)(2,1)S(1)} %get-tuple-element.102), channel_id=1, source_target_pairs={{0,8},{2,10},{4,12},{6,14},{8,0},{10,2},{12,4},{14,6},{16,24},{18,... | collective-permute-start | bytes 2457608 | tf_op jit(solution)/shard_map/ppermute | solution.py:494
  806.6 57.2 %collective-permute-start.53 = (bf16[160,2560]{1,0:T(8,128)(2,1)S(1)}, bf16[160,2560]{1,0:T(8,128)(2,1)S(1)}, u32[]{:S(2)}, u32[]{:S(2)}) collective-permute-start(bf16[160,2560]{1,0:T(8,128)(2,1)S(1)} %get-tuple-element.104), channel_id=1, source_target_pairs={{0,16},{2,18},{4,20},{6,22},{8,24},{10,26},{12,28},{14,30},{16,0},... | collective-permute-start | bytes 2457608 | tf_op jit(solution)/shard_map/ppermute | solution.py:494
  807.9 55.9 %collective-permute-start.54 = (bf16[160,2560]{1,0:T(8,128)(2,1)S(1)}, bf16[160,2560]{1,0:T(8,128)(2,1)S(1)}, u32[]{:S(2)}, u32[]{:S(2)}) collective-permute-start(bf16[160,2560]{1,0:T(8,128)(2,1)S(1)} %get-tuple-element.103), channel_id=1, source_target_pairs={{0,24},{2,26},{4,28},{6,30},{8,16},{10,18},{12,20},{14,22},{16,8},... | collective-permute-start | bytes 2457608 | tf_op jit(solution)/shard_map/ppermute | solution.py:494
  865.5 37.5 %collective-permute-start.55 = (bf16[160,2560]{1,0:T(8,128)(2,1)S(1)}, bf16[160,2560]{1,0:T(8,128)(2,1)S(1)}, u32[]{:S(2)}, u32[]{:S(2)}) collective-permute-start(bf16[160,2560]{1,0:T(8,128)(2,1)S(1)} %fusion.31), channel_id=1, source_target_pairs={{1,0},{0,1},{3,2},{2,3},{5,4},{4,5},{7,6},{6,7},{9,8},{8,9},{11,10... | collective-permute-start | bytes 2457608 | tf_op jit(solution)/shard_map/ppermute | solution.py:500
  884.0 49.1 %collective-permute-start.60 = (bf16[640,640]{1,0:T(8,128)(2,1)S(1)}, bf16[640,640]{1,0:T(8,128)(2,1)S(1)}, u32[]{:S(2)}, u32[]{:S(2)}) collective-permute-start(bf16[640,640]{1,0:T(8,128)(2,1)S(1)} %get-tuple-element.99), channel_id=1, source_target_pairs={{0,8},{2,10},{4,12},{6,14},{8,0},{10,2},{12,4},{14,6},{16,24},{18,... | collective-permute-start | bytes 2457608 | tf_op jit(solution)/shard_map/ppermute | solution.py:494
  900.5 57.2 %collective-permute-start.61 = (bf16[640,640]{1,0:T(8,128)(2,1)S(1)}, bf16[640,640]{1,0:T(8,128)(2,1)S(1)}, u32[]{:S(2)}, u32[]{:S(2)}) collective-permute-start(bf16[640,640]{1,0:T(8,128)(2,1)S(1)} %get-tuple-element.101), channel_id=1, source_target_pairs={{0,16},{2,18},{4,20},{6,22},{8,24},{10,26},{12,28},{14,30},{16,0},... | collective-permute-start | bytes 2457608 | tf_op jit(solution)/shard_map/ppermute | solution.py:494
  901.6 56.1 %collective-permute-start.62 = (bf16[640,640]{1,0:T(8,128)(2,1)S(1)}, bf16[640,640]{1,0:T(8,128)(2,1)S(1)}, u32[]{:S(2)}, u32[]{:S(2)}) collective-permute-start(bf16[640,640]{1,0:T(8,128)(2,1)S(1)} %get-tuple-element.100), channel_id=1, source_target_pairs={{0,24},{2,26},{4,28},{6,30},{8,16},{10,18},{12,20},{14,22},{16,8},... | collective-permute-start | bytes 2457608 | tf_op jit(solution)/shard_map/ppermute | solution.py:494
  903.2 57.4 %collective-permute-start.56 = (bf16[80,2560]{1,0:T(8,128)(2,1)S(1)}, bf16[80,2560]{1,0:T(8,128)(2,1)S(1)}, u32[]{:S(2)}, u32[]{:S(2)}) collective-permute-start(bf16[80,2560]{1,0:T(8,128)(2,1)S(1)} %dynamic-slice_bitcast_fusion.2), channel_id=1, source_target_pairs={{0,2},{2,0},{4,6},{6,4},{8,10},{10,8},{12,14},{14,12},{16,18},{18,... | collective-permute-start | bytes 1228808 | tf_op jit(solution)/shard_map/ppermute | solution.py:494
  (95 other events, 1483.6 us)

commit v2 on v1

v2 whole, which is shorter than its diff:
```python
import functools
import math

import jax
import jax.numpy as jnp
from jax import lax
from jax.experimental import pallas as pl
from jax.experimental.pallas import tpu as pltpu
from jax.sharding import PartitionSpec as P

HEADS = 20
HEAD_DIM = 64
HD = HEAD_DIM
EPS = 1e-05
NEG = -1e30
LOG2E = math.log2(math.e)
C2 = LOG2E / math.sqrt(HEAD_DIM)
F32 = jnp.float32
BF = jnp.bfloat16
NN = (((1,), (0,)), ((), ()))
NT = (((1,), (1,)), ((), ()))
TN = (((0,), (0,)), ((), ()))
VMEM_LIMIT = 56 * 2**20
SHARE = 20


def dot(a, b, dims):
    return lax.dot_general(a, b, dims, preferred_element_type=F32)


def head_sumsq(x,hp16):
    W=x.shape[1]
    sq=x.astype(F32)*x.astype(F32)
    row=lax.broadcasted_iota(jnp.int32,(hp16,W),0); col=lax.broadcasted_iota(jnp.int32,(hp16,W),1)
    ones=jnp.where(row==col//HD,1.0,0.0).astype(BF)
    return lax.dot_general(ones,sq.astype(BF),NT,preferred_element_type=F32)

def fwd_kernel(flags,cq,ck,q,k,v,*rest,first,tq,tk,heads):
    if first:
        accT_o,m_o,l_o,qm,vT,bias,acc,m,l,kn=rest
    else:
        accT_i,m_i,l_i,o_o,lse_o,qm,vT,bias,acc,m,l,kn=rest
    r=pl.program_id(0); qi=pl.program_id(1)
    nk=k.shape[1]//tk
    hp16=m.shape[0]
    @pl.when(qi==0)
    def _():
        vT[...]=v[0].T
        kn[...]=jnp.broadcast_to(jnp.sqrt(jnp.max(head_sumsq(k[0],hp16),1,keepdims=True)),kn.shape)
    lane=lax.broadcasted_iota(jnp.int32,(tq,128),1)
    for hp in range(heads//2):
        qp=q[0,:,hp*128:(hp+1)*128]
        qm[2*hp]=jnp.where(lane<64,qp,0).astype(BF)
        qm[2*hp+1]=jnp.where(lane>=64,qp,0).astype(BF)
    bound=jnp.sqrt(head_sumsq(q[0],hp16))*kn[:,0:1]*(C2*1.02)
    safe=jnp.max(bound)<50.0
    if first:
        m0=bound
    else:
        m0=jnp.maximum(bound,m_i[0])
    def loop(online):
        if first:
            acc[...]=jnp.zeros_like(acc); l[...]=jnp.zeros_like(l)
            m[...]=jnp.full_like(m,NEG) if online else m0
        elif online:
            acc[...]=accT_i[0]; m[...]=m_i[0]; l[...]=l_i[0]
        else:
            al=jnp.exp2(m_i[0]-m0)
            m[...]=m0; l[...]=al*l_i[0]
            for hh in range(heads):
                hs=slice(hh*HD,(hh+1)*HD)
                acc[hs,:]=al[hh:hh+1,:]*accT_i[0,hs,:]
        def body(kt,masked):
            ks=pl.ds(pl.multiple_of(kt*tk,tk),tk)
            if online:
                @pl.loop(0,heads//2)
                def _(hp):
                    kp=k[0,ks,pl.ds(pl.multiple_of(hp*128,128),128)]
                    for j in range(2):
                        hh=2*hp+j
                        s=lax.dot_general(kp,qm[hh],NT,preferred_element_type=F32)*C2+bias[...]
                        mp=m[pl.ds(hh,1),:]
                        mn=jnp.maximum(mp,jnp.max(s,0,keepdims=True))
                        p=jnp.exp2(s-mn)
                        al=jnp.exp2(mp-mn)
                        m[pl.ds(hh,1),:]=mn
                        l[pl.ds(hh,1),:]=al*l[pl.ds(hh,1),:]+jnp.sum(p,0,keepdims=True)
                        hs=pl.ds(pl.multiple_of(hh*HD,HD),HD)
                        acc[hs,:]=al*acc[hs,:]+lax.dot_general(vT[hs,ks],p.astype(BF),NN,preferred_element_type=F32)
                return
            def score(hh):
                s=lax.dot_general(k[0,ks,(hh//2)*128:(hh//2+1)*128],qm[hh],NT,preferred_element_type=F32)*C2
                if masked: s=s+bias[...]
                return s
            s=score(0); pp=None
            for hh in range(heads+1):
                if hh+1<heads: sn=score(hh+1)
                if pp is not None:
                    hs=slice((hh-1)*HD,hh*HD)
                    acc[hs,:]+=lax.dot_general(vT[hs,ks],pp,NN,preferred_element_type=F32)
                if hh<heads:
                    p=jnp.exp2(s-m[hh:hh+1,:])
                    l[hh:hh+1,:]+=jnp.sum(p,0,keepdims=True)
                    pp=p.astype(BF)
                s=sn
        @pl.loop(0,nk)
        def _(kt):
            f=flags[r,qi,kt]
            def mask():
                ks=pl.ds(pl.multiple_of(kt*tk,tk),tk)
                bias[...]=jnp.where(ck[0,ks,0:1]==cq[0,0:1,:],0.0,NEG)
            if online:
                @pl.when(f>0)
                def _():
                    mask(); body(kt,True)
            else:
                @pl.when(f==1)
                def _():
                    mask(); body(kt,True)
                @pl.when(f==2)
                def _(): body(kt,False)
    @pl.when(safe)
    def _(): loop(False)
    @pl.when(jnp.logical_not(safe))
    def _(): loop(True)
    if first:
        accT_o[0]=acc[...]; m_o[0]=m[...]; l_o[0]=l[...]
    else:
        for hp in range(heads//2):
            parts=[]
            for hh in (2*hp,2*hp+1):
                parts.append(acc[hh*HD:(hh+1)*HD,:]/l[hh:hh+1,:])
            o_o[0,:,hp*128:(hp+1)*128]=jnp.concatenate(parts,0).T.astype(BF)
        lse_o[0]=m[...]+jnp.log2(l[...])

def attn_fwd(flags,cq,ck,q,kv,kb,state,tq,tk,heads):
    nr,S,_=q.shape; W=heads*HD; Sk=kv.shape[1]; hp16=-(-heads//8)*8
    first=state is None
    qs=lambda r,i,*_:(r,i,0); ts=lambda r,i,*_:(r,0,i); ks=lambda r,i,*_:(r,0,0)
    stspec=[pl.BlockSpec((1,W,tq),ts),pl.BlockSpec((1,hp16,tq),ts),pl.BlockSpec((1,hp16,tq),ts)]
    ins=[pl.BlockSpec((1,1,tq),ts),pl.BlockSpec((1,Sk,128),ks),pl.BlockSpec((1,tq,W),qs),pl.BlockSpec((1,Sk,W),lambda r,i,*_:(r,0,kb)),pl.BlockSpec((1,Sk,W),lambda r,i,*_:(r,0,kb+1))]
    if first:
        outs=stspec
        osh=[jax.ShapeDtypeStruct((nr,W,S),F32)]+[jax.ShapeDtypeStruct((nr,hp16,S),F32)]*2
    else:
        ins=ins+stspec
        outs=[pl.BlockSpec((1,tq,W),qs),pl.BlockSpec((1,hp16,tq),ts)]
        osh=[jax.ShapeDtypeStruct((nr,S,W),BF),jax.ShapeDtypeStruct((nr,hp16,S),F32)]
    fl=4*nr*S*Sk*W
    return pl.pallas_call(functools.partial(fwd_kernel,first=first,tq=tq,tk=tk,heads=heads),
        out_shape=osh,
        grid_spec=pltpu.PrefetchScalarGridSpec(num_scalar_prefetch=1,grid=(nr,S//tq),in_specs=ins,out_specs=outs,
          scratch_shapes=[pltpu.VMEM((heads,tq,128),BF),pltpu.VMEM((W,Sk),BF),pltpu.VMEM((tk,tq),F32),pltpu.VMEM((W,tq),F32),pltpu.VMEM((hp16,tq),F32),pltpu.VMEM((hp16,tq),F32),pltpu.VMEM((hp16,128),F32)]),
        compiler_params=pltpu.CompilerParams(dimension_semantics=("arbitrary","arbitrary"),vmem_limit_bytes=VMEM_LIMIT),
        cost_estimate=pl.CostEstimate(flops=fl//SHARE,bytes_accessed=nr*(S*W*2+2*Sk*W*2+S*W*4)//SHARE,transcendentals=0),
        name="attn_fwd_a" if first else "attn_fwd_b",
    )(flags,cq,ck,q,kv,kv,*(state or ()))

def bwd_kernel(flags,cq,ck,q,k,v,do,o,lse,*rest,first,tq,tk,heads):
    if first:
        dqT_o,dkv_o,qm,dom,kT,bias,dqT,dk,dv,delta=rest
    else:
        dqT_i,dqkv_o,qm,dom,kT,bias,dqT,dk,dv,delta=rest
    r=pl.program_id(0); qi=pl.program_id(1); nq=pl.num_programs(1)
    nk=k.shape[1]//tk
    @pl.when(qi==0)
    def _():
        kT[...]=k[0].T
        dk[...]=jnp.zeros_like(dk); dv[...]=jnp.zeros_like(dv)
    lane=lax.broadcasted_iota(jnp.int32,(tq,128),1)
    for hp in range(heads//2):
        c=slice(hp*128,(hp+1)*128)
        qp=q[0,:,c]*jnp.asarray(0.125,BF); dp_=do[0,:,c]
        qm[2*hp]=jnp.where(lane<64,qp,0).astype(BF)
        qm[2*hp+1]=jnp.where(lane>=64,qp,0).astype(BF)
        dom[2*hp]=jnp.where(lane<64,dp_,0).astype(BF)
        dom[2*hp+1]=jnp.where(lane>=64,dp_,0).astype(BF)
    W=heads*HD
    prod=do[0].astype(F32)*o[0].astype(F32)
    hi=prod.astype(BF); lo=(prod-hi.astype(F32)).astype(BF)
    hp16=delta.shape[0]
    row=lax.broadcasted_iota(jnp.int32,(hp16,W),0); col=lax.broadcasted_iota(jnp.int32,(hp16,W),1)
    ones=jnp.where(row==col//HD,1.0,0.0).astype(BF)
    delta[...]=lax.dot_general(ones,hi,NT,preferred_element_type=F32)+lax.dot_general(ones,lo,NT,preferred_element_type=F32)
    if first: dqT[...]=jnp.zeros_like(dqT)
    else: dqT[...]=dqT_i[0]
    def body(kt):
        ks=pl.ds(pl.multiple_of(kt*tk,tk),tk)
        def col(hh): return slice((hh//2)*128,(hh//2+1)*128)
        def score(hh):
            s=lax.dot_general(k[0,ks,col(hh)],qm[hh],NT,preferred_element_type=F32)*LOG2E+bias[...]
            return s,lax.dot_general(v[0,ks,col(hh)],dom[hh],NT,preferred_element_type=F32)
        nxt=score(0); prev=None
        for hh in range(heads+1):
            cur=nxt
            if hh+1<heads: nxt=score(hh+1)
            if prev is not None:
                h1=hh-1; pb,dsb=prev
                hs=slice(h1*HD,(h1+1)*HD)
                dqT[hs,:]+=lax.dot_general(kT[hs,ks],dsb,NN,preferred_element_type=F32)
                dv[ks,col(h1)]+=jnp.dot(pb,dom[h1],preferred_element_type=F32)
                dk[ks,col(h1)]+=jnp.dot(dsb,qm[h1],preferred_element_type=F32)
            if hh<heads:
                s,dp=cur
                p=jnp.exp2(s-lse[0,hh:hh+1,:])
                ds=p*(dp-delta[hh:hh+1,:])
                prev=(p.astype(BF),ds.astype(BF))
    @pl.loop(0,nk)
    def _(kt):
        f=flags[r,qi,kt]
        @pl.when(f>0)
        def _():
            ks=pl.ds(pl.multiple_of(kt*tk,tk),tk)
            bias[...]=jnp.where(ck[0,ks,0:1]==cq[0,0:1,:],0.0,NEG)
            body(kt)
    if first: dqT_o[0]=dqT[...]
    else: dqkv_o[0,pl.ds(pl.multiple_of(qi*tq,tq),tq),0:W]=(dqT[...]*0.125).T.astype(BF)
    @pl.when(qi==nq-1)
    def _():
        out,at=(dkv_o,0) if first else (dqkv_o,W)
        out[0,:,at:at+W]=dk[...].astype(BF); out[0,:,at+W:at+2*W]=dv[...].astype(BF)

def attn_bwd(flags,cq,ck,q,kv,kb,do,o,lse,dqT,tq,tk,heads):
    nr,S,_=q.shape; W=heads*HD; Sk=kv.shape[1]; hp16=lse.shape[1]
    first=dqT is None
    qs=lambda r,i,*_:(r,i,0); ts=lambda r,i,*_:(r,0,i); ks=lambda r,i,*_:(r,0,0)
    ins=[pl.BlockSpec((1,1,tq),ts),pl.BlockSpec((1,Sk,128),ks),pl.BlockSpec((1,tq,W),qs),pl.BlockSpec((1,Sk,W),lambda r,i,*_:(r,0,kb)),pl.BlockSpec((1,Sk,W),lambda r,i,*_:(r,0,kb+1)),
         pl.BlockSpec((1,tq,W),qs),pl.BlockSpec((1,tq,W),qs),pl.BlockSpec((1,hp16,tq),ts)]
    if first:
        outs=[pl.BlockSpec((1,W,tq),ts),pl.BlockSpec((1,Sk,2*W),ks)]; osh=[jax.ShapeDtypeStruct((nr,W,S),F32),jax.ShapeDtypeStruct((nr,Sk,2*W),BF)]
        extra=()
    else:
        ins=ins+[pl.BlockSpec((1,W,tq),ts)]
        outs=[pl.BlockSpec((1,Sk,3*W),ks)]; osh=[jax.ShapeDtypeStruct((nr,Sk,3*W),BF)]
        extra=(dqT,)
    fl=10*nr*S*Sk*W
    return pl.pallas_call(functools.partial(bwd_kernel,first=first,tq=tq,tk=tk,heads=heads),
        out_shape=osh,
        grid_spec=pltpu.PrefetchScalarGridSpec(num_scalar_prefetch=1,grid=(nr,S//tq),in_specs=ins,out_specs=outs,
          scratch_shapes=[pltpu.VMEM((heads,tq,128),BF),pltpu.VMEM((heads,tq,128),BF),pltpu.VMEM((W,Sk),BF),pltpu.VMEM((tk,tq),F32),pltpu.VMEM((W,tq),F32),
             pltpu.VMEM((Sk,W),F32),pltpu.VMEM((Sk,W),F32),pltpu.VMEM((hp16,tq),F32)]),
        compiler_params=pltpu.CompilerParams(dimension_semantics=("arbitrary","arbitrary"),vmem_limit_bytes=VMEM_LIMIT),
        cost_estimate=pl.CostEstimate(flops=fl//SHARE,bytes_accessed=nr*(3*S*W*2+4*Sk*W*2+S*W*4)//SHARE,transcendentals=0),
        name="attn_bwd_a" if first else "attn_bwd_b",
    )(flags,cq,ck,q,kv,kv,do,o,lse,*extra)


def ffn_kernel(core, acts, w, b, d_act, act_o, theirs_o, mine_o, sum_o):
    del core
    step = pl.program_id(0)
    half = pl.num_programs(0) // 2
    rows = acts.shape[0]
    chunk = min(256, rows)
    count = rows // chunk

    def product(i):
        return dot(acts[i * chunk : (i + 1) * chunk, :], w[...], NN) + b[...]

    pre = product(0)
    total = None
    for i in range(count):
        following = product(i + 1) if i + 1 < count else None
        at = slice(i * chunk, (i + 1) * chunk)
        cdf = 0.5 + 0.5 * lax.erf(pre * math.sqrt(0.5))
        pdf = jnp.exp(-0.5 * pre * pre) * (1.0 / math.sqrt(2.0 * math.pi))
        act_o[at, :] = (pre * cdf).astype(BF)
        d_pre = (d_act[at, :].astype(F32) * (cdf + pre * pdf)).astype(BF)

        @pl.when(step < half)
        def _():
            theirs_o[at, :] = d_pre

        @pl.when(step >= half)
        def _():
            mine_o[at, :] = d_pre

        part = jnp.sum(d_pre.astype(F32), axis=0, keepdims=True)
        total = part if total is None else total + part
        pre = following
    sum_o[...] = total


def ffn_call(core, acts, w, b, d_act):
    rows, width = acts.shape
    ff = w.shape[1]
    tile = 512
    half = ff // 2 // tile

    def place(i, core):
        return jnp.where(i < half, 1 - core[0], core[0]) * half + lax.rem(i, half)

    col = lambda i, core: (0, place(i, core))
    return pl.pallas_call(
        ffn_kernel,
        out_shape=[
            jax.ShapeDtypeStruct((rows, ff), BF),
            jax.ShapeDtypeStruct((rows, ff // 2), BF),
            jax.ShapeDtypeStruct((rows, ff // 2), BF),
            jax.ShapeDtypeStruct((1, ff), F32),
        ],
        grid_spec=pltpu.PrefetchScalarGridSpec(
            num_scalar_prefetch=1,
            grid=(2 * half,),
            in_specs=[
                pl.BlockSpec((rows, width), lambda i, core: (0, 0)),
                pl.BlockSpec((width, tile), col),
                pl.BlockSpec((1, tile), col),
                pl.BlockSpec((rows, tile), col),
            ],
            out_specs=[
                pl.BlockSpec((rows, tile), col),
                pl.BlockSpec((rows, tile), lambda i, core: (0, jnp.minimum(i, half - 1))),
                pl.BlockSpec((rows, tile), lambda i, core: (0, jnp.maximum(i - half, 0))),
                pl.BlockSpec((1, tile), col),
            ],
        ),
        compiler_params=pltpu.CompilerParams(vmem_limit_bytes=VMEM_LIMIT),
        cost_estimate=pl.CostEstimate(
            flops=2 * rows * width * ff // SHARE,
            bytes_accessed=2 * (rows * width + width * ff + 3 * rows * ff) // SHARE,
            transcendentals=0,
        ),
        name="ffn",
    )(core, acts, w, b, d_act)


def store_blocks(where, acc, outs, first, second, halved):
    rows = acc.shape[0] // (first * second)
    for one in range(first):
        for two in range(second):
            block = lax.bitwise_xor(two * first + one, where[0]) * rows
            if halved:
                for part in range(2):
                    at = block + lax.bitwise_xor(where[2], part) * (rows // 2)
                    piece = acc[pl.ds(pl.multiple_of(at, 16), rows // 2), :]
                    outs[part][one, two] = piece.astype(BF)
            else:
                outs[one][two] = acc[pl.ds(pl.multiple_of(block, 16), rows), :].astype(BF)


def grad_kernel(where, *refs, groups, first, second, halved):
    ins = refs[: sum(2 * g for g in groups)]
    acc = refs[-1]
    height = acc.shape[0] // len(groups)
    at = 0
    for index, pairs in enumerate(groups):
        total = None
        for _ in range(pairs):
            part = dot(ins[at][...], ins[at + 1][...], TN)
            total = part if total is None else total + part
            at += 2
        acc[index * height : (index + 1) * height, :] = total
    store_blocks(where, acc, refs[len(ins) : -1], first, second, halved)


def grad_call(where, groups, width, first, second, tile, halved, name):
    ins, flat, depth = [], [], 0
    for group in groups:
        for a, b, offset in group:
            ins.append(pl.BlockSpec(a.shape, lambda i, where: (0, 0)))
            if offset is None:
                index = lambda i, where: (0, where[1] * (width // tile) + i)
            else:
                index = lambda i, where, offset=offset: (0, offset // tile + i)
            ins.append(pl.BlockSpec((b.shape[0], tile), index))
            flat += [a, b]
            depth += a.shape[0]
    height = sum(g[0][0].shape[1] for g in groups)
    depth = depth // len(groups)
    rows = height // (first * second)
    if halved:
        shape, block = (first, second, rows // 2, width), (first, second, rows // 2, tile)
        outs = 2
        index = lambda i, where: (0, 0, 0, i)
    else:
        shape, block = (second, rows, width), (second, rows, tile)
        outs = first
        index = lambda i, where: (0, 0, i)
    return pl.pallas_call(
        functools.partial(
            grad_kernel, groups=[len(g) for g in groups], first=first, second=second, halved=halved
        ),
        out_shape=[jax.ShapeDtypeStruct(shape, BF)] * outs,
        grid_spec=pltpu.PrefetchScalarGridSpec(
            num_scalar_prefetch=1,
            grid=(width // tile,),
            in_specs=ins,
            out_specs=[pl.BlockSpec(block, index)] * outs,
            scratch_shapes=[pltpu.VMEM((height, tile), F32)],
        ),
        compiler_params=pltpu.CompilerParams(vmem_limit_bytes=VMEM_LIMIT),
        cost_estimate=pl.CostEstimate(
            flops=2 * depth * height * width // SHARE,
            bytes_accessed=2 * (depth * (height + width) + height * width) // SHARE,
            transcendentals=0,
        ),
        name=name,
    )(where, *flat)


def back_kernel(where, a1, b1, a2, b2, out1, out2, acc):
    acc[...] = dot(a1[...], b1[...], TN) + dot(a2[...], b2[...], TN)
    rows = acc.shape[0] // 2
    for part, out in enumerate((out1, out2)):
        at = lax.bitwise_xor(where[2], part) * rows
        out[0, 0] = acc[pl.ds(pl.multiple_of(at, 16), rows), :].astype(BF)


def back_call(where, own, mate, first, second, name):
    (a1, b1), (a2, b2) = own, mate
    tokens, ff = a1.shape
    rows = ff // (first * second)
    width = b2.shape[1]

    def block(i, where):
        return (0, lax.bitwise_xor(lax.rem(i, second) * first + i // second, where[0]))

    return pl.pallas_call(
        back_kernel,
        out_shape=[jax.ShapeDtypeStruct((first, second, rows // 2, width), BF)] * 2,
        grid_spec=pltpu.PrefetchScalarGridSpec(
            num_scalar_prefetch=1,
            grid=(first * second,),
            in_specs=[
                pl.BlockSpec((tokens, rows), block),
                pl.BlockSpec((tokens, width), lambda i, where: (0, where[1])),
                pl.BlockSpec((tokens, rows), block),
                pl.BlockSpec((tokens, width), lambda i, where: (0, 0)),
            ],
            out_specs=[
                pl.BlockSpec(
                    (1, 1, rows // 2, width), lambda i, where: (i // second, lax.rem(i, second), 0, 0)
                )
            ]
            * 2,
            scratch_shapes=[pltpu.VMEM((rows, width), F32)],
        ),
        compiler_params=pltpu.CompilerParams(vmem_limit_bytes=VMEM_LIMIT),
        cost_estimate=pl.CostEstimate(
            flops=4 * tokens * ff * width // SHARE,
            bytes_accessed=2 * (2 * tokens * (ff + width) + ff * width) // SHARE,
            transcendentals=0,
        ),
        name=name,
    )(where, a1, b1, a2, b2)


def product_kernel(a, b, *rest, dims):
    total = dot(a[...], b[...], dims)
    for term in rest[:-1]:
        total = total + term[...]
    rest[-1][...] = total.astype(rest[-1].dtype)


def product(a, b, dims, name, terms=()):
    rows, depth = a.shape
    turned = dims == NT
    width = b.shape[0] if turned else b.shape[1]
    tile = 256
    if turned:
        b_spec = pl.BlockSpec((tile, depth), lambda i: (i, 0))
    else:
        b_spec = pl.BlockSpec((depth, tile), lambda i: (0, i))
    return pl.pallas_call(
        functools.partial(product_kernel, dims=dims),
        out_shape=jax.ShapeDtypeStruct((rows, width), BF),
        grid=(width // tile,),
        in_specs=[pl.BlockSpec(a.shape, lambda i: (0, 0), pipeline_mode=pl.Buffered(1)), b_spec]
        + [pl.BlockSpec((t.shape[0], tile), lambda i: (0, i)) for t in terms],
        out_specs=pl.BlockSpec((rows, tile), lambda i: (0, i)),
        compiler_params=pltpu.CompilerParams(vmem_limit_bytes=VMEM_LIMIT),
        cost_estimate=pl.CostEstimate(
            flops=2 * rows * depth * width // SHARE,
            bytes_accessed=2 * (rows * depth + depth * width + rows * width) // SHARE,
            transcendentals=0,
        ),
        name=name,
    )(a, b, *terms)


def tile_flags(queries, keys, tq, tk):
    q_first, q_last = queries[:, ::tq], queries[:, tq - 1 :: tq]
    k_first, k_last = keys[:, ::tk], keys[:, tk - 1 :: tk]
    meet = (q_first[:, :, None] <= k_last[:, None, :]) & (k_first[:, None, :] <= q_last[:, :, None])
    whole = (
        (q_first == q_last)[:, :, None]
        & (k_first == k_last)[:, None, :]
        & (q_first[:, :, None] == k_first[:, None, :])
    )
    return jnp.where(whole, 2, jnp.where(meet, 1, 0)).astype(jnp.int32)


def layer_norm_parts(values):
    centred = values - jnp.mean(values, axis=-1, keepdims=True)
    rstd = lax.rsqrt(jnp.mean(centred * centred, axis=-1, keepdims=True) + EPS)
    return centred * rstd, rstd


def layer_norm_back(d_norm, gain, xhat, rstd):
    e = d_norm * gain
    return rstd * (
        e - jnp.mean(e, axis=-1, keepdims=True) - xhat * jnp.mean(e * xhat, axis=-1, keepdims=True)
    )


def on_device(
    tokens,
    cell_start,
    norm1_gain,
    norm1_bias,
    w_qkv,
    bias_q,
    bias_v,
    w_out,
    bias_out,
    norm2_gain,
    norm2_bias,
    w_in,
    bias_in,
    w_back,
    bias_back,
    cotangent,
):
    rows, seg, width = tokens.shape
    count = rows * seg
    ff = w_in.shape[1]
    half = width // 2
    wide = lax.axis_size("wide")
    group = lax.axis_size("blk")
    place = lax.axis_index("wide")
    member = lax.axis_index("blk")
    core = place % 2
    chips = wide // 2
    first = 2 if chips <= 8 else 4
    second = chips // first
    heads = HEADS // 2
    tq, tk = min(512, seg), min(256, seg)
    halves = group == 2 and ff // chips % 128 == 0
    where = jnp.stack([place // 2, core, member]).astype(jnp.int32)
    where_out = jnp.stack([lax.bitwise_xor(place // 2, core * (chips // 2)), core, member]).astype(jnp.int32)

    def after(value, *earlier):
        return lax.optimization_barrier((value, earlier))[0]

    def across(array, by):
        return lax.ppermute(array, "wide", [(i, i ^ by) for i in range(wide)])

    def to_mate(array):
        return across(array, 1)

    def from_ahead(array, by):
        return lax.ppermute(array, "blk", [((i + by) % group, i) for i in range(group)])

    def to_ahead(array, by):
        return lax.ppermute(array, "blk", [(i, (i + by) % group) for i in range(group)])

    def from_all_ahead(array):
        parts = [from_ahead(array, by) for by in range(1, group)]
        return parts[0] if len(parts) == 1 else jnp.concatenate(parts, axis=1)

    def cut(array, start, size, axis):
        return lax.dynamic_slice_in_dim(array, start, size, axis)

    def paired(array):
        return jnp.concatenate([array, to_mate(array)], axis=0)

    inputs = tokens.astype(F32).reshape(count, width)
    xhat1, rstd1 = layer_norm_parts(inputs)
    acts = (xhat1 * norm1_gain + norm1_bias).astype(BF).reshape(tokens.shape)
    cells = paired(cell_start)
    far_cells = from_all_ahead(cells)
    acts = after(acts, far_cells)
    far_own = from_all_ahead(acts)
    acts_pair = paired(acts).reshape(2 * count, width)
    w_own = jnp.concatenate([cut(w_qkv, part * width + core * half, half, 1) for part in range(3)], axis=1)
    b_own = jnp.concatenate([cut(bias_q, core * half, half, 0), jnp.zeros((half,), F32), cut(bias_v, core * half, half, 0)])

    def columns(array):
        return jnp.broadcast_to(array[:, :, None], array.shape + (128,))

    qkv = (dot(acts_pair, w_own, NN) + b_own).astype(BF).reshape(2 * rows, seg, 3 * half)
    near_flags = tile_flags(cells, cells, tq, tk)
    far_flags = tile_flags(cells, far_cells, tq, tk)
    cell_rows = cells[:, None, :]
    near_columns, far_columns = columns(cells), columns(far_cells)
    state = attn_fwd(near_flags, cell_rows, near_columns, qkv, qkv, 1, None, tq, tk, heads)
    d_out = cotangent.reshape(count, width)
    far_own = after(far_own, state)
    far_mate = to_mate(far_own)
    d_act = dot(after(d_out, far_own, state), w_back, NT).astype(BF)

    far_mate = after(far_mate, d_act)
    far_pair = jnp.concatenate([far_own, far_mate], axis=0)
    far_len = far_pair.shape[1]
    far_pair = far_pair.reshape(-1, width)
    far_kv = (dot(far_pair, w_own[:, half:], NN) + b_own[half:]).astype(BF).reshape(2 * rows, far_len, 2 * half)
    attended, stats = attn_fwd(far_flags, cell_rows, far_columns, qkv, far_kv, 0, state, tq, tk, heads)
    mine, theirs = attended[:rows].reshape(count, half), attended[rows:].reshape(count, half)
    own_rest = to_mate(theirs)
    mate_rest = to_mate(mine)
    w_out_own = cut(w_out, core * half, half, 0)
    w_out_mate = cut(w_out, (1 - core) * half, half, 0)
    middle = inputs + (dot(mine, w_out_own, NN) + dot(own_rest, w_out_mate, NN)) + bias_out

    xhat2, rstd2 = layer_norm_parts(middle)
    acts2 = (xhat2 * norm2_gain + norm2_bias).astype(BF)
    acts2_mate = to_mate(acts2)
    d_out_mate = to_mate(cut(d_out, (1 - core) * half, half, 1))
    act, d_pre_theirs, d_pre_mine, d_pre_sum = ffn_call(where[1:], acts2, w_in, bias_in.reshape(1, ff), d_act)
    d_pre_mate = to_mate(d_pre_theirs)
    act_mate = to_mate(act)
    w_in_mine = cut(w_in, core * (ff // 2), ff // 2, 1)
    w_in_theirs = cut(w_in, (1 - core) * (ff // 2), ff // 2, 1)
    d_norm2 = dot(d_pre_theirs, w_in_theirs, NT) + dot(d_pre_mine, w_in_mine, NT)
    grad_out = d_out.astype(F32)
    d_middle = grad_out + layer_norm_back(d_norm2, norm2_gain, xhat2, rstd2)
    d_z = d_middle.astype(BF)
    d_att_theirs = dot(d_z, w_out_mate, NT).astype(BF)
    d_att_mine = dot(d_z, w_out_own, NT).astype(BF)
    d_att_mate = to_mate(d_att_theirs)
    d_z_mate = to_mate(cut(d_z, (1 - core) * half, half, 1))

    def send(parts):
        return [across(parts[one], 2 * one) for one in range(1, first)]

    def add_first(parts, received):
        sums = []
        for two in range(second):
            total = parts[0][two].astype(F32)
            for part in received:
                total = total + part[two].astype(F32)
            sums.append(total.astype(BF))
        return sums

    def send_second(sums):
        return [across(sums[two], 2 * first * two) for two in range(1, second)]

    def add_second(sums, received):
        total = sums[0].astype(F32)
        for part in received:
            total = total + part.astype(F32)
        return total.astype(BF)

    def add_half(parts, received):
        return [(parts[0][one].astype(F32) + received[one].astype(F32)).astype(BF) for one in range(first)]

    def start(parts):
        return from_ahead(parts[1], 1) if halves else send(parts)

    def middle_step(parts, received):
        if not halves:
            return parts, received
        sums = add_half(parts, received)
        return sums, send(sums)

    def over_row(total, other):
        if group == 2:
            return (total.astype(F32) + other.astype(F32)).astype(BF)
        return lax.psum(total, "blk")

    def ahead(total):
        return from_ahead(total, 1) if group == 2 else None

    def join_halves(total, other):
        return jnp.concatenate([jnp.where(member == 0, total, other), jnp.where(member == 0, other, total)], axis=0)

    def finish(total):
        split = total.reshape(2, -1, total.shape[-1])
        given = lax.dynamic_index_in_dim(split, 1 - core, 0, keepdims=False)
        kept = lax.dynamic_index_in_dim(split, core, 0, keepdims=False)
        other = to_mate(given)
        low, high = jnp.where(core == 0, kept, other), jnp.where(core == 0, other, kept)
        return [low.astype(F32), high.astype(F32)]

    act_held, act_mate = after((act, act_mate), d_att_theirs, d_att_mine)
    if halves:
        grad_back = back_call(where, (act_held, d_out), (act_mate, d_out_mate), first, second, "grad_back")
        back_in = from_ahead(grad_back[1], 1)
    else:
        whole = dot(act_held, cut(d_out, core * half, half, 1), TN) + dot(act_mate, d_out_mate, TN)
        whole = whole.astype(BF).reshape(second, first, ff // chips, half)
        grad_back = [
            jnp.stack([
                whole.reshape(chips, ff // chips, half)[lax.bitwise_xor(two * first + one, where[0])]
                for two in range(second)
            ])
            for one in range(first)
        ]
        back_in = send(grad_back)
    acts2_held = after(acts2, grad_back)
    grad_in = grad_call(
        where, [[(acts2_held, d_pre_mine, 0), (acts2_mate, d_pre_mate, 0)]], ff // 2, first, second, 512, False, "grad_in"
    )
    in_in = send(grad_in)

    d_att = jnp.concatenate([d_att_mine, d_att_mate], axis=0).reshape(2 * rows, seg, half)
    d_z_mate, mate_rest = after((d_z_mate, mate_rest), grad_in)
    d_att = after(d_att, grad_in, d_z_mate, mate_rest)
    d_qT, far_dkv = attn_bwd(
        far_flags, cell_rows, far_columns, qkv, far_kv, 0, d_att, attended, stats, None, tq, tk, heads
    )
    if halves:
        back_sums = add_half(grad_back, after(back_in, d_qT))
        back_in = send(back_sums)
    else:
        back_sums = grad_back
    far_dkv_flat = after(far_dkv, back_sums).reshape(-1, 2 * half)
    far_part = product(far_dkv_flat, w_own[:, half:], NT, "far_norm").reshape(2 * rows, far_len, width)
    far_given = to_mate(far_part[rows:])
    in_sums = add_first(grad_in, after(in_in, far_part))
    in_more = send_second(in_sums)
    far_sum = (far_part[:rows].astype(F32) + after(far_given, in_sums).astype(F32)).astype(BF)
    far_back = [to_ahead(far_sum[:, by * seg : (by + 1) * seg], by + 1) for by in range(group - 1)]
    d_qT = after(d_qT, in_sums, back_sums, far_sum)
    d_qkv, = attn_bwd(
        near_flags, cell_rows, near_columns, qkv, qkv, 1, d_att, attended, stats, d_qT, tq, tk, heads
    )
    back_two = add_first(back_sums, after(back_in, d_qkv))
    back_more = send_second(back_two)
    d_z_held = after(d_z, back_two)
    grad_o = grad_call(
        where_out,
        [
            [(mine, d_z_held, None), (theirs, d_z_mate, 0)],
            [(own_rest, d_z_held, None), (mate_rest, d_z_mate, 0)],
        ],
        half, first, second, half, halves, "grad_out",
    )
    out_in = start(grad_o)
    d_qkv_flat = d_qkv.reshape(2 * count, 3 * half)
    held = after(d_qkv_flat, grad_o)

    def grad_part(part, halved, name, held):
        pairs = [(acts_pair, held, part * half)]
        if part:
            pairs.append((far_pair, far_dkv_flat, (part - 1) * half))
        tile = half if far_len <= 2 * seg else 128
        return grad_call(where, [pairs], half, first, second, tile, halved, name)

    grad_v = grad_part(2, halves, "grad_v", held)
    v_in = start(grad_v)
    in_total = add_second(in_sums, after(in_more, grad_v))
    in_row = ahead(in_total)
    held = after(held, in_total)
    grad_k = grad_part(1, halves, "grad_k", held)
    k_in = start(grad_k)
    out_half, out_in = middle_step(grad_o, after(out_in, grad_k))
    held = after(held, grad_k, out_half)
    grad_q = grad_part(0, halves, "grad_q", held)
    q_in = start(grad_q)
    v_half, v_in = middle_step(grad_v, after(v_in, grad_q))
    held = after(held, grad_q, v_half)
    near_part = product(held, w_own, NT, "near_norm")
    near_given = to_mate(near_part[count:])
    back_total = add_second(back_two, after(back_more, near_part))
    back_row = ahead(back_total)
    k_half, k_in = middle_step(grad_k, after(k_in, near_part))
    out_two = add_first(out_half, after(out_in, near_part))
    out_more = send_second(out_two)
    act_late = after(act_held, back_total, k_half, out_two)
    mixed = product(act_late, w_back, NN, "mixed", (middle, bias_back.reshape(1, width))).reshape(tokens.shape)
    q_half, q_in = middle_step(grad_q, after(q_in, mixed))
    v_two = add_first(v_half, after(v_in, mixed))
    v_more = send_second(v_two)
    k_two = add_first(k_half, after(k_in, v_two))
    k_more = send_second(k_two)
    d_norm1, = after((near_part[:count].astype(F32),), mixed, q_half, v_two, k_two)
    d_norm1 = d_norm1 + near_given.astype(F32)
    for part in far_back:
        d_norm1 = d_norm1 + part.reshape(count, width).astype(F32)
    grad_tokens = (d_middle + layer_norm_back(d_norm1, norm1_gain, xhat1, rstd1)).reshape(tokens.shape)

    def vectors(parts):
        packed = jnp.concatenate([p.reshape(wide, -1) for p in parts], axis=1)
        total = packed
        for stride, size in ((2 * first, second), (2, first), (1, 2)):
            total = total.reshape(-1, size, stride, packed.shape[1])
            spot = (place // stride) % size
            kept = lax.dynamic_index_in_dim(total, spot, 1, keepdims=False)
            for by in range(1, size):
                given = lax.dynamic_index_in_dim(total, spot ^ by, 1, keepdims=False)
                kept = kept + across(given, by * stride)
            total = kept.reshape(stride, packed.shape[1])
        total = total.reshape(-1)
        total = total + from_ahead(total, 1) if group == 2 else lax.psum(total, "blk")
        out, at = [], 0
        for p in parts:
            size = p.size // wide
            out.append(total[at : at + size])
            at += size
        return out

    def widened(array):
        return lax.dynamic_update_slice_in_dim(jnp.zeros((width,), F32), array, core * half, 0)

    far_v_sum = jnp.sum(far_dkv_flat[:, half:].astype(F32), axis=0)
    small = vectors(
        [
            jnp.sum(d_norm1 * xhat1, axis=0),
            jnp.sum(d_norm1, axis=0),
            widened(jnp.sum(d_qkv_flat[:, :half].astype(F32), axis=0)),
            widened(jnp.sum(d_qkv_flat[:, 2 * half :].astype(F32), axis=0) + far_v_sum),
            jnp.sum(d_z.astype(F32), axis=0),
            jnp.sum(d_norm2 * xhat2, axis=0),
            jnp.sum(d_norm2, axis=0),
            d_pre_sum,
            jnp.sum(grad_out, axis=0),
        ]
    )
    q_two = add_first(q_half, after(q_in, d_norm1))
    q_more = send_second(q_two)

    def rest(total, row=None):
        row = ahead(total) if row is None else row
        return join_halves(total, row) if halves else over_row(total, row)

    in_row, back_row = after((in_row, back_row), q_two)
    in_total, back_total = over_row(in_total, in_row), rest(back_total, back_row)
    out_total = rest(add_second(out_two, after(out_more, q_two)))
    v_total = rest(add_second(v_two, after(v_more, q_two)))
    k_total = rest(add_second(k_two, after(k_more, q_two)))
    q_total = rest(add_second(q_two, q_more))

    def matrix(*totals):
        return jnp.concatenate([piece for total in totals for piece in finish(total)], axis=1)

    return (
        mixed,
        grad_tokens,
        small[0],
        small[1],
        matrix(q_total, k_total, v_total),
        small[2],
        small[3],
        matrix(out_total),
        small[4],
        small[5],
        small[6],
        matrix(in_total),
        small[7],
        matrix(back_total),
        small[8],
    )


def solution(mesh):
    spread = P("wide", "blk", None)
    placed = (spread, P("wide", "blk")) + (P(),) * 13 + (spread,)
    matrix, vector = P("wide", None), P("wide")
    return jax.shard_map(
        on_device,
        mesh=mesh,
        in_specs=placed,
        out_specs=(
            spread, spread, vector, vector, matrix, vector, vector, matrix, vector, vector, vector,
            matrix, vector, matrix, vector,
        ),
        check_vma=False,
    )
```

time: 995 us -> 709 us (0.71); the launches traced: 978 us -> 716 us
  waiting for transfers between devices: 247 us -> 43.8 us
  matrix products: 190 us -> 84 us
  starting transfers between devices: 144 us -> 102 us
  Pallas kernels: 307 us -> 347 us
  other arithmetic: 67.2 us -> 107 us
  local copies, waits for them, and re-layouts: 20.3 us -> 31 us
    ppermute x53 -> x48, waiting for transfers between devices: 170 us -> 32.5 us  [across(): return lax.ppermute(array, 'wide', [(i, i ^ by) for i in range(wide)])]
    dot_general x28 -> x9, matrix products: 190 us -> 84 us  [dot(): return lax.dot_general(a, b, dims, preferred_element_type=F32)]
    pallas_call x7 -> x9, Pallas kernels: 99.2 us -> 145 us  [the longest x5 72.7 us: grad_call(): pl.pallas_call(functools.partial(grad_kernel, groups=[len(g) for g in gro...]
    ppermute x53 -> x48, starting transfers between devices: 127 us -> 87 us  [across(): return lax.ppermute(array, 'wide', [(i, i ^ by) for i in range(wide)])]
    ppermute x11 -> x14, waiting for transfers between devices: 47.7 us -> 11.2 us  [from_ahead(): lax.ppermute(array, 'blk', [((i + by) % group, i) for i in range(group)])]
    ppermute x1, waiting for transfers between devices: 29.6 us -> 0.01 us  [to_ahead(): lax.ppermute(array, 'blk', [(i, (i + by) % group) for i in range(group)])]
    concatenate x6 -> x17, other arithmetic: 6.3 us -> 22.5 us  [the longest x2 8.42 us: on_device(): jnp.concatenate([cut(w_qkv, part * width + core * half, half, 1) for part...]
    convert_element_type x19 -> x20, other arithmetic: 21.5 us -> 36 us  [the longest x6 12.1 us: add_first(): sums.append(total.astype(BF))]
  transfers between devices with their start and end apart: 65 -> 63, of which waited for: 23 -> 13; matrix products, arithmetic and copies ran while one was open for 26% -> 27% of each run, Pallas kernels for 30% -> 39%
where the time goes in v2:
time: 709 us; the launch traced here: 716 us
  Pallas kernels  347 us (49%)
  other arithmetic  107 us (15%)
  starting transfers between devices  102 us (14%)
  matrix products  84 us (12%)
  waiting for transfers between devices  43.8 us (6%)
  local copies, waits for them, and re-layouts  31 us (4%)
    pallas_call x2, Pallas kernels, attn_bwd(): pl.pallas_call(functools.partial(bwd_kernel, first=first, tq=tq, tk=tk, h...  105 us
    ppermute x48, starting transfers between devices, across(): return lax.ppermute(array, 'wide', [(i, i ^ by) for i in range(wide)])  87 us
    dot_general x9, matrix products, dot(): return lax.dot_general(a, b, dims, preferred_element_type=F32)  84 us
    pallas_call x5, Pallas kernels, grad_call(): pl.pallas_call(functools.partial(grad_kernel, groups=[len(g) for g in gro...  72.7 us
    pallas_call x2, Pallas kernels, attn_fwd(): pl.pallas_call(functools.partial(fwd_kernel, first=first, tq=tq, tk=tk, h...  58.1 us
    pallas_call x3, Pallas kernels, product(): pl.pallas_call(functools.partial(product_kernel, dims=dims), out_shape=ja...  49 us
    pallas_call x1, Pallas kernels, ffn_call(): pl.pallas_call(ffn_kernel, out_shape=[jax.ShapeDtypeStruct((rows, ff), BF...  38.3 us
    ppermute x48, waiting for transfers between devices, across(): return lax.ppermute(array, 'wide', [(i, i ^ by) for i in range(wide)])  32.5 us
  transfers between devices with their start and end apart: 63, of which 13 were waited for; matrix products, arithmetic and copies ran while one was open for 27% of the time, Pallas kernels for 39%

profile of v2, /device:TPU:0, one launch (start us, length us, event | category | flops | bytes accessed | tf_op | source)
XLA Modules:
  0.0 716.1 jit_solution(2446040999375915121)
XLA Ops:
  23.6 13.5 %add_convert_fusion = bf16[2048,1920]{1,0:T(8,128)(2,1)} fusion(f32[1920]{0:T(1024)S(1)} %pad_maximum_fusion.10, bf16[2048,1280]{1,0:T(8,128)(2,1)S(1)} %bitcast.317, bf16[1280,640]{1,0:T(8,128)(2,1)S(1)} %copy-done.10, bf16[1280,640]{1,0:T(8,128)(2,1)S(1)} %copy-done.13, bf16[1280,640]{1,0:T(8,128)(2,1)S(1)} %copy-done.17), kind=kOutput, calls=%fused_computation | convolution fusion | flops 10088939520 | bytes 18030080 | tf_op jit(solution)/shard_map/dot_general | solution.py:28
  38.5 32.0 %attn_fwd_a.1 = (f32[2,640,1024]{2,1,0:T(8,128)}, f32[2,16,1024]{2,1,0:T(8,128)}, f32[2,16,1024]{2,1,0:T(8,128)}) custom-call(s32[2,2,4]{2,1,0:T(2,128)} %get-tuple-element.239.flags, s32[2,1,1024]{2,1,0:T(1,128)} %broadcast_in_dim.26.cq, s32[2,1024,128]{2,1,0:T(8,128)} %broadcast_in_dim.29.ck, bf16[2,1024,1920]{2,1,0:T(8,128)(2,1)} %bitcast.304, ...), custom_call_target="tpu_custom_call" | custom-call | flops 268435456 | bytes 655360 | tf_op jit(solution)/shard_map/attn_fwd_a/pallas_call | solution.py:150
  70.4 6.8 collective-permute-done.3
  77.3 20.6 %convolution_convert_fusion.d_act = bf16[1024,5120]{1,0:T(8,128)(2,1)} fusion(bf16[1024,1280]{1,0:T(8,128)(2,1)S(1)} %bitcast.339, bf16[5120,1280]{1,0:T(8,128)(2,1)} %b.1), kind=kOutput, calls=%fused_computation.2 | convolution fusion | flops 13427015680 | bytes 26214400 | tf_op jit(solution)/shard_map/dot_general | solution.py:28
  101.4 8.6 %add_convert_fusion.1 = bf16[2048,1280]{1,0:T(8,128)(2,1)} fusion(bf16[2048,1280]{1,0:T(8,128)(2,1)S(1)} %bitcast.331, f32[1280]{0:T(1024)S(1)} %concatenate.92, bf16[1280,640]{1,0:T(8,128)(2,1)S(1)} %copy-done.11, bf16[1280,640]{1,0:T(8,128)(2,1)S(1)} %copy-done.14), kind=kOutput, calls=%fused_computation.1 | convolution fusion | flops 6722682880 | bytes 13767680 | tf_op jit(solution)/shard_map/dot_general | solution.py:28
  111.3 26.1 %attn_fwd_b.1 = (bf16[2,1024,640]{2,1,0:T(8,128)(2,1)}, f32[2,16,1024]{2,1,0:T(8,128)}) custom-call(s32[2,2,4]{2,1,0:T(2,128)} %get-tuple-element.240.flags, s32[2,1,1024]{2,1,0:T(1,128)} %broadcast_in_dim.26.cq, s32[2,1024,128]{2,1,0:T(8,128)} %broadcast_in_dim.27.ck, bf16[2,1024,1920]{2,1,0:T(8,128)(2,1)} %bitcast.307, bf16[2,1024,1280]{2,1,0:T(8,128)(2,1)} %bitcast.323, ...), custom_call_target="tpu_custom_call" | custom-call | flops 268435456 | bytes 655360 | tf_op jit(solution)/shard_map/attn_fwd_b/pallas_call | solution.py:150
  152.9 38.3 %ffn.1 = (bf16[1024,5120]{1,0:T(8,128)(2,1)}, bf16[1024,2560]{1,0:T(8,128)(2,1)}, bf16[1024,2560]{1,0:T(8,128)(2,1)}, f32[1,5120]{1,0:T(1,128)}) custom-call(s32[2]{0:T(128)} %pad_add_fusion.1.core, bf16[1024,1280]{1,0:T(8,128)(2,1)} %add_convert_fusion.2.acts.refs_0_, bf16[1280,5120]{1,0:T(8,128)(2,1)} %w.1, f32[1,5120]{1,0:T(1,128)} %bitcast.356, ...), custom_call_target="tpu_custom_call" | custom-call | flops 671088640 | bytes 2359296 | tf_op jit(solution)/shard_map/ffn/pallas_call | solution.py:293
  194.2 12.5 %fusion = f32[1024,1280]{1,0:T(8,128)} fusion(bf16[1024,2560]{1,0:T(8,128)(2,1)} %get-tuple-element.95.refs_1_, bf16[1280,5120]{1,0:T(8,128)(2,1)} %w.1, s32[]{:T(128)S(6)} %select_n.227), kind=kOutput, calls=%fused_computation.6 | convolution fusion | flops 6710886400 | bytes 17039364 | tf_op jit(solution)/shard_map/dot_general | solution.py:28
  206.7 14.3 %multiply_reduce_fusion = (f32[1280]{0:T(1024)S(1)}, f32[1024]{0:T(1024)S(1)}, f32[1024]{0:T(1024)S(1)}, f32[1280]{0:T(1024)S(1)}, f32[1024,1280]{1,0:T(8,128)}) fusion(f32[1024,1280]{1,0:T(8,128)} %copy-done.2, f32[1024]{0:T(1024)S(1)} %add_rsqrt_fusion, f32[1024]{0:T(1024)S(1)} %broadcast_multiply_fusion.4, f32[1280]{0:T(1024)S(1)} %copy-done.45, ...), kind=kOutput, calls=%fused_computation.36 | convolution fusion | flops 6723989504 | bytes 27556868 | tf_op jit(solution)/shard_map/dot_general | solution.py:28
  221.0 6.1 convert_reduce_fusion.2
  233.8 23.4 %grad_back.1 = (bf16[2,4,320,640]{3,2,1,0:T(8,128)(2,1)}, bf16[2,4,320,640]{3,2,1,0:T(8,128)(2,1)}) custom-call(s32[3]{0:T(128)} %add_add_fusion.where, bf16[1024,5120]{1,0:T(8,128)(2,1)} %get-tuple-element.137.a1.a, bf16[1024,1280]{1,0:T(8,128)(2,1)} %bitcast.338, bf16[1024,5120]{1,0:T(8,128)(2,1)} %collective-permute-done.6.a2, ...), custom_call_target="tpu_custom_call" | custom-call | flops 671088640 | bytes 1507328 | tf_op jit(solution)/shard_map/grad_back/pallas_call | solution.py:418
  259.9 20.6 %grad_in.1 = (bf16[4,160,2560]{2,1,0:T(8,128)(2,1)}, bf16[4,160,2560]{2,1,0:T(8,128)(2,1)}) custom-call(s32[3]{0:T(128)} %add_add_fusion.where, bf16[1024,1280]{1,0:T(8,128)(2,1)} %add_convert_fusion.2.acts.refs_0_, bf16[1024,2560]{1,0:T(8,128)(2,1)} %get-tuple-element.95.refs_1_, bf16[1024,1280]{1,0:T(8,128)(2,1)} %collective-permute-done.10.refs_2_, ...), custom_call_target="tpu_custom_call" | custom-call | flops 671088640 | bytes 1114112 | tf_op jit(solution)/shard_map/grad_in/pallas_call | solution.py:379
  286.4 45.7 %attn_bwd_a.1 = (f32[2,640,1024]{2,1,0:T(8,128)}, bf16[2,1024,1280]{2,1,0:T(8,128)(2,1)}) custom-call(s32[2,2,4]{2,1,0:T(2,128)} %get-tuple-element.240.flags, s32[2,1,1024]{2,1,0:T(1,128)} %broadcast_in_dim.26.cq, s32[2,1024,128]{2,1,0:T(8,128)} %broadcast_in_dim.27.ck, bf16[2,1024,1920]{2,1,0:T(8,128)(2,1)} %bitcast.308, bf16[2,1024,1280]{2,1,0:T(8,128)(2,1)} %bitcast.325, ...), custom_call_target="tpu_custom_call" | custom-call | flops 671088640 | bytes 1179648 | tf_op jit(solution)/shard_map/attn_bwd_a/pallas_call | solution.py:237
  336.6 11.7 %far_norm.1 = bf16[2048,1280]{1,0:T(8,128)(2,1)} custom-call(bf16[2048,1280]{1,0:T(8,128)(2,1)} %bitcast.327, bf16[1280,1280]{1,0:T(8,128)(2,1)} %pad_maximum_fusion.3.b), custom_call_target="tpu_custom_call" | custom-call | flops 335544320 | bytes 688128 | tf_op jit(solution)/shard_map/far_norm/pallas_call | solution.py:464
  353.1 6.4 pad_maximum_fusion.2.b
  364.7 9.2 %collective-permute-start.20 = (bf16[160,2560]{1,0:T(8,128)(2,1)}, bf16[160,2560]{1,0:T(8,128)(2,1)}, u32[]{:S(2)}, u32[]{:S(2)}) collective-permute-start(bf16[160,2560]{1,0:T(8,128)(2,1)} %get-tuple-element.176), channel_id=1, source_target_pairs={{0,8},{2,10},{4,12},{6,14},{8,0},{10,2},{12,4},{14,6},{16,24},{18,... | collective-permute-start | bytes 2457608 | tf_op jit(solution)/shard_map/ppermute | solution.py:546
  373.9 21.0 %collective-permute-start.21 = (bf16[160,2560]{1,0:T(8,128)(2,1)}, bf16[160,2560]{1,0:T(8,128)(2,1)}, u32[]{:S(2)}, u32[]{:S(2)}) collective-permute-start(bf16[160,2560]{1,0:T(8,128)(2,1)} %get-tuple-element.175), channel_id=1, source_target_pairs={{0,16},{2,18},{4,20},{6,22},{8,24},{10,26},{12,28},{14,30},{16,0},... | collective-permute-start | bytes 2457608 | tf_op jit(solution)/shard_map/ppermute | solution.py:546
  400.4 59.6 %attn_bwd_b.1 = bf16[2,1024,1920]{2,1,0:T(8,128)(2,1)} custom-call(s32[2,2,4]{2,1,0:T(2,128)} %get-tuple-element.239.flags, s32[2,1,1024]{2,1,0:T(1,128)} %broadcast_in_dim.26.cq, s32[2,1024,128]{2,1,0:T(8,128)} %broadcast_in_dim.29.ck, bf16[2,1024,1920]{2,1,0:T(8,128)(2,1)} %bitcast.309, bf16[2,1024,1920]{2,1,0:T(8,128)(2,1)} %bitcast.310, ...), custom_call_target="tpu_custom_call" | custom-call | flops 671088640 | bytes 1179648 | tf_op jit(solution)/shard_map/attn_bwd_b/pallas_call | solution.py:237
  462.9 10.2 %grad_out.1 = (bf16[2,4,80,640]{3,2,1,0:T(8,128)(2,1)}, bf16[2,4,80,640]{3,2,1,0:T(8,128)(2,1)}) custom-call(s32[3]{0:T(128)} %add_add_fusion.1.where, bf16[1024,640]{1,0:T(8,128)(2,1)} %get-tuple-element.187.refs_0_, bf16[1024,1280]{1,0:T(8,128)(2,1)} %copy-done.7, bf16[1024,640]{1,0:T(8,128)(2,1)} %get-tuple-element.188.refs_2_, ...), custom_call_target="tpu_custom_call" | custom-call | flops 167772160 | bytes 475136 | tf_op jit(solution)/shard_map/grad_out/pallas_call | solution.py:379
  475.0 15.8 %grad_v.1 = (bf16[2,4,80,640]{3,2,1,0:T(8,128)(2,1)}, bf16[2,4,80,640]{3,2,1,0:T(8,128)(2,1)}) custom-call(s32[3]{0:T(128)} %add_add_fusion.where, bf16[2048,1280]{1,0:T(8,128)(2,1)} %bitcast.318, bf16[2048,1920]{1,0:T(8,128)(2,1)} %bitcast.312, bf16[2048,1280]{1,0:T(8,128)(2,1)} %bitcast.332, bf16[2048,1280]{1,0:T(8,128)(2,1)} %bitcast.328), custom_call_target="tpu_custom_call" | custom-call | flops 335544320 | bytes 868352 | tf_op jit(solution)/shard_map/grad_v/pallas_call | solution.py:379
  493.9 16.4 %grad_k.1 = (bf16[2,4,80,640]{3,2,1,0:T(8,128)(2,1)}, bf16[2,4,80,640]{3,2,1,0:T(8,128)(2,1)}) custom-call(s32[3]{0:T(128)} %add_add_fusion.where, bf16[2048,1280]{1,0:T(8,128)(2,1)} %bitcast.319, bf16[2048,1920]{1,0:T(8,128)(2,1)} %bitcast.313, bf16[2048,1280]{1,0:T(8,128)(2,1)} %bitcast.333, bf16[2048,1280]{1,0:T(8,128)(2,1)} %bitcast.329), custom_call_target="tpu_custom_call" | custom-call | flops 335544320 | bytes 868352 | tf_op jit(solution)/shard_map/grad_k/pallas_call | solution.py:379
  513.3 9.6 %grad_q.1 = (bf16[2,4,80,640]{3,2,1,0:T(8,128)(2,1)}, bf16[2,4,80,640]{3,2,1,0:T(8,128)(2,1)}) custom-call(s32[3]{0:T(128)} %add_add_fusion.where, bf16[2048,1280]{1,0:T(8,128)(2,1)} %bitcast.320, bf16[2048,1920]{1,0:T(8,128)(2,1)} %bitcast.314), custom_call_target="tpu_custom_call" | custom-call | flops 167772160 | bytes 475136 | tf_op jit(solution)/shard_map/grad_q/pallas_call | solution.py:379
  524.0 16.5 %near_norm.1 = bf16[2048,1280]{1,0:T(8,128)(2,1)} custom-call(bf16[2048,1920]{1,0:T(8,128)(2,1)} %bitcast.315, bf16[1280,1920]{1,0:T(8,128)(2,1)} %pad_maximum_fusion.2.b), custom_call_target="tpu_custom_call" | custom-call | flops 503316480 | bytes 901120 | tf_op jit(solution)/shard_map/near_norm/pallas_call | solution.py:464
  540.5 6.2 fusion.97
  554.1 7.2 %collective-permute-start.17 = (bf16[320,640]{1,0:T(8,128)(2,1)}, bf16[320,640]{1,0:T(8,128)(2,1)}, u32[]{:S(2)}, u32[]{:S(2)}) collective-permute-start(bf16[320,640]{1,0:T(8,128)(2,1)} %get-tuple-element.185), channel_id=1, source_target_pairs={{0,8},{2,10},{4,12},{6,14},{8,0},{10,2},{12,4},{14,6},{16,24},{18,... | collective-permute-start | bytes 1228808 | tf_op jit(solution)/shard_map/ppermute | solution.py:546
  569.0 6.7 collective-permute-done.17
  580.5 12.0 %collective-permute-done.18 = bf16[320,640]{1,0:T(8,128)(2,1)} collective-permute-done((bf16[320,640]{1,0:T(8,128)(2,1)}, bf16[320,640]{1,0:T(8,128)(2,1)}, u32[]{:S(2)}, u32[]{:S(2)}) %collective-permute-start.18) | collective-permute-done | bytes 409632 | tf_op jit(solution)/shard_map/ppermute | solution.py:546
  600.3 20.8 %mixed.1 = bf16[1024,1280]{1,0:T(8,128)(2,1)} custom-call(bf16[1024,5120]{1,0:T(8,128)(2,1)} %get-tuple-element.137.a1.a, bf16[5120,1280]{1,0:T(8,128)(2,1)} %b.1, f32[1024,1280]{1,0:T(8,128)} %copy-done.2, f32[1,1280]{1,0:T(1,128)} %reshape.427.rest_1_), custom_call_target="tpu_custom_call" | custom-call | flops 671088640 | bytes 1310720 | tf_op jit(solution)/shard_map/mixed/pallas_call | solution.py:464
  626.0 8.2 %fusion.16 = (f32[1280]{0:T(1024)S(1)}, f32[1024]{0:T(1024)}, f32[1024]{0:T(1024)}, f32[1280]{0:T(1024)S(1)}, f32[1024,1280]{1,0:T(8,128)}) fusion(bf16[1,1024,1280]{2,1,0:T(8,128)(2,1)S(1)} %copy-done.5, f32[1024]{0:T(1024)S(1)} %copy-done.44, f32[1024]{0:T(1024)S(1)} %copy-done.40, f32[1280]{0:T(1024)S(1)} %copy-done.42, ...), kind=kLoop, calls=%fused_computation.24 | loop fusion | flops 18345472 | bytes 18381824 | tf_op jit(solution)/shard_map/reduce_sum | solution.py:799
  637.9 8.0 %collective-permute-start.32 = (f32[1,4,960]{2,1,0:T(4,128)S(1)}, f32[1,4,960]{2,1,0:T(4,128)S(1)}, u32[]{:S(2)}, u32[]{:S(2)}) collective-permute-start(f32[1,4,960]{2,1,0:T(4,128)S(1)} %get-tuple-element.228), channel_id=1, source_target_pairs={{0,8},{2,10},{4,12},{6,14},{8,0},{10,2},{12,4},{14,6},{16,24},{18,... | collective-permute-start | bytes 46088 | tf_op jit(solution)/shard_map/ppermute | solution.py:546
  661.7 7.3 %fusion.15 = f32[1,1024,1280]{2,1,0:T(8,128)} fusion(f32[1024,1280]{1,0:T(8,128)} %get-tuple-element.169, bf16[1,1024,1280]{2,1,0:T(8,128)(2,1)} %param.16, f32[1024,1280]{1,0:T(8,128)} %get-tuple-element.170, f32[1024]{0:T(1024)S(1)} %broadcast_multiply_fusion, f32[1024]{0:T(1024)S(1)} %broadcast_multiply_fusion.1, f32[1280]{0:T(1024)} %param.18, ...), kind=kLoop, calls=%fused_computation.23 | loop fusion | flops 11796480 | bytes 18371584 | tf_op jit(solution)/shard_map/reshape | solution.py:771
  685.3 6.8 collective-permute-start.45
  (362 shorter events, 186.1 us)
Async XLA Ops:
  17.7 59.6 %collective-permute-start.3 = (bf16[1,1024,1280]{2,1,0:T(8,128)(2,1)}, bf16[1,1024,1280]{2,1,0:T(8,128)(2,1)}, u32[]{:S(2)}, u32[]{:S(2)}) collective-permute-start(bf16[1,1024,1280]{2,1,0:T(8,128)(2,1)} %fusion.22), channel_id=1, source_target_pairs={{1,0},{0,1},{3,2},{2,3},{5,4},{4,5},{7,6},{6,7},{9,8},{8,9},{11,10... | collective-permute-start | bytes 7864328 | tf_op jit(solution)/shard_map/ppermute | solution.py:552
  77.3 20.6 %collective-permute-start.4 = (bf16[1,1024,1280]{2,1,0:T(8,128)(2,1)}, bf16[1,1024,1280]{2,1,0:T(8,128)(2,1)}, u32[]{:S(2)}, u32[]{:S(2)}) collective-permute-start(bf16[1,1024,1280]{2,1,0:T(8,128)(2,1)} %collective-permute-done.3), channel_id=1, source_target_pairs={{0,2},{2,0},{4,6},{6,4},{8,10},{10,8},{12,14},{14,12},{16,18},{18,... | collective-permute-start | bytes 7864328 | tf_op jit(solution)/shard_map/ppermute | solution.py:546
  191.3 42.5 %collective-permute-start.6 = (bf16[1024,5120]{1,0:T(8,128)(2,1)}, bf16[1024,5120]{1,0:T(8,128)(2,1)}, u32[]{:S(2)}, u32[]{:S(2)}) collective-permute-start(bf16[1024,5120]{1,0:T(8,128)(2,1)} %get-tuple-element.137.a1.a), channel_id=1, source_target_pairs={{0,2},{2,0},{4,6},{6,4},{8,10},{10,8},{12,14},{14,12},{16,18},{18,... | collective-permute-start | bytes 31457288 | tf_op jit(solution)/shard_map/ppermute | solution.py:546
  192.6 41.2 %collective-permute-start.7 = (bf16[1024,640]{1,0:T(8,128)(2,1)}, bf16[1024,640]{1,0:T(8,128)(2,1)}, u32[]{:S(2)}, u32[]{:S(2)}) collective-permute-start(bf16[1024,640]{1,0:T(8,128)(2,1)} %dynamic-slice_bitcast_fusion), channel_id=1, source_target_pairs={{0,2},{2,0},{4,6},{6,4},{8,10},{10,8},{12,14},{14,12},{16,18},{18,... | collective-permute-start | bytes 3932168 | tf_op jit(solution)/shard_map/ppermute | solution.py:546
  193.7 66.1 %collective-permute-start.10 = (bf16[1024,1280]{1,0:T(8,128)(2,1)}, bf16[1024,1280]{1,0:T(8,128)(2,1)}, u32[]{:S(2)}, u32[]{:S(2)}) collective-permute-start(bf16[1024,1280]{1,0:T(8,128)(2,1)} %add_convert_fusion.2.acts.refs_0_), channel_id=1, source_target_pairs={{0,2},{2,0},{4,6},{6,4},{8,10},{10,8},{12,14},{14,12},{16,18},{18,... | collective-permute-start | bytes 7864328 | tf_op jit(solution)/shard_map/ppermute | solution.py:546
  193.7 66.2 %collective-permute-start.11 = (bf16[1024,2560]{1,0:T(8,128)(2,1)}, bf16[1024,2560]{1,0:T(8,128)(2,1)}, u32[]{:S(2)}, u32[]{:S(2)}) collective-permute-start(bf16[1024,2560]{1,0:T(8,128)(2,1)} %get-tuple-element.94), channel_id=1, source_target_pairs={{0,2},{2,0},{4,6},{6,4},{8,10},{10,8},{12,14},{14,12},{16,18},{18,... | collective-permute-start | bytes 15728648 | tf_op jit(solution)/shard_map/ppermute | solution.py:546
  257.3 74.8 %collective-permute-start.8 = (bf16[2,4,320,640]{3,2,1,0:T(8,128)(2,1)}, bf16[2,4,320,640]{3,2,1,0:T(8,128)(2,1)}, u32[]{:S(2)}, u32[]{:S(2)}) collective-permute-start(bf16[2,4,320,640]{3,2,1,0:T(8,128)(2,1)} %get-tuple-element.99), channel_id=1, source_target_pairs={{1,0},{0,1},{3,2},{2,3},{5,4},{4,5},{7,6},{6,7},{9,8},{8,9},{11,10... | collective-permute-start | bytes 9830408 | tf_op jit(solution)/shard_map/ppermute | solution.py:552
  258.0 25.3 %collective-permute-start.9 = (bf16[1024,640]{1,0:T(8,128)(2,1)}, bf16[1024,640]{1,0:T(8,128)(2,1)}, u32[]{:S(2)}, u32[]{:S(2)}) collective-permute-start(bf16[1024,640]{1,0:T(8,128)(2,1)} %convolution_convert_fusion.2), channel_id=1, source_target_pairs={{0,2},{2,0},{4,6},{6,4},{8,10},{10,8},{12,14},{14,12},{16,18},{18,... | collective-permute-start | bytes 3932168 | tf_op jit(solution)/shard_map/ppermute | solution.py:546
  258.2 28.2 %collective-permute-start.13 = (bf16[1024,640]{1,0:T(8,128)(2,1)S(1)}, bf16[1024,640]{1,0:T(8,128)(2,1)}, u32[]{:S(2)}, u32[]{:S(2)}) collective-permute-start(bf16[1024,640]{1,0:T(8,128)(2,1)S(1)} %copy-done.18), channel_id=1, source_target_pairs={{0,2},{2,0},{4,6},{6,4},{8,10},{10,8},{12,14},{14,12},{16,18},{18,... | collective-permute-start | bytes 3932168 | tf_op jit(solution)/shard_map/ppermute | solution.py:546
  259.7 26.7 %collective-permute-start.12 = (bf16[1024,640]{1,0:T(8,128)(2,1)}, bf16[1024,640]{1,0:T(8,128)(2,1)}, u32[]{:S(2)}, u32[]{:S(2)}) collective-permute-start(bf16[1024,640]{1,0:T(8,128)(2,1)} %constant_dynamic-slice_fusion.2), channel_id=1, source_target_pairs={{0,2},{2,0},{4,6},{6,4},{8,10},{10,8},{12,14},{14,12},{16,18},{18,... | collective-permute-start | bytes 3932168 | tf_op jit(solution)/shard_map/ppermute | solution.py:546
  280.5 80.2 %collective-permute-start.15 = (bf16[4,160,2560]{2,1,0:T(8,128)(2,1)}, bf16[4,160,2560]{2,1,0:T(8,128)(2,1)}, u32[]{:S(2)}, u32[]{:S(2)}) collective-permute-start(bf16[4,160,2560]{2,1,0:T(8,128)(2,1)} %get-tuple-element.102), channel_id=1, source_target_pairs={{0,4},{2,6},{4,0},{6,2},{8,12},{10,14},{12,8},{14,10},{16,20},{18,... | collective-permute-start | bytes 9830408 | tf_op jit(solution)/shard_map/ppermute | solution.py:546
  351.7 44.7 %collective-permute-start.16 = (bf16[1,1024,1280]{2,1,0:T(8,128)(2,1)}, bf16[1,1024,1280]{2,1,0:T(8,128)(2,1)}, u32[]{:S(2)}, u32[]{:S(2)}) collective-permute-start(bf16[1,1024,1280]{2,1,0:T(8,128)(2,1)} %slice_bitcast_fusion), channel_id=1, source_target_pairs={{0,2},{2,0},{4,6},{6,4},{8,10},{10,8},{12,14},{14,12},{16,18},{18,... | collective-permute-start | bytes 7864328 | tf_op jit(solution)/shard_map/ppermute | solution.py:546
  359.5 100.5 %collective-permute-start.14 = (bf16[4,320,640]{2,1,0:T(8,128)(2,1)S(1)}, bf16[4,320,640]{2,1,0:T(8,128)(2,1)}, u32[]{:S(2)}, u32[]{:S(2)}) collective-permute-start(bf16[4,320,640]{2,1,0:T(8,128)(2,1)S(1)} %copy-done.21), channel_id=1, source_target_pairs={{0,4},{2,6},{4,0},{6,2},{8,12},{10,14},{12,8},{14,10},{16,20},{18,... | collective-permute-start | bytes 4915208 | tf_op jit(solution)/shard_map/ppermute | solution.py:546
  364.7 126.1 %collective-permute-start.20 = (bf16[160,2560]{1,0:T(8,128)(2,1)}, bf16[160,2560]{1,0:T(8,128)(2,1)}, u32[]{:S(2)}, u32[]{:S(2)}) collective-permute-start(bf16[160,2560]{1,0:T(8,128)(2,1)} %get-tuple-element.176), channel_id=1, source_target_pairs={{0,8},{2,10},{4,12},{6,14},{8,0},{10,2},{12,4},{14,6},{16,24},{18,... | collective-permute-start | bytes 2457608 | tf_op jit(solution)/shard_map/ppermute | solution.py:546
  373.9 117.0 %collective-permute-start.21 = (bf16[160,2560]{1,0:T(8,128)(2,1)}, bf16[160,2560]{1,0:T(8,128)(2,1)}, u32[]{:S(2)}, u32[]{:S(2)}) collective-permute-start(bf16[160,2560]{1,0:T(8,128)(2,1)} %get-tuple-element.175), channel_id=1, source_target_pairs={{0,16},{2,18},{4,20},{6,22},{8,24},{10,26},{12,28},{14,30},{16,0},... | collective-permute-start | bytes 2457608 | tf_op jit(solution)/shard_map/ppermute | solution.py:546
  394.9 96.0 %collective-permute-start.22 = (bf16[160,2560]{1,0:T(8,128)(2,1)S(1)}, bf16[160,2560]{1,0:T(8,128)(2,1)}, u32[]{:S(2)}, u32[]{:S(2)}) collective-permute-start(bf16[160,2560]{1,0:T(8,128)(2,1)S(1)} %get-tuple-element.174), channel_id=1, source_target_pairs={{0,24},{2,26},{4,28},{6,30},{8,16},{10,18},{12,20},{14,22},{16,8},... | collective-permute-start | bytes 2457608 | tf_op jit(solution)/shard_map/ppermute | solution.py:546
  400.4 225.5 %collective-permute-start.31 = (bf16[1,1024,1280]{2,1,0:T(8,128)(2,1)}, bf16[1,1024,1280]{2,1,0:T(8,128)(2,1)}, u32[]{:S(2)}, u32[]{:S(2)}) collective-permute-start(bf16[1,1024,1280]{2,1,0:T(8,128)(2,1)} %fusion.23), channel_id=1, source_target_pairs={{0,1},{1,0},{2,3},{3,2},{4,5},{5,4},{6,7},{7,6},{8,9},{9,8},{10,11... | collective-permute-start | bytes 7864328 | tf_op jit(solution)/shard_map/ppermute | solution.py:555
  473.1 39.1 %collective-permute-start.23 = (bf16[2,4,80,640]{3,2,1,0:T(8,128)(2,1)}, bf16[2,4,80,640]{3,2,1,0:T(8,128)(2,1)S(1)}, u32[]{:S(2)}, u32[]{:S(2)}) collective-permute-start(bf16[2,4,80,640]{3,2,1,0:T(8,128)(2,1)} %get-tuple-element.116), channel_id=1, source_target_pairs={{1,0},{0,1},{3,2},{2,3},{5,4},{4,5},{7,6},{6,7},{9,8},{8,9},{11,10... | collective-permute-start | bytes 2457608 | tf_op jit(solution)/shard_map/ppermute | solution.py:552
  490.8 32.1 %collective-permute-start.24 = (bf16[2,4,80,640]{3,2,1,0:T(8,128)(2,1)}, bf16[2,4,80,640]{3,2,1,0:T(8,128)(2,1)S(1)}, u32[]{:S(2)}, u32[]{:S(2)}) collective-permute-start(bf16[2,4,80,640]{3,2,1,0:T(8,128)(2,1)} %get-tuple-element.119), channel_id=1, source_target_pairs={{1,0},{0,1},{3,2},{2,3},{5,4},{4,5},{7,6},{6,7},{9,8},{8,9},{11,10... | collective-permute-start | bytes 2457608 | tf_op jit(solution)/shard_map/ppermute | solution.py:552
  510.3 51.0 %collective-permute-start.25 = (bf16[2,4,80,640]{3,2,1,0:T(8,128)(2,1)}, bf16[2,4,80,640]{3,2,1,0:T(8,128)(2,1)}, u32[]{:S(2)}, u32[]{:S(2)}) collective-permute-start(bf16[2,4,80,640]{3,2,1,0:T(8,128)(2,1)} %get-tuple-element.125), channel_id=1, source_target_pairs={{1,0},{0,1},{3,2},{2,3},{5,4},{4,5},{7,6},{6,7},{9,8},{8,9},{11,10... | collective-permute-start | bytes 2457608 | tf_op jit(solution)/shard_map/ppermute | solution.py:552
  546.7 79.2 %collective-permute-start.30 = (bf16[1024,1280]{1,0:T(8,128)(2,1)}, bf16[1024,1280]{1,0:T(8,128)(2,1)}, u32[]{:S(2)}, u32[]{:S(2)}) collective-permute-start(bf16[1024,1280]{1,0:T(8,128)(2,1)} %get-tuple-element.180), channel_id=1, source_target_pairs={{0,2},{2,0},{4,6},{6,4},{8,10},{10,8},{12,14},{14,12},{16,18},{18,... | collective-permute-start | bytes 7864328 | tf_op jit(solution)/shard_map/ppermute | solution.py:546
  554.1 21.6 %collective-permute-start.17 = (bf16[320,640]{1,0:T(8,128)(2,1)}, bf16[320,640]{1,0:T(8,128)(2,1)}, u32[]{:S(2)}, u32[]{:S(2)}) collective-permute-start(bf16[320,640]{1,0:T(8,128)(2,1)} %get-tuple-element.185), channel_id=1, source_target_pairs={{0,8},{2,10},{4,12},{6,14},{8,0},{10,2},{12,4},{14,6},{16,24},{18,... | collective-permute-start | bytes 1228808 | tf_op jit(solution)/shard_map/ppermute | solution.py:546
  561.3 31.1 %collective-permute-start.18 = (bf16[320,640]{1,0:T(8,128)(2,1)}, bf16[320,640]{1,0:T(8,128)(2,1)}, u32[]{:S(2)}, u32[]{:S(2)}) collective-permute-start(bf16[320,640]{1,0:T(8,128)(2,1)} %get-tuple-element.184), channel_id=1, source_target_pairs={{0,16},{2,18},{4,20},{6,22},{8,24},{10,26},{12,28},{14,30},{16,0},... | collective-permute-start | bytes 1228808 | tf_op jit(solution)/shard_map/ppermute | solution.py:546
  561.3 31.2 %collective-permute-start.19 = (bf16[320,640]{1,0:T(8,128)(2,1)}, bf16[320,640]{1,0:T(8,128)(2,1)}, u32[]{:S(2)}, u32[]{:S(2)}) collective-permute-start(bf16[320,640]{1,0:T(8,128)(2,1)} %get-tuple-element.183), channel_id=1, source_target_pairs={{0,24},{2,26},{4,28},{6,30},{8,16},{10,18},{12,20},{14,22},{16,8},... | collective-permute-start | bytes 1228808 | tf_op jit(solution)/shard_map/ppermute | solution.py:546
  575.7 20.8 %collective-permute-start.26 = (bf16[4,80,640]{2,1,0:T(8,128)(2,1)}, bf16[4,80,640]{2,1,0:T(8,128)(2,1)S(1)}, u32[]{:S(2)}, u32[]{:S(2)}) collective-permute-start(bf16[4,80,640]{2,1,0:T(8,128)(2,1)} %get-tuple-element.196), channel_id=1, source_target_pairs={{0,4},{2,6},{4,0},{6,2},{8,12},{10,14},{12,8},{14,10},{16,20},{18,... | collective-permute-start | bytes 1228808 | tf_op jit(solution)/shard_map/ppermute | solution.py:546
  592.4 28.7 %collective-permute-start.28 = (bf16[4,80,640]{2,1,0:T(8,128)(2,1)}, bf16[4,80,640]{2,1,0:T(8,128)(2,1)S(1)}, u32[]{:S(2)}, u32[]{:S(2)}) collective-permute-start(bf16[4,80,640]{2,1,0:T(8,128)(2,1)} %get-tuple-element.194), channel_id=1, source_target_pairs={{0,4},{2,6},{4,0},{6,2},{8,12},{10,14},{12,8},{14,10},{16,20},{18,... | collective-permute-start | bytes 1228808 | tf_op jit(solution)/shard_map/ppermute | solution.py:546
  592.6 32.3 %collective-permute-start.27 = (bf16[2,4,80,640]{3,2,1,0:T(8,128)(2,1)}, bf16[2,4,80,640]{3,2,1,0:T(8,128)(2,1)S(1)}, u32[]{:S(2)}, u32[]{:S(2)}) collective-permute-start(bf16[2,4,80,640]{3,2,1,0:T(8,128)(2,1)} %get-tuple-element.129), channel_id=1, source_target_pairs={{1,0},{0,1},{3,2},{2,3},{5,4},{4,5},{7,6},{6,7},{9,8},{8,9},{11,10... | collective-permute-start | bytes 2457608 | tf_op jit(solution)/shard_map/ppermute | solution.py:552
  596.5 27.6 %collective-permute-start.29 = (bf16[4,80,640]{2,1,0:T(8,128)(2,1)S(1)}, bf16[4,80,640]{2,1,0:T(8,128)(2,1)S(1)}, u32[]{:S(2)}, u32[]{:S(2)}) collective-permute-start(bf16[4,80,640]{2,1,0:T(8,128)(2,1)S(1)} %get-tuple-element.192), channel_id=1, source_target_pairs={{0,4},{2,6},{4,0},{6,2},{8,12},{10,14},{12,8},{14,10},{16,20},{18,... | collective-permute-start | bytes 1228808 | tf_op jit(solution)/shard_map/ppermute | solution.py:546
  621.2 57.9 %collective-permute-start.59 = (bf16[160,2560]{1,0:T(8,128)(2,1)}, bf16[160,2560]{1,0:T(8,128)(2,1)}, u32[]{:S(2)}, u32[]{:S(2)}) collective-permute-start(bf16[160,2560]{1,0:T(8,128)(2,1)} %add_convert_fusion.6), channel_id=1, source_target_pairs={{1,0},{0,1},{3,2},{2,3},{5,4},{4,5},{7,6},{6,7},{9,8},{8,9},{11,10... | collective-permute-start | bytes 2457608 | tf_op jit(solution)/shard_map/ppermute | solution.py:552
  624.1 55.1 %collective-permute-start.60 = (bf16[320,640]{1,0:T(8,128)(2,1)}, bf16[320,640]{1,0:T(8,128)(2,1)}, u32[]{:S(2)}, u32[]{:S(2)}) collective-permute-start(bf16[320,640]{1,0:T(8,128)(2,1)} %add_convert_fusion.17), channel_id=1, source_target_pairs={{1,0},{0,1},{3,2},{2,3},{5,4},{4,5},{7,6},{6,7},{9,8},{8,9},{11,10... | collective-permute-start | bytes 1228808 | tf_op jit(solution)/shard_map/ppermute | solution.py:552
  650.5 21.3 %collective-permute-start.39 = (bf16[80,640]{1,0:T(8,128)(2,1)}, bf16[80,640]{1,0:T(8,128)(2,1)}, u32[]{:S(2)}, u32[]{:S(2)}) collective-permute-start(bf16[80,640]{1,0:T(8,128)(2,1)} %get-tuple-element.203), channel_id=1, source_target_pairs={{0,8},{2,10},{4,12},{6,14},{8,0},{10,2},{12,4},{14,6},{16,24},{18,... | collective-permute-start | bytes 307208 | tf_op jit(solution)/shard_map/ppermute | solution.py:546
  651.3 20.6 %collective-permute-start.40 = (bf16[80,640]{1,0:T(8,128)(2,1)}, bf16[80,640]{1,0:T(8,128)(2,1)}, u32[]{:S(2)}, u32[]{:S(2)}) collective-permute-start(bf16[80,640]{1,0:T(8,128)(2,1)} %get-tuple-element.205), channel_id=1, source_target_pairs={{0,16},{2,18},{4,20},{6,22},{8,24},{10,26},{12,28},{14,30},{16,0},... | collective-permute-start | bytes 307208 | tf_op jit(solution)/shard_map/ppermute | solution.py:546
  (90 other events, 1264.0 us)

commit v3 on v2

v3 whole, which is shorter than its diff:
```python
import functools
import math

import jax
import jax.numpy as jnp
from jax import lax
from jax.experimental import pallas as pl
from jax.experimental.pallas import tpu as pltpu
from jax.sharding import PartitionSpec as P

HEADS = 20
HEAD_DIM = 64
HD = HEAD_DIM
EPS = 1e-05
NEG = -1e30
LOG2E = math.log2(math.e)
C2 = LOG2E / math.sqrt(HEAD_DIM)
F32 = jnp.float32
BF = jnp.bfloat16
NN = (((1,), (0,)), ((), ()))
NT = (((1,), (1,)), ((), ()))
TN = (((0,), (0,)), ((), ()))
VMEM_LIMIT = 56 * 2**20
SHARE = 20
VR = HD + 16


def dot(a, b, dims):
    return lax.dot_general(a, b, dims, preferred_element_type=F32)


def head_sumsq(x,hp16):
    W=x.shape[1]
    sq=x.astype(F32)*x.astype(F32)
    row=lax.broadcasted_iota(jnp.int32,(hp16,W),0); col=lax.broadcasted_iota(jnp.int32,(hp16,W),1)
    ones=jnp.where(row==col//HD,1.0,0.0).astype(BF)
    return lax.dot_general(ones,sq.astype(BF),NT,preferred_element_type=F32)

def fwd_kernel(flags,cq,ck,q,k,v,*rest,first,tq,tk,heads):
    if first:
        accT_o,m_o,l_o,qm,vT,bias,acc,m,l,kn=rest
    else:
        accT_i,m_i,l_i,o_o,lse_o,qm,vT,bias,acc,m,l,kn=rest
    r=pl.program_id(0); qi=pl.program_id(1)
    nk=k.shape[1]//tk
    hp16=m.shape[0]
    @pl.when(qi==0)
    def _():
        for hh in range(heads):
            vT[hh*VR:hh*VR+HD,:]=v[0,:,hh*HD:(hh+1)*HD].T
            vT[hh*VR+HD:(hh+1)*VR,:]=jnp.ones((VR-HD,vT.shape[1]),BF)
        kn[...]=jnp.broadcast_to(jnp.sqrt(jnp.max(head_sumsq(k[0],hp16),1,keepdims=True)),kn.shape)
    lane=lax.broadcasted_iota(jnp.int32,(tq,128),1)
    for hp in range(heads//2):
        qp=q[0,:,hp*128:(hp+1)*128]
        qm[2*hp]=jnp.where(lane<64,qp,0).astype(BF)
        qm[2*hp+1]=jnp.where(lane>=64,qp,0).astype(BF)
    bound=jnp.sqrt(head_sumsq(q[0],hp16))*kn[:,0:1]*(C2*1.02)
    safe=jnp.max(bound)<50.0
    if first:
        m0=bound
    else:
        m0=jnp.maximum(bound,m_i[0])
    def loop(online):
        if first:
            acc[...]=jnp.zeros_like(acc); l[...]=jnp.zeros_like(l)
            m[...]=jnp.full_like(m,NEG) if online else m0
        elif online:
            acc[...]=accT_i[0]; m[...]=m_i[0]; l[...]=l_i[0]
        else:
            al=jnp.exp2(m_i[0]-m0)
            m[...]=m0; l[...]=al*l_i[0]
            for hh in range(heads):
                hs=slice(hh*HD,(hh+1)*HD)
                acc[hs,:]=al[hh:hh+1,:]*accT_i[0,hs,:]
        def body(kt,masked):
            ks=pl.ds(pl.multiple_of(kt*tk,tk),tk)
            if online:
                @pl.loop(0,heads//2)
                def _(hp):
                    kp=k[0,ks,pl.ds(pl.multiple_of(hp*128,128),128)]
                    for j in range(2):
                        hh=2*hp+j
                        s=lax.dot_general(kp,qm[hh],NT,preferred_element_type=F32)*C2+bias[...]
                        mp=m[pl.ds(hh,1),:]
                        mn=jnp.maximum(mp,jnp.max(s,0,keepdims=True))
                        p=jnp.exp2(s-mn)
                        al=jnp.exp2(mp-mn)
                        m[pl.ds(hh,1),:]=mn
                        l[pl.ds(hh,1),:]=al*l[pl.ds(hh,1),:]+jnp.sum(p,0,keepdims=True)
                        hs=pl.ds(pl.multiple_of(hh*HD,HD),HD)
                        vs=pl.ds(pl.multiple_of(hh*VR,16),HD)
                        acc[hs,:]=al*acc[hs,:]+lax.dot_general(vT[vs,ks],p.astype(BF),NN,preferred_element_type=F32)
                return
            def score(hh):
                s=lax.dot_general(k[0,ks,(hh//2)*128:(hh//2+1)*128],qm[hh],NT,preferred_element_type=F32)*C2
                if masked: s=s+bias[...]
                return s
            s=score(0); pp=None
            for hh in range(heads+1):
                if hh+1<heads: sn=score(hh+1)
                if pp is not None:
                    h1=hh-1
                    both=lax.dot_general(vT[h1*VR:(h1+1)*VR,ks],pp,NN,preferred_element_type=F32)
                    acc[h1*HD:(h1+1)*HD,:]+=both[:HD]
                    l[h1:h1+1,:]+=both[HD:HD+1]
                if hh<heads:
                    p=jnp.exp2(s-m[hh:hh+1,:])
                    pp=p.astype(BF)
                s=sn
        @pl.loop(0,nk)
        def _(kt):
            f=flags[r,qi,kt]
            def mask():
                ks=pl.ds(pl.multiple_of(kt*tk,tk),tk)
                bias[...]=jnp.where(ck[0,ks,0:1]==cq[0,0:1,:],0.0,NEG)
            if online:
                @pl.when(f>0)
                def _():
                    mask(); body(kt,True)
            else:
                @pl.when(f==1)
                def _():
                    mask(); body(kt,True)
                @pl.when(f==2)
                def _(): body(kt,False)
    @pl.when(safe)
    def _(): loop(False)
    @pl.when(jnp.logical_not(safe))
    def _(): loop(True)
    if first:
        accT_o[0]=acc[...]; m_o[0]=m[...]; l_o[0]=l[...]
    else:
        for hp in range(heads//2):
            parts=[]
            for hh in (2*hp,2*hp+1):
                parts.append(acc[hh*HD:(hh+1)*HD,:]/l[hh:hh+1,:])
            o_o[0,:,hp*128:(hp+1)*128]=jnp.concatenate(parts,0).T.astype(BF)
        lse_o[0]=m[...]+jnp.log2(l[...])

def attn_fwd(flags,cq,ck,q,kv,kb,state,tq,tk,heads):
    nr,S,_=q.shape; W=heads*HD; Sk=kv.shape[1]; hp16=-(-heads//8)*8
    first=state is None
    qs=lambda r,i,*_:(r,i,0); ts=lambda r,i,*_:(r,0,i); ks=lambda r,i,*_:(r,0,0)
    stspec=[pl.BlockSpec((1,W,tq),ts),pl.BlockSpec((1,hp16,tq),ts),pl.BlockSpec((1,hp16,tq),ts)]
    ins=[pl.BlockSpec((1,1,tq),ts),pl.BlockSpec((1,Sk,128),ks),pl.BlockSpec((1,tq,W),qs),pl.BlockSpec((1,Sk,W),lambda r,i,*_:(r,0,kb)),pl.BlockSpec((1,Sk,W),lambda r,i,*_:(r,0,kb+1))]
    if first:
        outs=stspec
        osh=[jax.ShapeDtypeStruct((nr,W,S),F32)]+[jax.ShapeDtypeStruct((nr,hp16,S),F32)]*2
    else:
        ins=ins+stspec
        outs=[pl.BlockSpec((1,tq,W),qs),pl.BlockSpec((1,hp16,tq),ts)]
        osh=[jax.ShapeDtypeStruct((nr,S,W),BF),jax.ShapeDtypeStruct((nr,hp16,S),F32)]
    fl=4*nr*S*Sk*W
    return pl.pallas_call(functools.partial(fwd_kernel,first=first,tq=tq,tk=tk,heads=heads),
        out_shape=osh,
        grid_spec=pltpu.PrefetchScalarGridSpec(num_scalar_prefetch=1,grid=(nr,S//tq),in_specs=ins,out_specs=outs,
          scratch_shapes=[pltpu.VMEM((heads,tq,128),BF),pltpu.VMEM((heads*VR,Sk),BF),pltpu.VMEM((tk,tq),F32),pltpu.VMEM((W,tq),F32),pltpu.VMEM((hp16,tq),F32),pltpu.VMEM((hp16,tq),F32),pltpu.VMEM((hp16,128),F32)]),
        compiler_params=pltpu.CompilerParams(dimension_semantics=("arbitrary","arbitrary"),vmem_limit_bytes=VMEM_LIMIT),
        cost_estimate=pl.CostEstimate(flops=fl//SHARE,bytes_accessed=nr*(S*W*2+2*Sk*W*2+S*W*4)//SHARE,transcendentals=0),
        name="attn_fwd_a" if first else "attn_fwd_b",
    )(flags,cq,ck,q,kv,kv,*(state or ()))

def bwd_kernel(flags,cq,ck,q,k,v,do_own,do_mate,o,lse,*rest,spans,tq,tk):
    first=len(spans)==2
    if first:
        dqT_o,*dkv_o,qm,dom,kT,bias,dqT,dk,dv,delta=rest
    else:
        dqT_i,dqkv_o,qm,dom,kT,bias,dqT,dk,dv,delta=rest
    r=pl.program_id(0); qi=pl.program_id(1); nq=pl.num_programs(1)
    nk=k.shape[1]//tk
    low=spans[0][0]; heads=sum(b-a for a,b in spans)
    W=heads*HD; c0=low*HD
    @pl.when(qi==0)
    def _():
        kT[...]=k[0,:,c0:c0+W].T
        dk[...]=jnp.zeros_like(dk); dv[...]=jnp.zeros_like(dv)
    own=r<pl.num_programs(0)//2
    lane=lax.broadcasted_iota(jnp.int32,(tq,128),1)
    for hp in range(heads//2):
        c=slice(c0+hp*128,c0+(hp+1)*128)
        qp=q[0,:,c]*jnp.asarray(0.125,BF); dp_=jnp.where(own,do_own[0,:,c],do_mate[0,:,c])
        qm[2*hp]=jnp.where(lane<64,qp,0).astype(BF)
        qm[2*hp+1]=jnp.where(lane>=64,qp,0).astype(BF)
        dom[2*hp]=jnp.where(lane<64,dp_,0).astype(BF)
        dom[2*hp+1]=jnp.where(lane>=64,dp_,0).astype(BF)
    prod=jnp.where(own,do_own[0,:,c0:c0+W],do_mate[0,:,c0:c0+W]).astype(F32)*o[0,:,c0:c0+W].astype(F32)
    hi=prod.astype(BF); lo=(prod-hi.astype(F32)).astype(BF)
    n16=delta.shape[0]
    row=lax.broadcasted_iota(jnp.int32,(n16,W),0); col_=lax.broadcasted_iota(jnp.int32,(n16,W),1)
    ones=jnp.where(row==col_//HD,1.0,0.0).astype(BF)
    delta[...]=lax.dot_general(ones,hi,NT,preferred_element_type=F32)+lax.dot_general(ones,lo,NT,preferred_element_type=F32)
    if first: dqT[...]=jnp.zeros_like(dqT)
    else: dqT[...]=dqT_i[0,c0:c0+W,:]
    def body(kt):
        ks=pl.ds(pl.multiple_of(kt*tk,tk),tk)
        def col(hh): return slice((hh//2)*128,(hh//2+1)*128)
        def wide(hh): return slice(c0+(hh//2)*128,c0+(hh//2+1)*128)
        def score(hh):
            s=lax.dot_general(k[0,ks,wide(hh)],qm[hh],NT,preferred_element_type=F32)*LOG2E+bias[...]
            return s,lax.dot_general(v[0,ks,wide(hh)],dom[hh],NT,preferred_element_type=F32)
        nxt=score(0); prev=None
        for hh in range(heads+1):
            cur=nxt
            if hh+1<heads: nxt=score(hh+1)
            if prev is not None:
                h1=hh-1; pb,dsb=prev
                hs=slice(h1*HD,(h1+1)*HD)
                dqT[hs,:]+=lax.dot_general(kT[hs,ks],dsb,NN,preferred_element_type=F32)
                dv[ks,col(h1)]+=jnp.dot(pb,dom[h1],preferred_element_type=F32)
                dk[ks,col(h1)]+=jnp.dot(dsb,qm[h1],preferred_element_type=F32)
            if hh<heads:
                s,dp=cur
                at=low+hh
                p=jnp.exp2(s-lse[0,at:at+1,:])
                ds=p*(dp-delta[hh:hh+1,:])
                prev=(p.astype(BF),ds.astype(BF))
    @pl.loop(0,nk)
    def _(kt):
        f=flags[r,qi,kt]
        @pl.when(f>0)
        def _():
            ks=pl.ds(pl.multiple_of(kt*tk,tk),tk)
            bias[...]=jnp.where(ck[0,ks,0:1]==cq[0,0:1,:],0.0,NEG)
            body(kt)
    if first: dqT_o[0]=dqT[...]
    else: dqkv_o[0,pl.ds(pl.multiple_of(qi*tq,tq),tq),0:W]=(dqT[...]*0.125).T.astype(BF)
    @pl.when(qi==nq-1)
    def _():
        if first:
            for (a,b),out in zip(spans,dkv_o):
                n=(b-a)*HD; at=(a-low)*HD
                out[0,:,0:n]=dk[:,at:at+n].astype(BF); out[0,:,n:2*n]=dv[:,at:at+n].astype(BF)
        else:
            dqkv_o[0,:,W:2*W]=dk[...].astype(BF); dqkv_o[0,:,2*W:3*W]=dv[...].astype(BF)

def attn_bwd(flags,cq,ck,q,kv,kb,do,o,lse,dqT,tq,tk,full,spans,name):
    nr,S,_=q.shape; F=full*HD; Sk=kv.shape[1]; n16=lse.shape[1]
    heads=sum(b-a for a,b in spans); W=heads*HD
    first=dqT is None
    qs=lambda r,i,*_:(r,i,0); ts=lambda r,i,*_:(r,0,i); ks=lambda r,i,*_:(r,0,0)
    ins=[pl.BlockSpec((1,1,tq),ts),pl.BlockSpec((1,Sk,128),ks),pl.BlockSpec((1,tq,F),qs),pl.BlockSpec((1,Sk,F),lambda r,i,*_:(r,0,kb)),pl.BlockSpec((1,Sk,F),lambda r,i,*_:(r,0,kb+1)),
         pl.BlockSpec((1,tq,F),lambda r,i,*_:(jnp.minimum(r,nr//2-1),jnp.where(r<nr//2,i,S//tq-1),0)),
         pl.BlockSpec((1,tq,F),lambda r,i,*_:(jnp.maximum(r-nr//2,0),jnp.where(r<nr//2,0,i),0)),
         pl.BlockSpec((1,tq,F),qs),pl.BlockSpec((1,n16,tq),ts)]
    if first:
        widths=[2*(b-a)*HD for a,b in spans]
        outs=[pl.BlockSpec((1,F,tq),ts)]+[pl.BlockSpec((1,Sk,n),ks) for n in widths]
        osh=[jax.ShapeDtypeStruct((nr,F,S),F32)]+[jax.ShapeDtypeStruct((nr,Sk,n),BF) for n in widths]
        extra=()
    else:
        ins=ins+[pl.BlockSpec((1,F,tq),ts)]
        outs=[pl.BlockSpec((1,Sk,3*W),ks)]; osh=[jax.ShapeDtypeStruct((nr,Sk,3*W),BF)]
        extra=(dqT,)
    fl=10*nr*S*Sk*W
    return pl.pallas_call(functools.partial(bwd_kernel,spans=spans,tq=tq,tk=tk),
        out_shape=osh,
        grid_spec=pltpu.PrefetchScalarGridSpec(num_scalar_prefetch=1,grid=(nr,S//tq),in_specs=ins,out_specs=outs,
          scratch_shapes=[pltpu.VMEM((heads,tq,128),BF),pltpu.VMEM((heads,tq,128),BF),pltpu.VMEM((W,Sk),BF),pltpu.VMEM((tk,tq),F32),pltpu.VMEM((W,tq),F32),
             pltpu.VMEM((Sk,W),F32),pltpu.VMEM((Sk,W),F32),pltpu.VMEM((n16,tq),F32)]),
        compiler_params=pltpu.CompilerParams(dimension_semantics=("arbitrary","arbitrary"),vmem_limit_bytes=VMEM_LIMIT),
        cost_estimate=pl.CostEstimate(flops=fl//SHARE,bytes_accessed=nr*(3*S*W*2+4*Sk*W*2+S*W*4)//SHARE,transcendentals=0),
        name=name,
    )(flags,cq,ck,q,kv,kv,*do,o,lse,*extra)


def ffn_kernel(where, acts, w, b, d_act, *rest):
    act_o, d_pre_o, sum_o = rest[-3:]
    rows = acts.shape[0]
    chunk = min(256, rows)
    count = rows // chunk

    def product(i):
        return dot(acts[i * chunk : (i + 1) * chunk, :], w[...], NN) + b[...]

    pre = product(0)
    total = None
    for i in range(count):
        following = product(i + 1) if i + 1 < count else None
        at = slice(i * chunk, (i + 1) * chunk)
        cdf = 0.5 + 0.5 * lax.erf(pre * math.sqrt(0.5))
        pdf = jnp.exp(-0.5 * pre * pre) * (1.0 / math.sqrt(2.0 * math.pi))
        act_o[at, :] = (pre * cdf).astype(BF)
        d_pre = (d_act[at, :].astype(F32) * (cdf + pre * pdf)).astype(BF)
        d_pre_o[at, :] = d_pre
        part = jnp.sum(d_pre.astype(F32), axis=0, keepdims=True)
        total = part if total is None else total + part
        pre = following
    sum_o[...] = total


def ffn_call(where, acts, w, b, d_act, earlier, name):
    rows, width = acts.shape
    ff = w.shape[1]
    tile = 512
    steps = ff // 2 // tile
    mine = bool(earlier)

    def place(i, where):
        return (where[1] if mine else 1 - where[1]) * steps + i

    col = lambda i, where: (0, place(i, where))
    return pl.pallas_call(
        ffn_kernel,
        out_shape=[
            jax.ShapeDtypeStruct((rows, ff), BF),
            jax.ShapeDtypeStruct((rows, ff // 2), BF),
            jax.ShapeDtypeStruct((1, ff), F32),
        ],
        grid_spec=pltpu.PrefetchScalarGridSpec(
            num_scalar_prefetch=1,
            grid=(steps,),
            in_specs=[
                pl.BlockSpec((rows, width), lambda i, where: (0, 0)),
                pl.BlockSpec((width, tile), col),
                pl.BlockSpec((1, tile), col),
                pl.BlockSpec((rows, tile), col),
            ]
            + [pl.BlockSpec(memory_space=pl.ANY)] * len(earlier),
            out_specs=[
                pl.BlockSpec((rows, tile), col),
                pl.BlockSpec((rows, tile), lambda i, where: (0, i)),
                pl.BlockSpec((1, tile), col),
            ],
        ),
        input_output_aliases={5: 0, 6: 2} if mine else {},
        compiler_params=pltpu.CompilerParams(vmem_limit_bytes=VMEM_LIMIT),
        cost_estimate=pl.CostEstimate(
            flops=rows * width * ff // SHARE,
            bytes_accessed=(2 * rows * width + width * ff + 3 * rows * ff) // SHARE,
            transcendentals=0,
        ),
        name=name,
    )(where, acts, w, b, d_act, *earlier)


def store_blocks(where, acc, outs, first, second, halved):
    rows = acc.shape[0] // (first * second)
    for one in range(first):
        for two in range(second):
            block = lax.bitwise_xor(two * first + one, where[0]) * rows
            if halved:
                for part in range(2):
                    at = block + lax.bitwise_xor(where[2], part) * (rows // 2)
                    piece = acc[pl.ds(pl.multiple_of(at, 16), rows // 2), :]
                    outs[part][one, two] = piece.astype(BF)
            else:
                outs[one][two] = acc[pl.ds(pl.multiple_of(block, 16), rows), :].astype(BF)


def grad_kernel(where, *refs, groups, first, second, halved, outs):
    acc = refs[-1]
    ins = refs[: sum(2 * g for g in groups)]
    height = acc.shape[0] // len(groups)
    at = 0
    for index, pairs in enumerate(groups):
        total = None
        for _ in range(pairs):
            part = dot(ins[at][...], ins[at + 1][...], TN)
            total = part if total is None else total + part
            at += 2
        acc[index * height : (index + 1) * height, :] = total
    store_blocks(where, acc, refs[-1 - outs : -1], first, second, halved)


def grad_call(where, groups, width, first, second, tile, halved, name, into=()):
    ins, flat, depth = [], [], 0
    for group in groups:
        for a, b, offset in group:
            ins.append(pl.BlockSpec(a.shape, lambda i, where: (0, 0)))
            if offset is None:
                index = lambda i, where: (0, where[1] * (width // tile) + i)
            else:
                index = lambda i, where, offset=offset: (0, offset // tile + i)
            ins.append(pl.BlockSpec((b.shape[0], tile), index))
            flat += [a, b]
            depth += a.shape[0]
    height = sum(g[0][0].shape[1] for g in groups)
    depth = depth // len(groups)
    rows = height // (first * second)
    if halved:
        shape, block = (first, second, rows // 2, width), (first, second, rows // 2, tile)
        outs = 2
        index = lambda i, where: (0, 0, 0, i)
    else:
        shape, block = (second, rows, width), (second, rows, tile)
        outs = first
        index = lambda i, where: (0, 0, i)
    if into:
        shape = into[0].shape
        row = shape[2] * 2 // rows - 1
        index = lambda i, where: (0, 0, row, i)
    return pl.pallas_call(
        functools.partial(
            grad_kernel, groups=[len(g) for g in groups], first=first, second=second, halved=halved, outs=outs
        ),
        out_shape=[jax.ShapeDtypeStruct(shape, BF)] * outs,
        grid_spec=pltpu.PrefetchScalarGridSpec(
            num_scalar_prefetch=1,
            grid=(width // tile,),
            in_specs=ins + [pl.BlockSpec(memory_space=pl.ANY)] * len(into),
            out_specs=[pl.BlockSpec(block, index)] * outs,
            scratch_shapes=[pltpu.VMEM((height, tile), F32)],
        ),
        input_output_aliases={1 + len(flat) + i: i for i in range(len(into))},
        compiler_params=pltpu.CompilerParams(vmem_limit_bytes=VMEM_LIMIT),
        cost_estimate=pl.CostEstimate(
            flops=2 * depth * height * width // SHARE,
            bytes_accessed=2 * (depth * (height + width) + height * width) // SHARE,
            transcendentals=0,
        ),
        name=name,
    )(where, *flat, *into)


def qkv_kernel(where, near_a, near_b, far_a, far_b, *refs, first, second, halved):
    *outs, sum_o, acc = refs
    acc[...] = dot(near_a[...], near_b[...], TN)
    sum_o[...] = jnp.sum(near_b[...].astype(F32), axis=0, keepdims=True)

    @pl.when(pl.program_id(0) > 0)
    def _():
        acc[...] += dot(far_a[...], far_b[...], TN)
        sum_o[...] += jnp.sum(far_b[...].astype(F32), axis=0, keepdims=True)

    store_blocks(where, acc, outs, first, second, halved)


def qkv_call(where, near, far, first, second, halved, name):
    (near_a, near_b), (far_a, far_b) = near, far
    height = near_a.shape[1]
    width = near_b.shape[1]
    tile = width // 3
    rows = height // (first * second)
    if halved:
        shape, block = (first, second, rows // 2, width), (first, second, rows // 2, tile)
        outs = 2
        index = lambda i, where: (0, 0, 0, i)
    else:
        shape, block = (second, rows, width), (second, rows, tile)
        outs = first
        index = lambda i, where: (0, 0, i)
    once = pl.Buffered(1)
    return pl.pallas_call(
        functools.partial(qkv_kernel, first=first, second=second, halved=halved),
        out_shape=[jax.ShapeDtypeStruct(shape, BF)] * outs + [jax.ShapeDtypeStruct((1, width), F32)],
        grid_spec=pltpu.PrefetchScalarGridSpec(
            num_scalar_prefetch=1,
            grid=(3,),
            in_specs=[
                pl.BlockSpec(near_a.shape, lambda i, where: (0, 0), pipeline_mode=once),
                pl.BlockSpec((near_b.shape[0], tile), lambda i, where: (0, i)),
                pl.BlockSpec(far_a.shape, lambda i, where: (0, 0), pipeline_mode=once),
                pl.BlockSpec((far_b.shape[0], tile), lambda i, where: (0, jnp.maximum(i - 1, 0))),
            ],
            out_specs=[pl.BlockSpec(block, index)] * outs + [pl.BlockSpec((1, tile), lambda i, where: (0, i))],
            scratch_shapes=[pltpu.VMEM((height, tile), F32)],
        ),
        compiler_params=pltpu.CompilerParams(vmem_limit_bytes=VMEM_LIMIT),
        cost_estimate=pl.CostEstimate(
            flops=2 * (near_a.shape[0] + far_a.shape[0]) * height * width // SHARE,
            bytes_accessed=2 * ((near_a.shape[0] + far_a.shape[0]) * (height + width) + height * width) // SHARE,
            transcendentals=0,
        ),
        name=name,
    )(where, near_a, near_b, far_a, far_b)


def back_kernel(where, a1, b1, a2, b2, out1, out2, acc):
    acc[...] = dot(a1[...], b1[...], TN) + dot(a2[...], b2[...], TN)
    rows = acc.shape[0] // 2
    for part, out in enumerate((out1, out2)):
        at = lax.bitwise_xor(where[2], part) * rows
        out[0, 0] = acc[pl.ds(pl.multiple_of(at, 16), rows), :].astype(BF)


def back_call(where, own, mate, first, second, extra, name):
    (a1, b1), (a2, b2) = own, mate
    tokens, ff = a1.shape
    rows = ff // (first * second)
    width = b2.shape[1] // 2

    def block(i, where):
        return (0, lax.bitwise_xor(lax.rem(i, second) * first + i // second, where[0]))

    return pl.pallas_call(
        back_kernel,
        out_shape=[jax.ShapeDtypeStruct((first, second, rows // 2 + extra, width), BF)] * 2,
        grid_spec=pltpu.PrefetchScalarGridSpec(
            num_scalar_prefetch=1,
            grid=(first * second,),
            in_specs=[
                pl.BlockSpec((tokens, rows), block),
                pl.BlockSpec((tokens, width), lambda i, where: (0, where[1])),
                pl.BlockSpec((tokens, rows), block),
                pl.BlockSpec((tokens, width), lambda i, where: (0, where[1])),
            ],
            out_specs=[
                pl.BlockSpec(
                    (1, 1, rows // 2, width), lambda i, where: (i // second, lax.rem(i, second), 0, 0)
                )
            ]
            * 2,
            scratch_shapes=[pltpu.VMEM((rows, width), F32)],
        ),
        compiler_params=pltpu.CompilerParams(vmem_limit_bytes=VMEM_LIMIT),
        cost_estimate=pl.CostEstimate(
            flops=4 * tokens * ff * width // SHARE,
            bytes_accessed=2 * (2 * tokens * (ff + width) + ff * width) // SHARE,
            transcendentals=0,
        ),
        name=name,
    )(where, a1, b1, a2, b2)


def product_kernel(*refs, dims, parts):
    total = dot(refs[0][...], refs[1][...], dims)
    for i in range(1, parts):
        total = total + dot(refs[2 * i][...], refs[2 * i + 1][...], dims)
    for term in refs[2 * parts : -1]:
        total = total + term[...]
    refs[-1][...] = total.astype(refs[-1].dtype)


def product(pairs, dims, name, terms=()):
    tile = 256
    turned = dims == NT
    rows = pairs[0][0].shape[0]
    width = pairs[0][1].shape[0 if turned else 1]
    ins, flat, depth = [], [], 0
    for a, b in pairs:
        ins.append(pl.BlockSpec(a.shape, lambda i: (0, 0), pipeline_mode=pl.Buffered(1)))
        if turned:
            ins.append(pl.BlockSpec((tile, b.shape[1]), lambda i: (i, 0)))
        else:
            ins.append(pl.BlockSpec((b.shape[0], tile), lambda i: (0, i)))
        flat += [a, b]
        depth += a.shape[1]
    return pl.pallas_call(
        functools.partial(product_kernel, dims=dims, parts=len(pairs)),
        out_shape=jax.ShapeDtypeStruct((rows, width), BF),
        grid=(width // tile,),
        in_specs=ins + [pl.BlockSpec((t.shape[0], tile), lambda i: (0, i)) for t in terms],
        out_specs=pl.BlockSpec((rows, tile), lambda i: (0, i)),
        compiler_params=pltpu.CompilerParams(vmem_limit_bytes=VMEM_LIMIT),
        cost_estimate=pl.CostEstimate(
            flops=2 * rows * depth * width // SHARE,
            bytes_accessed=2 * (rows * depth + depth * width + rows * width) // SHARE,
            transcendentals=0,
        ),
        name=name,
    )(*flat, *terms)


def tile_flags(queries, keys, tq, tk):
    q_first, q_last = queries[:, ::tq], queries[:, tq - 1 :: tq]
    k_first, k_last = keys[:, ::tk], keys[:, tk - 1 :: tk]
    meet = (q_first[:, :, None] <= k_last[:, None, :]) & (k_first[:, None, :] <= q_last[:, :, None])
    whole = (
        (q_first == q_last)[:, :, None]
        & (k_first == k_last)[:, None, :]
        & (q_first[:, :, None] == k_first[:, None, :])
    )
    return jnp.where(whole, 2, jnp.where(meet, 1, 0)).astype(jnp.int32)


def layer_norm_parts(values):
    centred = values - jnp.mean(values, axis=-1, keepdims=True)
    rstd = lax.rsqrt(jnp.mean(centred * centred, axis=-1, keepdims=True) + EPS)
    return centred * rstd, rstd


def layer_norm_back(d_norm, gain, xhat, rstd):
    e = d_norm * gain
    return rstd * (
        e - jnp.mean(e, axis=-1, keepdims=True) - xhat * jnp.mean(e * xhat, axis=-1, keepdims=True)
    )


def on_device(
    tokens,
    cell_start,
    norm1_gain,
    norm1_bias,
    w_qkv,
    bias_q,
    bias_v,
    w_out,
    bias_out,
    norm2_gain,
    norm2_bias,
    w_in,
    bias_in,
    w_back,
    bias_back,
    cotangent,
):
    rows, seg, width = tokens.shape
    count = rows * seg
    ff = w_in.shape[1]
    half = width // 2
    wide = lax.axis_size("wide")
    group = lax.axis_size("blk")
    place = lax.axis_index("wide")
    member = lax.axis_index("blk")
    core = place % 2
    chips = wide // 2
    first = 2 if chips <= 8 else 4
    second = chips // first
    heads = HEADS // 2
    early = 6
    spans = ((0, early), (early, heads))
    tq, tk = min(512, seg), min(256, seg)
    halves = group == 2 and ff // chips % 128 == 0
    where = jnp.stack([place // 2, core, member]).astype(jnp.int32)
    where_out = jnp.stack([lax.bitwise_xor(place // 2, core * (chips // 2)), core, member]).astype(jnp.int32)

    def after(value, *earlier):
        return lax.optimization_barrier((value, earlier))[0]

    def across(array, by):
        return lax.ppermute(array, "wide", [(i, i ^ by) for i in range(wide)])

    def to_mate(array):
        return across(array, 1)

    def from_ahead(array, by):
        return lax.ppermute(array, "blk", [((i + by) % group, i) for i in range(group)])

    def to_ahead(array, by):
        return lax.ppermute(array, "blk", [(i, (i + by) % group) for i in range(group)])

    def from_all_ahead(array):
        parts = [from_ahead(array, by) for by in range(1, group)]
        return parts[0] if len(parts) == 1 else jnp.concatenate(parts, axis=1)

    def cut(array, start, size, axis):
        return lax.dynamic_slice_in_dim(array, start, size, axis)

    def paired(array):
        return jnp.concatenate([array, to_mate(array)], axis=0)

    inputs = tokens.astype(F32).reshape(count, width)
    xhat1, rstd1 = layer_norm_parts(inputs)
    acts = (xhat1 * norm1_gain + norm1_bias).astype(BF).reshape(tokens.shape)
    cells = paired(cell_start)
    far_cells = from_all_ahead(cells)
    acts = after(acts, far_cells)
    far_own = from_all_ahead(acts)
    acts_pair = paired(acts).reshape(2 * count, width)
    w_own = jnp.concatenate([cut(w_qkv, part * width + core * half, half, 1) for part in range(3)], axis=1)
    b_own = jnp.concatenate([cut(bias_q, core * half, half, 0), jnp.zeros((half,), F32), cut(bias_v, core * half, half, 0)])

    def own_columns(span):
        return [w_own[:, part * half + span[0] * HD : part * half + span[1] * HD] for part in range(3)]

    w_early, w_late = (jnp.concatenate(own_columns(span), axis=1) for span in spans)

    def columns(array):
        return jnp.broadcast_to(array[:, :, None], array.shape + (128,))

    qkv = (dot(acts_pair, w_own, NN) + b_own).astype(BF).reshape(2 * rows, seg, 3 * half)
    near_flags = tile_flags(cells, cells, tq, tk)
    far_flags = tile_flags(cells, far_cells, tq, tk)
    cell_rows = cells[:, None, :]
    near_columns, far_columns = columns(cells), columns(far_cells)
    state = attn_fwd(near_flags, cell_rows, near_columns, qkv, qkv, 1, None, tq, tk, heads)
    d_out = cotangent.reshape(count, width)
    d_out_mate = to_mate(after(d_out, acts_pair))
    far_own = after(far_own, state)
    far_mate = to_mate(far_own)
    d_act = dot(after(d_out, far_own, state), w_back, NT).astype(BF)

    far_mate = after(far_mate, d_act)
    far_pair = jnp.concatenate([far_own, far_mate], axis=0)
    far_len = far_pair.shape[1]
    far_pair = far_pair.reshape(-1, width)
    far_kv = (dot(far_pair, w_own[:, half:], NN) + b_own[half:]).astype(BF).reshape(2 * rows, far_len, 2 * half)
    attended, stats = attn_fwd(far_flags, cell_rows, far_columns, qkv, far_kv, 0, state, tq, tk, heads)
    mine, theirs = attended[:rows].reshape(count, half), attended[rows:].reshape(count, half)
    own_rest = to_mate(theirs)
    mate_rest = to_mate(mine)
    w_out_own = cut(w_out, core * half, half, 0)
    w_out_mate = cut(w_out, (1 - core) * half, half, 0)
    middle = inputs + (dot(mine, w_out_own, NN) + dot(own_rest, w_out_mate, NN)) + bias_out

    xhat2, rstd2 = layer_norm_parts(middle)
    acts2 = (xhat2 * norm2_gain + norm2_bias).astype(BF)
    acts2_mate = to_mate(acts2)
    b_in = bias_in.reshape(1, ff)
    act_part, d_pre_theirs, sum_part = ffn_call(where, acts2, w_in, b_in, d_act, (), "ffn_theirs")
    d_pre_mate = to_mate(d_pre_theirs)
    act, d_pre_mine, d_pre_sum = ffn_call(where, acts2, w_in, b_in, d_act, (act_part, sum_part), "ffn_mine")
    act_mate = to_mate(act)
    w_in_mine = cut(w_in, core * (ff // 2), ff // 2, 1)
    w_in_theirs = cut(w_in, (1 - core) * (ff // 2), ff // 2, 1)
    d_norm2 = dot(d_pre_theirs, w_in_theirs, NT) + dot(d_pre_mine, w_in_mine, NT)
    grad_out = d_out.astype(F32)
    d_middle = grad_out + layer_norm_back(d_norm2, norm2_gain, xhat2, rstd2)
    d_z = d_middle.astype(BF)
    d_att_theirs = dot(d_z, w_out_mate, NT).astype(BF)
    d_att_mine = dot(d_z, w_out_own, NT).astype(BF)
    d_att_mate = to_mate(d_att_theirs)
    d_z_mate = to_mate(d_z)

    def send(parts):
        return [across(parts[one], 2 * one) for one in range(1, first)]

    def add_first(parts, received):
        sums = []
        for two in range(second):
            total = parts[0][two].astype(F32)
            for part in received:
                total = total + part[two].astype(F32)
            sums.append(total.astype(BF))
        return sums

    def send_second(sums):
        return [across(sums[two], 2 * first * two) for two in range(1, second)]

    def add_second(sums, received):
        total = sums[0].astype(F32)
        for part in received:
            total = total + part.astype(F32)
        return total.astype(BF)

    def start(parts):
        return from_ahead(parts[1], 1) if halves else send(parts)

    def middle_step(parts, received):
        if not halves:
            return parts, received
        sums = [(parts[0][one].astype(F32) + received[one].astype(F32)).astype(BF) for one in range(first)]
        return sums, send(sums)

    def ahead(total):
        return from_ahead(total, 1) if group == 2 else None

    def over_row(total, other):
        if group == 2:
            return (total.astype(F32) + other.astype(F32)).astype(BF)
        return lax.psum(total, "blk")

    def by_core(total, other, sizes):
        if halves:
            kept = jnp.where(member == core, total, other)
            return kept, jnp.where(member == core, other, total)
        total = over_row(total, other)
        parts, at = [], 0
        for size in sizes:
            parts.append(total[at : at + size].reshape(2, size // 2, total.shape[1]))
            at += size
        split = jnp.concatenate(parts, axis=1)
        return (lax.dynamic_index_in_dim(split, i, 0, keepdims=False) for i in (core, 1 - core))

    def swap(split):
        kept, given = split
        other = to_mate(given)
        return jnp.where(core == 0, kept, other).astype(F32), jnp.where(core == 0, other, kept).astype(F32)

    d_pre_held, d_pre_mate = after((d_pre_mine, d_pre_mate), d_att_theirs, d_att_mine)
    grad_in = grad_call(
        where, [[(acts2, d_pre_held, 0), (acts2_mate, d_pre_mate, 0)]], ff // 2, first, second, 512, False, "grad_in"
    )
    in_in = send(grad_in)
    act_held, act_mate, mate_rest, d_z_mate = after((act, act_mate, mate_rest, d_z_mate), grad_in)

    def grad_o(into):
        return grad_call(
            where_out,
            [
                [(mine, d_z, None), (theirs, d_z_mate, None)],
                [(own_rest, d_z, None), (mate_rest, d_z_mate, None)],
            ],
            half, first, second, half, halves, "grad_out", into,
        )

    back_rows, out_rows = ff // chips, width // chips
    if halves:
        grad_b = back_call(
            where, (act_held, d_out), (act_mate, d_out_mate), first, second, out_rows // 2, "grad_back"
        )
        grad_b = grad_o(tuple(grad_b))
    else:
        whole = dot(act_held, cut(d_out, core * half, half, 1), TN) + dot(act_mate, cut(d_out_mate, core * half, half, 1), TN)
        whole = whole.astype(BF).reshape(chips, back_rows, half)
        grad_b = [
            jnp.concatenate([
                jnp.stack([whole[lax.bitwise_xor(two * first + one, where[0])] for two in range(second)]), other
            ], axis=1)
            for one, other in enumerate(grad_o(()))
        ]
    b_in = start(grad_b)

    back_tq = min(256, seg)
    near_flags, far_flags = tile_flags(cells, cells, back_tq, tk), tile_flags(cells, far_cells, back_tq, tk)
    d_att = after((d_att_mine.reshape(rows, seg, half), d_att_mate.reshape(rows, seg, half)), grad_b)
    d_qT, far_early, far_late = attn_bwd(
        far_flags, cell_rows, far_columns, qkv, far_kv, 0, d_att, attended, stats, None, back_tq, tk, heads, spans, "attn_bwd_far"
    )
    in_sums = add_first(grad_in, after(in_in, d_qT))
    in_more = send_second(in_sums)
    far_early, far_late = after((far_early, far_late), in_sums)
    far_early, far_late = (f.reshape(-1, f.shape[-1]) for f in (far_early, far_late))
    n_early, n_late = early * HD, (heads - early) * HD
    far_part = product([(far_early, w_early[:, n_early:]), (far_late, w_late[:, n_late:])], NT, "far_norm")
    far_part = far_part.reshape(2 * rows, far_len, width)
    far_given = to_mate(far_part[rows:])
    far_sum = (far_part[:rows].astype(F32) + after(far_given, in_sums, far_part).astype(F32)).astype(BF)
    far_back = [to_ahead(far_sum[:, by * seg : (by + 1) * seg], by + 1) for by in range(group - 1)]
    d_qT = after(d_qT, far_sum)

    def near_back(span, name, *earlier):
        (out,) = attn_bwd(
            near_flags, cell_rows, near_columns, qkv, qkv, 1, d_att, attended, stats, after(d_qT, earlier), back_tq, tk, heads,
            (span,), name,
        )
        return out.reshape(2 * count, -1)

    near_early = near_back(spans[0], "attn_bwd_early")
    b_sums, b_in = middle_step(grad_b, after(b_in, near_early))
    in_total = add_second(in_sums, after(in_more, b_sums))
    in_row = ahead(in_total)
    near_early = after(near_early, b_sums, in_total)
    *grad_e, sum_e = qkv_call(where, (acts_pair, near_early), (far_pair, far_early), first, second, halves, "grad_early")
    grad_e, in_row, far_back = after((grad_e, in_row, far_back), grad_e)
    e_in = start(grad_e)
    near_late = near_back(spans[1], "attn_bwd_late", grad_e, far_back)
    b_two = add_first(b_sums, after(b_in, near_late))
    b_more = send_second(b_two)
    near_late = after(near_late, b_two)
    *grad_l, sum_l = qkv_call(where, (acts_pair, near_late), (far_pair, far_late), first, second, halves, "grad_late")
    l_in = start(grad_l)
    e_sums, e_in = middle_step(grad_e, after(e_in, grad_l))
    act_late = after(act_held, e_sums)
    mixed = product([(act_late, w_back)], NN, "mixed", (middle, bias_back.reshape(1, width))).reshape(tokens.shape)
    l_sums, l_in = middle_step(grad_l, after(l_in, mixed))
    b_total = add_second(b_two, after(b_more, l_sums))
    b_row = ahead(b_total)
    e_two = add_first(e_sums, after(e_in, b_total))
    e_more = send_second(e_two)
    near_part = product(
        [(after(near_early, l_sums, e_two), w_early), (near_late, w_late)], NT, "near_norm"
    )
    near_given = to_mate(near_part[count:])
    l_two = add_first(l_sums, after(l_in, near_part))
    e_total = add_second(e_two, after(e_more, l_two))
    l_more = send_second(l_two)
    e_row = ahead(e_total)
    (d_norm1,) = after((near_part[:count].astype(F32),), l_two, e_total)
    d_norm1 = d_norm1 + near_given.astype(F32)
    for part in far_back:
        d_norm1 = d_norm1 + part.reshape(count, width).astype(F32)
    grad_tokens = (d_middle + layer_norm_back(d_norm1, norm1_gain, xhat1, rstd1)).reshape(tokens.shape)

    def vectors(parts, *covers):
        packed = jnp.concatenate([p.reshape(wide, -1) for p in parts], axis=1)
        total = packed
        covers = iter(covers)
        for stride, size in ((2 * first, second), (2, first), (1, 2)):
            total = total.reshape(-1, size, stride, packed.shape[1])
            spot = (place // stride) % size
            kept = lax.dynamic_index_in_dim(total, spot, 1, keepdims=False)
            given = [
                across(lax.dynamic_index_in_dim(total, spot ^ by, 1, keepdims=False), by * stride)
                for by in range(1, size)
            ]
            given = after(given, next(covers))
            for part in given:
                kept = kept + part
            total = kept.reshape(stride, packed.shape[1])
        total = total.reshape(-1)
        total = total + after(from_ahead(total, 1), next(covers)) if group == 2 else lax.psum(total, "blk")
        out, at = [], 0
        for p in parts:
            size = p.size // wide
            out.append(total[at : at + size])
            at += size
        return out

    def widened(part):
        n = sum_e.shape[1] // 3, sum_l.shape[1] // 3
        own = jnp.concatenate([s[0, part * m : (part + 1) * m] for s, m in zip((sum_e, sum_l), n)])
        return lax.dynamic_update_slice_in_dim(jnp.zeros((width,), F32), own, core * half, 0)

    in_low, in_high = swap(by_core(after(in_total, d_norm1), in_row, [width // chips])) if not halves else (None, None)
    if halves:
        in_whole = over_row(after(in_total, d_norm1), in_row).reshape(2, -1, in_total.shape[1])
        in_low, in_high = swap([lax.dynamic_index_in_dim(in_whole, i, 0, keepdims=False) for i in (core, 1 - core)])
    b_low, b_high = swap(by_core(after(b_total, d_norm1), b_row, [back_rows, out_rows]))
    e_low, e_high = swap(by_core(e_total, e_row, [out_rows]))
    l_total = add_second(l_two, l_more)
    l_low, l_high = swap(by_core(l_total, ahead(l_total), [out_rows]))

    def part_columns(part):
        return [
            array[:, part * n : (part + 1) * n]
            for array, n in ((e_low, n_early), (l_low, n_late), (e_high, n_early), (l_high, n_late))
        ]

    share = ff // wide
    grad_w_in = jnp.concatenate([in_low, in_high], axis=1)
    grad_w_back = jnp.concatenate([b_low[:share], b_high[:share]], axis=1)
    grad_w_out = jnp.concatenate([b_low[share:], b_high[share:]], axis=1)
    small = vectors(
        [
            jnp.sum(d_norm1 * xhat1, axis=0),
            jnp.sum(d_norm1, axis=0),
            widened(0),
            widened(2),
            jnp.sum(d_z.astype(F32), axis=0),
            jnp.sum(d_norm2 * xhat2, axis=0),
            jnp.sum(d_norm2, axis=0),
            d_pre_sum,
            jnp.sum(grad_out, axis=0),
        ],
        grad_tokens,
        grad_w_in,
        grad_w_back,
        grad_w_out,
    )
    return (
        mixed,
        grad_tokens,
        small[0],
        small[1],
        jnp.concatenate([piece for part in range(3) for piece in part_columns(part)], axis=1),
        small[2],
        small[3],
        grad_w_out,
        small[4],
        small[5],
        small[6],
        grad_w_in,
        small[7],
        grad_w_back,
        small[8],
    )


def solution(mesh):
    spread = P("wide", "blk", None)
    placed = (spread, P("wide", "blk")) + (P(),) * 13 + (spread,)
    matrix, vector = P("wide", None), P("wide")
    return jax.shard_map(
        on_device,
        mesh=mesh,
        in_specs=placed,
        out_specs=(
            spread, spread, vector, vector, matrix, vector, vector, matrix, vector, vector, vector,
            matrix, vector, matrix, vector,
        ),
        check_vma=False,
    )
```

time: 709 us -> 665 us (0.938); the launches traced: 716 us -> 664 us
  other arithmetic: 107 us -> 81.2 us
  Pallas kernels: 347 us -> 324 us
  starting transfers between devices: 102 us -> 90.2 us
    pallas_call x5 -> x2, Pallas kernels: 72.7 us -> 30.6 us  [grad_call(): pl.pallas_call(functools.partial(grad_kernel, groups=[len(g) for g in gro...]
    pallas_call x5 -> x8, Pallas kernels: 154 us -> 183 us  [the longest x3 97 us: attn_bwd(): pl.pallas_call(functools.partial(bwd_kernel, spans=spans, tq=tq, tk=tk),...]
    ppermute x48 -> x38, starting transfers between devices: 87 us -> 74.5 us  [across(): return lax.ppermute(array, 'wide', [(i, i ^ by) for i in range(wide)])]
    ppermute x14 -> x10, waiting for transfers between devices: 11.2 us -> 22 us  [from_ahead(): lax.ppermute(array, 'blk', [((i + by) % group, i) for i in range(group)])]
    ppermute x48 -> x38, waiting for transfers between devices: 32.5 us -> 27.3 us  [across(): return lax.ppermute(array, 'wide', [(i, i ^ by) for i in range(wide)])]
    concatenate x13 -> x7, other arithmetic: 16.2 us -> 11.2 us  [the longest x4 7.8 us: on_device(): jnp.concatenate(own_columns(span), axis=1)]
    pallas_call x1 -> x2, Pallas kernels: 38.3 us -> 34.4 us  [ffn_call(): pl.pallas_call(ffn_kernel, out_shape=[jax.ShapeDtypeStruct((rows, ff), BF...]
    ppermute x14 -> x10, starting transfers between devices: 15.1 us -> 14.2 us  [from_ahead(): lax.ppermute(array, 'blk', [((i + by) % group, i) for i in range(group)])]
  transfers between devices with their start and end apart: 63 -> 49, of which waited for: 13 -> 9; matrix products, arithmetic and copies ran while one was open for 27% -> 25% of each run, Pallas kernels for 39% -> 40%
where the time goes in v3:
time: 665 us; the launch traced here: 664 us
  Pallas kernels  324 us (49%)
  starting transfers between devices  90.2 us (14%)
  matrix products  87.3 us (13%)
  other arithmetic  81.2 us (12%)
  waiting for transfers between devices  49.4 us (7%)
  local copies, waits for them, and re-layouts  30.2 us (5%)
    pallas_call x3, Pallas kernels, attn_bwd(): pl.pallas_call(functools.partial(bwd_kernel, spans=spans, tq=tq, tk=tk),...  97 us
    dot_general x9, matrix products, dot(): return lax.dot_general(a, b, dims, preferred_element_type=F32)  87.3 us
    ppermute x38, starting transfers between devices, across(): return lax.ppermute(array, 'wide', [(i, i ^ by) for i in range(wide)])  74.5 us
    pallas_call x2, Pallas kernels, attn_fwd(): pl.pallas_call(functools.partial(fwd_kernel, first=first, tq=tq, tk=tk, h...  53.2 us
    pallas_call x3, Pallas kernels, product(): pl.pallas_call(functools.partial(product_kernel, dims=dims, parts=len(pai...  49.1 us
    pallas_call x2, Pallas kernels, qkv_call(): pl.pallas_call(functools.partial(qkv_kernel, first=first, second=second,...  36.5 us
    pallas_call x2, Pallas kernels, ffn_call(): pl.pallas_call(ffn_kernel, out_shape=[jax.ShapeDtypeStruct((rows, ff), BF...  34.4 us
    pallas_call x2, Pallas kernels, grad_call(): pl.pallas_call(functools.partial(grad_kernel, groups=[len(g) for g in gro...  30.6 us
  transfers between devices with their start and end apart: 49, of which 9 were waited for; matrix products, arithmetic and copies ran while one was open for 25% of the time, Pallas kernels for 40%

profile of v3, /device:TPU:0, one launch (start us, length us, event | category | flops | bytes accessed | tf_op | source)
XLA Modules:
  0.0 664.0 jit_solution(7292448281979975246)
XLA Ops:
  21.9 13.5 %add_convert_fusion = bf16[2048,1920]{1,0:T(8,128)(2,1)} fusion(f32[1920]{0:T(1024)S(1)} %pad_maximum_fusion.8, bf16[2048,1280]{1,0:T(8,128)(2,1)S(1)} %bitcast.223, bf16[1280,640]{1,0:T(8,128)(2,1)S(1)} %copy-done.26, bf16[1280,640]{1,0:T(8,128)(2,1)S(1)} %copy-done.28, bf16[1280,640]{1,0:T(8,128)(2,1)S(1)} %copy-done.30), kind=kOutput, calls=%fused_computation | convolution fusion | flops 10088939520 | bytes 18030080 | tf_op jit(solution)/shard_map/dot_general | solution.py:29
  36.8 31.6 %attn_fwd_a.1 = (f32[2,640,1024]{2,1,0:T(8,128)}, f32[2,16,1024]{2,1,0:T(8,128)}, f32[2,16,1024]{2,1,0:T(8,128)}) custom-call(s32[2,2,4]{2,1,0:T(2,128)} %get-tuple-element.243.flags, s32[2,1,1024]{2,1,0:T(1,128)} %broadcast_in_dim.38.cq, s32[2,1024,128]{2,1,0:T(8,128)} %broadcast_in_dim.41.ck, bf16[2,1024,1920]{2,1,0:T(8,128)(2,1)} %bitcast.206, ...), custom_call_target="tpu_custom_call" | custom-call | flops 268435456 | bytes 655360 | tf_op jit(solution)/shard_map/attn_fwd_a/pallas_call | solution.py:155
  68.4 7.1 %collective-permute-done.3 = bf16[1,1024,1280]{2,1,0:T(8,128)(2,1)} collective-permute-done((bf16[1,1024,1280]{2,1,0:T(8,128)(2,1)}, bf16[1,1024,1280]{2,1,0:T(8,128)(2,1)}, u32[]{:S(2)}, u32[]{:S(2)}) %collective-permute-start.3) | collective-permute-done | bytes 2621472 | tf_op jit(solution)/shard_map/ppermute | solution.py:628
  75.6 20.0 %convolution_convert_fusion.d_act = bf16[1024,5120]{1,0:T(8,128)(2,1)} fusion(bf16[1024,1280]{1,0:T(8,128)(2,1)} %bitcast.6.b1, bf16[5120,1280]{1,0:T(8,128)(2,1)} %refs_1_.1), kind=kOutput, calls=%fused_computation.2 | convolution fusion | flops 13427015680 | bytes 26214400 | tf_op jit(solution)/shard_map/dot_general | solution.py:29
  98.3 8.8 %add_convert_fusion.1 = bf16[2048,1280]{1,0:T(8,128)(2,1)} fusion(bf16[2048,1280]{1,0:T(8,128)(2,1)S(1)} %bitcast.226, f32[1280]{0:T(1024)S(1)} %concatenate.82, bf16[1280,640]{1,0:T(8,128)(2,1)S(1)} %copy-done.27, bf16[1280,640]{1,0:T(8,128)(2,1)S(1)} %copy-done.29), kind=kOutput, calls=%fused_computation.1 | convolution fusion | flops 6722682880 | bytes 13767680 | tf_op jit(solution)/shard_map/dot_general | solution.py:29
  108.4 21.6 %attn_fwd_b.1 = (bf16[2,1024,640]{2,1,0:T(8,128)(2,1)}, f32[2,16,1024]{2,1,0:T(8,128)}) custom-call(s32[2,2,4]{2,1,0:T(2,128)} %get-tuple-element.244.flags, s32[2,1,1024]{2,1,0:T(1,128)} %broadcast_in_dim.38.cq, s32[2,1024,128]{2,1,0:T(8,128)} %broadcast_in_dim.39.ck, bf16[2,1024,1920]{2,1,0:T(8,128)(2,1)} %bitcast.209, bf16[2,1024,1280]{2,1,0:T(8,128)(2,1)} %bitcast.219, ...), custom_call_target="tpu_custom_call" | custom-call | flops 268435456 | bytes 655360 | tf_op jit(solution)/shard_map/attn_fwd_b/pallas_call | solution.py:155
  145.4 17.5 %ffn_theirs.1 = (bf16[1024,5120]{1,0:T(8,128)(2,1)}, bf16[1024,2560]{1,0:T(8,128)(2,1)}, f32[1,5120]{1,0:T(1,128)}) custom-call(s32[3]{0:T(128)} %add_add_fusion.where, bf16[1024,1280]{1,0:T(8,128)(2,1)} %add_convert_fusion.2.acts.refs_0_, bf16[1280,5120]{1,0:T(8,128)(2,1)} %w.3, f32[1,5120]{1,0:T(1,128)} %bitcast.246, ...), custom_call_target="tpu_custom_call" | custom-call | flops 335544320 | bytes 1245184 | tf_op jit(solution)/shard_map/ffn_theirs/pallas_call | solution.py:303
  162.8 16.9 %ffn_mine.1 = (bf16[1024,5120]{1,0:T(8,128)(2,1)}, bf16[1024,2560]{1,0:T(8,128)(2,1)}, f32[1,5120]{1,0:T(1,128)}) custom-call(s32[3]{0:T(128)} %add_add_fusion.where, bf16[1024,1280]{1,0:T(8,128)(2,1)} %add_convert_fusion.2.acts.refs_0_, bf16[1280,5120]{1,0:T(8,128)(2,1)} %w.3, f32[1,5120]{1,0:T(1,128)} %bitcast.247, ...), custom_call_target="tpu_custom_call", output_to_operand_aliasing={{0}: (5, {}), {2}: (6, {})} | custom-call | flops 335544320 | bytes 1245184 | tf_op jit(solution)/shard_map/ffn_mine/pallas_call | solution.py:303
  180.3 12.5 %fusion = f32[1024,1280]{1,0:T(8,128)} fusion(bf16[1024,2560]{1,0:T(8,128)(2,1)} %get-tuple-element.105.refs_1_, bf16[1280,5120]{1,0:T(8,128)(2,1)} %w.3, s32[]{:T(128)S(6)} %select_n.202), kind=kOutput, calls=%fused_computation.6 | convolution fusion | flops 6710886400 | bytes 17039364 | tf_op jit(solution)/shard_map/dot_general | solution.py:29
  192.8 14.7 %multiply_reduce_fusion = (f32[1280]{0:T(1024)S(1)}, f32[1024]{0:T(1024)S(1)}, f32[1024]{0:T(1024)S(1)}, f32[1280]{0:T(1024)S(1)}, f32[1024,1280]{1,0:T(8,128)S(1)}) fusion(f32[1024,1280]{1,0:T(8,128)} %copy-done.1, f32[1024]{0:T(1024)S(1)} %add_rsqrt_fusion, f32[1024]{0:T(1024)S(1)} %broadcast_multiply_fusion.4, f32[1280]{0:T(1024)S(1)} %copy-done.42, ...), kind=kOutput, calls=%fused_computation.36 | convolution fusion | flops 6723989504 | bytes 27556868 | tf_op jit(solution)/shard_map/dot_general | solution.py:29
  207.5 5.8 convert_reduce_fusion.2
  223.4 20.3 %grad_in.1 = (bf16[4,160,2560]{2,1,0:T(8,128)(2,1)}, bf16[4,160,2560]{2,1,0:T(8,128)(2,1)}) custom-call(s32[3]{0:T(128)} %add_add_fusion.where, bf16[1024,1280]{1,0:T(8,128)(2,1)} %add_convert_fusion.2.acts.refs_0_, bf16[1024,2560]{1,0:T(8,128)(2,1)} %get-tuple-element.105.refs_1_, bf16[1024,1280]{1,0:T(8,128)(2,1)} %collective-permute-done.10.refs_2_, ...), custom_call_target="tpu_custom_call" | custom-call | flops 671088640 | bytes 1114112 | tf_op jit(solution)/shard_map/grad_in/pallas_call | solution.py:393
  243.7 8.6 %collective-permute-start.13 = (bf16[4,160,2560]{2,1,0:T(8,128)(2,1)}, bf16[4,160,2560]{2,1,0:T(8,128)(2,1)}, u32[]{:S(2)}, u32[]{:S(2)}) collective-permute-start(bf16[4,160,2560]{2,1,0:T(8,128)(2,1)} %get-tuple-element.108), channel_id=1, source_target_pairs={{0,4},{2,6},{4,0},{6,2},{8,12},{10,14},{12,8},{14,10},{16,20},{18,... | collective-permute-start | bytes 9830408 | tf_op jit(solution)/shard_map/ppermute | solution.py:622
  255.5 7.6 %collective-permute-done.7.refs_6_ = bf16[1024,640]{1,0:T(8,128)(2,1)} collective-permute-done((bf16[1024,640]{1,0:T(8,128)(2,1)}, bf16[1024,640]{1,0:T(8,128)(2,1)}, u32[]{:S(2)}, u32[]{:S(2)}) %collective-permute-start.7) | collective-permute-done | bytes 1310752 | tf_op jit(solution)/shard_map/ppermute | solution.py:622
  271.4 23.1 %grad_back.1 = (bf16[2,4,400,640]{3,2,1,0:T(8,128)(2,1)}, bf16[2,4,400,640]{3,2,1,0:T(8,128)(2,1)}) custom-call(s32[3]{0:T(128)} %add_add_fusion.where, bf16[1024,5120]{1,0:T(8,128)(2,1)} %get-tuple-element.145.a1.refs_0_, bf16[1024,1280]{1,0:T(8,128)(2,1)} %bitcast.6.b1, bf16[1024,5120]{1,0:T(8,128)(2,1)} %collective-permute-done.6.a2, ...), custom_call_target="tpu_custom_call" | custom-call | flops 671088640 | bytes 1507328 | tf_op jit(solution)/shard_map/grad_back/pallas_call | solution.py:486
  294.5 10.3 %grad_out.1 = (bf16[2,4,400,640]{3,2,1,0:T(8,128)(2,1)}, bf16[2,4,400,640]{3,2,1,0:T(8,128)(2,1)}) custom-call(s32[3]{0:T(128)} %add_add_fusion.1.where, bf16[1024,640]{1,0:T(8,128)(2,1)} %get-tuple-element.209.refs_0_, bf16[1024,1280]{1,0:T(8,128)(2,1)} %get-tuple-element.182.refs_1_.refs_5_, ...), custom_call_target="tpu_custom_call", output_to_operand_aliasing={{0}: (9, {}), {1}: (10, {})} | custom-call | flops 167772160 | bytes 475136 | tf_op jit(solution)/shard_map/grad_out/pallas_call | solution.py:393
  310.2 30.9 %attn_bwd_far.1 = (f32[2,640,1024]{2,1,0:T(8,128)}, bf16[2,1024,768]{2,1,0:T(8,128)(2,1)}, bf16[2,1024,512]{2,1,0:T(8,128)(2,1)}) custom-call(s32[2,4,4]{2,1,0:T(4,128)} %get-tuple-element.241.flags, s32[2,1,1024]{2,1,0:T(1,128)} %broadcast_in_dim.38.cq, s32[2,1024,128]{2,1,0:T(8,128)} %broadcast_in_dim.39.ck, bf16[2,1024,1920]{2,1,0:T(8,128)(2,1)} %bitcast.210, ...), custom_call_target="tpu_custom_call" | custom-call | flops 671088640 | bytes 1179648 | tf_op jit(solution)/shard_map/attn_bwd_far/pallas_call | solution.py:256
  346.3 11.7 %far_norm.1 = bf16[2048,1280]{1,0:T(8,128)(2,1)} custom-call(bf16[2048,768]{1,0:T(8,128)(2,1)} %bitcast.233, bf16[1280,768]{1,0:T(8,128)(2,1)} %pad_maximum_fusion.3.refs_1_, bf16[2048,512]{1,0:T(8,128)(2,1)} %bitcast.241, bf16[1280,512]{1,0:T(8,128)(2,1)} %pad_maximum_fusion.6.refs_3_), custom_call_target="tpu_custom_call" | custom-call | flops 335544320 | bytes 688128 | tf_op jit(solution)/shard_map/far_norm/pallas_call | solution.py:539
  377.4 37.6 %attn_bwd_early.1 = bf16[2,1024,1152]{2,1,0:T(8,128)(2,1)} custom-call(s32[2,4,4]{2,1,0:T(4,128)} %get-tuple-element.242.flags, s32[2,1,1024]{2,1,0:T(1,128)} %broadcast_in_dim.38.cq, s32[2,1024,128]{2,1,0:T(8,128)} %broadcast_in_dim.41.ck, bf16[2,1024,1920]{2,1,0:T(8,128)(2,1)} %bitcast.211, bf16[2,1024,1920]{2,1,0:T(8,128)(2,1)} %bitcast.212, ...), custom_call_target="tpu_custom_call" | custom-call | flops 402653184 | bytes 707788 | tf_op jit(solution)/shard_map/attn_bwd_early/pallas_call | solution.py:256
  420.3 18.0 %collective-permute-start.22 = (bf16[4,400,640]{2,1,0:T(8,128)(2,1)}, bf16[4,400,640]{2,1,0:T(8,128)(2,1)}, u32[]{:S(2)}, u32[]{:S(2)}) collective-permute-start(bf16[4,400,640]{2,1,0:T(8,128)(2,1)} %get-tuple-element.194), channel_id=1, source_target_pairs={{0,4},{2,6},{4,0},{6,2},{8,12},{10,14},{12,8},{14,10},{16,20},{18,... | collective-permute-start | bytes 6144008 | tf_op jit(solution)/shard_map/ppermute | solution.py:622
  440.5 22.0 %grad_early.1 = (bf16[2,4,80,1152]{3,2,1,0:T(8,128)(2,1)}, bf16[2,4,80,1152]{3,2,1,0:T(8,128)(2,1)}, f32[1,1152]{1,0:T(1,128)}) custom-call(s32[3]{0:T(128)} %add_add_fusion.where, bf16[2048,1280]{1,0:T(8,128)(2,1)} %bitcast.224, bf16[2048,1152]{1,0:T(8,128)(2,1)} %bitcast.229, bf16[2048,1280]{1,0:T(8,128)(2,1)} %bitcast.227, bf16[2048,768]{1,0:T(8,128)(2,1)} %bitcast.234), custom_call_target="tpu_custom_call" | custom-call | flops 603979776 | bytes 1143603 | tf_op jit(solution)/shard_map/grad_early/pallas_call | solution.py:444
  462.5 9.6 %collective-permute-done.19 = bf16[160,2560]{1,0:T(8,128)(2,1)S(1)} collective-permute-done((bf16[160,2560]{1,0:T(8,128)(2,1)S(1)}, bf16[160,2560]{1,0:T(8,128)(2,1)S(1)}, u32[]{:S(2)}, u32[]{:S(2)}) %collective-permute-start.19) | collective-permute-done | bytes 819232 | tf_op jit(solution)/shard_map/ppermute | solution.py:628
  482.2 28.4 %attn_bwd_late.1 = bf16[2,1024,768]{2,1,0:T(8,128)(2,1)} custom-call(s32[2,4,4]{2,1,0:T(4,128)} %get-tuple-element.242.flags, s32[2,1,1024]{2,1,0:T(1,128)} %broadcast_in_dim.38.cq, s32[2,1024,128]{2,1,0:T(8,128)} %broadcast_in_dim.41.ck, bf16[2,1024,1920]{2,1,0:T(8,128)(2,1)} %bitcast.214, bf16[2,1024,1920]{2,1,0:T(8,128)(2,1)} %bitcast.215, ...), custom_call_target="tpu_custom_call" | custom-call | flops 268435456 | bytes 471859 | tf_op jit(solution)/shard_map/attn_bwd_late/pallas_call | solution.py:256
  513.7 5.4 collective-permute-start.26
  520.6 14.5 %grad_late.1 = (bf16[2,4,80,768]{3,2,1,0:T(8,128)(2,1)}, bf16[2,4,80,768]{3,2,1,0:T(8,128)(2,1)}, f32[1,768]{1,0:T(1,128)}) custom-call(s32[3]{0:T(128)} %add_add_fusion.where, bf16[2048,1280]{1,0:T(8,128)(2,1)} %bitcast.225, bf16[2048,768]{1,0:T(8,128)(2,1)} %bitcast.231, bf16[2048,1280]{1,0:T(8,128)(2,1)} %bitcast.228, bf16[2048,512]{1,0:T(8,128)(2,1)} %bitcast.242), custom_call_target="tpu_custom_call" | custom-call | flops 402653184 | bytes 937164 | tf_op jit(solution)/shard_map/grad_late/pallas_call | solution.py:444
  538.5 12.8 %collective-permute-start.24 = (bf16[4,80,1152]{2,1,0:T(8,128)(2,1)}, bf16[4,80,1152]{2,1,0:T(8,128)(2,1)}, u32[]{:S(2)}, u32[]{:S(2)}) collective-permute-start(bf16[4,80,1152]{2,1,0:T(8,128)(2,1)} %get-tuple-element.207), channel_id=1, source_target_pairs={{0,4},{2,6},{4,0},{6,2},{8,12},{10,14},{12,8},{14,10},{16,20},{18,... | collective-permute-start | bytes 2211848 | tf_op jit(solution)/shard_map/ppermute | solution.py:622
  551.7 20.8 %mixed.1 = bf16[1024,1280]{1,0:T(8,128)(2,1)} custom-call(bf16[1024,5120]{1,0:T(8,128)(2,1)} %get-tuple-element.145.a1.refs_0_, bf16[5120,1280]{1,0:T(8,128)(2,1)} %refs_1_.1, f32[1024,1280]{1,0:T(8,128)} %copy-done.1, f32[1,1280]{1,0:T(1,128)} %reshape.354.refs_3_), custom_call_target="tpu_custom_call" | custom-call | flops 671088640 | bytes 1310720 | tf_op jit(solution)/shard_map/mixed/pallas_call | solution.py:539
  578.6 16.6 %near_norm.1 = bf16[2048,1280]{1,0:T(8,128)(2,1)} custom-call(bf16[2048,1152]{1,0:T(8,128)(2,1)} %bitcast.230, bf16[1280,1152]{1,0:T(8,128)(2,1)} %pad_maximum_fusion.2.refs_1_, bf16[2048,768]{1,0:T(8,128)(2,1)} %bitcast.232, bf16[1280,768]{1,0:T(8,128)(2,1)} %pad_maximum_fusion.4.refs_3_), custom_call_target="tpu_custom_call" | custom-call | flops 503316480 | bytes 901120 | tf_op jit(solution)/shard_map/near_norm/pallas_call | solution.py:539
  604.2 8.2 %collective-permute-done.45 = bf16[80,768]{1,0:T(8,128)(2,1)S(1)} collective-permute-done((bf16[80,768]{1,0:T(8,128)(2,1)S(1)}, bf16[80,768]{1,0:T(8,128)(2,1)S(1)}, u32[]{:S(2)}, u32[]{:S(2)}) %collective-permute-start.45) | collective-permute-done | bytes 122912 | tf_op jit(solution)/shard_map/ppermute | solution.py:622
  615.6 5.3 collective-permute-done.30
  628.5 6.9 %fusion.16 = (f32[1280]{0:T(1024)S(1)}, f32[1024]{0:T(1024)S(1)}, f32[1024]{0:T(1024)S(1)}, f32[1280]{0:T(1024)S(1)}, f32[1024,1280]{1,0:T(8,128)}) fusion(bf16[1,1024,1280]{2,1,0:T(8,128)(2,1)S(1)} %copy-done.4, f32[1024]{0:T(1024)S(1)} %copy-done.41, f32[1024]{0:T(1024)S(1)} %copy-done.36, f32[1280]{0:T(1024)S(1)} %copy-done.39, ...), kind=kLoop, calls=%fused_computation.24 | loop fusion | flops 18345472 | bytes 18381824 | tf_op jit(solution)/shard_map/reduce_sum | solution.py:907
  644.5 7.2 %fusion.15 = f32[1,1024,1280]{2,1,0:T(8,128)} fusion(f32[1024,1280]{1,0:T(8,128)} %get-tuple-element.183, bf16[1,1024,1280]{2,1,0:T(8,128)(2,1)} %param.16, f32[1024,1280]{1,0:T(8,128)} %get-tuple-element.184, f32[1024]{0:T(1024)S(1)} %broadcast_multiply_fusion, f32[1024]{0:T(1024)S(1)} %broadcast_multiply_fusion.1, f32[1280]{0:T(1024)S(1)} %copy-done.39, ...), kind=kLoop, calls=%fused_computation.23 | loop fusion | flops 11796480 | bytes 18371584 | tf_op jit(solution)/shard_map/reshape | solution.py:854
  (343 shorter events, 166.1 us)
Async XLA Ops:
  16.0 59.6 %collective-permute-start.3 = (bf16[1,1024,1280]{2,1,0:T(8,128)(2,1)}, bf16[1,1024,1280]{2,1,0:T(8,128)(2,1)}, u32[]{:S(2)}, u32[]{:S(2)}) collective-permute-start(bf16[1,1024,1280]{2,1,0:T(8,128)(2,1)} %fusion.22), channel_id=1, source_target_pairs={{1,0},{0,1},{3,2},{2,3},{5,4},{4,5},{7,6},{6,7},{9,8},{8,9},{11,10... | collective-permute-start | bytes 7864328 | tf_op jit(solution)/shard_map/ppermute | solution.py:628
  75.6 20.0 %collective-permute-start.4 = (bf16[1,1024,1280]{2,1,0:T(8,128)(2,1)}, bf16[1,1024,1280]{2,1,0:T(8,128)(2,1)S(1)}, u32[]{:S(2)}, u32[]{:S(2)}) collective-permute-start(bf16[1,1024,1280]{2,1,0:T(8,128)(2,1)} %collective-permute-done.3), channel_id=1, source_target_pairs={{0,2},{2,0},{4,6},{6,4},{8,10},{10,8},{12,14},{14,12},{16,18},{18,... | collective-permute-start | bytes 7864328 | tf_op jit(solution)/shard_map/ppermute | solution.py:622
  179.7 91.7 %collective-permute-start.6 = (bf16[1024,5120]{1,0:T(8,128)(2,1)}, bf16[1024,5120]{1,0:T(8,128)(2,1)}, u32[]{:S(2)}, u32[]{:S(2)}) collective-permute-start(bf16[1024,5120]{1,0:T(8,128)(2,1)} %get-tuple-element.145.a1.refs_0_), channel_id=1, source_target_pairs={{0,2},{2,0},{4,6},{6,4},{8,10},{10,8},{12,14},{14,12},{16,18},{18,... | collective-permute-start | bytes 31457288 | tf_op jit(solution)/shard_map/ppermute | solution.py:622
  179.7 43.7 %collective-permute-start.9 = (bf16[1024,2560]{1,0:T(8,128)(2,1)}, bf16[1024,2560]{1,0:T(8,128)(2,1)}, u32[]{:S(2)}, u32[]{:S(2)}) collective-permute-start(bf16[1024,2560]{1,0:T(8,128)(2,1)} %get-tuple-element.103), channel_id=1, source_target_pairs={{0,2},{2,0},{4,6},{6,4},{8,10},{10,8},{12,14},{14,12},{16,18},{18,... | collective-permute-start | bytes 15728648 | tf_op jit(solution)/shard_map/ppermute | solution.py:622
  180.2 43.2 %collective-permute-start.10 = (bf16[1024,1280]{1,0:T(8,128)(2,1)}, bf16[1024,1280]{1,0:T(8,128)(2,1)}, u32[]{:S(2)}, u32[]{:S(2)}) collective-permute-start(bf16[1024,1280]{1,0:T(8,128)(2,1)} %add_convert_fusion.2.acts.refs_0_), channel_id=1, source_target_pairs={{0,2},{2,0},{4,6},{6,4},{8,10},{10,8},{12,14},{14,12},{16,18},{18,... | collective-permute-start | bytes 7864328 | tf_op jit(solution)/shard_map/ppermute | solution.py:622
  243.7 97.5 %collective-permute-start.13 = (bf16[4,160,2560]{2,1,0:T(8,128)(2,1)}, bf16[4,160,2560]{2,1,0:T(8,128)(2,1)}, u32[]{:S(2)}, u32[]{:S(2)}) collective-permute-start(bf16[4,160,2560]{2,1,0:T(8,128)(2,1)} %get-tuple-element.108), channel_id=1, source_target_pairs={{0,4},{2,6},{4,0},{6,2},{8,12},{10,14},{12,8},{14,10},{16,20},{18,... | collective-permute-start | bytes 9830408 | tf_op jit(solution)/shard_map/ppermute | solution.py:622
  252.3 19.2 %collective-permute-start.8 = (bf16[1024,1280]{1,0:T(8,128)(2,1)}, bf16[1024,1280]{1,0:T(8,128)(2,1)}, u32[]{:S(2)}, u32[]{:S(2)}) collective-permute-start(bf16[1024,1280]{1,0:T(8,128)(2,1)} %get-tuple-element.182.refs_1_.refs_5_), channel_id=1, source_target_pairs={{0,2},{2,0},{4,6},{6,4},{8,10},{10,8},{12,14},{14,12},{16,18},{18,... | collective-permute-start | bytes 7864328 | tf_op jit(solution)/shard_map/ppermute | solution.py:622
  252.5 19.0 %collective-permute-start.12 = (bf16[1024,1280]{1,0:T(8,128)(2,1)}, bf16[1024,1280]{1,0:T(8,128)(2,1)}, u32[]{:S(2)}, u32[]{:S(2)}) collective-permute-start(bf16[1024,1280]{1,0:T(8,128)(2,1)} %bitcast.6.b1), channel_id=1, source_target_pairs={{0,2},{2,0},{4,6},{6,4},{8,10},{10,8},{12,14},{14,12},{16,18},{18,... | collective-permute-start | bytes 7864328 | tf_op jit(solution)/shard_map/ppermute | solution.py:622
  263.2 46.0 %collective-permute-start.11 = (bf16[1024,640]{1,0:T(8,128)(2,1)S(1)}, bf16[1024,640]{1,0:T(8,128)(2,1)S(1)}, u32[]{:S(2)}, u32[]{:S(2)}) collective-permute-start(bf16[1024,640]{1,0:T(8,128)(2,1)S(1)} %copy-done.63), channel_id=1, source_target_pairs={{0,2},{2,0},{4,6},{6,4},{8,10},{10,8},{12,14},{14,12},{16,18},{18,... | collective-permute-start | bytes 3932168 | tf_op jit(solution)/shard_map/ppermute | solution.py:622
  304.9 110.1 %collective-permute-start.15 = (bf16[2,4,400,640]{3,2,1,0:T(8,128)(2,1)}, bf16[2,4,400,640]{3,2,1,0:T(8,128)(2,1)}, u32[]{:S(2)}, u32[]{:S(2)}) collective-permute-start(bf16[2,4,400,640]{3,2,1,0:T(8,128)(2,1)} %get-tuple-element.117), channel_id=1, source_target_pairs={{1,0},{0,1},{3,2},{2,3},{5,4},{4,5},{7,6},{6,7},{9,8},{8,9},{11,10... | collective-permute-start | bytes 12288008 | tf_op jit(solution)/shard_map/ppermute | solution.py:628
  367.2 105.9 %collective-permute-start.20 = (bf16[1,1024,1280]{2,1,0:T(8,128)(2,1)}, bf16[1,1024,1280]{2,1,0:T(8,128)(2,1)}, u32[]{:S(2)}, u32[]{:S(2)}) collective-permute-start(bf16[1,1024,1280]{2,1,0:T(8,128)(2,1)} %fusion.23), channel_id=1, source_target_pairs={{0,1},{1,0},{2,3},{3,2},{4,5},{5,4},{6,7},{7,6},{8,9},{9,8},{10,11... | collective-permute-start | bytes 7864328 | tf_op jit(solution)/shard_map/ppermute | solution.py:631
  368.6 69.7 %collective-permute-start.16 = (bf16[160,2560]{1,0:T(8,128)(2,1)}, bf16[160,2560]{1,0:T(8,128)(2,1)}, u32[]{:S(2)}, u32[]{:S(2)}) collective-permute-start(bf16[160,2560]{1,0:T(8,128)(2,1)} %get-tuple-element.198), channel_id=1, source_target_pairs={{0,8},{2,10},{4,12},{6,14},{8,0},{10,2},{12,4},{14,6},{16,24},{18,... | collective-permute-start | bytes 2457608 | tf_op jit(solution)/shard_map/ppermute | solution.py:622
  370.9 67.4 %collective-permute-start.17 = (bf16[160,2560]{1,0:T(8,128)(2,1)}, bf16[160,2560]{1,0:T(8,128)(2,1)}, u32[]{:S(2)}, u32[]{:S(2)}) collective-permute-start(bf16[160,2560]{1,0:T(8,128)(2,1)} %get-tuple-element.197), channel_id=1, source_target_pairs={{0,16},{2,18},{4,20},{6,22},{8,24},{10,26},{12,28},{14,30},{16,0},... | collective-permute-start | bytes 2457608 | tf_op jit(solution)/shard_map/ppermute | solution.py:622
  375.9 62.4 %collective-permute-start.18 = (bf16[160,2560]{1,0:T(8,128)(2,1)}, bf16[160,2560]{1,0:T(8,128)(2,1)}, u32[]{:S(2)}, u32[]{:S(2)}) collective-permute-start(bf16[160,2560]{1,0:T(8,128)(2,1)} %get-tuple-element.196), channel_id=1, source_target_pairs={{0,24},{2,26},{4,28},{6,30},{8,16},{10,18},{12,20},{14,22},{16,8},... | collective-permute-start | bytes 2457608 | tf_op jit(solution)/shard_map/ppermute | solution.py:622
  420.3 90.3 %collective-permute-start.22 = (bf16[4,400,640]{2,1,0:T(8,128)(2,1)}, bf16[4,400,640]{2,1,0:T(8,128)(2,1)}, u32[]{:S(2)}, u32[]{:S(2)}) collective-permute-start(bf16[4,400,640]{2,1,0:T(8,128)(2,1)} %get-tuple-element.194), channel_id=1, source_target_pairs={{0,4},{2,6},{4,0},{6,2},{8,12},{10,14},{12,8},{14,10},{16,20},{18,... | collective-permute-start | bytes 6144008 | tf_op jit(solution)/shard_map/ppermute | solution.py:622
  440.4 31.7 %collective-permute-start.19 = (bf16[160,2560]{1,0:T(8,128)(2,1)S(1)}, bf16[160,2560]{1,0:T(8,128)(2,1)S(1)}, u32[]{:S(2)}, u32[]{:S(2)}) collective-permute-start(bf16[160,2560]{1,0:T(8,128)(2,1)S(1)} %add_convert_fusion.6), channel_id=1, source_target_pairs={{1,0},{0,1},{3,2},{2,3},{5,4},{4,5},{7,6},{6,7},{9,8},{8,9},{11,10... | collective-permute-start | bytes 2457608 | tf_op jit(solution)/shard_map/ppermute | solution.py:628
  473.1 62.7 %collective-permute-start.21 = (bf16[2,4,80,1152]{3,2,1,0:T(8,128)(2,1)}, bf16[2,4,80,1152]{3,2,1,0:T(8,128)(2,1)}, u32[]{:S(2)}, u32[]{:S(2)}) collective-permute-start(bf16[2,4,80,1152]{3,2,1,0:T(8,128)(2,1)} %get-tuple-element.137), channel_id=1, source_target_pairs={{1,0},{0,1},{3,2},{2,3},{5,4},{4,5},{7,6},{6,7},{9,8},{8,9},{11,10... | collective-permute-start | bytes 4423688 | tf_op jit(solution)/shard_map/ppermute | solution.py:628
  513.7 60.5 %collective-permute-start.25 = (bf16[400,640]{1,0:T(8,128)(2,1)}, bf16[400,640]{1,0:T(8,128)(2,1)}, u32[]{:S(2)}, u32[]{:S(2)}) collective-permute-start(bf16[400,640]{1,0:T(8,128)(2,1)} %get-tuple-element.204), channel_id=1, source_target_pairs={{0,8},{2,10},{4,12},{6,14},{8,0},{10,2},{12,4},{14,6},{16,24},{18,... | collective-permute-start | bytes 1536008 | tf_op jit(solution)/shard_map/ppermute | solution.py:622
  513.7 60.5 %collective-permute-start.26 = (bf16[400,640]{1,0:T(8,128)(2,1)}, bf16[400,640]{1,0:T(8,128)(2,1)}, u32[]{:S(2)}, u32[]{:S(2)}) collective-permute-start(bf16[400,640]{1,0:T(8,128)(2,1)} %get-tuple-element.203), channel_id=1, source_target_pairs={{0,16},{2,18},{4,20},{6,22},{8,24},{10,26},{12,28},{14,30},{16,0},... | collective-permute-start | bytes 1536008 | tf_op jit(solution)/shard_map/ppermute | solution.py:622
  519.1 55.1 %collective-permute-start.27 = (bf16[400,640]{1,0:T(8,128)(2,1)}, bf16[400,640]{1,0:T(8,128)(2,1)}, u32[]{:S(2)}, u32[]{:S(2)}) collective-permute-start(bf16[400,640]{1,0:T(8,128)(2,1)} %get-tuple-element.202), channel_id=1, source_target_pairs={{0,24},{2,26},{4,28},{6,30},{8,16},{10,18},{12,20},{14,22},{16,8},... | collective-permute-start | bytes 1536008 | tf_op jit(solution)/shard_map/ppermute | solution.py:622
  535.0 37.5 %collective-permute-start.23 = (bf16[2,4,80,768]{3,2,1,0:T(8,128)(2,1)}, bf16[2,4,80,768]{3,2,1,0:T(8,128)(2,1)}, u32[]{:S(2)}, u32[]{:S(2)}) collective-permute-start(bf16[2,4,80,768]{3,2,1,0:T(8,128)(2,1)} %get-tuple-element.143), channel_id=1, source_target_pairs={{1,0},{0,1},{3,2},{2,3},{5,4},{4,5},{7,6},{6,7},{9,8},{8,9},{11,10... | collective-permute-start | bytes 2949128 | tf_op jit(solution)/shard_map/ppermute | solution.py:628
  538.5 37.8 %collective-permute-start.24 = (bf16[4,80,1152]{2,1,0:T(8,128)(2,1)}, bf16[4,80,1152]{2,1,0:T(8,128)(2,1)}, u32[]{:S(2)}, u32[]{:S(2)}) collective-permute-start(bf16[4,80,1152]{2,1,0:T(8,128)(2,1)} %get-tuple-element.207), channel_id=1, source_target_pairs={{0,4},{2,6},{4,0},{6,2},{8,12},{10,14},{12,8},{14,10},{16,20},{18,... | collective-permute-start | bytes 2211848 | tf_op jit(solution)/shard_map/ppermute | solution.py:622
  574.1 21.1 %collective-permute-start.28 = (bf16[4,80,768]{2,1,0:T(8,128)(2,1)S(1)}, bf16[4,80,768]{2,1,0:T(8,128)(2,1)S(1)}, u32[]{:S(2)}, u32[]{:S(2)}) collective-permute-start(bf16[4,80,768]{2,1,0:T(8,128)(2,1)S(1)} %get-tuple-element.211), channel_id=1, source_target_pairs={{0,4},{2,6},{4,0},{6,2},{8,12},{10,14},{12,8},{14,10},{16,20},{18,... | collective-permute-start | bytes 1474568 | tf_op jit(solution)/shard_map/ppermute | solution.py:622
  575.8 59.6 %collective-permute-start.39 = (bf16[400,640]{1,0:T(8,128)(2,1)S(1)}, bf16[400,640]{1,0:T(8,128)(2,1)S(1)}, u32[]{:S(2)}, u32[]{:S(2)}) collective-permute-start(bf16[400,640]{1,0:T(8,128)(2,1)S(1)} %add_convert_fusion.13), channel_id=1, source_target_pairs={{1,0},{0,1},{3,2},{2,3},{5,4},{4,5},{7,6},{6,7},{9,8},{8,9},{11,10... | collective-permute-start | bytes 1536008 | tf_op jit(solution)/shard_map/ppermute | solution.py:628
  577.8 37.1 %collective-permute-start.29 = (bf16[80,1152]{1,0:T(8,128)(2,1)S(1)}, bf16[80,1152]{1,0:T(8,128)(2,1)S(1)}, u32[]{:S(2)}, u32[]{:S(2)}) collective-permute-start(bf16[80,1152]{1,0:T(8,128)(2,1)S(1)} %get-tuple-element.217), channel_id=1, source_target_pairs={{0,8},{2,10},{4,12},{6,14},{8,0},{10,2},{12,4},{14,6},{16,24},{18,... | collective-permute-start | bytes 552968 | tf_op jit(solution)/shard_map/ppermute | solution.py:622
  596.6 15.7 %collective-permute-start.45 = (bf16[80,768]{1,0:T(8,128)(2,1)S(1)}, bf16[80,768]{1,0:T(8,128)(2,1)S(1)}, u32[]{:S(2)}, u32[]{:S(2)}) collective-permute-start(bf16[80,768]{1,0:T(8,128)(2,1)S(1)} %get-tuple-element.223), channel_id=1, source_target_pairs={{0,16},{2,18},{4,20},{6,22},{8,24},{10,26},{12,28},{14,30},{16,0},... | collective-permute-start | bytes 368648 | tf_op jit(solution)/shard_map/ppermute | solution.py:622
  598.6 16.1 %collective-permute-start.46 = (bf16[80,768]{1,0:T(8,128)(2,1)S(1)}, bf16[80,768]{1,0:T(8,128)(2,1)S(1)}, u32[]{:S(2)}, u32[]{:S(2)}) collective-permute-start(bf16[80,768]{1,0:T(8,128)(2,1)S(1)} %get-tuple-element.222), channel_id=1, source_target_pairs={{0,24},{2,26},{4,28},{6,30},{8,16},{10,18},{12,20},{14,22},{16,8},... | collective-permute-start | bytes 368648 | tf_op jit(solution)/shard_map/ppermute | solution.py:622
  602.9 18.0 %collective-permute-start.30 = (bf16[80,1152]{1,0:T(8,128)(2,1)S(1)}, bf16[80,1152]{1,0:T(8,128)(2,1)S(1)}, u32[]{:S(2)}, u32[]{:S(2)}) collective-permute-start(bf16[80,1152]{1,0:T(8,128)(2,1)S(1)} %get-tuple-element.216), channel_id=1, source_target_pairs={{0,16},{2,18},{4,20},{6,22},{8,24},{10,26},{12,28},{14,30},{16,0},... | collective-permute-start | bytes 552968 | tf_op jit(solution)/shard_map/ppermute | solution.py:622
  614.7 13.7 %collective-permute-start.32 = (bf16[1024,1280]{1,0:T(8,128)(2,1)S(1)}, bf16[1024,1280]{1,0:T(8,128)(2,1)S(1)}, u32[]{:S(2)}, u32[]{:S(2)}) collective-permute-start(bf16[1024,1280]{1,0:T(8,128)(2,1)S(1)} %get-tuple-element.200), channel_id=1, source_target_pairs={{0,2},{2,0},{4,6},{6,4},{8,10},{10,8},{12,14},{14,12},{16,18},{18,... | collective-permute-start | bytes 7864328 | tf_op jit(solution)/shard_map/ppermute | solution.py:622
  636.4 19.7 %collective-permute-start.40 = (bf16[400,640]{1,0:T(8,128)(2,1)}, bf16[400,640]{1,0:T(8,128)(2,1)}, u32[]{:S(2)}, u32[]{:S(2)}) collective-permute-start(bf16[400,640]{1,0:T(8,128)(2,1)} %broadcast_select_fusion), channel_id=1, source_target_pairs={{0,2},{2,0},{4,6},{6,4},{8,10},{10,8},{12,14},{14,12},{16,18},{18,... | collective-permute-start | bytes 1536008 | tf_op jit(solution)/shard_map/ppermute | solution.py:622
  638.5 15.1 %collective-permute-start.37 = (bf16[80,2560]{1,0:T(8,128)(2,1)}, bf16[80,2560]{1,0:T(8,128)(2,1)}, u32[]{:S(2)}, u32[]{:S(2)}) collective-permute-start(bf16[80,2560]{1,0:T(8,128)(2,1)} %dynamic-slice_bitcast_fusion), channel_id=1, source_target_pairs={{0,2},{2,0},{4,6},{6,4},{8,10},{10,8},{12,14},{14,12},{16,18},{18,... | collective-permute-start | bytes 1228808 | tf_op jit(solution)/shard_map/ppermute | solution.py:622
  639.2 12.5 %collective-permute-start.33 = (f32[1,4,960]{2,1,0:T(4,128)S(1)}, f32[1,4,960]{2,1,0:T(4,128)S(1)}, u32[]{:S(2)}, u32[]{:S(2)}) collective-permute-start(f32[1,4,960]{2,1,0:T(4,128)S(1)} %get-tuple-element.230), channel_id=1, source_target_pairs={{0,8},{2,10},{4,12},{6,14},{8,0},{10,2},{12,4},{14,6},{16,24},{18,... | collective-permute-start | bytes 46088 | tf_op jit(solution)/shard_map/ppermute | solution.py:622
  (84 other events, 843.9 us)

commit v4 on v3

--- a/solution.py
+++ b/solution.py
@@ -21,7 +21,7 @@
 NT = (((1,), (1,)), ((), ()))
 TN = (((0,), (0,)), ((), ()))
 VMEM_LIMIT = 56 * 2**20
-SHARE = 20
+SHARE = 1000
 VR = HD + 16
 
 
@@ -513,31 +513,38 @@
     )(where, a1, b1, a2, b2)
 
 
-def product_kernel(*refs, dims, parts):
-    total = dot(refs[0][...], refs[1][...], dims)
-    for i in range(1, parts):
-        total = total + dot(refs[2 * i][...], refs[2 * i + 1][...], dims)
-    for term in refs[2 * parts : -1]:
+def product_kernel(*refs, dims, spans):
+    parts = len(spans) if spans else 1
+    total = None
+    for i in range(parts):
+        b = refs[parts]
+        if spans:
+            b = jnp.concatenate([b[:, low:high] for low, high in spans[i]], axis=1)
+        else:
+            b = b[...]
+        part = dot(refs[i][...], b, dims)
+        total = part if total is None else total + part
+    for term in refs[parts + 1 : -1]:
         total = total + term[...]
     refs[-1][...] = total.astype(refs[-1].dtype)
 
 
-def product(pairs, dims, name, terms=()):
+def product(parts, b, dims, name, spans=None, terms=(), half=None):
     tile = 256
     turned = dims == NT
-    rows = pairs[0][0].shape[0]
-    width = pairs[0][1].shape[0 if turned else 1]
-    ins, flat, depth = [], [], 0
-    for a, b in pairs:
-        ins.append(pl.BlockSpec(a.shape, lambda i: (0, 0), pipeline_mode=pl.Buffered(1)))
-        if turned:
-            ins.append(pl.BlockSpec((tile, b.shape[1]), lambda i: (i, 0)))
-        else:
-            ins.append(pl.BlockSpec((b.shape[0], tile), lambda i: (0, i)))
-        flat += [a, b]
-        depth += a.shape[1]
+    rows = parts[0].shape[0] // (1 if half is None else 2)
+    place = half or 0
+    width = b.shape[0 if turned else 1]
+    depth = sum(a.shape[1] for a in parts)
+    ins = [
+        pl.BlockSpec((rows, a.shape[1]), lambda i: (place, 0), pipeline_mode=pl.Buffered(1)) for a in parts
+    ]
+    if turned:
+        ins.append(pl.BlockSpec((tile, b.shape[1]), lambda i: (i, 0)))
+    else:
+        ins.append(pl.BlockSpec((b.shape[0], tile), lambda i: (0, i)))
     return pl.pallas_call(
-        functools.partial(product_kernel, dims=dims, parts=len(pairs)),
+        functools.partial(product_kernel, dims=dims, spans=spans),
         out_shape=jax.ShapeDtypeStruct((rows, width), BF),
         grid=(width // tile,),
         in_specs=ins + [pl.BlockSpec((t.shape[0], tile), lambda i: (0, i)) for t in terms],
@@ -549,7 +556,7 @@
             transcendentals=0,
         ),
         name=name,
-    )(*flat, *terms)
+    )(*parts, b, *terms)
 
 
 def tile_flags(queries, keys, tq, tk):
@@ -651,10 +658,11 @@
     w_own = jnp.concatenate([cut(w_qkv, part * width + core * half, half, 1) for part in range(3)], axis=1)
     b_own = jnp.concatenate([cut(bias_q, core * half, half, 0), jnp.zeros((half,), F32), cut(bias_v, core * half, half, 0)])
 
-    def own_columns(span):
-        return [w_own[:, part * half + span[0] * HD : part * half + span[1] * HD] for part in range(3)]
-
-    w_early, w_late = (jnp.concatenate(own_columns(span), axis=1) for span in spans)
+    def own_columns(span, parts):
+        return tuple((part * half + span[0] * HD, part * half + span[1] * HD) for part in parts)
+
+    near_spans = tuple(own_columns(span, (0, 1, 2)) for span in spans)
+    far_spans = tuple(own_columns(span, (1, 2)) for span in spans)
 
     def columns(array):
         return jnp.broadcast_to(array[:, :, None], array.shape + (128,))
@@ -669,7 +677,7 @@
     d_out_mate = to_mate(after(d_out, acts_pair))
     far_own = after(far_own, state)
     far_mate = to_mate(far_own)
-    d_act = dot(after(d_out, far_own, state), w_back, NT).astype(BF)
+    d_act = dot(after(d_out, far_own, state, d_out_mate), w_back, NT).astype(BF)
 
     far_mate = after(far_mate, d_act)
     far_pair = jnp.concatenate([far_own, far_mate], axis=0)
@@ -690,7 +698,12 @@
     b_in = bias_in.reshape(1, ff)
     act_part, d_pre_theirs, sum_part = ffn_call(where, acts2, w_in, b_in, d_act, (), "ffn_theirs")
     d_pre_mate = to_mate(d_pre_theirs)
-    act, d_pre_mine, d_pre_sum = ffn_call(where, acts2, w_in, b_in, d_act, (act_part, sum_part), "ffn_mine")
+    act_part, acts2_mate, mate_rest = after((act_part, acts2_mate, mate_rest), d_pre_theirs)
+    act, d_pre_mine, d_pre_sum = ffn_call(
+        where, after(acts2, acts2_mate, mate_rest), w_in, b_in, d_act, (act_part, sum_part), "ffn_mine"
+    )
+    d_pre_mine, d_pre_mate = after((d_pre_mine, d_pre_mate), d_pre_sum)
+    d_pre_theirs = after(d_pre_theirs, d_pre_mate)
     act_mate = to_mate(act)
     w_in_mine = cut(w_in, core * (ff // 2), ff // 2, 1)
     w_in_theirs = cut(w_in, (1 - core) * (ff // 2), ff // 2, 1)
@@ -707,22 +720,26 @@
         return [across(parts[one], 2 * one) for one in range(1, first)]
 
     def add_first(parts, received):
-        sums = []
-        for two in range(second):
-            total = parts[0][two].astype(F32)
+        def added(at):
+            total = parts[0][at].astype(F32)
             for part in received:
-                total = total + part[two].astype(F32)
-            sums.append(total.astype(BF))
-        return sums
-
-    def send_second(sums):
-        return [across(sums[two], 2 * first * two) for two in range(1, second)]
-
-    def add_second(sums, received):
-        total = sums[0].astype(F32)
-        for part in received:
-            total = total + part.astype(F32)
-        return total.astype(BF)
+                total = total + part[at].astype(F32)
+            return total.astype(BF)
+
+        return added(slice(0, second // 2)), added(slice(second // 2, second))
+
+    def send_second(pair):
+        return across(pair[1], first * second)
+
+    def add_second(pair, received):
+        kept, got = pair[0].astype(F32), received.astype(F32)
+        return tuple((kept[at] + got[at]).astype(BF) for at in range(2))
+
+    def send_third(pair):
+        return across(pair[1], 2 * first)
+
+    def add_third(pair, received):
+        return (pair[0].astype(F32) + received.astype(F32)).astype(BF)
 
     def start(parts):
         return from_ahead(parts[1], 1) if halves else send(parts)
@@ -758,12 +775,12 @@
         other = to_mate(given)
         return jnp.where(core == 0, kept, other).astype(F32), jnp.where(core == 0, other, kept).astype(F32)
 
-    d_pre_held, d_pre_mate = after((d_pre_mine, d_pre_mate), d_att_theirs, d_att_mine)
+    d_pre_held = after(d_pre_mine, d_att_theirs, d_att_mine)
     grad_in = grad_call(
         where, [[(acts2, d_pre_held, 0), (acts2_mate, d_pre_mate, 0)]], ff // 2, first, second, 512, False, "grad_in"
     )
     in_in = send(grad_in)
-    act_held, act_mate, mate_rest, d_z_mate = after((act, act_mate, mate_rest, d_z_mate), grad_in)
+    act_held, act_mate, d_z_mate = after((act, act_mate, d_z_mate), grad_in)
 
     def grad_o(into):
         return grad_call(
@@ -803,10 +820,11 @@
     far_early, far_late = after((far_early, far_late), in_sums)
     far_early, far_late = (f.reshape(-1, f.shape[-1]) for f in (far_early, far_late))
     n_early, n_late = early * HD, (heads - early) * HD
-    far_part = product([(far_early, w_early[:, n_early:]), (far_late, w_late[:, n_late:])], NT, "far_norm")
-    far_part = far_part.reshape(2 * rows, far_len, width)
-    far_given = to_mate(far_part[rows:])
-    far_sum = (far_part[:rows].astype(F32) + after(far_given, in_sums, far_part).astype(F32)).astype(BF)
+    far_theirs = product([far_early, far_late], w_own, NT, "far_norm_theirs", far_spans, half=1)
+    far_given = to_mate(far_theirs)
+    far_mine = product([after(far_early, far_theirs), far_late], w_own, NT, "far_norm_mine", far_spans, half=0)
+    far_sum = (far_mine.astype(F32) + after(far_given, in_sums, far_mine).astype(F32)).astype(BF)
+    far_sum = far_sum.reshape(rows, far_len, width)
     far_back = [to_ahead(far_sum[:, by * seg : (by + 1) * seg], by + 1) for by in range(group - 1)]
     d_qT = after(d_qT, far_sum)
 
@@ -819,38 +837,49 @@
 
     near_early = near_back(spans[0], "attn_bwd_early")
     b_sums, b_in = middle_step(grad_b, after(b_in, near_early))
-    in_total = add_second(in_sums, after(in_more, b_sums))
+    in_two = add_second(in_sums, after(in_more, b_sums))
+    in_last = send_third(in_two)
+    near_early = after(near_early, b_sums, in_two)
+    *grad_e, sum_e = qkv_call(where, (acts_pair, near_early), (far_pair, far_early), first, second, halves, "grad_early")
+    in_total = add_third(in_two, after(in_last, grad_e))
     in_row = ahead(in_total)
-    near_early = after(near_early, b_sums, in_total)
-    *grad_e, sum_e = qkv_call(where, (acts_pair, near_early), (far_pair, far_early), first, second, halves, "grad_early")
-    grad_e, in_row, far_back = after((grad_e, in_row, far_back), grad_e)
+    grad_e, far_back = after((grad_e, far_back), in_total)
     e_in = start(grad_e)
     near_late = near_back(spans[1], "attn_bwd_late", grad_e, far_back)
     b_two = add_first(b_sums, after(b_in, near_late))
     b_more = send_second(b_two)
-    near_late = after(near_late, b_two)
+    e_sums, e_in = middle_step(grad_e, after(e_in, b_two))
+    in_row = after(in_row, e_sums)
+    near_late = after(near_late, b_two, e_sums, in_row)
     *grad_l, sum_l = qkv_call(where, (acts_pair, near_late), (far_pair, far_late), first, second, halves, "grad_late")
     l_in = start(grad_l)
-    e_sums, e_in = middle_step(grad_e, after(e_in, grad_l))
-    act_late = after(act_held, e_sums)
-    mixed = product([(act_late, w_back)], NN, "mixed", (middle, bias_back.reshape(1, width))).reshape(tokens.shape)
-    l_sums, l_in = middle_step(grad_l, after(l_in, mixed))
-    b_total = add_second(b_two, after(b_more, l_sums))
+    near_held = after(near_early, grad_l)
+    near_theirs = product([near_held, near_late], w_own, NT, "near_norm_theirs", near_spans, half=1)
+    near_mine = product([after(near_held, near_theirs), near_late], w_own, NT, "near_norm_mine", near_spans, half=0)
+    e_two = add_first(e_sums, after(e_in, near_mine))
+    e_more = send_second(e_two)
+    b_three = add_second(b_two, after(b_more, e_two))
+    b_last = send_third(b_three)
+    l_sums, l_in = middle_step(grad_l, after(l_in, b_three))
+    near_given = to_mate(after(near_theirs, near_mine))
+    act_late = after(act_held, e_two, b_three, l_sums)
+    mixed = product([act_late], w_back, NN, "mixed", terms=(middle, bias_back.reshape(1, width))).reshape(tokens.shape)
+    l_two = add_first(l_sums, after(l_in, mixed))
+    l_more = send_second(l_two)
+    e_three = add_second(e_two, after(e_more, l_two))
+    e_last = send_third(e_three)
+    b_total = add_third(b_three, after(b_last, e_three))
     b_row = ahead(b_total)
-    e_two = add_first(e_sums, after(e_in, b_total))
-    e_more = send_second(e_two)
-    near_part = product(
-        [(after(near_early, l_sums, e_two), w_early), (near_late, w_late)], NT, "near_norm"
-    )
-    near_given = to_mate(near_part[count:])
-    l_two = add_first(l_sums, after(l_in, near_part))
-    e_total = add_second(e_two, after(e_more, l_two))
-    l_more = send_second(l_two)
-    e_row = ahead(e_total)
-    (d_norm1,) = after((near_part[:count].astype(F32),), l_two, e_total)
-    d_norm1 = d_norm1 + near_given.astype(F32)
+    near_mine, near_given = after((near_mine, near_given), l_two, e_three, b_total)
+    d_norm1 = near_mine.astype(F32) + near_given.astype(F32)
     for part in far_back:
         d_norm1 = d_norm1 + part.reshape(count, width).astype(F32)
+    norm1_sums = (jnp.sum(d_norm1 * xhat1, axis=0), jnp.sum(d_norm1, axis=0))
+    e_total = add_third(e_three, after(e_last, norm1_sums))
+    e_row = ahead(e_total)
+    l_three = add_second(l_two, after(l_more, e_total))
+    l_last = send_third(l_three)
+    xhat1 = after(xhat1, l_three, e_total)
     grad_tokens = (d_middle + layer_norm_back(d_norm1, norm1_gain, xhat1, rstd1)).reshape(tokens.shape)
 
     def vectors(parts, *covers):
@@ -883,13 +912,13 @@
         own = jnp.concatenate([s[0, part * m : (part + 1) * m] for s, m in zip((sum_e, sum_l), n)])
         return lax.dynamic_update_slice_in_dim(jnp.zeros((width,), F32), own, core * half, 0)
 
-    in_low, in_high = swap(by_core(after(in_total, d_norm1), in_row, [width // chips])) if not halves else (None, None)
+    in_low, in_high = swap(by_core(after(in_total, grad_tokens), in_row, [width // chips])) if not halves else (None, None)
     if halves:
-        in_whole = over_row(after(in_total, d_norm1), in_row).reshape(2, -1, in_total.shape[1])
+        in_whole = over_row(after(in_total, grad_tokens), in_row).reshape(2, -1, in_total.shape[1])
         in_low, in_high = swap([lax.dynamic_index_in_dim(in_whole, i, 0, keepdims=False) for i in (core, 1 - core)])
-    b_low, b_high = swap(by_core(after(b_total, d_norm1), b_row, [back_rows, out_rows]))
-    e_low, e_high = swap(by_core(e_total, e_row, [out_rows]))
-    l_total = add_second(l_two, l_more)
+    b_low, b_high = swap(by_core(after(b_total, grad_tokens), b_row, [back_rows, out_rows]))
+    e_low, e_high = swap(by_core(after(e_total, grad_tokens), e_row, [out_rows]))
+    l_total = add_third(l_three, after(l_last, grad_tokens))
     l_low, l_high = swap(by_core(l_total, ahead(l_total), [out_rows]))
 
     def part_columns(part):
@@ -904,8 +933,7 @@
     grad_w_out = jnp.concatenate([b_low[share:], b_high[share:]], axis=1)
     small = vectors(
         [
-            jnp.sum(d_norm1 * xhat1, axis=0),
-            jnp.sum(d_norm1, axis=0),
+            *norm1_sums,
             widened(0),
             widened(2),
             jnp.sum(d_z.astype(F32), axis=0),

time: 665 us -> 658 us (0.989)
  starting transfers between devices: 90.2 us -> 53 us
  Pallas kernels: 324 us -> 361 us
  local copies, waits for them, and re-layouts: 30.2 us -> 23 us
    ppermute x38 -> x34, starting transfers between devices: 74.5 us -> 33.2 us  [across(): return lax.ppermute(array, 'wide', [(i, i ^ by) for i in range(wide)])]
    pallas_call x3, Pallas kernels: 97 us -> 121 us  [attn_bwd(): pl.pallas_call(functools.partial(bwd_kernel, spans=spans, tq=tq, tk=tk),...]
    pallas_call x3 -> x5, Pallas kernels: 49.1 us -> 57.3 us  [product(): pl.pallas_call(functools.partial(product_kernel, dims=dims, spans=spans),...]
    slice x3 -> x0, local copies, waits for them, and re-layouts: 7.68 us -> none  [the longest x2 5.62 us: own_columns(): w_own[:, part * half + span[0] * HD:part * half + span[1] * HD]]
    ppermute x38 -> x34, waiting for transfers between devices: 27.3 us -> 33.4 us  [across(): return lax.ppermute(array, 'wide', [(i, i ^ by) for i in range(wide)])]
    convert_element_type x9 -> x16, other arithmetic: 15.8 us -> 15.3 us  [the longest x8 12.9 us: add_second(): kept, got = (pair[0].astype(F32), received.astype(F32))]
  transfers between devices with their start and end apart: 49 -> 45, of which waited for: 9 -> 11; matrix products, arithmetic and copies ran while one was open for 25% -> 24% of each run, Pallas kernels for 40% -> 48%
where the time goes in v4:
time: 658 us; the launch traced here: 661 us
  Pallas kernels  361 us (55%)
  matrix products  88.9 us (14%)
  other arithmetic  81 us (12%)
  starting transfers between devices  53 us (8%)
  waiting for transfers between devices  51.4 us (8%)
  local copies, waits for them, and re-layouts  23 us (3%)
    pallas_call x3, Pallas kernels, attn_bwd(): pl.pallas_call(functools.partial(bwd_kernel, spans=spans, tq=tq, tk=tk),...  121 us
    dot_general x9, matrix products, dot(): return lax.dot_general(a, b, dims, preferred_element_type=F32)  88.9 us
    pallas_call x2, Pallas kernels, attn_fwd(): pl.pallas_call(functools.partial(fwd_kernel, first=first, tq=tq, tk=tk, h...  57.9 us
    pallas_call x5, Pallas kernels, product(): pl.pallas_call(functools.partial(product_kernel, dims=dims, spans=spans),...  57.3 us
    pallas_call x2, Pallas kernels, qkv_call(): pl.pallas_call(functools.partial(qkv_kernel, first=first, second=second,...  36.8 us
    pallas_call x2, Pallas kernels, ffn_call(): pl.pallas_call(ffn_kernel, out_shape=[jax.ShapeDtypeStruct((rows, ff), BF...  35 us
    ppermute x34, waiting for transfers between devices, across(): return lax.ppermute(array, 'wide', [(i, i ^ by) for i in range(wide)])  33.4 us
    ppermute x34, starting transfers between devices, across(): return lax.ppermute(array, 'wide', [(i, i ^ by) for i in range(wide)])  33.2 us
  transfers between devices with their start and end apart: 45, of which 11 were waited for; matrix products, arithmetic and copies ran while one was open for 24% of the time, Pallas kernels for 48%

profile of v4, /device:TPU:0, one launch (start us, length us, event | category | flops | bytes accessed | tf_op | source)
XLA Modules:
  0.0 660.8 jit_solution(17908241422349573647)
XLA Ops:
  23.4 13.5 %add_convert_fusion = bf16[2048,1920]{1,0:T(8,128)(2,1)} fusion(f32[1920]{0:T(1024)S(1)} %pad_maximum_fusion.5, bf16[2048,1280]{1,0:T(8,128)(2,1)S(1)} %bitcast.172, bf16[1280,640]{1,0:T(8,128)(2,1)S(1)} %copy-done.21, bf16[1280,640]{1,0:T(8,128)(2,1)S(1)} %copy-done.23, bf16[1280,640]{1,0:T(8,128)(2,1)S(1)} %copy-done.19), kind=kOutput, calls=%fused_computation | convolution fusion | flops 10088939520 | bytes 18030080 | tf_op jit(solution)/shard_map/dot_general | solution.py:29
  38.3 32.0 %attn_fwd_a.1 = (f32[2,640,1024]{2,1,0:T(8,128)}, f32[2,16,1024]{2,1,0:T(8,128)}, f32[2,16,1024]{2,1,0:T(8,128)}) custom-call(s32[2,2,4]{2,1,0:T(2,128)} %get-tuple-element.258.flags, s32[2,1,1024]{2,1,0:T(1,128)} %broadcast_in_dim.38.cq, s32[2,1024,128]{2,1,0:T(8,128)} %broadcast_in_dim.41.ck, bf16[2,1024,1920]{2,1,0:T(8,128)(2,1)} %bitcast.149, ...), custom_call_target="tpu_custom_call" | custom-call | flops 5368709 | bytes 13107 | tf_op jit(solution)/shard_map/attn_fwd_a/pallas_call | solution.py:155
  70.3 5.3 collective-permute-done.3
  75.6 20.6 %convolution_convert_fusion.d_act = bf16[1024,5120]{1,0:T(8,128)(2,1)} fusion(bf16[1024,1280]{1,0:T(8,128)(2,1)S(1)} %bitcast.194, bf16[5120,1280]{1,0:T(8,128)(2,1)} %refs_1_.1), kind=kOutput, calls=%fused_computation.2 | convolution fusion | flops 13427015680 | bytes 26214400 | tf_op jit(solution)/shard_map/dot_general | solution.py:29
  99.6 8.7 %add_convert_fusion.1 = bf16[2048,1280]{1,0:T(8,128)(2,1)} fusion(bf16[2048,1280]{1,0:T(8,128)(2,1)S(1)} %bitcast.175, f32[1280]{0:T(1024)S(1)} %concatenate.70, bf16[1280,640]{1,0:T(8,128)(2,1)S(1)} %copy-done.22, bf16[1280,640]{1,0:T(8,128)(2,1)S(1)} %copy-done.24), kind=kOutput, calls=%fused_computation.1 | convolution fusion | flops 6722682880 | bytes 13767680 | tf_op jit(solution)/shard_map/dot_general | solution.py:29
  109.7 25.9 %attn_fwd_b.1 = (bf16[2,1024,640]{2,1,0:T(8,128)(2,1)}, f32[2,16,1024]{2,1,0:T(8,128)}) custom-call(s32[2,2,4]{2,1,0:T(2,128)} %get-tuple-element.259.flags, s32[2,1,1024]{2,1,0:T(1,128)} %broadcast_in_dim.38.cq, s32[2,1024,128]{2,1,0:T(8,128)} %broadcast_in_dim.39.ck, bf16[2,1024,1920]{2,1,0:T(8,128)(2,1)} %bitcast.152, bf16[2,1024,1280]{2,1,0:T(8,128)(2,1)} %bitcast.162, ...), custom_call_target="tpu_custom_call" | custom-call | flops 5368709 | bytes 13107 | tf_op jit(solution)/shard_map/attn_fwd_b/pallas_call | solution.py:155
  151.0 17.9 %ffn_theirs.1 = (bf16[1024,5120]{1,0:T(8,128)(2,1)}, bf16[1024,2560]{1,0:T(8,128)(2,1)}, f32[1,5120]{1,0:T(1,128)}) custom-call(s32[3]{0:T(128)} %add_add_fusion.where, bf16[1024,1280]{1,0:T(8,128)(2,1)} %add_convert_fusion.3.acts.refs_0_, bf16[1280,5120]{1,0:T(8,128)(2,1)} %w.3, f32[1,5120]{1,0:T(1,128)} %bitcast.198, ...), custom_call_target="tpu_custom_call" | custom-call | flops 6710886 | bytes 24903 | tf_op jit(solution)/shard_map/ffn_theirs/pallas_call | solution.py:303
  169.5 13.3 %collective-permute-done.8.refs_6_ = bf16[1024,640]{1,0:T(8,128)(2,1)S(1)} collective-permute-done((bf16[1024,640]{1,0:T(8,128)(2,1)S(1)}, bf16[1024,640]{1,0:T(8,128)(2,1)S(1)}, u32[]{:S(2)}, u32[]{:S(2)}) %collective-permute-start.8) | collective-permute-done | bytes 1310752 | tf_op jit(solution)/shard_map/ppermute | solution.py:629
  184.8 17.1 %ffn_mine.1 = (bf16[1024,5120]{1,0:T(8,128)(2,1)}, bf16[1024,2560]{1,0:T(8,128)(2,1)}, f32[1,5120]{1,0:T(1,128)}) custom-call(s32[3]{0:T(128)} %add_add_fusion.where, bf16[1024,1280]{1,0:T(8,128)(2,1)} %add_convert_fusion.3.acts.refs_0_, bf16[1280,5120]{1,0:T(8,128)(2,1)} %w.3, f32[1,5120]{1,0:T(1,128)} %bitcast.199, ...), custom_call_target="tpu_custom_call", output_to_operand_aliasing={{0}: (5, {}), {2}: (6, {})} | custom-call | flops 6710886 | bytes 24903 | tf_op jit(solution)/shard_map/ffn_mine/pallas_call | solution.py:303
  202.2 12.5 %fusion.2 = f32[1024,1280]{1,0:T(8,128)} fusion(bf16[1024,2560]{1,0:T(8,128)(2,1)} %get-tuple-element.122, bf16[1280,5120]{1,0:T(8,128)(2,1)} %w.3, s32[]{:T(128)S(6)} %select_n.201), kind=kOutput, calls=%fused_computation.8 | convolution fusion | flops 6710886400 | bytes 17039364 | tf_op jit(solution)/shard_map/dot_general | solution.py:29
  214.6 15.8 %multiply_reduce_fusion = (f32[1280]{0:T(1024)S(1)}, f32[1024]{0:T(1024)S(1)}, f32[1024]{0:T(1024)S(1)}, f32[1280]{0:T(1024)S(1)}, f32[1024,1280]{1,0:T(8,128)}) fusion(f32[1024,1280]{1,0:T(8,128)} %copy-done.2, f32[1024]{0:T(1024)S(1)} %add_rsqrt_fusion, f32[1024]{0:T(1024)S(1)} %broadcast_multiply_fusion.4, f32[1280]{0:T(1024)S(1)} %copy-done.42, ...), kind=kOutput, calls=%fused_computation.25 | convolution fusion | flops 6723989504 | bytes 27556868 | tf_op jit(solution)/shard_map/dot_general | solution.py:29
  230.4 6.6 convert_reduce_fusion.2
  237.0 5.1 convolution_convert_fusion.2
  247.1 20.4 %grad_in.1 = (bf16[4,160,2560]{2,1,0:T(8,128)(2,1)}, bf16[4,160,2560]{2,1,0:T(8,128)(2,1)}) custom-call(s32[3]{0:T(128)} %add_add_fusion.where, bf16[1024,1280]{1,0:T(8,128)(2,1)} %add_convert_fusion.3.acts.refs_0_, bf16[1024,2560]{1,0:T(8,128)(2,1)} %get-tuple-element.124.refs_1_, bf16[1024,1280]{1,0:T(8,128)(2,1)} %copy-done.30, ...), custom_call_target="tpu_custom_call" | custom-call | flops 13421772 | bytes 22282 | tf_op jit(solution)/shard_map/grad_in/pallas_call | solution.py:393
  274.8 22.9 %grad_back.1 = (bf16[2,4,400,640]{3,2,1,0:T(8,128)(2,1)}, bf16[2,4,400,640]{3,2,1,0:T(8,128)(2,1)}) custom-call(s32[3]{0:T(128)} %add_add_fusion.where, bf16[1024,5120]{1,0:T(8,128)(2,1)} %get-tuple-element.167.a1.refs_0_, bf16[1024,1280]{1,0:T(8,128)(2,1)} %bitcast.192, bf16[1024,5120]{1,0:T(8,128)(2,1)} %collective-permute-done.9.a2, ...), custom_call_target="tpu_custom_call" | custom-call | flops 13421772 | bytes 30146 | tf_op jit(solution)/shard_map/grad_back/pallas_call | solution.py:486
  297.7 10.3 %grad_out.1 = (bf16[2,4,400,640]{3,2,1,0:T(8,128)(2,1)}, bf16[2,4,400,640]{3,2,1,0:T(8,128)(2,1)}) custom-call(s32[3]{0:T(128)} %add_add_fusion.1.where, bf16[1024,640]{1,0:T(8,128)(2,1)} %get-tuple-element.225.refs_0_, bf16[1024,1280]{1,0:T(8,128)(2,1)} %get-tuple-element.200.refs_1_.refs_5_, ...), custom_call_target="tpu_custom_call", output_to_operand_aliasing={{0}: (9, {}), {1}: (10, {})} | custom-call | flops 3355443 | bytes 9502 | tf_op jit(solution)/shard_map/grad_out/pallas_call | solution.py:393
  313.2 47.5 %attn_bwd_far.1 = (f32[2,640,1024]{2,1,0:T(8,128)}, bf16[2,1024,768]{2,1,0:T(8,128)(2,1)}, bf16[2,1024,512]{2,1,0:T(8,128)(2,1)}) custom-call(s32[2,4,4]{2,1,0:T(4,128)} %get-tuple-element.256.flags, s32[2,1,1024]{2,1,0:T(1,128)} %broadcast_in_dim.38.cq, s32[2,1024,128]{2,1,0:T(8,128)} %broadcast_in_dim.39.ck, bf16[2,1024,1920]{2,1,0:T(8,128)(2,1)} %bitcast.153, ...), custom_call_target="tpu_custom_call" | custom-call | flops 13421772 | bytes 23592 | tf_op jit(solution)/shard_map/attn_bwd_far/pallas_call | solution.py:256
  365.7 8.3 %far_norm_theirs.1 = bf16[1024,1280]{1,0:T(8,128)(2,1)} custom-call(bf16[2048,768]{1,0:T(8,128)(2,1)} %bitcast.178, bf16[2048,512]{1,0:T(8,128)(2,1)} %bitcast.183, bf16[1280,1920]{1,0:T(8,128)(2,1)} %pad_maximum_fusion.2.refs_2_), custom_call_target="tpu_custom_call" | custom-call | flops 3355443 | bytes 8519 | tf_op jit(solution)/shard_map/far_norm_theirs/pallas_call | solution.py:546
  374.0 8.4 %far_norm_mine.1 = bf16[1024,1280]{1,0:T(8,128)(2,1)} custom-call(bf16[2048,768]{1,0:T(8,128)(2,1)} %bitcast.179, bf16[2048,512]{1,0:T(8,128)(2,1)} %bitcast.184, bf16[1280,1920]{1,0:T(8,128)(2,1)} %pad_maximum_fusion.2.refs_2_), custom_call_target="tpu_custom_call" | custom-call | flops 3355443 | bytes 8519 | tf_op jit(solution)/shard_map/far_norm_mine/pallas_call | solution.py:546
  387.5 41.8 %attn_bwd_early.1 = bf16[2,1024,1152]{2,1,0:T(8,128)(2,1)} custom-call(s32[2,4,4]{2,1,0:T(4,128)} %get-tuple-element.257.flags, s32[2,1,1024]{2,1,0:T(1,128)} %broadcast_in_dim.38.cq, s32[2,1024,128]{2,1,0:T(8,128)} %broadcast_in_dim.41.ck, bf16[2,1024,1920]{2,1,0:T(8,128)(2,1)} %bitcast.154, bf16[2,1024,1920]{2,1,0:T(8,128)(2,1)} %bitcast.155, ...), custom_call_target="tpu_custom_call" | custom-call | flops 8053063 | bytes 14155 | tf_op jit(solution)/shard_map/attn_bwd_early/pallas_call | solution.py:256
  429.4 5.2 fusion.21
  434.6 14.0 %collective-permute-done.16 = bf16[2,160,2560]{2,1,0:T(8,128)(2,1)} collective-permute-done((bf16[2,160,2560]{2,1,0:T(8,128)(2,1)}, bf16[2,160,2560]{2,1,0:T(8,128)(2,1)}, u32[]{:S(2)}, u32[]{:S(2)}) %collective-permute-start.16) | collective-permute-done | bytes 1638432 | tf_op jit(solution)/shard_map/ppermute | solution.py:629
  451.0 5.8 collective-permute-start.18
  456.8 22.1 %grad_early.1 = (bf16[2,4,80,1152]{3,2,1,0:T(8,128)(2,1)}, bf16[2,4,80,1152]{3,2,1,0:T(8,128)(2,1)}, f32[1,1152]{1,0:T(1,128)}) custom-call(s32[3]{0:T(128)} %add_add_fusion.where, bf16[2048,1280]{1,0:T(8,128)(2,1)} %bitcast.173, bf16[2048,1152]{1,0:T(8,128)(2,1)} %bitcast.166, bf16[2048,1280]{1,0:T(8,128)(2,1)} %bitcast.176, bf16[2048,768]{1,0:T(8,128)(2,1)} %bitcast.180), custom_call_target="tpu_custom_call" | custom-call | flops 12079595 | bytes 22872 | tf_op jit(solution)/shard_map/grad_early/pallas_call | solution.py:444
  483.8 31.2 %attn_bwd_late.1 = bf16[2,1024,768]{2,1,0:T(8,128)(2,1)} custom-call(s32[2,4,4]{2,1,0:T(4,128)} %get-tuple-element.257.flags, s32[2,1,1024]{2,1,0:T(1,128)} %broadcast_in_dim.38.cq, s32[2,1024,128]{2,1,0:T(8,128)} %broadcast_in_dim.41.ck, bf16[2,1024,1920]{2,1,0:T(8,128)(2,1)} %bitcast.157, bf16[2,1024,1920]{2,1,0:T(8,128)(2,1)} %bitcast.158, ...), custom_call_target="tpu_custom_call" | custom-call | flops 5368709 | bytes 9437 | tf_op jit(solution)/shard_map/attn_bwd_late/pallas_call | solution.py:256
  519.7 5.1 collective-permute-start.21
  527.9 5.8 collective-permute-done.22
  533.7 14.7 %grad_late.1 = (bf16[2,4,80,768]{3,2,1,0:T(8,128)(2,1)}, bf16[2,4,80,768]{3,2,1,0:T(8,128)(2,1)}, f32[1,768]{1,0:T(1,128)}) custom-call(s32[3]{0:T(128)} %add_add_fusion.where, bf16[2048,1280]{1,0:T(8,128)(2,1)} %bitcast.174, bf16[2048,768]{1,0:T(8,128)(2,1)} %bitcast.169, bf16[2048,1280]{1,0:T(8,128)(2,1)} %bitcast.177, bf16[2048,512]{1,0:T(8,128)(2,1)} %bitcast.185), custom_call_target="tpu_custom_call" | custom-call | flops 8053063 | bytes 18743 | tf_op jit(solution)/shard_map/grad_late/pallas_call | solution.py:444
  552.4 9.9 %near_norm_theirs.1 = bf16[1024,1280]{1,0:T(8,128)(2,1)} custom-call(bf16[2048,1152]{1,0:T(8,128)(2,1)} %bitcast.167, bf16[2048,768]{1,0:T(8,128)(2,1)} %bitcast.170, bf16[1280,1920]{1,0:T(8,128)(2,1)} %pad_maximum_fusion.2.refs_2_), custom_call_target="tpu_custom_call" | custom-call | flops 5033164 | bytes 11468 | tf_op jit(solution)/shard_map/near_norm_theirs/pallas_call | solution.py:546
  562.3 9.9 %near_norm_mine.1 = bf16[1024,1280]{1,0:T(8,128)(2,1)} custom-call(bf16[2048,1152]{1,0:T(8,128)(2,1)} %bitcast.168, bf16[2048,768]{1,0:T(8,128)(2,1)} %bitcast.171, bf16[1280,1920]{1,0:T(8,128)(2,1)} %pad_maximum_fusion.2.refs_2_), custom_call_target="tpu_custom_call" | custom-call | flops 5033164 | bytes 11468 | tf_op jit(solution)/shard_map/near_norm_mine/pallas_call | solution.py:546
  584.9 20.9 %mixed.1 = bf16[1024,1280]{1,0:T(8,128)(2,1)} custom-call(bf16[1024,5120]{1,0:T(8,128)(2,1)} %get-tuple-element.167.a1.refs_0_, bf16[5120,1280]{1,0:T(8,128)(2,1)} %refs_1_.1, f32[1024,1280]{1,0:T(8,128)} %copy-done.2, f32[1,1280]{1,0:T(1,128)} %reshape.287.refs_3_), custom_call_target="tpu_custom_call" | custom-call | flops 13421772 | bytes 26214 | tf_op jit(solution)/shard_map/mixed/pallas_call | solution.py:546
  624.3 5.3 add_bitcast_fusion
  (344 shorter events, 155.1 us)
Async XLA Ops:
  15.9 59.6 %collective-permute-start.3 = (bf16[1,1024,1280]{2,1,0:T(8,128)(2,1)}, bf16[1,1024,1280]{2,1,0:T(8,128)(2,1)}, u32[]{:S(2)}, u32[]{:S(2)}) collective-permute-start(bf16[1,1024,1280]{2,1,0:T(8,128)(2,1)} %fusion.13), channel_id=1, source_target_pairs={{1,0},{0,1},{3,2},{2,3},{5,4},{4,5},{7,6},{6,7},{9,8},{8,9},{11,10... | collective-permute-start | bytes 7864328 | tf_op jit(solution)/shard_map/ppermute | solution.py:635
  20.6 55.0 %collective-permute-start.5 = (bf16[1024,1280]{1,0:T(8,128)(2,1)S(1)}, bf16[1024,1280]{1,0:T(8,128)(2,1)}, u32[]{:S(2)}, u32[]{:S(2)}) collective-permute-start(bf16[1024,1280]{1,0:T(8,128)(2,1)S(1)} %bitcast.193), channel_id=1, source_target_pairs={{0,2},{2,0},{4,6},{6,4},{8,10},{10,8},{12,14},{14,12},{16,18},{18,... | collective-permute-start | bytes 7864328 | tf_op jit(solution)/shard_map/ppermute | solution.py:629
  75.6 20.6 %collective-permute-start.4 = (bf16[1,1024,1280]{2,1,0:T(8,128)(2,1)}, bf16[1,1024,1280]{2,1,0:T(8,128)(2,1)}, u32[]{:S(2)}, u32[]{:S(2)}) collective-permute-start(bf16[1,1024,1280]{2,1,0:T(8,128)(2,1)} %collective-permute-done.3), channel_id=1, source_target_pairs={{0,2},{2,0},{4,6},{6,4},{8,10},{10,8},{12,14},{14,12},{16,18},{18,... | collective-permute-start | bytes 7864328 | tf_op jit(solution)/shard_map/ppermute | solution.py:629
  168.9 33.2 %collective-permute-start.10 = (bf16[1024,2560]{1,0:T(8,128)(2,1)}, bf16[1024,2560]{1,0:T(8,128)(2,1)}, u32[]{:S(2)}, u32[]{:S(2)}) collective-permute-start(bf16[1024,2560]{1,0:T(8,128)(2,1)} %get-tuple-element.122), channel_id=1, source_target_pairs={{0,2},{2,0},{4,6},{6,4},{8,10},{10,8},{12,14},{14,12},{16,18},{18,... | collective-permute-start | bytes 15728648 | tf_op jit(solution)/shard_map/ppermute | solution.py:629
  168.9 13.9 %collective-permute-start.7 = (bf16[1024,1280]{1,0:T(8,128)(2,1)S(1)}, bf16[1024,1280]{1,0:T(8,128)(2,1)S(1)}, u32[]{:S(2)}, u32[]{:S(2)}) collective-permute-start(bf16[1024,1280]{1,0:T(8,128)(2,1)S(1)} %copy-done.8), channel_id=1, source_target_pairs={{0,2},{2,0},{4,6},{6,4},{8,10},{10,8},{12,14},{14,12},{16,18},{18,... | collective-permute-start | bytes 7864328 | tf_op jit(solution)/shard_map/ppermute | solution.py:629
  169.4 13.4 %collective-permute-start.8 = (bf16[1024,640]{1,0:T(8,128)(2,1)S(1)}, bf16[1024,640]{1,0:T(8,128)(2,1)S(1)}, u32[]{:S(2)}, u32[]{:S(2)}) collective-permute-start(bf16[1024,640]{1,0:T(8,128)(2,1)S(1)} %copy-done.25), channel_id=1, source_target_pairs={{0,2},{2,0},{4,6},{6,4},{8,10},{10,8},{12,14},{14,12},{16,18},{18,... | collective-permute-start | bytes 3932168 | tf_op jit(solution)/shard_map/ppermute | solution.py:629
  201.9 72.9 %collective-permute-start.9 = (bf16[1024,5120]{1,0:T(8,128)(2,1)}, bf16[1024,5120]{1,0:T(8,128)(2,1)}, u32[]{:S(2)}, u32[]{:S(2)}) collective-permute-start(bf16[1024,5120]{1,0:T(8,128)(2,1)} %get-tuple-element.167.a1.refs_0_), channel_id=1, source_target_pairs={{0,2},{2,0},{4,6},{6,4},{8,10},{10,8},{12,14},{14,12},{16,18},{18,... | collective-permute-start | bytes 31457288 | tf_op jit(solution)/shard_map/ppermute | solution.py:629
  267.6 93.1 %collective-permute-start.13 = (bf16[4,160,2560]{2,1,0:T(8,128)(2,1)}, bf16[4,160,2560]{2,1,0:T(8,128)(2,1)}, u32[]{:S(2)}, u32[]{:S(2)}) collective-permute-start(bf16[4,160,2560]{2,1,0:T(8,128)(2,1)} %get-tuple-element.126), channel_id=1, source_target_pairs={{0,4},{2,6},{4,0},{6,2},{8,12},{10,14},{12,8},{14,10},{16,20},{18,... | collective-permute-start | bytes 9830408 | tf_op jit(solution)/shard_map/ppermute | solution.py:629
  267.8 44.3 %collective-permute-start.12 = (bf16[1024,640]{1,0:T(8,128)(2,1)}, bf16[1024,640]{1,0:T(8,128)(2,1)S(1)}, u32[]{:S(2)}, u32[]{:S(2)}) collective-permute-start(bf16[1024,640]{1,0:T(8,128)(2,1)} %convolution_convert_fusion.2), channel_id=1, source_target_pairs={{0,2},{2,0},{4,6},{6,4},{8,10},{10,8},{12,14},{14,12},{16,18},{18,... | collective-permute-start | bytes 3932168 | tf_op jit(solution)/shard_map/ppermute | solution.py:629
  308.1 121.3 %collective-permute-start.15 = (bf16[2,4,400,640]{3,2,1,0:T(8,128)(2,1)}, bf16[2,4,400,640]{3,2,1,0:T(8,128)(2,1)}, u32[]{:S(2)}, u32[]{:S(2)}) collective-permute-start(bf16[2,4,400,640]{3,2,1,0:T(8,128)(2,1)} %get-tuple-element.133), channel_id=1, source_target_pairs={{1,0},{0,1},{3,2},{2,3},{5,4},{4,5},{7,6},{6,7},{9,8},{8,9},{11,10... | collective-permute-start | bytes 12288008 | tf_op jit(solution)/shard_map/ppermute | solution.py:635
  374.0 8.4 %collective-permute-start.14 = (bf16[1024,1280]{1,0:T(8,128)(2,1)}, bf16[1024,1280]{1,0:T(8,128)(2,1)S(1)}, u32[]{:S(2)}, u32[]{:S(2)}) collective-permute-start(bf16[1024,1280]{1,0:T(8,128)(2,1)} %far_norm_theirs.1), channel_id=1, source_target_pairs={{0,2},{2,0},{4,6},{6,4},{8,10},{10,8},{12,14},{14,12},{16,18},{18,... | collective-permute-start | bytes 7864328 | tf_op jit(solution)/shard_map/ppermute | solution.py:629
  374.0 74.5 %collective-permute-start.16 = (bf16[2,160,2560]{2,1,0:T(8,128)(2,1)}, bf16[2,160,2560]{2,1,0:T(8,128)(2,1)}, u32[]{:S(2)}, u32[]{:S(2)}) collective-permute-start(bf16[2,160,2560]{2,1,0:T(8,128)(2,1)} %get-tuple-element.217), channel_id=1, source_target_pairs={{0,16},{2,18},{4,20},{6,22},{8,24},{10,26},{12,28},{14,30},{16,0},... | collective-permute-start | bytes 4915208 | tf_op jit(solution)/shard_map/ppermute | solution.py:629
  386.3 92.8 %collective-permute-start.17 = (bf16[1,1024,1280]{2,1,0:T(8,128)(2,1)}, bf16[1,1024,1280]{2,1,0:T(8,128)(2,1)S(1)}, u32[]{:S(2)}, u32[]{:S(2)}) collective-permute-start(bf16[1,1024,1280]{2,1,0:T(8,128)(2,1)} %fusion.20), channel_id=1, source_target_pairs={{0,1},{1,0},{2,3},{3,2},{4,5},{5,4},{6,7},{7,6},{8,9},{9,8},{10,11... | collective-permute-start | bytes 7864328 | tf_op jit(solution)/shard_map/ppermute | solution.py:638
  451.0 27.9 %collective-permute-start.18 = (bf16[160,2560]{1,0:T(8,128)(2,1)S(1)}, bf16[160,2560]{1,0:T(8,128)(2,1)S(1)}, u32[]{:S(2)}, u32[]{:S(2)}) collective-permute-start(bf16[160,2560]{1,0:T(8,128)(2,1)S(1)} %get-tuple-element.215), channel_id=1, source_target_pairs={{0,8},{2,10},{4,12},{6,14},{8,0},{10,2},{12,4},{14,6},{16,24},{18,... | collective-permute-start | bytes 2457608 | tf_op jit(solution)/shard_map/ppermute | solution.py:629
  456.7 58.2 %collective-permute-start.20 = (bf16[4,400,640]{2,1,0:T(8,128)(2,1)}, bf16[4,400,640]{2,1,0:T(8,128)(2,1)S(1)}, u32[]{:S(2)}, u32[]{:S(2)}) collective-permute-start(bf16[4,400,640]{2,1,0:T(8,128)(2,1)} %get-tuple-element.213), channel_id=1, source_target_pairs={{0,4},{2,6},{4,0},{6,2},{8,12},{10,14},{12,8},{14,10},{16,20},{18,... | collective-permute-start | bytes 6144008 | tf_op jit(solution)/shard_map/ppermute | solution.py:629
  479.1 38.1 %collective-permute-start.19 = (bf16[2,4,80,1152]{3,2,1,0:T(8,128)(2,1)}, bf16[2,4,80,1152]{3,2,1,0:T(8,128)(2,1)}, u32[]{:S(2)}, u32[]{:S(2)}) collective-permute-start(bf16[2,4,80,1152]{3,2,1,0:T(8,128)(2,1)} %get-tuple-element.153), channel_id=1, source_target_pairs={{1,0},{0,1},{3,2},{2,3},{5,4},{4,5},{7,6},{6,7},{9,8},{8,9},{11,10... | collective-permute-start | bytes 4423688 | tf_op jit(solution)/shard_map/ppermute | solution.py:635
  483.7 50.0 %collective-permute-start.22 = (bf16[160,2560]{1,0:T(8,128)(2,1)S(1)}, bf16[160,2560]{1,0:T(8,128)(2,1)}, u32[]{:S(2)}, u32[]{:S(2)}) collective-permute-start(bf16[160,2560]{1,0:T(8,128)(2,1)S(1)} %add_convert_fusion.9), channel_id=1, source_target_pairs={{1,0},{0,1},{3,2},{2,3},{5,4},{4,5},{7,6},{6,7},{9,8},{8,9},{11,10... | collective-permute-start | bytes 2457608 | tf_op jit(solution)/shard_map/ppermute | solution.py:635
  519.7 52.5 %collective-permute-start.21 = (bf16[4,80,1152]{2,1,0:T(8,128)(2,1)}, bf16[4,80,1152]{2,1,0:T(8,128)(2,1)S(1)}, u32[]{:S(2)}, u32[]{:S(2)}) collective-permute-start(bf16[4,80,1152]{2,1,0:T(8,128)(2,1)} %get-tuple-element.222), channel_id=1, source_target_pairs={{0,4},{2,6},{4,0},{6,2},{8,12},{10,14},{12,8},{14,10},{16,20},{18,... | collective-permute-start | bytes 2211848 | tf_op jit(solution)/shard_map/ppermute | solution.py:629
  524.8 48.6 %collective-permute-start.23 = (bf16[2,400,640]{2,1,0:T(8,128)(2,1)}, bf16[2,400,640]{2,1,0:T(8,128)(2,1)S(1)}, u32[]{:S(2)}, u32[]{:S(2)}) collective-permute-start(bf16[2,400,640]{2,1,0:T(8,128)(2,1)} %get-tuple-element.220), channel_id=1, source_target_pairs={{0,16},{2,18},{4,20},{6,22},{8,24},{10,26},{12,28},{14,30},{16,0},... | collective-permute-start | bytes 3072008 | tf_op jit(solution)/shard_map/ppermute | solution.py:629
  548.4 27.1 %collective-permute-start.24 = (bf16[2,4,80,768]{3,2,1,0:T(8,128)(2,1)}, bf16[2,4,80,768]{3,2,1,0:T(8,128)(2,1)}, u32[]{:S(2)}, u32[]{:S(2)}) collective-permute-start(bf16[2,4,80,768]{3,2,1,0:T(8,128)(2,1)} %get-tuple-element.161), channel_id=1, source_target_pairs={{1,0},{0,1},{3,2},{2,3},{5,4},{4,5},{7,6},{6,7},{9,8},{8,9},{11,10... | collective-permute-start | bytes 2949128 | tf_op jit(solution)/shard_map/ppermute | solution.py:635
  572.2 40.2 %collective-permute-start.25 = (bf16[1024,1280]{1,0:T(8,128)(2,1)}, bf16[1024,1280]{1,0:T(8,128)(2,1)}, u32[]{:S(2)}, u32[]{:S(2)}) collective-permute-start(bf16[1024,1280]{1,0:T(8,128)(2,1)} %near_norm_theirs.1), channel_id=1, source_target_pairs={{0,2},{2,0},{4,6},{6,4},{8,10},{10,8},{12,14},{14,12},{16,18},{18,... | collective-permute-start | bytes 7864328 | tf_op jit(solution)/shard_map/ppermute | solution.py:629
  577.7 28.1 %collective-permute-start.26 = (bf16[4,80,768]{2,1,0:T(8,128)(2,1)}, bf16[4,80,768]{2,1,0:T(8,128)(2,1)}, u32[]{:S(2)}, u32[]{:S(2)}) collective-permute-start(bf16[4,80,768]{2,1,0:T(8,128)(2,1)} %get-tuple-element.228), channel_id=1, source_target_pairs={{0,4},{2,6},{4,0},{6,2},{8,12},{10,14},{12,8},{14,10},{16,20},{18,... | collective-permute-start | bytes 1474568 | tf_op jit(solution)/shard_map/ppermute | solution.py:629
  579.7 27.6 %collective-permute-start.27 = (bf16[2,80,1152]{2,1,0:T(8,128)(2,1)}, bf16[2,80,1152]{2,1,0:T(8,128)(2,1)}, u32[]{:S(2)}, u32[]{:S(2)}) collective-permute-start(bf16[2,80,1152]{2,1,0:T(8,128)(2,1)} %get-tuple-element.233), channel_id=1, source_target_pairs={{0,16},{2,18},{4,20},{6,22},{8,24},{10,26},{12,28},{14,30},{16,0},... | collective-permute-start | bytes 1105928 | tf_op jit(solution)/shard_map/ppermute | solution.py:629
  584.5 26.0 %collective-permute-start.28 = (bf16[400,640]{1,0:T(8,128)(2,1)}, bf16[400,640]{1,0:T(8,128)(2,1)S(1)}, u32[]{:S(2)}, u32[]{:S(2)}) collective-permute-start(bf16[400,640]{1,0:T(8,128)(2,1)} %get-tuple-element.218), channel_id=1, source_target_pairs={{0,8},{2,10},{4,12},{6,14},{8,0},{10,2},{12,4},{14,6},{16,24},{18,... | collective-permute-start | bytes 1536008 | tf_op jit(solution)/shard_map/ppermute | solution.py:629
  607.1 13.1 %collective-permute-start.29 = (bf16[2,80,768]{2,1,0:T(8,128)(2,1)S(1)}, bf16[2,80,768]{2,1,0:T(8,128)(2,1)S(1)}, u32[]{:S(2)}, u32[]{:S(2)}) collective-permute-start(bf16[2,80,768]{2,1,0:T(8,128)(2,1)S(1)} %get-tuple-element.238), channel_id=1, source_target_pairs={{0,16},{2,18},{4,20},{6,22},{8,24},{10,26},{12,28},{14,30},{16,0},... | collective-permute-start | bytes 737288 | tf_op jit(solution)/shard_map/ppermute | solution.py:629
  610.6 26.6 %collective-permute-start.37 = (bf16[400,640]{1,0:T(8,128)(2,1)S(1)}, bf16[400,640]{1,0:T(8,128)(2,1)}, u32[]{:S(2)}, u32[]{:S(2)}) collective-permute-start(bf16[400,640]{1,0:T(8,128)(2,1)S(1)} %add_convert_fusion.12), channel_id=1, source_target_pairs={{1,0},{0,1},{3,2},{2,3},{5,4},{4,5},{7,6},{6,7},{9,8},{8,9},{11,10... | collective-permute-start | bytes 1536008 | tf_op jit(solution)/shard_map/ppermute | solution.py:635
  616.0 27.5 %collective-permute-start.40 = (bf16[80,1152]{1,0:T(8,128)(2,1)S(1)}, bf16[80,1152]{1,0:T(8,128)(2,1)S(1)}, u32[]{:S(2)}, u32[]{:S(2)}) collective-permute-start(bf16[80,1152]{1,0:T(8,128)(2,1)S(1)} %add_convert_fusion.15), channel_id=1, source_target_pairs={{1,0},{0,1},{3,2},{2,3},{5,4},{4,5},{7,6},{6,7},{9,8},{8,9},{11,10... | collective-permute-start | bytes 552968 | tf_op jit(solution)/shard_map/ppermute | solution.py:635
  620.3 22.8 %collective-permute-start.42 = (bf16[80,768]{1,0:T(8,128)(2,1)S(1)}, bf16[80,768]{1,0:T(8,128)(2,1)S(1)}, u32[]{:S(2)}, u32[]{:S(2)}) collective-permute-start(bf16[80,768]{1,0:T(8,128)(2,1)S(1)} %get-tuple-element.236), channel_id=1, source_target_pairs={{0,8},{2,10},{4,12},{6,14},{8,0},{10,2},{12,4},{14,6},{16,24},{18,... | collective-permute-start | bytes 368648 | tf_op jit(solution)/shard_map/ppermute | solution.py:629
  631.2 9.2 %collective-permute-start.31 = (f32[1,4,960]{2,1,0:T(4,128)S(1)}, f32[1,4,960]{2,1,0:T(4,128)S(1)}, u32[]{:S(2)}, u32[]{:S(2)}) collective-permute-start(f32[1,4,960]{2,1,0:T(4,128)S(1)} %get-tuple-element.245), channel_id=1, source_target_pairs={{0,8},{2,10},{4,12},{6,14},{8,0},{10,2},{12,4},{14,6},{16,24},{18,... | collective-permute-start | bytes 46088 | tf_op jit(solution)/shard_map/ppermute | solution.py:629
  640.5 12.3 %collective-permute-start.38 = (bf16[400,640]{1,0:T(8,128)(2,1)}, bf16[400,640]{1,0:T(8,128)(2,1)}, u32[]{:S(2)}, u32[]{:S(2)}) collective-permute-start(bf16[400,640]{1,0:T(8,128)(2,1)} %broadcast_select_fusion), channel_id=1, source_target_pairs={{0,2},{2,0},{4,6},{6,4},{8,10},{10,8},{12,14},{14,12},{16,18},{18,... | collective-permute-start | bytes 1536008 | tf_op jit(solution)/shard_map/ppermute | solution.py:629
  640.5 9.3 %collective-permute-start.35 = (bf16[80,2560]{1,0:T(8,128)(2,1)}, bf16[80,2560]{1,0:T(8,128)(2,1)}, u32[]{:S(2)}, u32[]{:S(2)}) collective-permute-start(bf16[80,2560]{1,0:T(8,128)(2,1)} %dynamic-slice_bitcast_fusion), channel_id=1, source_target_pairs={{0,2},{2,0},{4,6},{6,4},{8,10},{10,8},{12,14},{14,12},{16,18},{18,... | collective-permute-start | bytes 1228808 | tf_op jit(solution)/shard_map/ppermute | solution.py:629
  642.8 9.7 %collective-permute-start.34 = (f32[1,2,960]{2,1,0:T(2,128)S(1)}, f32[1,2,960]{2,1,0:T(2,128)S(1)}, u32[]{:S(2)}, u32[]{:S(2)}) collective-permute-start(f32[1,2,960]{2,1,0:T(2,128)S(1)} %dynamic-slice_bitcast_fusion.4), channel_id=1, source_target_pairs={{0,4},{2,6},{4,0},{6,2},{8,12},{10,14},{12,8},{14,10},{16,20},{18,... | collective-permute-start | bytes 23048 | tf_op jit(solution)/shard_map/ppermute | solution.py:629
  (82 other events, 888.3 us)

commit v5 on v4

--- a/solution.py
+++ b/solution.py
@@ -21,7 +21,7 @@
 NT = (((1,), (1,)), ((), ()))
 TN = (((0,), (0,)), ((), ()))
 VMEM_LIMIT = 56 * 2**20
-SHARE = 1000
+SHARE = 10
 VR = HD + 16
 
 
@@ -264,29 +264,92 @@
     )(flags,cq,ck,q,kv,kv,*do,o,lse,*extra)
 
 
-def ffn_kernel(where, acts, w, b, d_act, *rest):
-    act_o, d_pre_o, sum_o = rest[-3:]
-    rows = acts.shape[0]
+def ffn_kernel(where, acts, w, b, d_act, *rest, last):
+    step = pl.program_id(0)
+    final = pl.num_programs(0) - 1
+    rows, width = acts.shape
     chunk = min(256, rows)
     count = rows // chunk
+    if last:
+        ins, outs, scratch = rest[:7], rest[7:15], rest[15:]
+        _, _, acc_i, middle_i, d_out_i, w_out_i, gain = ins
+        act_o, d_pre_o, sum_o, mid_o, d_z_o, theirs_o, mine_o, sums_o = outs
+        acc, part, middle, d_out, w_out, d_z, att, in_sem, out_sem = scratch
+        loads = [
+            pltpu.make_async_copy(source, target, in_sem.at[n])
+            for n, (source, target) in enumerate(
+                ((acc_i, part), (middle_i, middle), (d_out_i, d_out), (w_out_i, w_out))
+            )
+        ]
+
+        @pl.when(step == 0)
+        def _():
+            for load in loads:
+                load.start()
+    else:
+        act_o, d_pre_o, sum_o, acc = rest
+
+    @pl.when(step == 0)
+    def _():
+        acc[...] = jnp.zeros_like(acc)
+
+    def span(i):
+        return slice(i * chunk, (i + 1) * chunk)
 
     def product(i):
-        return dot(acts[i * chunk : (i + 1) * chunk, :], w[...], NN) + b[...]
+        return dot(acts[span(i), :], w[...], NN) + b[...]
 
     pre = product(0)
-    total = None
-    for i in range(count):
+    total, held = None, None
+    for i in range(count + 1):
         following = product(i + 1) if i + 1 < count else None
-        at = slice(i * chunk, (i + 1) * chunk)
-        cdf = 0.5 + 0.5 * lax.erf(pre * math.sqrt(0.5))
-        pdf = jnp.exp(-0.5 * pre * pre) * (1.0 / math.sqrt(2.0 * math.pi))
-        act_o[at, :] = (pre * cdf).astype(BF)
-        d_pre = (d_act[at, :].astype(F32) * (cdf + pre * pdf)).astype(BF)
-        d_pre_o[at, :] = d_pre
-        part = jnp.sum(d_pre.astype(F32), axis=0, keepdims=True)
-        total = part if total is None else total + part
+        if held is not None:
+            acc[span(i - 1), :] += dot(held, w[...], NT)
+        if i < count:
+            at = span(i)
+            cdf = 0.5 + 0.5 * lax.erf(pre * math.sqrt(0.5))
+            pdf = jnp.exp(-0.5 * pre * pre) * (1.0 / math.sqrt(2.0 * math.pi))
+            act_o[at, :] = (pre * cdf).astype(BF)
+            held = (d_act[at, :].astype(F32) * (cdf + pre * pdf)).astype(BF)
+            d_pre_o[at, :] = held
+            summed = jnp.sum(held.astype(F32), axis=0, keepdims=True)
+            total = summed if total is None else total + summed
         pre = following
     sum_o[...] = total
+    if not last:
+        return
+
+    @pl.when(step == final)
+    def _():
+        for load in loads:
+            load.wait()
+        half = width // 2
+        sums, stores = None, []
+        for i in range(count):
+            at = span(i)
+            d_norm = acc[at, :] + part[at, :]
+            xhat, rstd = layer_norm_parts(middle[at, :])
+            d_mid = d_out[at, :].astype(F32) + layer_norm_back(d_norm, gain[...], xhat, rstd)
+            low = d_mid.astype(BF)
+            part[at, :] = d_mid
+            d_z[at, :] = low
+            for side in range(2):
+                first = pl.multiple_of(lax.bitwise_xor(where[1], 1 - side) * half, half)
+                att[side, at, :] = dot(low, w_out[pl.ds(first, half), :], NT).astype(BF)
+            new = [low.astype(F32), d_norm * xhat, d_norm]
+            new = jnp.concatenate([jnp.sum(n, axis=0, keepdims=True) for n in new], axis=0)
+            sums = new if sums is None else sums + new
+            pairs = ((part, mid_o), (d_z, d_z_o), (att.at[0], theirs_o), (att.at[1], mine_o))
+            for n, (source, target) in enumerate(pairs):
+                store = pltpu.make_async_copy(
+                    source.at[pl.ds(i * chunk, chunk)], target.at[pl.ds(i * chunk, chunk)], out_sem.at[4 * i + n]
+                )
+                store.start()
+                stores.append(store)
+        sums_o[0:3, :] = sums
+        sums_o[3:8, :] = jnp.zeros((5, width), F32)
+        for store in stores:
+            store.wait()
 
 
 def ffn_call(where, acts, w, b, d_act, earlier, name):
@@ -294,39 +357,66 @@
     ff = w.shape[1]
     tile = 512
     steps = ff // 2 // tile
-    mine = bool(earlier)
+    last = bool(earlier)
+    chunk = min(256, rows)
 
     def place(i, where):
-        return (where[1] if mine else 1 - where[1]) * steps + i
+        return (where[1] if last else 1 - where[1]) * steps + i
 
     col = lambda i, where: (0, place(i, where))
+    whole = pl.BlockSpec((rows, width), lambda i, where: (0, 0))
+    anywhere = pl.BlockSpec(memory_space=pl.ANY)
+    out_shape = [
+        jax.ShapeDtypeStruct((rows, ff), BF),
+        jax.ShapeDtypeStruct((rows, ff // 2), BF),
+        jax.ShapeDtypeStruct((1, ff), F32),
+    ]
+    out_specs = [
+        pl.BlockSpec((rows, tile), col),
+        pl.BlockSpec((rows, tile), lambda i, where: (0, i)),
+        pl.BlockSpec((1, tile), col),
+    ]
+    ins = [
+        pl.BlockSpec((rows, width), lambda i, where: (0, 0), pipeline_mode=pl.Buffered(1)),
+        pl.BlockSpec((width, tile), col),
+        pl.BlockSpec((1, tile), col),
+        pl.BlockSpec((rows, tile), col),
+    ]
+    scratch = []
+    if last:
+        ins += [anywhere] * 6 + [pl.BlockSpec((1, width), lambda i, where: (0, 0))]
+        out_shape += [
+            jax.ShapeDtypeStruct((rows, width), F32),
+            jax.ShapeDtypeStruct((rows, width), BF),
+            jax.ShapeDtypeStruct((rows, width // 2), BF),
+            jax.ShapeDtypeStruct((rows, width // 2), BF),
+            jax.ShapeDtypeStruct((8, width), F32),
+        ]
+        out_specs += [anywhere] * 4 + [pl.BlockSpec((8, width), lambda i, where: (0, 0))]
+        scratch = [
+            pltpu.VMEM((rows, width), F32),
+            pltpu.VMEM((rows, width), F32),
+            pltpu.VMEM((rows, width), F32),
+            pltpu.VMEM((rows, width), BF),
+            pltpu.VMEM((width, width), BF),
+            pltpu.VMEM((rows, width), BF),
+            pltpu.VMEM((2, rows, width // 2), BF),
+            pltpu.SemaphoreType.DMA((4,)),
+            pltpu.SemaphoreType.DMA((4 * (rows // chunk),)),
+        ]
+    else:
+        out_shape.append(jax.ShapeDtypeStruct((rows, width), F32))
+        out_specs.append(whole)
     return pl.pallas_call(
-        ffn_kernel,
-        out_shape=[
-            jax.ShapeDtypeStruct((rows, ff), BF),
-            jax.ShapeDtypeStruct((rows, ff // 2), BF),
-            jax.ShapeDtypeStruct((1, ff), F32),
-        ],
+        functools.partial(ffn_kernel, last=last),
+        out_shape=out_shape,
         grid_spec=pltpu.PrefetchScalarGridSpec(
-            num_scalar_prefetch=1,
-            grid=(steps,),
-            in_specs=[
-                pl.BlockSpec((rows, width), lambda i, where: (0, 0)),
-                pl.BlockSpec((width, tile), col),
-                pl.BlockSpec((1, tile), col),
-                pl.BlockSpec((rows, tile), col),
-            ]
-            + [pl.BlockSpec(memory_space=pl.ANY)] * len(earlier),
-            out_specs=[
-                pl.BlockSpec((rows, tile), col),
-                pl.BlockSpec((rows, tile), lambda i, where: (0, i)),
-                pl.BlockSpec((1, tile), col),
-            ],
+            num_scalar_prefetch=1, grid=(steps,), in_specs=ins, out_specs=out_specs, scratch_shapes=scratch
         ),
-        input_output_aliases={5: 0, 6: 2} if mine else {},
+        input_output_aliases={5: 0, 6: 2} if last else {},
         compiler_params=pltpu.CompilerParams(vmem_limit_bytes=VMEM_LIMIT),
         cost_estimate=pl.CostEstimate(
-            flops=rows * width * ff // SHARE,
+            flops=2 * rows * width * ff // SHARE,
             bytes_accessed=(2 * rows * width + width * ff + 3 * rows * ff) // SHARE,
             transcendentals=0,
         ),
@@ -530,7 +620,7 @@
 
 
 def product(parts, b, dims, name, spans=None, terms=(), half=None):
-    tile = 256
+    tile = 256 if sum(a.shape[1] for a in parts) > 2560 else 640
     turned = dims == NT
     rows = parts[0].shape[0] // (1 if half is None else 2)
     place = half or 0
@@ -692,27 +782,20 @@
     w_out_mate = cut(w_out, (1 - core) * half, half, 0)
     middle = inputs + (dot(mine, w_out_own, NN) + dot(own_rest, w_out_mate, NN)) + bias_out
 
-    xhat2, rstd2 = layer_norm_parts(middle)
+    xhat2, _ = layer_norm_parts(middle)
     acts2 = (xhat2 * norm2_gain + norm2_bias).astype(BF)
     acts2_mate = to_mate(acts2)
     b_in = bias_in.reshape(1, ff)
-    act_part, d_pre_theirs, sum_part = ffn_call(where, acts2, w_in, b_in, d_act, (), "ffn_theirs")
+    act_part, d_pre_theirs, sum_part, norm_part = ffn_call(
+        where, after(acts2, mate_rest), w_in, b_in, d_act, (), "ffn_theirs"
+    )
     d_pre_mate = to_mate(d_pre_theirs)
-    act_part, acts2_mate, mate_rest = after((act_part, acts2_mate, mate_rest), d_pre_theirs)
-    act, d_pre_mine, d_pre_sum = ffn_call(
-        where, after(acts2, acts2_mate, mate_rest), w_in, b_in, d_act, (act_part, sum_part), "ffn_mine"
+    act, d_pre_mine, d_pre_sum, d_middle, d_z, d_att_theirs, d_att_mine, z_sums = ffn_call(
+        where, acts2, w_in, b_in, d_act,
+        (act_part, sum_part, norm_part, middle, d_out, w_out, norm2_gain.reshape(1, width)), "ffn_mine",
     )
-    d_pre_mine, d_pre_mate = after((d_pre_mine, d_pre_mate), d_pre_sum)
-    d_pre_theirs = after(d_pre_theirs, d_pre_mate)
-    act_mate = to_mate(act)
-    w_in_mine = cut(w_in, core * (ff // 2), ff // 2, 1)
-    w_in_theirs = cut(w_in, (1 - core) * (ff // 2), ff // 2, 1)
-    d_norm2 = dot(d_pre_theirs, w_in_theirs, NT) + dot(d_pre_mine, w_in_mine, NT)
+    act_mate = to_mate(after(act, d_pre_mate, acts2_mate))
     grad_out = d_out.astype(F32)
-    d_middle = grad_out + layer_norm_back(d_norm2, norm2_gain, xhat2, rstd2)
-    d_z = d_middle.astype(BF)
-    d_att_theirs = dot(d_z, w_out_mate, NT).astype(BF)
-    d_att_mine = dot(d_z, w_out_own, NT).astype(BF)
     d_att_mate = to_mate(d_att_theirs)
     d_z_mate = to_mate(d_z)
 
@@ -775,7 +858,7 @@
         other = to_mate(given)
         return jnp.where(core == 0, kept, other).astype(F32), jnp.where(core == 0, other, kept).astype(F32)
 
-    d_pre_held = after(d_pre_mine, d_att_theirs, d_att_mine)
+    d_pre_held = d_pre_mine
     grad_in = grad_call(
         where, [[(acts2, d_pre_held, 0), (acts2_mate, d_pre_mate, 0)]], ff // 2, first, second, 512, False, "grad_in"
     )
@@ -849,8 +932,7 @@
     b_two = add_first(b_sums, after(b_in, near_late))
     b_more = send_second(b_two)
     e_sums, e_in = middle_step(grad_e, after(e_in, b_two))
-    in_row = after(in_row, e_sums)
-    near_late = after(near_late, b_two, e_sums, in_row)
+    near_late = after(near_late, b_two, e_sums)
     *grad_l, sum_l = qkv_call(where, (acts_pair, near_late), (far_pair, far_late), first, second, halves, "grad_late")
     l_in = start(grad_l)
     near_held = after(near_early, grad_l)
@@ -862,7 +944,8 @@
     b_last = send_third(b_three)
     l_sums, l_in = middle_step(grad_l, after(l_in, b_three))
     near_given = to_mate(after(near_theirs, near_mine))
-    act_late = after(act_held, e_two, b_three, l_sums)
+    in_row = after(in_row, near_mine)
+    act_late = after(act_held, e_two, b_three, l_sums, in_row)
     mixed = product([act_late], w_back, NN, "mixed", terms=(middle, bias_back.reshape(1, width))).reshape(tokens.shape)
     l_two = add_first(l_sums, after(l_in, mixed))
     l_more = send_second(l_two)
@@ -936,9 +1019,9 @@
             *norm1_sums,
             widened(0),
             widened(2),
-            jnp.sum(d_z.astype(F32), axis=0),
-            jnp.sum(d_norm2 * xhat2, axis=0),
-            jnp.sum(d_norm2, axis=0),
+            z_sums[0],
+            z_sums[1],
+            z_sums[2],
             d_pre_sum,
             jnp.sum(grad_out, axis=0),
         ],

time: 658 us -> 607 us (0.922); the launches traced: 661 us -> 602 us
  matrix products: 88.9 us -> 50.7 us
  waiting for transfers between devices: 51.4 us -> 33.5 us
  starting transfers between devices: 53 us -> 41.6 us
  Pallas kernels: 361 us -> 371 us
  other arithmetic: 81 us -> 73.5 us
    dot_general x9 -> x5, matrix products: 88.9 us -> 50.7 us  [dot(): return lax.dot_general(a, b, dims, preferred_element_type=F32)]
    pallas_call x2, Pallas kernels: 35 us -> 53.8 us  [ffn_call(): pl.pallas_call(functools.partial(ffn_kernel, last=last), out_shape=out_sh...]
    ppermute x34, starting transfers between devices: 33.2 us -> 20.7 us  [across(): return lax.ppermute(array, 'wide', [(i, i ^ by) for i in range(wide)])]
    ppermute x34, waiting for transfers between devices: 33.4 us -> 23.4 us  [across(): return lax.ppermute(array, 'wide', [(i, i ^ by) for i in range(wide)])]
    pallas_call x3, Pallas kernels: 121 us -> 112 us  [attn_bwd(): pl.pallas_call(functools.partial(bwd_kernel, spans=spans, tq=tq, tk=tk),...]
    ppermute x10, waiting for transfers between devices: 18 us -> 10.1 us  [from_ahead(): lax.ppermute(array, 'blk', [((i + by) % group, i) for i in range(group)])]
  transfers between devices with their start and end apart: 45 -> 45, of which waited for: 11 -> 11; matrix products, arithmetic and copies ran while one was open for 24% -> 21% of each run, Pallas kernels for 48% -> 54%
where the time goes in v5:
time: 607 us; the launch traced here: 602 us
  Pallas kernels  371 us (61%)
  other arithmetic  73.5 us (12%)
  matrix products  50.7 us (8%)
  starting transfers between devices  41.6 us (7%)
  waiting for transfers between devices  33.5 us (6%)
  local copies, waits for them, and re-layouts  29 us (5%)
    pallas_call x3, Pallas kernels, attn_bwd(): pl.pallas_call(functools.partial(bwd_kernel, spans=spans, tq=tq, tk=tk),...  112 us
    pallas_call x5, Pallas kernels, product(): pl.pallas_call(functools.partial(product_kernel, dims=dims, spans=spans),...  58.8 us
    pallas_call x2, Pallas kernels, attn_fwd(): pl.pallas_call(functools.partial(fwd_kernel, first=first, tq=tq, tk=tk, h...  55.8 us
    pallas_call x2, Pallas kernels, ffn_call(): pl.pallas_call(functools.partial(ffn_kernel, last=last), out_shape=out_sh...  53.8 us
    dot_general x5, matrix products, dot(): return lax.dot_general(a, b, dims, preferred_element_type=F32)  50.7 us
    pallas_call x2, Pallas kernels, qkv_call(): pl.pallas_call(functools.partial(qkv_kernel, first=first, second=second,...  36.7 us
    pallas_call x2, Pallas kernels, grad_call(): pl.pallas_call(functools.partial(grad_kernel, groups=[len(g) for g in gro...  31.1 us
    ppermute x34, waiting for transfers between devices, across(): return lax.ppermute(array, 'wide', [(i, i ^ by) for i in range(wide)])  23.4 us
  transfers between devices with their start and end apart: 45, of which 11 were waited for; matrix products, arithmetic and copies ran while one was open for 21% of the time, Pallas kernels for 54%

profile of v5, /device:TPU:0, one launch (start us, length us, event | category | flops | bytes accessed | tf_op | source)
XLA Modules:
  0.0 601.6 jit_solution(17162617877092507458)
XLA Ops:
  9.0 4.8 constant_dynamic-slice_fusion.3
  22.5 13.2 %add_convert_fusion = bf16[2048,1920]{1,0:T(8,128)(2,1)} fusion(f32[1920]{0:T(1024)S(1)} %pad_maximum_fusion.5, bf16[2048,1280]{1,0:T(8,128)(2,1)S(1)} %bitcast.163, bf16[1280,640]{1,0:T(8,128)(2,1)S(1)} %copy-done.18, bf16[1280,640]{1,0:T(8,128)(2,1)S(1)} %copy-done.20, bf16[1280,640]{1,0:T(8,128)(2,1)S(1)} %copy-done.16), kind=kOutput, calls=%fused_computation | convolution fusion | flops 10088939520 | bytes 18030080 | tf_op jit(solution)/shard_map/dot_general | solution.py:29
  37.1 32.7 %attn_fwd_a.1 = (f32[2,640,1024]{2,1,0:T(8,128)}, f32[2,16,1024]{2,1,0:T(8,128)}, f32[2,16,1024]{2,1,0:T(8,128)}) custom-call(s32[2,2,4]{2,1,0:T(2,128)} %get-tuple-element.253.flags, s32[2,1,1024]{2,1,0:T(1,128)} %broadcast_in_dim.40.cq, s32[2,1024,128]{2,1,0:T(8,128)} %broadcast_in_dim.43.ck, bf16[2,1024,1920]{2,1,0:T(8,128)(2,1)} %bitcast.142, ...), custom_call_target="tpu_custom_call" | custom-call | flops 536870912 | bytes 1310720 | tf_op jit(solution)/shard_map/attn_fwd_a/pallas_call | solution.py:155
  69.8 4.7 collective-permute-done.3
  74.5 20.6 %convolution_convert_fusion.d_act = bf16[1024,5120]{1,0:T(8,128)(2,1)} fusion(bf16[1024,1280]{1,0:T(8,128)(2,1)S(1)} %bitcast.175, bf16[5120,1280]{1,0:T(8,128)(2,1)} %refs_1_.1), kind=kOutput, calls=%fused_computation.2 | convolution fusion | flops 13427015680 | bytes 26214400 | tf_op jit(solution)/shard_map/dot_general | solution.py:29
  97.8 9.0 %add_convert_fusion.1 = bf16[2048,1280]{1,0:T(8,128)(2,1)} fusion(bf16[2048,1280]{1,0:T(8,128)(2,1)S(1)} %bitcast.166, f32[1280]{0:T(1024)S(1)} %concatenate.70, bf16[1280,640]{1,0:T(8,128)(2,1)S(1)} %copy-done.19, bf16[1280,640]{1,0:T(8,128)(2,1)S(1)} %copy-done.21), kind=kOutput, calls=%fused_computation.1 | convolution fusion | flops 6722682880 | bytes 13767680 | tf_op jit(solution)/shard_map/dot_general | solution.py:29
  108.1 23.1 %attn_fwd_b.1 = (bf16[2,1024,640]{2,1,0:T(8,128)(2,1)}, f32[2,16,1024]{2,1,0:T(8,128)}) custom-call(s32[2,2,4]{2,1,0:T(2,128)} %get-tuple-element.254.flags, s32[2,1,1024]{2,1,0:T(1,128)} %broadcast_in_dim.40.cq, s32[2,1024,128]{2,1,0:T(8,128)} %broadcast_in_dim.41.ck, bf16[2,1024,1920]{2,1,0:T(8,128)(2,1)} %bitcast.145, bf16[2,1024,1280]{2,1,0:T(8,128)(2,1)} %bitcast.153, ...), custom_call_target="tpu_custom_call" | custom-call | flops 536870912 | bytes 1310720 | tf_op jit(solution)/shard_map/attn_fwd_b/pallas_call | solution.py:155
  135.8 3.8 fusion.20
  139.7 4.1 fusion.57
  148.1 23.7 %ffn_theirs.1 = (bf16[1024,5120]{1,0:T(8,128)(2,1)}, bf16[1024,2560]{1,0:T(8,128)(2,1)}, f32[1,5120]{1,0:T(1,128)}, f32[1024,1280]{1,0:T(8,128)}) custom-call(s32[3]{0:T(128)} %add_add_fusion.where, bf16[1024,1280]{1,0:T(8,128)(2,1)} %add_convert_fusion.3.acts.refs_0_, bf16[1280,5120]{1,0:T(8,128)(2,1)} %w.3, f32[1,5120]{1,0:T(1,128)} %bitcast.190, ...), custom_call_target="tpu_custom_call" | custom-call | flops 1342177280 | bytes 2490368 | tf_op jit(solution)/shard_map/ffn_theirs/pallas_call | solution.py:410
  173.2 30.1 %ffn_mine.1 = (bf16[1024,5120]{1,0:T(8,128)(2,1)}, bf16[1024,2560]{1,0:T(8,128)(2,1)}, f32[1,5120]{1,0:T(1,128)}, f32[1024,1280]{1,0:T(8,128)}, bf16[1024,1280]{...) custom-call(s32[3]{0:T(128)} %add_add_fusion.where, ...), custom_call_target="tpu_custom_call", output_to_operand_aliasing={{0}: (5, {}), {2}: (6, {})} | custom-call | flops 1342177280 | bytes 2490368 | tf_op jit(solution)/shard_map/ffn_mine/pallas_call | solution.py:410
  205.6 20.6 %grad_in.1 = (bf16[4,160,2560]{2,1,0:T(8,128)(2,1)}, bf16[4,160,2560]{2,1,0:T(8,128)(2,1)}) custom-call(s32[3]{0:T(128)} %add_add_fusion.where, bf16[1024,1280]{1,0:T(8,128)(2,1)} %add_convert_fusion.3.acts.refs_0_, bf16[1024,2560]{1,0:T(8,128)(2,1)} %get-tuple-element.119.refs_1_, bf16[1024,1280]{1,0:T(8,128)(2,1)} %collective-permute-done.9.refs_2_, ...), custom_call_target="tpu_custom_call" | custom-call | flops 1342177280 | bytes 2228224 | tf_op jit(solution)/shard_map/grad_in/pallas_call | solution.py:483
  228.9 4.7 pad_maximum_fusion.2.refs_2_
  234.8 22.9 %grad_back.1 = (bf16[2,4,400,640]{3,2,1,0:T(8,128)(2,1)}, bf16[2,4,400,640]{3,2,1,0:T(8,128)(2,1)}) custom-call(s32[3]{0:T(128)} %add_add_fusion.where, bf16[1024,5120]{1,0:T(8,128)(2,1)} %get-tuple-element.164.a1.refs_0_, bf16[1024,1280]{1,0:T(8,128)(2,1)} %bitcast.173, bf16[1024,5120]{1,0:T(8,128)(2,1)} %collective-permute-done.10.a2, ...), custom_call_target="tpu_custom_call" | custom-call | flops 1342177280 | bytes 3014656 | tf_op jit(solution)/shard_map/grad_back/pallas_call | solution.py:576
  257.7 10.5 %grad_out.1 = (bf16[2,4,400,640]{3,2,1,0:T(8,128)(2,1)}, bf16[2,4,400,640]{3,2,1,0:T(8,128)(2,1)}) custom-call(s32[3]{0:T(128)} %add_add_fusion.1.where, bf16[1024,640]{1,0:T(8,128)(2,1)} %get-tuple-element.220.refs_0_, bf16[1024,1280]{1,0:T(8,128)(2,1)} %get-tuple-element.118.refs_1_.refs_5_, ...), custom_call_target="tpu_custom_call", output_to_operand_aliasing={{0}: (9, {}), {1}: (10, {})} | custom-call | flops 335544320 | bytes 950272 | tf_op jit(solution)/shard_map/grad_out/pallas_call | solution.py:483
  268.2 6.7 %collective-permute-start.15 = (bf16[2,4,400,640]{3,2,1,0:T(8,128)(2,1)}, bf16[2,4,400,640]{3,2,1,0:T(8,128)(2,1)}, u32[]{:S(2)}, u32[]{:S(2)}) collective-permute-start(bf16[2,4,400,640]{3,2,1,0:T(8,128)(2,1)} %get-tuple-element.130), channel_id=1, source_target_pairs={{1,0},{0,1},{3,2},{2,3},{5,4},{4,5},{7,6},{6,7},{9,8},{8,9},{11,10... | collective-permute-start | bytes 12288008 | tf_op jit(solution)/shard_map/ppermute | solution.py:725
  276.1 39.0 %attn_bwd_far.1 = (f32[2,640,1024]{2,1,0:T(8,128)}, bf16[2,1024,768]{2,1,0:T(8,128)(2,1)}, bf16[2,1024,512]{2,1,0:T(8,128)(2,1)}) custom-call(s32[2,4,4]{2,1,0:T(4,128)} %get-tuple-element.251.flags, s32[2,1,1024]{2,1,0:T(1,128)} %broadcast_in_dim.40.cq, s32[2,1024,128]{2,1,0:T(8,128)} %broadcast_in_dim.41.ck, bf16[2,1024,1920]{2,1,0:T(8,128)(2,1)} %bitcast.146, ...), custom_call_target="tpu_custom_call" | custom-call | flops 1342177280 | bytes 2359296 | tf_op jit(solution)/shard_map/attn_bwd_far/pallas_call | solution.py:256
  315.2 5.0 fusion.54
  320.2 8.3 %far_norm_theirs.1 = bf16[1024,1280]{1,0:T(8,128)(2,1)} custom-call(bf16[2048,768]{1,0:T(8,128)(2,1)} %bitcast.169, bf16[2048,512]{1,0:T(8,128)(2,1)} %bitcast.176, bf16[1280,1920]{1,0:T(8,128)(2,1)} %pad_maximum_fusion.2.refs_2_), custom_call_target="tpu_custom_call" | custom-call | flops 335544320 | bytes 851968 | tf_op jit(solution)/shard_map/far_norm_theirs/pallas_call | solution.py:636
  328.5 8.0 %far_norm_mine.1 = bf16[1024,1280]{1,0:T(8,128)(2,1)} custom-call(bf16[2048,768]{1,0:T(8,128)(2,1)} %bitcast.170, bf16[2048,512]{1,0:T(8,128)(2,1)} %bitcast.177, bf16[1280,1920]{1,0:T(8,128)(2,1)} %pad_maximum_fusion.2.refs_2_), custom_call_target="tpu_custom_call" | custom-call | flops 335544320 | bytes 851968 | tf_op jit(solution)/shard_map/far_norm_mine/pallas_call | solution.py:636
  336.5 3.9 fusion.13
  342.2 41.9 %attn_bwd_early.1 = bf16[2,1024,1152]{2,1,0:T(8,128)(2,1)} custom-call(s32[2,4,4]{2,1,0:T(4,128)} %get-tuple-element.252.flags, s32[2,1,1024]{2,1,0:T(1,128)} %broadcast_in_dim.40.cq, s32[2,1024,128]{2,1,0:T(8,128)} %broadcast_in_dim.43.ck, bf16[2,1024,1920]{2,1,0:T(8,128)(2,1)} %bitcast.147, bf16[2,1024,1920]{2,1,0:T(8,128)(2,1)} %bitcast.148, ...), custom_call_target="tpu_custom_call" | custom-call | flops 805306368 | bytes 1415577 | tf_op jit(solution)/shard_map/attn_bwd_early/pallas_call | solution.py:256
  384.1 5.1 fusion.14
  389.2 13.8 %collective-permute-done.16 = bf16[2,160,2560]{2,1,0:T(8,128)(2,1)} collective-permute-done((bf16[2,160,2560]{2,1,0:T(8,128)(2,1)}, bf16[2,160,2560]{2,1,0:T(8,128)(2,1)}, u32[]{:S(2)}, u32[]{:S(2)}) %collective-permute-start.16) | collective-permute-done | bytes 1638432 | tf_op jit(solution)/shard_map/ppermute | solution.py:719
  405.6 22.0 %grad_early.1 = (bf16[2,4,80,1152]{3,2,1,0:T(8,128)(2,1)}, bf16[2,4,80,1152]{3,2,1,0:T(8,128)(2,1)}, f32[1,1152]{1,0:T(1,128)}) custom-call(s32[3]{0:T(128)} %add_add_fusion.where, bf16[2048,1280]{1,0:T(8,128)(2,1)} %bitcast.164, bf16[2048,1152]{1,0:T(8,128)(2,1)} %bitcast.157, bf16[2048,1280]{1,0:T(8,128)(2,1)} %bitcast.167, bf16[2048,768]{1,0:T(8,128)(2,1)} %bitcast.171), custom_call_target="tpu_custom_call" | custom-call | flops 1207959552 | bytes 2287206 | tf_op jit(solution)/shard_map/grad_early/pallas_call | solution.py:534
  430.0 31.2 %attn_bwd_late.1 = bf16[2,1024,768]{2,1,0:T(8,128)(2,1)} custom-call(s32[2,4,4]{2,1,0:T(4,128)} %get-tuple-element.252.flags, s32[2,1,1024]{2,1,0:T(1,128)} %broadcast_in_dim.40.cq, s32[2,1024,128]{2,1,0:T(8,128)} %broadcast_in_dim.43.ck, bf16[2,1024,1920]{2,1,0:T(8,128)(2,1)} %bitcast.150, bf16[2,1024,1920]{2,1,0:T(8,128)(2,1)} %bitcast.151, ...), custom_call_target="tpu_custom_call" | custom-call | flops 536870912 | bytes 943718 | tf_op jit(solution)/shard_map/attn_bwd_late/pallas_call | solution.py:256
  475.5 14.7 %grad_late.1 = (bf16[2,4,80,768]{3,2,1,0:T(8,128)(2,1)}, bf16[2,4,80,768]{3,2,1,0:T(8,128)(2,1)}, f32[1,768]{1,0:T(1,128)}) custom-call(s32[3]{0:T(128)} %add_add_fusion.where, bf16[2048,1280]{1,0:T(8,128)(2,1)} %bitcast.165, bf16[2048,768]{1,0:T(8,128)(2,1)} %bitcast.160, bf16[2048,1280]{1,0:T(8,128)(2,1)} %bitcast.168, bf16[2048,512]{1,0:T(8,128)(2,1)} %bitcast.178), custom_call_target="tpu_custom_call" | custom-call | flops 805306368 | bytes 1874329 | tf_op jit(solution)/shard_map/grad_late/pallas_call | solution.py:534
  492.2 10.7 %near_norm_theirs.1 = bf16[1024,1280]{1,0:T(8,128)(2,1)} custom-call(bf16[2048,1152]{1,0:T(8,128)(2,1)} %bitcast.158, bf16[2048,768]{1,0:T(8,128)(2,1)} %bitcast.161, bf16[1280,1920]{1,0:T(8,128)(2,1)} %pad_maximum_fusion.2.refs_2_), custom_call_target="tpu_custom_call" | custom-call | flops 503316480 | bytes 1146880 | tf_op jit(solution)/shard_map/near_norm_theirs/pallas_call | solution.py:636
  502.9 10.8 %near_norm_mine.1 = bf16[1024,1280]{1,0:T(8,128)(2,1)} custom-call(bf16[2048,1152]{1,0:T(8,128)(2,1)} %bitcast.159, bf16[2048,768]{1,0:T(8,128)(2,1)} %bitcast.162, bf16[1280,1920]{1,0:T(8,128)(2,1)} %pad_maximum_fusion.2.refs_2_), custom_call_target="tpu_custom_call" | custom-call | flops 503316480 | bytes 1146880 | tf_op jit(solution)/shard_map/near_norm_mine/pallas_call | solution.py:636
  524.5 21.0 %mixed.1 = bf16[1024,1280]{1,0:T(8,128)(2,1)} custom-call(bf16[1024,5120]{1,0:T(8,128)(2,1)} %get-tuple-element.164.a1.refs_0_, bf16[5120,1280]{1,0:T(8,128)(2,1)} %refs_1_.1, f32[1024,1280]{1,0:T(8,128)} %copy-done, f32[1,1280]{1,0:T(1,128)} %reshape.277.refs_3_), custom_call_target="tpu_custom_call" | custom-call | flops 1342177280 | bytes 2621440 | tf_op jit(solution)/shard_map/mixed/pallas_call | solution.py:636
  561.3 3.8 multiply_reduce_fusion.3
  565.1 5.3 add_bitcast_fusion
  (309 shorter events, 119.7 us)
Async XLA Ops:
  8.8 8.3 %collective-permute-start.2 = (bf16[1,1024,1280]{2,1,0:T(8,128)(2,1)S(1)}, bf16[1,1024,1280]{2,1,0:T(8,128)(2,1)}, u32[]{:S(2)}, u32[]{:S(2)}) collective-permute-start(bf16[1,1024,1280]{2,1,0:T(8,128)(2,1)S(1)} %fusion.9), channel_id=1, source_target_pairs={{0,2},{2,0},{4,6},{6,4},{8,10},{10,8},{12,14},{14,12},{16,18},{18,... | collective-permute-start | bytes 7864328 | tf_op jit(solution)/shard_map/ppermute | solution.py:719
  14.8 59.7 %collective-permute-start.3 = (bf16[1,1024,1280]{2,1,0:T(8,128)(2,1)S(1)}, bf16[1,1024,1280]{2,1,0:T(8,128)(2,1)}, u32[]{:S(2)}, u32[]{:S(2)}) collective-permute-start(bf16[1,1024,1280]{2,1,0:T(8,128)(2,1)S(1)} %fusion.9), channel_id=1, source_target_pairs={{1,0},{0,1},{3,2},{2,3},{5,4},{4,5},{7,6},{6,7},{9,8},{8,9},{11,10... | collective-permute-start | bytes 7864328 | tf_op jit(solution)/shard_map/ppermute | solution.py:725
  19.6 54.9 %collective-permute-start.5 = (bf16[1024,1280]{1,0:T(8,128)(2,1)S(1)}, bf16[1024,1280]{1,0:T(8,128)(2,1)}, u32[]{:S(2)}, u32[]{:S(2)}) collective-permute-start(bf16[1024,1280]{1,0:T(8,128)(2,1)S(1)} %bitcast.174), channel_id=1, source_target_pairs={{0,2},{2,0},{4,6},{6,4},{8,10},{10,8},{12,14},{14,12},{16,18},{18,... | collective-permute-start | bytes 7864328 | tf_op jit(solution)/shard_map/ppermute | solution.py:719
  74.5 20.6 %collective-permute-start.4 = (bf16[1,1024,1280]{2,1,0:T(8,128)(2,1)}, bf16[1,1024,1280]{2,1,0:T(8,128)(2,1)S(1)}, u32[]{:S(2)}, u32[]{:S(2)}) collective-permute-start(bf16[1,1024,1280]{2,1,0:T(8,128)(2,1)} %collective-permute-done.3), channel_id=1, source_target_pairs={{0,2},{2,0},{4,6},{6,4},{8,10},{10,8},{12,14},{14,12},{16,18},{18,... | collective-permute-start | bytes 7864328 | tf_op jit(solution)/shard_map/ppermute | solution.py:719
  135.8 11.2 %collective-permute-start.7 = (bf16[1024,640]{1,0:T(8,128)(2,1)}, bf16[1024,640]{1,0:T(8,128)(2,1)S(1)}, u32[]{:S(2)}, u32[]{:S(2)}) collective-permute-start(bf16[1024,640]{1,0:T(8,128)(2,1)} %get-tuple-element.220.refs_0_), channel_id=1, source_target_pairs={{0,2},{2,0},{4,6},{6,4},{8,10},{10,8},{12,14},{14,12},{16,18},{18,... | collective-permute-start | bytes 3932168 | tf_op jit(solution)/shard_map/ppermute | solution.py:719
  171.8 31.5 %collective-permute-start.8 = (bf16[1024,2560]{1,0:T(8,128)(2,1)}, bf16[1024,2560]{1,0:T(8,128)(2,1)S(1)}, u32[]{:S(2)}, u32[]{:S(2)}) collective-permute-start(bf16[1024,2560]{1,0:T(8,128)(2,1)} %get-tuple-element.116), channel_id=1, source_target_pairs={{0,2},{2,0},{4,6},{6,4},{8,10},{10,8},{12,14},{14,12},{16,18},{18,... | collective-permute-start | bytes 15728648 | tf_op jit(solution)/shard_map/ppermute | solution.py:719
  172.5 30.8 %collective-permute-start.9 = (bf16[1024,1280]{1,0:T(8,128)(2,1)S(1)}, bf16[1024,1280]{1,0:T(8,128)(2,1)}, u32[]{:S(2)}, u32[]{:S(2)}) collective-permute-start(bf16[1024,1280]{1,0:T(8,128)(2,1)S(1)} %copy-done.7), channel_id=1, source_target_pairs={{0,2},{2,0},{4,6},{6,4},{8,10},{10,8},{12,14},{14,12},{16,18},{18,... | collective-permute-start | bytes 7864328 | tf_op jit(solution)/shard_map/ppermute | solution.py:719
  203.3 31.5 %collective-permute-start.10 = (bf16[1024,5120]{1,0:T(8,128)(2,1)}, bf16[1024,5120]{1,0:T(8,128)(2,1)}, u32[]{:S(2)}, u32[]{:S(2)}) collective-permute-start(bf16[1024,5120]{1,0:T(8,128)(2,1)} %get-tuple-element.164.a1.refs_0_), channel_id=1, source_target_pairs={{0,2},{2,0},{4,6},{6,4},{8,10},{10,8},{12,14},{14,12},{16,18},{18,... | collective-permute-start | bytes 31457288 | tf_op jit(solution)/shard_map/ppermute | solution.py:719
  226.1 89.0 %collective-permute-start.13 = (bf16[4,160,2560]{2,1,0:T(8,128)(2,1)}, bf16[4,160,2560]{2,1,0:T(8,128)(2,1)}, u32[]{:S(2)}, u32[]{:S(2)}) collective-permute-start(bf16[4,160,2560]{2,1,0:T(8,128)(2,1)} %get-tuple-element.121), channel_id=1, source_target_pairs={{0,4},{2,6},{4,0},{6,2},{8,12},{10,14},{12,8},{14,10},{16,20},{18,... | collective-permute-start | bytes 9830408 | tf_op jit(solution)/shard_map/ppermute | solution.py:719
  228.0 46.9 %collective-permute-start.12 = (bf16[1024,640]{1,0:T(8,128)(2,1)}, bf16[1024,640]{1,0:T(8,128)(2,1)S(1)}, u32[]{:S(2)}, u32[]{:S(2)}) collective-permute-start(bf16[1024,640]{1,0:T(8,128)(2,1)} %get-tuple-element.124), channel_id=1, source_target_pairs={{0,2},{2,0},{4,6},{6,4},{8,10},{10,8},{12,14},{14,12},{16,18},{18,... | collective-permute-start | bytes 3932168 | tf_op jit(solution)/shard_map/ppermute | solution.py:719
  268.2 115.9 %collective-permute-start.15 = (bf16[2,4,400,640]{3,2,1,0:T(8,128)(2,1)}, bf16[2,4,400,640]{3,2,1,0:T(8,128)(2,1)}, u32[]{:S(2)}, u32[]{:S(2)}) collective-permute-start(bf16[2,4,400,640]{3,2,1,0:T(8,128)(2,1)} %get-tuple-element.130), channel_id=1, source_target_pairs={{1,0},{0,1},{3,2},{2,3},{5,4},{4,5},{7,6},{6,7},{9,8},{8,9},{11,10... | collective-permute-start | bytes 12288008 | tf_op jit(solution)/shard_map/ppermute | solution.py:725
  328.5 74.5 %collective-permute-start.16 = (bf16[2,160,2560]{2,1,0:T(8,128)(2,1)}, bf16[2,160,2560]{2,1,0:T(8,128)(2,1)}, u32[]{:S(2)}, u32[]{:S(2)}) collective-permute-start(bf16[2,160,2560]{2,1,0:T(8,128)(2,1)} %get-tuple-element.213), channel_id=1, source_target_pairs={{0,16},{2,18},{4,20},{6,22},{8,24},{10,26},{12,28},{14,30},{16,0},... | collective-permute-start | bytes 4915208 | tf_op jit(solution)/shard_map/ppermute | solution.py:719
  340.4 87.5 %collective-permute-start.17 = (bf16[1,1024,1280]{2,1,0:T(8,128)(2,1)}, bf16[1,1024,1280]{2,1,0:T(8,128)(2,1)S(1)}, u32[]{:S(2)}, u32[]{:S(2)}) collective-permute-start(bf16[1,1024,1280]{2,1,0:T(8,128)(2,1)} %fusion.13), channel_id=1, source_target_pairs={{0,1},{1,0},{2,3},{3,2},{4,5},{5,4},{6,7},{7,6},{8,9},{9,8},{10,11... | collective-permute-start | bytes 7864328 | tf_op jit(solution)/shard_map/ppermute | solution.py:728
  405.5 22.2 %collective-permute-start.18 = (bf16[160,2560]{1,0:T(8,128)(2,1)S(1)}, bf16[160,2560]{1,0:T(8,128)(2,1)S(1)}, u32[]{:S(2)}, u32[]{:S(2)}) collective-permute-start(bf16[160,2560]{1,0:T(8,128)(2,1)S(1)} %get-tuple-element.211), channel_id=1, source_target_pairs={{0,8},{2,10},{4,12},{6,14},{8,0},{10,2},{12,4},{14,6},{16,24},{18,... | collective-permute-start | bytes 2457608 | tf_op jit(solution)/shard_map/ppermute | solution.py:719
  405.5 55.7 %collective-permute-start.20 = (bf16[4,400,640]{2,1,0:T(8,128)(2,1)}, bf16[4,400,640]{2,1,0:T(8,128)(2,1)S(1)}, u32[]{:S(2)}, u32[]{:S(2)}) collective-permute-start(bf16[4,400,640]{2,1,0:T(8,128)(2,1)} %get-tuple-element.209), channel_id=1, source_target_pairs={{0,4},{2,6},{4,0},{6,2},{8,12},{10,14},{12,8},{14,10},{16,20},{18,... | collective-permute-start | bytes 6144008 | tf_op jit(solution)/shard_map/ppermute | solution.py:719
  427.9 35.6 %collective-permute-start.19 = (bf16[2,4,80,1152]{3,2,1,0:T(8,128)(2,1)}, bf16[2,4,80,1152]{3,2,1,0:T(8,128)(2,1)}, u32[]{:S(2)}, u32[]{:S(2)}) collective-permute-start(bf16[2,4,80,1152]{3,2,1,0:T(8,128)(2,1)} %get-tuple-element.150), channel_id=1, source_target_pairs={{1,0},{0,1},{3,2},{2,3},{5,4},{4,5},{7,6},{6,7},{9,8},{8,9},{11,10... | collective-permute-start | bytes 4423688 | tf_op jit(solution)/shard_map/ppermute | solution.py:725
  429.8 83.9 %collective-permute-start.24 = (bf16[160,2560]{1,0:T(8,128)(2,1)S(1)}, bf16[160,2560]{1,0:T(8,128)(2,1)}, u32[]{:S(2)}, u32[]{:S(2)}) collective-permute-start(bf16[160,2560]{1,0:T(8,128)(2,1)S(1)} %add_convert_fusion.9), channel_id=1, source_target_pairs={{1,0},{0,1},{3,2},{2,3},{5,4},{4,5},{7,6},{6,7},{9,8},{8,9},{11,10... | collective-permute-start | bytes 2457608 | tf_op jit(solution)/shard_map/ppermute | solution.py:725
  466.5 47.3 %collective-permute-start.21 = (bf16[4,80,1152]{2,1,0:T(8,128)(2,1)}, bf16[4,80,1152]{2,1,0:T(8,128)(2,1)}, u32[]{:S(2)}, u32[]{:S(2)}) collective-permute-start(bf16[4,80,1152]{2,1,0:T(8,128)(2,1)} %get-tuple-element.218), channel_id=1, source_target_pairs={{0,4},{2,6},{4,0},{6,2},{8,12},{10,14},{12,8},{14,10},{16,20},{18,... | collective-permute-start | bytes 2211848 | tf_op jit(solution)/shard_map/ppermute | solution.py:719
  468.5 47.4 %collective-permute-start.22 = (bf16[2,400,640]{2,1,0:T(8,128)(2,1)}, bf16[2,400,640]{2,1,0:T(8,128)(2,1)}, u32[]{:S(2)}, u32[]{:S(2)}) collective-permute-start(bf16[2,400,640]{2,1,0:T(8,128)(2,1)} %get-tuple-element.216), channel_id=1, source_target_pairs={{0,16},{2,18},{4,20},{6,22},{8,24},{10,26},{12,28},{14,30},{16,0},... | collective-permute-start | bytes 3072008 | tf_op jit(solution)/shard_map/ppermute | solution.py:719
  490.2 28.2 %collective-permute-start.23 = (bf16[2,4,80,768]{3,2,1,0:T(8,128)(2,1)}, bf16[2,4,80,768]{3,2,1,0:T(8,128)(2,1)S(1)}, u32[]{:S(2)}, u32[]{:S(2)}) collective-permute-start(bf16[2,4,80,768]{3,2,1,0:T(8,128)(2,1)} %get-tuple-element.157), channel_id=1, source_target_pairs={{1,0},{0,1},{3,2},{2,3},{5,4},{4,5},{7,6},{6,7},{9,8},{8,9},{11,10... | collective-permute-start | bytes 2949128 | tf_op jit(solution)/shard_map/ppermute | solution.py:725
  513.7 35.6 %collective-permute-start.25 = (bf16[1024,1280]{1,0:T(8,128)(2,1)}, bf16[1024,1280]{1,0:T(8,128)(2,1)}, u32[]{:S(2)}, u32[]{:S(2)}) collective-permute-start(bf16[1024,1280]{1,0:T(8,128)(2,1)} %near_norm_theirs.1), channel_id=1, source_target_pairs={{0,2},{2,0},{4,6},{6,4},{8,10},{10,8},{12,14},{14,12},{16,18},{18,... | collective-permute-start | bytes 7864328 | tf_op jit(solution)/shard_map/ppermute | solution.py:719
  519.8 25.7 %collective-permute-start.26 = (bf16[4,80,768]{2,1,0:T(8,128)(2,1)}, bf16[4,80,768]{2,1,0:T(8,128)(2,1)}, u32[]{:S(2)}, u32[]{:S(2)}) collective-permute-start(bf16[4,80,768]{2,1,0:T(8,128)(2,1)} %get-tuple-element.223), channel_id=1, source_target_pairs={{0,4},{2,6},{4,0},{6,2},{8,12},{10,14},{12,8},{14,10},{16,20},{18,... | collective-permute-start | bytes 1474568 | tf_op jit(solution)/shard_map/ppermute | solution.py:719
  521.4 25.5 %collective-permute-start.27 = (bf16[2,80,1152]{2,1,0:T(8,128)(2,1)}, bf16[2,80,1152]{2,1,0:T(8,128)(2,1)S(1)}, u32[]{:S(2)}, u32[]{:S(2)}) collective-permute-start(bf16[2,80,1152]{2,1,0:T(8,128)(2,1)} %get-tuple-element.228), channel_id=1, source_target_pairs={{0,16},{2,18},{4,20},{6,22},{8,24},{10,26},{12,28},{14,30},{16,0},... | collective-permute-start | bytes 1105928 | tf_op jit(solution)/shard_map/ppermute | solution.py:719
  522.6 26.4 %collective-permute-start.28 = (bf16[400,640]{1,0:T(8,128)(2,1)}, bf16[400,640]{1,0:T(8,128)(2,1)S(1)}, u32[]{:S(2)}, u32[]{:S(2)}) collective-permute-start(bf16[400,640]{1,0:T(8,128)(2,1)} %get-tuple-element.214), channel_id=1, source_target_pairs={{0,8},{2,10},{4,12},{6,14},{8,0},{10,2},{12,4},{14,6},{16,24},{18,... | collective-permute-start | bytes 1536008 | tf_op jit(solution)/shard_map/ppermute | solution.py:719
  546.8 13.6 %collective-permute-start.29 = (bf16[2,80,768]{2,1,0:T(8,128)(2,1)S(1)}, bf16[2,80,768]{2,1,0:T(8,128)(2,1)S(1)}, u32[]{:S(2)}, u32[]{:S(2)}) collective-permute-start(bf16[2,80,768]{2,1,0:T(8,128)(2,1)S(1)} %get-tuple-element.233), channel_id=1, source_target_pairs={{0,16},{2,18},{4,20},{6,22},{8,24},{10,26},{12,28},{14,30},{16,0},... | collective-permute-start | bytes 737288 | tf_op jit(solution)/shard_map/ppermute | solution.py:719
  547.1 9.3 %collective-permute-start.30 = (bf16[80,1152]{1,0:T(8,128)(2,1)S(1)}, bf16[80,1152]{1,0:T(8,128)(2,1)S(1)}, u32[]{:S(2)}, u32[]{:S(2)}) collective-permute-start(bf16[80,1152]{1,0:T(8,128)(2,1)S(1)} %get-tuple-element.227), channel_id=1, source_target_pairs={{0,8},{2,10},{4,12},{6,14},{8,0},{10,2},{12,4},{14,6},{16,24},{18,... | collective-permute-start | bytes 552968 | tf_op jit(solution)/shard_map/ppermute | solution.py:719
  549.1 26.7 %collective-permute-start.37 = (bf16[400,640]{1,0:T(8,128)(2,1)S(1)}, bf16[400,640]{1,0:T(8,128)(2,1)}, u32[]{:S(2)}, u32[]{:S(2)}) collective-permute-start(bf16[400,640]{1,0:T(8,128)(2,1)S(1)} %add_convert_fusion.12), channel_id=1, source_target_pairs={{1,0},{0,1},{3,2},{2,3},{5,4},{4,5},{7,6},{6,7},{9,8},{8,9},{11,10... | collective-permute-start | bytes 1536008 | tf_op jit(solution)/shard_map/ppermute | solution.py:725
  556.4 29.2 %collective-permute-start.40 = (bf16[80,1152]{1,0:T(8,128)(2,1)S(1)}, bf16[80,1152]{1,0:T(8,128)(2,1)S(1)}, u32[]{:S(2)}, u32[]{:S(2)}) collective-permute-start(bf16[80,1152]{1,0:T(8,128)(2,1)S(1)} %add_convert_fusion.15), channel_id=1, source_target_pairs={{1,0},{0,1},{3,2},{2,3},{5,4},{4,5},{7,6},{6,7},{9,8},{8,9},{11,10... | collective-permute-start | bytes 552968 | tf_op jit(solution)/shard_map/ppermute | solution.py:725
  561.2 21.9 %collective-permute-start.42 = (bf16[80,768]{1,0:T(8,128)(2,1)}, bf16[80,768]{1,0:T(8,128)(2,1)}, u32[]{:S(2)}, u32[]{:S(2)}) collective-permute-start(bf16[80,768]{1,0:T(8,128)(2,1)} %get-tuple-element.231), channel_id=1, source_target_pairs={{0,8},{2,10},{4,12},{6,14},{8,0},{10,2},{12,4},{14,6},{16,24},{18,... | collective-permute-start | bytes 368648 | tf_op jit(solution)/shard_map/ppermute | solution.py:719
  580.1 13.6 %collective-permute-start.38 = (bf16[400,640]{1,0:T(8,128)(2,1)}, bf16[400,640]{1,0:T(8,128)(2,1)}, u32[]{:S(2)}, u32[]{:S(2)}) collective-permute-start(bf16[400,640]{1,0:T(8,128)(2,1)} %broadcast_select_fusion), channel_id=1, source_target_pairs={{0,2},{2,0},{4,6},{6,4},{8,10},{10,8},{12,14},{14,12},{16,18},{18,... | collective-permute-start | bytes 1536008 | tf_op jit(solution)/shard_map/ppermute | solution.py:719
  580.1 10.7 %collective-permute-start.35 = (bf16[80,2560]{1,0:T(8,128)(2,1)}, bf16[80,2560]{1,0:T(8,128)(2,1)}, u32[]{:S(2)}, u32[]{:S(2)}) collective-permute-start(bf16[80,2560]{1,0:T(8,128)(2,1)} %dynamic-slice_bitcast_fusion), channel_id=1, source_target_pairs={{0,2},{2,0},{4,6},{6,4},{8,10},{10,8},{12,14},{14,12},{16,18},{18,... | collective-permute-start | bytes 1228808 | tf_op jit(solution)/shard_map/ppermute | solution.py:719
  581.4 12.0 %collective-permute-start.34 = (f32[1,2,960]{2,1,0:T(2,128)S(1)}, f32[1,2,960]{2,1,0:T(2,128)S(1)}, u32[]{:S(2)}, u32[]{:S(2)}) collective-permute-start(f32[1,2,960]{2,1,0:T(2,128)S(1)} %dynamic-slice_bitcast_fusion.4), channel_id=1, source_target_pairs={{0,4},{2,6},{4,0},{6,2},{8,12},{10,14},{12,8},{14,10},{16,20},{18,... | collective-permute-start | bytes 23048 | tf_op jit(solution)/shard_map/ppermute | solution.py:719
  (67 other events, 547.2 us)

commit v6 on v5

--- a/solution.py
+++ b/solution.py
@@ -21,6 +21,11 @@
 NT = (((1,), (1,)), ((), ()))
 TN = (((0,), (0,)), ((), ()))
 VMEM_LIMIT = 56 * 2**20
+
+
+def room(mebibytes, rows):
+    return mebibytes * 2**20 if rows <= 2048 else VMEM_LIMIT
+
 SHARE = 10
 VR = HD + 16
 
@@ -28,6 +33,12 @@
 def dot(a, b, dims):
     return lax.dot_general(a, b, dims, preferred_element_type=F32)
 
+
+def own_map(nr,last):
+    return lambda r,i,*_:(jnp.minimum(r,nr//2-1),jnp.where(r<nr//2,i,last-1),0)
+
+def mate_map(nr):
+    return lambda r,i,*_:(jnp.maximum(r-nr//2,0),jnp.where(r<nr//2,0,i),0)
 
 def head_sumsq(x,hp16):
     W=x.shape[1]
@@ -40,7 +51,7 @@
     if first:
         accT_o,m_o,l_o,qm,vT,bias,acc,m,l,kn=rest
     else:
-        accT_i,m_i,l_i,o_o,lse_o,qm,vT,bias,acc,m,l,kn=rest
+        accT_i,m_i,l_i,o_own,o_mate,lse_o,qm,vT,bias,acc,m,l,kn=rest
     r=pl.program_id(0); qi=pl.program_id(1)
     nk=k.shape[1]//tk
     hp16=m.shape[0]
@@ -135,7 +146,11 @@
             parts=[]
             for hh in (2*hp,2*hp+1):
                 parts.append(acc[hh*HD:(hh+1)*HD,:]/l[hh:hh+1,:])
-            o_o[0,:,hp*128:(hp+1)*128]=jnp.concatenate(parts,0).T.astype(BF)
+            low=jnp.concatenate(parts,0).T.astype(BF)
+            @pl.when(r<pl.num_programs(0)//2)
+            def _(): o_own[0,:,hp*128:(hp+1)*128]=low
+            @pl.when(r>=pl.num_programs(0)//2)
+            def _(): o_mate[0,:,hp*128:(hp+1)*128]=low
         lse_o[0]=m[...]+jnp.log2(l[...])
 
 def attn_fwd(flags,cq,ck,q,kv,kb,state,tq,tk,heads):
@@ -149,19 +164,19 @@
         osh=[jax.ShapeDtypeStruct((nr,W,S),F32)]+[jax.ShapeDtypeStruct((nr,hp16,S),F32)]*2
     else:
         ins=ins+stspec
-        outs=[pl.BlockSpec((1,tq,W),qs),pl.BlockSpec((1,hp16,tq),ts)]
-        osh=[jax.ShapeDtypeStruct((nr,S,W),BF),jax.ShapeDtypeStruct((nr,hp16,S),F32)]
+        outs=[pl.BlockSpec((1,tq,W),own_map(nr,S//tq)),pl.BlockSpec((1,tq,W),mate_map(nr)),pl.BlockSpec((1,hp16,tq),ts)]
+        osh=[jax.ShapeDtypeStruct((nr//2,S,W),BF)]*2+[jax.ShapeDtypeStruct((nr,hp16,S),F32)]
     fl=4*nr*S*Sk*W
     return pl.pallas_call(functools.partial(fwd_kernel,first=first,tq=tq,tk=tk,heads=heads),
         out_shape=osh,
         grid_spec=pltpu.PrefetchScalarGridSpec(num_scalar_prefetch=1,grid=(nr,S//tq),in_specs=ins,out_specs=outs,
           scratch_shapes=[pltpu.VMEM((heads,tq,128),BF),pltpu.VMEM((heads*VR,Sk),BF),pltpu.VMEM((tk,tq),F32),pltpu.VMEM((W,tq),F32),pltpu.VMEM((hp16,tq),F32),pltpu.VMEM((hp16,tq),F32),pltpu.VMEM((hp16,128),F32)]),
-        compiler_params=pltpu.CompilerParams(dimension_semantics=("arbitrary","arbitrary"),vmem_limit_bytes=VMEM_LIMIT),
+        compiler_params=pltpu.CompilerParams(dimension_semantics=("arbitrary","arbitrary"),vmem_limit_bytes=room(20, nr * Sk)),
         cost_estimate=pl.CostEstimate(flops=fl//SHARE,bytes_accessed=nr*(S*W*2+2*Sk*W*2+S*W*4)//SHARE,transcendentals=0),
         name="attn_fwd_a" if first else "attn_fwd_b",
     )(flags,cq,ck,q,kv,kv,*(state or ()))
 
-def bwd_kernel(flags,cq,ck,q,k,v,do_own,do_mate,o,lse,*rest,spans,tq,tk):
+def bwd_kernel(flags,cq,ck,q,k,v,do_own,do_mate,o_own,o_mate,lse,*rest,spans,tq,tk):
     first=len(spans)==2
     if first:
         dqT_o,*dkv_o,qm,dom,kT,bias,dqT,dk,dv,delta=rest
@@ -184,7 +199,7 @@
         qm[2*hp+1]=jnp.where(lane>=64,qp,0).astype(BF)
         dom[2*hp]=jnp.where(lane<64,dp_,0).astype(BF)
         dom[2*hp+1]=jnp.where(lane>=64,dp_,0).astype(BF)
-    prod=jnp.where(own,do_own[0,:,c0:c0+W],do_mate[0,:,c0:c0+W]).astype(F32)*o[0,:,c0:c0+W].astype(F32)
+    prod=jnp.where(own,do_own[0,:,c0:c0+W],do_mate[0,:,c0:c0+W]).astype(F32)*jnp.where(own,o_own[0,:,c0:c0+W],o_mate[0,:,c0:c0+W]).astype(F32)
     hi=prod.astype(BF); lo=(prod-hi.astype(F32)).astype(BF)
     n16=delta.shape[0]
     row=lax.broadcasted_iota(jnp.int32,(n16,W),0); col_=lax.broadcasted_iota(jnp.int32,(n16,W),1)
@@ -240,9 +255,7 @@
     first=dqT is None
     qs=lambda r,i,*_:(r,i,0); ts=lambda r,i,*_:(r,0,i); ks=lambda r,i,*_:(r,0,0)
     ins=[pl.BlockSpec((1,1,tq),ts),pl.BlockSpec((1,Sk,128),ks),pl.BlockSpec((1,tq,F),qs),pl.BlockSpec((1,Sk,F),lambda r,i,*_:(r,0,kb)),pl.BlockSpec((1,Sk,F),lambda r,i,*_:(r,0,kb+1)),
-         pl.BlockSpec((1,tq,F),lambda r,i,*_:(jnp.minimum(r,nr//2-1),jnp.where(r<nr//2,i,S//tq-1),0)),
-         pl.BlockSpec((1,tq,F),lambda r,i,*_:(jnp.maximum(r-nr//2,0),jnp.where(r<nr//2,0,i),0)),
-         pl.BlockSpec((1,tq,F),qs),pl.BlockSpec((1,n16,tq),ts)]
+         *[pl.BlockSpec((1,tq,F),own_map(nr,S//tq)),pl.BlockSpec((1,tq,F),mate_map(nr))]*2,pl.BlockSpec((1,n16,tq),ts)]
     if first:
         widths=[2*(b-a)*HD for a,b in spans]
         outs=[pl.BlockSpec((1,F,tq),ts)]+[pl.BlockSpec((1,Sk,n),ks) for n in widths]
@@ -258,10 +271,10 @@
         grid_spec=pltpu.PrefetchScalarGridSpec(num_scalar_prefetch=1,grid=(nr,S//tq),in_specs=ins,out_specs=outs,
           scratch_shapes=[pltpu.VMEM((heads,tq,128),BF),pltpu.VMEM((heads,tq,128),BF),pltpu.VMEM((W,Sk),BF),pltpu.VMEM((tk,tq),F32),pltpu.VMEM((W,tq),F32),
              pltpu.VMEM((Sk,W),F32),pltpu.VMEM((Sk,W),F32),pltpu.VMEM((n16,tq),F32)]),
-        compiler_params=pltpu.CompilerParams(dimension_semantics=("arbitrary","arbitrary"),vmem_limit_bytes=VMEM_LIMIT),
+        compiler_params=pltpu.CompilerParams(dimension_semantics=("arbitrary","arbitrary"),vmem_limit_bytes=room(28, nr * Sk)),
         cost_estimate=pl.CostEstimate(flops=fl//SHARE,bytes_accessed=nr*(3*S*W*2+4*Sk*W*2+S*W*4)//SHARE,transcendentals=0),
         name=name,
-    )(flags,cq,ck,q,kv,kv,*do,o,lse,*extra)
+    )(flags,cq,ck,q,kv,kv,*do,*o,lse,*extra)
 
 
 def ffn_kernel(where, acts, w, b, d_act, *rest, last):
@@ -414,7 +427,7 @@
             num_scalar_prefetch=1, grid=(steps,), in_specs=ins, out_specs=out_specs, scratch_shapes=scratch
         ),
         input_output_aliases={5: 0, 6: 2} if last else {},
-        compiler_params=pltpu.CompilerParams(vmem_limit_bytes=VMEM_LIMIT),
+        compiler_params=pltpu.CompilerParams(vmem_limit_bytes=room((52 if last else 22), rows)),
         cost_estimate=pl.CostEstimate(
             flops=2 * rows * width * ff // SHARE,
             bytes_accessed=(2 * rows * width + width * ff + 3 * rows * ff) // SHARE,
@@ -493,7 +506,7 @@
             scratch_shapes=[pltpu.VMEM((height, tile), F32)],
         ),
         input_output_aliases={1 + len(flat) + i: i for i in range(len(into))},
-        compiler_params=pltpu.CompilerParams(vmem_limit_bytes=VMEM_LIMIT),
+        compiler_params=pltpu.CompilerParams(vmem_limit_bytes=room(22, depth)),
         cost_estimate=pl.CostEstimate(
             flops=2 * depth * height * width // SHARE,
             bytes_accessed=2 * (depth * (height + width) + height * width) // SHARE,
@@ -546,7 +559,7 @@
             out_specs=[pl.BlockSpec(block, index)] * outs + [pl.BlockSpec((1, tile), lambda i, where: (0, i))],
             scratch_shapes=[pltpu.VMEM((height, tile), F32)],
         ),
-        compiler_params=pltpu.CompilerParams(vmem_limit_bytes=VMEM_LIMIT),
+        compiler_params=pltpu.CompilerParams(vmem_limit_bytes=room(27, far[0].shape[0])),
         cost_estimate=pl.CostEstimate(
             flops=2 * (near_a.shape[0] + far_a.shape[0]) * height * width // SHARE,
             bytes_accessed=2 * ((near_a.shape[0] + far_a.shape[0]) * (height + width) + height * width) // SHARE,
@@ -593,7 +606,7 @@
             * 2,
             scratch_shapes=[pltpu.VMEM((rows, width), F32)],
         ),
-        compiler_params=pltpu.CompilerParams(vmem_limit_bytes=VMEM_LIMIT),
+        compiler_params=pltpu.CompilerParams(vmem_limit_bytes=room(16, own[0].shape[0])),
         cost_estimate=pl.CostEstimate(
             flops=4 * tokens * ff * width // SHARE,
             bytes_accessed=2 * (2 * tokens * (ff + width) + ff * width) // SHARE,
@@ -601,6 +614,28 @@
         ),
         name=name,
     )(where, a1, b1, a2, b2)
+
+
+def own_kernel(where, w, out):
+    out[...] = w[...]
+
+
+def own_columns_call(where, w):
+    depth, width = w.shape
+    tile = width // 6
+    return pl.pallas_call(
+        own_kernel,
+        out_shape=jax.ShapeDtypeStruct((depth, width // 2), w.dtype),
+        grid_spec=pltpu.PrefetchScalarGridSpec(
+            num_scalar_prefetch=1,
+            grid=(2, 3),
+            in_specs=[pl.BlockSpec((depth // 2, tile), lambda j, i, where: (j, 2 * i + where[1]))],
+            out_specs=pl.BlockSpec((depth // 2, tile), lambda j, i, where: (j, i)),
+        ),
+        compiler_params=pltpu.CompilerParams(vmem_limit_bytes=12 * 2**20),
+        cost_estimate=pl.CostEstimate(flops=0, bytes_accessed=2 * depth * width // SHARE, transcendentals=0),
+        name="own_columns",
+    )(where, w)
 
 
 def product_kernel(*refs, dims, spans):
@@ -639,7 +674,7 @@
         grid=(width // tile,),
         in_specs=ins + [pl.BlockSpec((t.shape[0], tile), lambda i: (0, i)) for t in terms],
         out_specs=pl.BlockSpec((rows, tile), lambda i: (0, i)),
-        compiler_params=pltpu.CompilerParams(vmem_limit_bytes=VMEM_LIMIT),
+        compiler_params=pltpu.CompilerParams(vmem_limit_bytes=room(22, rows)),
         cost_estimate=pl.CostEstimate(
             flops=2 * rows * depth * width // SHARE,
             bytes_accessed=2 * (rows * depth + depth * width + rows * width) // SHARE,
@@ -745,7 +780,7 @@
     acts = after(acts, far_cells)
     far_own = from_all_ahead(acts)
     acts_pair = paired(acts).reshape(2 * count, width)
-    w_own = jnp.concatenate([cut(w_qkv, part * width + core * half, half, 1) for part in range(3)], axis=1)
+    w_own = own_columns_call(where, w_qkv)
     b_own = jnp.concatenate([cut(bias_q, core * half, half, 0), jnp.zeros((half,), F32), cut(bias_v, core * half, half, 0)])
 
     def own_columns(span, parts):
@@ -774,8 +809,8 @@
     far_len = far_pair.shape[1]
     far_pair = far_pair.reshape(-1, width)
     far_kv = (dot(far_pair, w_own[:, half:], NN) + b_own[half:]).astype(BF).reshape(2 * rows, far_len, 2 * half)
-    attended, stats = attn_fwd(far_flags, cell_rows, far_columns, qkv, far_kv, 0, state, tq, tk, heads)
-    mine, theirs = attended[:rows].reshape(count, half), attended[rows:].reshape(count, half)
+    *attended, stats = attn_fwd(far_flags, cell_rows, far_columns, qkv, far_kv, 0, state, tq, tk, heads)
+    mine, theirs = (part.reshape(count, half) for part in attended)
     own_rest = to_mate(theirs)
     mate_rest = to_mate(mine)
     w_out_own = cut(w_out, core * half, half, 0)
@@ -815,8 +850,7 @@
         return across(pair[1], first * second)
 
     def add_second(pair, received):
-        kept, got = pair[0].astype(F32), received.astype(F32)
-        return tuple((kept[at] + got[at]).astype(BF) for at in range(2))
+        return tuple((pair[0][at].astype(F32) + received[at].astype(F32)).astype(BF) for at in range(2))
 
     def send_third(pair):
         return across(pair[1], 2 * first)

time: 607 us -> 635 us (1.046)
  Pallas kernels: 371 us -> 319 us
  local copies, waits for them, and re-layouts: 29 us -> 75.1 us
  starting transfers between devices: 41.6 us -> 83.6 us
  waiting for transfers between devices: 33.5 us -> 26.7 us
    unnamed x119 -> x211, local copies, waits for them, and re-layouts: 7.08 us -> 64.3 us
    ppermute x34, starting transfers between devices: 20.7 us -> 63.7 us  [across(): return lax.ppermute(array, 'wide', [(i, i ^ by) for i in range(wide)])]
    pallas_call x3, Pallas kernels: 112 us -> 92.9 us  [attn_bwd(): pl.pallas_call(functools.partial(bwd_kernel, spans=spans, tq=tq, tk=tk),...]
    pallas_call x5, Pallas kernels: 58.8 us -> 40.8 us  [product(): pl.pallas_call(functools.partial(product_kernel, dims=dims, spans=spans),...]
    ppermute x34, waiting for transfers between devices: 23.4 us -> 14 us  [across(): return lax.ppermute(array, 'wide', [(i, i ^ by) for i in range(wide)])]
    pallas_call x2, Pallas kernels: 36.7 us -> 27.4 us  [qkv_call(): pl.pallas_call(functools.partial(qkv_kernel, first=first, second=second,...]
    convert_element_type x12 -> x8, other arithmetic: 16.4 us -> 20.2 us  [the longest x4 15 us: added(): return total.astype(BF)]
  transfers between devices with their start and end apart: 45 -> 45, of which waited for: 11 -> 11; matrix products, arithmetic and copies ran while one was open for 21% -> 19% of each run, Pallas kernels for 54% -> 44%
where the time goes in v6:
time: 635 us; the launch traced here: 627 us
  Pallas kernels  319 us (50%)
  starting transfers between devices  83.6 us (13%)
  local copies, waits for them, and re-layouts  75.1 us (12%)
  other arithmetic  73.8 us (12%)
  matrix products  45.5 us (7%)
  waiting for transfers between devices  26.7 us (4%)
    pallas_call x3, Pallas kernels, attn_bwd(): pl.pallas_call(functools.partial(bwd_kernel, spans=spans, tq=tq, tk=tk),...  92.9 us
    unnamed x211, local copies, waits for them, and re-layouts  64.3 us
    ppermute x34, starting transfers between devices, across(): return lax.ppermute(array, 'wide', [(i, i ^ by) for i in range(wide)])  63.7 us
    pallas_call x2, Pallas kernels, attn_fwd(): pl.pallas_call(functools.partial(fwd_kernel, first=first, tq=tq, tk=tk, h...  52.8 us
    pallas_call x2, Pallas kernels, ffn_call(): pl.pallas_call(functools.partial(ffn_kernel, last=last), out_shape=out_sh...  52.1 us
    dot_general x5, matrix products, dot(): return lax.dot_general(a, b, dims, preferred_element_type=F32)  45.5 us
    pallas_call x5, Pallas kernels, product(): pl.pallas_call(functools.partial(product_kernel, dims=dims, spans=spans),...  40.8 us
    pallas_call x2, Pallas kernels, grad_call(): pl.pallas_call(functools.partial(grad_kernel, groups=[len(g) for g in gro...  27.9 us
  transfers between devices with their start and end apart: 45, of which 11 were waited for; matrix products, arithmetic and copies ran while one was open for 19% of the time, Pallas kernels for 44%

profile of v6, /device:TPU:0, one launch (start us, length us, event | category | flops | bytes accessed | tf_op | source)
XLA Modules:
  0.0 626.5 jit_solution(5357036810928244419)
XLA Ops:
  25.9 11.5 %add_convert_fusion = bf16[2048,1920]{1,0:T(8,128)(2,1)S(1)} fusion(f32[1920]{0:T(1024)S(1)} %pad_maximum_fusion.4, bf16[2048,1280]{1,0:T(8,128)(2,1)S(1)} %bitcast.174, bf16[1280,1920]{1,0:T(8,128)(2,1)S(1)} %bitcast.157), kind=kOutput, calls=%fused_computation | convolution fusion | flops 10074193920 | bytes 18030080 | tf_op jit(solution)/shard_map/dot_general | solution.py:34
  37.8 28.9 %attn_fwd_a.1 = (f32[2,640,1024]{2,1,0:T(8,128)S(1)}, f32[2,16,1024]{2,1,0:T(8,128)S(1)}, f32[2,16,1024]{2,1,0:T(8,128)S(1)}) custom-call(s32[2,2,4]{2,1,0:T(2,128)S(1)} %get-tuple-element.246.flags, s32[2,1,1024]{2,1,0:T(1,128)S(1)} %broadcast_in_dim.40.cq, s32[2,1024,128]{2,1,0:T(8,128)S(1)} %broadcast_in_dim.43.ck, bf16[2,1024,1920]{2,1,0:T(8,128)(2,1)S(1)} %bitcast.141, ...), custom_call_target="tpu_custom_call" | custom-call | flops 536870912 | bytes 1310720 | tf_op jit(solution)/shard_map/attn_fwd_a/pallas_call | solution.py:170
  69.1 8.9 %collective-permute-done.3 = bf16[1,1024,1280]{2,1,0:T(8,128)(2,1)} collective-permute-done((bf16[1,1024,1280]{2,1,0:T(8,128)(2,1)}, bf16[1,1024,1280]{2,1,0:T(8,128)(2,1)}, u32[]{:S(2)}, u32[]{:S(2)}) %collective-permute-start.3) | collective-permute-done | bytes 2621472 | tf_op jit(solution)/shard_map/ppermute | solution.py:760
  79.7 20.1 %convolution_convert_fusion.d_act = bf16[1024,5120]{1,0:T(8,128)(2,1)} fusion(bf16[1024,1280]{1,0:T(8,128)(2,1)} %bitcast.185, bf16[5120,1280]{1,0:T(8,128)(2,1)} %refs_1_.1), kind=kOutput, calls=%fused_computation.2 | convolution fusion | flops 13427015680 | bytes 26214400 | tf_op jit(solution)/shard_map/dot_general | solution.py:34
  102.9 7.2 %add_convert_fusion.1 = bf16[2048,1280]{1,0:T(8,128)(2,1)S(1)} fusion(bf16[2048,1280]{1,0:T(8,128)(2,1)S(1)} %bitcast.177, f32[1280]{0:T(1024)S(1)} %concatenate.62, bf16[1280,1920]{1,0:T(8,128)(2,1)S(1)} %bitcast.157), kind=kOutput, calls=%fused_computation.1 | convolution fusion | flops 6716129280 | bytes 13770752 | tf_op jit(solution)/shard_map/dot_general | solution.py:34
  114.4 23.9 %attn_fwd_b.1 = (bf16[1,1024,640]{2,1,0:T(8,128)(2,1)S(1)}, bf16[1,1024,640]{2,1,0:T(8,128)(2,1)S(1)}, f32[2,16,1024]{2,1,0:T(8,128)S(1)}) custom-call(s32[2,2,4]{2,1,0:T(2,128)S(1)} %get-tuple-element.247.flags, s32[2,1,1024]{2,1,0:T(1,128)S(1)} %broadcast_in_dim.40.cq, s32[2,1024,128]{2,1,0:T(8,128)S(1)} %broadcast_in_dim.41.ck, ...), custom_call_target="tpu_custom_call" | custom-call | flops 536870912 | bytes 1310720 | tf_op jit(solution)/shard_map/attn_fwd_b/pallas_call | solution.py:170
  152.5 21.4 %ffn_theirs.1 = (bf16[1024,5120]{1,0:T(8,128)(2,1)S(1)}, bf16[1024,2560]{1,0:T(8,128)(2,1)}, f32[1,5120]{1,0:T(1,128)S(1)}, f32[1024,1280]{1,0:T(8,128)S(1)}) custom-call(s32[3]{0:T(128)S(1)} %add_add_fusion.where, bf16[1024,1280]{1,0:T(8,128)(2,1)S(1)} %add_convert_fusion.3.acts.refs_0_, bf16[1280,5120]{1,0:T(8,128)(2,1)} %w.5, f32[1,5120]{1,0:T(1,128)S(1)} %bitcast.199, ...), custom_call_target="tpu_custom_call" | custom-call | flops 1342177280 | bytes 2490368 | tf_op jit(solution)/shard_map/ffn_theirs/pallas_call | solution.py:423
  180.7 30.6 %ffn_mine.1 = (bf16[1024,5120]{1,0:T(8,128)(2,1)}, bf16[1024,2560]{1,0:T(8,128)(2,1)}, f32[1,5120]{1,0:T(1,128)S(1)}, f32[1024,1280]{1,0:T(8,128)}, bf16[1024,12...) custom-call(s32[3]{0:T(128)S(1)} %add_add_fusion.where, ...), custom_call_target="tpu_custom_call", output_to_operand_aliasing={{0}: (5, {}), {2}: (6, {})} | custom-call | flops 1342177280 | bytes 2490368 | tf_op jit(solution)/shard_map/ffn_mine/pallas_call | solution.py:423
  214.5 18.8 %grad_in.1 = (bf16[4,160,2560]{2,1,0:T(8,128)(2,1)S(1)}, bf16[4,160,2560]{2,1,0:T(8,128)(2,1)}) custom-call(s32[3]{0:T(128)S(1)} %add_add_fusion.where, bf16[1024,1280]{1,0:T(8,128)(2,1)S(1)} %copy-done.18, bf16[1024,2560]{1,0:T(8,128)(2,1)S(1)} %copy-done.47, bf16[1024,1280]{1,0:T(8,128)(2,1)S(1)} %collective-permute-done.9.refs_2_, ...), custom_call_target="tpu_custom_call" | custom-call | flops 1342177280 | bytes 2228224 | tf_op jit(solution)/shard_map/grad_in/pallas_call | solution.py:496
  236.8 4.6 collective-permute-done.11.refs_3_.refs_7_
  247.1 23.3 %grad_back.1 = (bf16[2,4,400,640]{3,2,1,0:T(8,128)(2,1)S(1)}, bf16[2,4,400,640]{3,2,1,0:T(8,128)(2,1)}) custom-call(s32[3]{0:T(128)S(1)} %add_add_fusion.where, bf16[1024,5120]{1,0:T(8,128)(2,1)S(1)} %copy-done.3, bf16[1024,1280]{1,0:T(8,128)(2,1)S(1)} %bitcast.188, bf16[1024,5120]{1,0:T(8,128)(2,1)} %collective-permute-done.10.a2, ...), custom_call_target="tpu_custom_call" | custom-call | flops 1342177280 | bytes 3014656 | tf_op jit(solution)/shard_map/grad_back/pallas_call | solution.py:589
  270.5 9.1 %grad_out.1 = (bf16[2,4,400,640]{3,2,1,0:T(8,128)(2,1)S(1)}, bf16[2,4,400,640]{3,2,1,0:T(8,128)(2,1)}) custom-call(s32[3]{0:T(128)S(1)} %add_add_fusion.1.where, bf16[1024,640]{1,0:T(8,128)(2,1)S(1)} %bitcast.190, bf16[1024,1280]{1,0:T(8,128)(2,1)} %get-tuple-element.120.refs_1_.refs_5_, ...), custom_call_target="tpu_custom_call", output_to_operand_aliasing={{0}: (9, {}), {1}: (10, {})} | custom-call | flops 335544320 | bytes 950272 | tf_op jit(solution)/shard_map/grad_out/pallas_call | solution.py:496
  281.6 33.1 %attn_bwd_far.1 = (f32[2,640,1024]{2,1,0:T(8,128)S(1)}, bf16[2,1024,768]{2,1,0:T(8,128)(2,1)S(1)}, bf16[2,1024,512]{2,1,0:T(8,128)(2,1)S(1)}) custom-call(s32[2,4,4]{2,1,0:T(4,128)S(1)} %get-tuple-element.244.flags, s32[2,1,1024]{2,1,0:T(1,128)S(1)} %broadcast_in_dim.40.cq, s32[2,1024,128]{2,1,0:T(8,128)S(1)} %copy-done.46, ...), custom_call_target="tpu_custom_call" | custom-call | flops 1342177280 | bytes 2359296 | tf_op jit(solution)/shard_map/attn_bwd_far/pallas_call | solution.py:269
  314.8 7.0 %add_convert_fusion.6 = (bf16[2,160,2560]{2,1,0:T(8,128)(2,1)}, bf16[2,160,2560]{2,1,0:T(8,128)(2,1)}) fusion(bf16[4,160,2560]{2,1,0:T(8,128)(2,1)} %collective-permute-done.13, bf16[4,160,2560]{2,1,0:T(8,128)(2,1)S(1)} %copy-done.52), kind=kLoop, calls=%fused_computation.30 | loop fusion | flops 6553600 | bytes 9830400 | tf_op jit(solution)/shard_map/convert_element_type | solution.py:845
  322.9 4.7 far_norm_theirs.1
  327.7 36.3 %collective-permute-start.16 = (bf16[2,160,2560]{2,1,0:T(8,128)(2,1)}, bf16[2,160,2560]{2,1,0:T(8,128)(2,1)}, u32[]{:S(2)}, u32[]{:S(2)}) collective-permute-start(bf16[2,160,2560]{2,1,0:T(8,128)(2,1)} %get-tuple-element.202), channel_id=1, source_target_pairs={{0,16},{2,18},{4,20},{6,22},{8,24},{10,26},{12,28},{14,30},{16,0},... | collective-permute-start | bytes 4915208 | tf_op jit(solution)/shard_map/ppermute | solution.py:754
  364.1 4.7 far_norm_mine.1
  373.0 34.2 %attn_bwd_early.1 = bf16[2,1024,1152]{2,1,0:T(8,128)(2,1)S(1)} custom-call(s32[2,4,4]{2,1,0:T(4,128)S(1)} %get-tuple-element.245.flags, s32[2,1,1024]{2,1,0:T(1,128)S(1)} %broadcast_in_dim.40.cq, s32[2,1024,128]{2,1,0:T(8,128)S(1)} %copy-done.37, bf16[2,1024,1920]{2,1,0:T(8,128)(2,1)S(1)} %bitcast.150, bf16[2,1024,1920]{2,1,0:T(8,128)(2,1)S(1)} %bitcast.151, ...), custom_call_target="tpu_custom_call" | custom-call | flops 805306368 | bytes 1415577 | tf_op jit(solution)/shard_map/attn_bwd_early/pallas_call | solution.py:269
  407.3 8.3 %fusion.12 = (bf16[4,400,640]{2,1,0:T(8,128)(2,1)}, bf16[1,4,400,640]{3,2,1,0:T(8,128)(2,1)}) fusion(bf16[2,4,400,640]{3,2,1,0:T(8,128)(2,1)} %collective-permute-done.15, bf16[2,4,400,640]{3,2,1,0:T(8,128)(2,1)} %copy-done.39), kind=kLoop, calls=%fused_computation.33 | loop fusion | flops 8192000 | bytes 12288000 | tf_op jit(solution)/shard_map/convert_element_type | solution.py:867
  420.5 17.8 %grad_early.1 = (bf16[2,4,80,1152]{3,2,1,0:T(8,128)(2,1)S(1)}, bf16[2,4,80,1152]{3,2,1,0:T(8,128)(2,1)}, f32[1,1152]{1,0:T(1,128)S(1)}) custom-call(s32[3]{0:T(128)S(1)} %add_add_fusion.where, bf16[2048,1280]{1,0:T(8,128)(2,1)S(1)} %bitcast.175, bf16[2048,1152]{1,0:T(8,128)(2,1)S(1)} %bitcast.168, bf16[2048,1280]{1,0:T(8,128)(2,1)S(1)} %bitcast.180, ...), custom_call_target="tpu_custom_call" | custom-call | flops 1207959552 | bytes 2287206 | tf_op jit(solution)/shard_map/grad_early/pallas_call | solution.py:547
  444.1 25.5 %attn_bwd_late.1 = bf16[2,1024,768]{2,1,0:T(8,128)(2,1)S(1)} custom-call(s32[2,4,4]{2,1,0:T(4,128)S(1)} %get-tuple-element.245.flags, s32[2,1,1024]{2,1,0:T(1,128)S(1)} %broadcast_in_dim.40.cq, s32[2,1024,128]{2,1,0:T(8,128)S(1)} %copy-done.38, bf16[2,1024,1920]{2,1,0:T(8,128)(2,1)S(1)} %bitcast.153, bf16[2,1024,1920]{2,1,0:T(8,128)(2,1)S(1)} %bitcast.154, ...), custom_call_target="tpu_custom_call" | custom-call | flops 536870912 | bytes 943718 | tf_op jit(solution)/shard_map/attn_bwd_late/pallas_call | solution.py:269
  469.7 4.5 fusion.13
  480.5 4.6 collective-permute-start.22
  496.5 9.6 %grad_late.1 = (bf16[2,4,80,768]{3,2,1,0:T(8,128)(2,1)S(1)}, bf16[2,4,80,768]{3,2,1,0:T(8,128)(2,1)S(1)}, f32[1,768]{1,0:T(1,128)S(1)}) custom-call(s32[3]{0:T(128)S(1)} %add_add_fusion.where, bf16[2048,1280]{1,0:T(8,128)(2,1)S(1)} %bitcast.176, bf16[2048,768]{1,0:T(8,128)(2,1)S(1)} %bitcast.171, bf16[2048,1280]{1,0:T(8,128)(2,1)S(1)} %bitcast.181, ...), custom_call_target="tpu_custom_call" | custom-call | flops 805306368 | bytes 1874329 | tf_op jit(solution)/shard_map/grad_late/pallas_call | solution.py:547
  506.1 5.1 collective-permute-start.23
  513.6 7.8 %near_norm_theirs.1 = bf16[1024,1280]{1,0:T(8,128)(2,1)} custom-call(bf16[2048,1152]{1,0:T(8,128)(2,1)S(1)} %bitcast.169, bf16[2048,768]{1,0:T(8,128)(2,1)S(1)} %bitcast.172, bf16[1280,1920]{1,0:T(8,128)(2,1)S(1)} %bitcast.161), custom_call_target="tpu_custom_call" | custom-call | flops 503316480 | bytes 1146880 | tf_op jit(solution)/shard_map/near_norm_theirs/pallas_call | solution.py:671
  521.4 6.9 %near_norm_mine.1 = bf16[1024,1280]{1,0:T(8,128)(2,1)S(1)} custom-call(bf16[2048,1152]{1,0:T(8,128)(2,1)S(1)} %bitcast.170, bf16[2048,768]{1,0:T(8,128)(2,1)S(1)} %bitcast.173, bf16[1280,1920]{1,0:T(8,128)(2,1)S(1)} %bitcast.161), custom_call_target="tpu_custom_call" | custom-call | flops 503316480 | bytes 1146880 | tf_op jit(solution)/shard_map/near_norm_mine/pallas_call | solution.py:671
  547.4 4.7 copy-done.40
  552.2 16.6 %mixed.1 = bf16[1024,1280]{1,0:T(8,128)(2,1)} custom-call(bf16[1024,5120]{1,0:T(8,128)(2,1)S(1)} %copy-done.4, bf16[5120,1280]{1,0:T(8,128)(2,1)S(1)} %copy-done.40, f32[1024,1280]{1,0:T(8,128)S(1)} %copy-done.6, f32[1,1280]{1,0:T(1,128)S(1)} %reshape.293.refs_3_), custom_call_target="tpu_custom_call" | custom-call | flops 1342177280 | bytes 2621440 | tf_op jit(solution)/shard_map/mixed/pallas_call | solution.py:671
  574.1 4.5 fusion.37
  583.8 4.6 multiply_reduce_fusion.3
  588.5 5.6 add_bitcast_fusion
  (402 shorter events, 169.2 us)
Async XLA Ops:
  9.7 10.1 %collective-permute-start.2 = (bf16[1,1024,1280]{2,1,0:T(8,128)(2,1)}, bf16[1,1024,1280]{2,1,0:T(8,128)(2,1)}, u32[]{:S(2)}, u32[]{:S(2)}) collective-permute-start(bf16[1,1024,1280]{2,1,0:T(8,128)(2,1)} %fusion.9), channel_id=1, source_target_pairs={{0,2},{2,0},{4,6},{6,4},{8,10},{10,8},{12,14},{14,12},{16,18},{18,... | collective-permute-start | bytes 7864328 | tf_op jit(solution)/shard_map/ppermute | solution.py:754
  18.4 59.6 %collective-permute-start.3 = (bf16[1,1024,1280]{2,1,0:T(8,128)(2,1)}, bf16[1,1024,1280]{2,1,0:T(8,128)(2,1)}, u32[]{:S(2)}, u32[]{:S(2)}) collective-permute-start(bf16[1,1024,1280]{2,1,0:T(8,128)(2,1)} %fusion.9), channel_id=1, source_target_pairs={{1,0},{0,1},{3,2},{2,3},{5,4},{4,5},{7,6},{6,7},{9,8},{8,9},{11,10... | collective-permute-start | bytes 7864328 | tf_op jit(solution)/shard_map/ppermute | solution.py:760
  23.2 54.9 %collective-permute-start.5 = (bf16[1024,1280]{1,0:T(8,128)(2,1)S(1)}, bf16[1024,1280]{1,0:T(8,128)(2,1)S(1)}, u32[]{:S(2)}, u32[]{:S(2)}) collective-permute-start(bf16[1024,1280]{1,0:T(8,128)(2,1)S(1)} %bitcast.187), channel_id=1, source_target_pairs={{0,2},{2,0},{4,6},{6,4},{8,10},{10,8},{12,14},{14,12},{16,18},{18,... | collective-permute-start | bytes 7864328 | tf_op jit(solution)/shard_map/ppermute | solution.py:754
  78.0 21.8 %collective-permute-start.4 = (bf16[1,1024,1280]{2,1,0:T(8,128)(2,1)}, bf16[1,1024,1280]{2,1,0:T(8,128)(2,1)}, u32[]{:S(2)}, u32[]{:S(2)}) collective-permute-start(bf16[1,1024,1280]{2,1,0:T(8,128)(2,1)} %collective-permute-done.3), channel_id=1, source_target_pairs={{0,2},{2,0},{4,6},{6,4},{8,10},{10,8},{12,14},{14,12},{16,18},{18,... | collective-permute-start | bytes 7864328 | tf_op jit(solution)/shard_map/ppermute | solution.py:754
  139.0 12.4 %collective-permute-start.7 = (bf16[1024,640]{1,0:T(8,128)(2,1)S(1)}, bf16[1024,640]{1,0:T(8,128)(2,1)S(1)}, u32[]{:S(2)}, u32[]{:S(2)}) collective-permute-start(bf16[1024,640]{1,0:T(8,128)(2,1)S(1)} %bitcast.189), channel_id=1, source_target_pairs={{0,2},{2,0},{4,6},{6,4},{8,10},{10,8},{12,14},{14,12},{16,18},{18,... | collective-permute-start | bytes 3932168 | tf_op jit(solution)/shard_map/ppermute | solution.py:754
  180.1 31.2 %collective-permute-start.8 = (bf16[1024,2560]{1,0:T(8,128)(2,1)}, bf16[1024,2560]{1,0:T(8,128)(2,1)}, u32[]{:S(2)}, u32[]{:S(2)}) collective-permute-start(bf16[1024,2560]{1,0:T(8,128)(2,1)} %get-tuple-element.118), channel_id=1, source_target_pairs={{0,2},{2,0},{4,6},{6,4},{8,10},{10,8},{12,14},{14,12},{16,18},{18,... | collective-permute-start | bytes 15728648 | tf_op jit(solution)/shard_map/ppermute | solution.py:754
  180.5 30.8 %collective-permute-start.9 = (bf16[1024,1280]{1,0:T(8,128)(2,1)S(1)}, bf16[1024,1280]{1,0:T(8,128)(2,1)S(1)}, u32[]{:S(2)}, u32[]{:S(2)}) collective-permute-start(bf16[1024,1280]{1,0:T(8,128)(2,1)S(1)} %add_convert_fusion.3.acts.refs_0_), channel_id=1, source_target_pairs={{0,2},{2,0},{4,6},{6,4},{8,10},{10,8},{12,14},{14,12},{16,18},{18,... | collective-permute-start | bytes 7864328 | tf_op jit(solution)/shard_map/ppermute | solution.py:754
  211.3 30.0 %collective-permute-start.10 = (bf16[1024,5120]{1,0:T(8,128)(2,1)}, bf16[1024,5120]{1,0:T(8,128)(2,1)}, u32[]{:S(2)}, u32[]{:S(2)}) collective-permute-start(bf16[1024,5120]{1,0:T(8,128)(2,1)} %get-tuple-element.166.a1.refs_0_), channel_id=1, source_target_pairs={{0,2},{2,0},{4,6},{6,4},{8,10},{10,8},{12,14},{14,12},{16,18},{18,... | collective-permute-start | bytes 31457288 | tf_op jit(solution)/shard_map/ppermute | solution.py:754
  235.0 79.8 %collective-permute-start.13 = (bf16[4,160,2560]{2,1,0:T(8,128)(2,1)}, bf16[4,160,2560]{2,1,0:T(8,128)(2,1)}, u32[]{:S(2)}, u32[]{:S(2)}) collective-permute-start(bf16[4,160,2560]{2,1,0:T(8,128)(2,1)} %get-tuple-element.123), channel_id=1, source_target_pairs={{0,4},{2,6},{4,0},{6,2},{8,12},{10,14},{12,8},{14,10},{16,20},{18,... | collective-permute-start | bytes 9830408 | tf_op jit(solution)/shard_map/ppermute | solution.py:754
  236.1 44.8 %collective-permute-start.12 = (bf16[1024,640]{1,0:T(8,128)(2,1)}, bf16[1024,640]{1,0:T(8,128)(2,1)}, u32[]{:S(2)}, u32[]{:S(2)}) collective-permute-start(bf16[1024,640]{1,0:T(8,128)(2,1)} %get-tuple-element.126), channel_id=1, source_target_pairs={{0,2},{2,0},{4,6},{6,4},{8,10},{10,8},{12,14},{14,12},{16,18},{18,... | collective-permute-start | bytes 3932168 | tf_op jit(solution)/shard_map/ppermute | solution.py:754
  279.6 127.7 %collective-permute-start.15 = (bf16[2,4,400,640]{3,2,1,0:T(8,128)(2,1)}, bf16[2,4,400,640]{3,2,1,0:T(8,128)(2,1)}, u32[]{:S(2)}, u32[]{:S(2)}) collective-permute-start(bf16[2,4,400,640]{3,2,1,0:T(8,128)(2,1)} %get-tuple-element.132), channel_id=1, source_target_pairs={{1,0},{0,1},{3,2},{2,3},{5,4},{4,5},{7,6},{6,7},{9,8},{8,9},{11,10... | collective-permute-start | bytes 12288008 | tf_op jit(solution)/shard_map/ppermute | solution.py:760
  327.6 41.2 %collective-permute-start.14 = (bf16[1024,1280]{1,0:T(8,128)(2,1)S(1)}, bf16[1024,1280]{1,0:T(8,128)(2,1)S(1)}, u32[]{:S(2)}, u32[]{:S(2)}) collective-permute-start(bf16[1024,1280]{1,0:T(8,128)(2,1)S(1)} %far_norm_theirs.1), channel_id=1, source_target_pairs={{0,2},{2,0},{4,6},{6,4},{8,10},{10,8},{12,14},{14,12},{16,18},{18,... | collective-permute-start | bytes 7864328 | tf_op jit(solution)/shard_map/ppermute | solution.py:754
  327.7 87.9 %collective-permute-start.16 = (bf16[2,160,2560]{2,1,0:T(8,128)(2,1)}, bf16[2,160,2560]{2,1,0:T(8,128)(2,1)}, u32[]{:S(2)}, u32[]{:S(2)}) collective-permute-start(bf16[2,160,2560]{2,1,0:T(8,128)(2,1)} %get-tuple-element.202), channel_id=1, source_target_pairs={{0,16},{2,18},{4,20},{6,22},{8,24},{10,26},{12,28},{14,30},{16,0},... | collective-permute-start | bytes 4915208 | tf_op jit(solution)/shard_map/ppermute | solution.py:754
  371.0 68.3 %collective-permute-start.17 = (bf16[1,1024,1280]{2,1,0:T(8,128)(2,1)}, bf16[1,1024,1280]{2,1,0:T(8,128)(2,1)}, u32[]{:S(2)}, u32[]{:S(2)}) collective-permute-start(bf16[1,1024,1280]{2,1,0:T(8,128)(2,1)} %fusion.11), channel_id=1, source_target_pairs={{0,1},{1,0},{2,3},{3,2},{4,5},{5,4},{6,7},{7,6},{8,9},{9,8},{10,11... | collective-permute-start | bytes 7864328 | tf_op jit(solution)/shard_map/ppermute | solution.py:763
  417.6 20.7 %collective-permute-start.18 = (bf16[160,2560]{1,0:T(8,128)(2,1)S(1)}, bf16[160,2560]{1,0:T(8,128)(2,1)S(1)}, u32[]{:S(2)}, u32[]{:S(2)}) collective-permute-start(bf16[160,2560]{1,0:T(8,128)(2,1)S(1)} %get-tuple-element.206), channel_id=1, source_target_pairs={{0,8},{2,10},{4,12},{6,14},{8,0},{10,2},{12,4},{14,6},{16,24},{18,... | collective-permute-start | bytes 2457608 | tf_op jit(solution)/shard_map/ppermute | solution.py:754
  417.6 52.0 %collective-permute-start.20 = (bf16[4,400,640]{2,1,0:T(8,128)(2,1)}, bf16[4,400,640]{2,1,0:T(8,128)(2,1)}, u32[]{:S(2)}, u32[]{:S(2)}) collective-permute-start(bf16[4,400,640]{2,1,0:T(8,128)(2,1)} %get-tuple-element.200), channel_id=1, source_target_pairs={{0,4},{2,6},{4,0},{6,2},{8,12},{10,14},{12,8},{14,10},{16,20},{18,... | collective-permute-start | bytes 6144008 | tf_op jit(solution)/shard_map/ppermute | solution.py:754
  439.4 35.5 %collective-permute-start.19 = (bf16[2,4,80,1152]{3,2,1,0:T(8,128)(2,1)}, bf16[2,4,80,1152]{3,2,1,0:T(8,128)(2,1)S(1)}, u32[]{:S(2)}, u32[]{:S(2)}) collective-permute-start(bf16[2,4,80,1152]{3,2,1,0:T(8,128)(2,1)} %get-tuple-element.152), channel_id=1, source_target_pairs={{1,0},{0,1},{3,2},{2,3},{5,4},{4,5},{7,6},{6,7},{9,8},{8,9},{11,10... | collective-permute-start | bytes 4423688 | tf_op jit(solution)/shard_map/ppermute | solution.py:760
  441.6 86.8 %collective-permute-start.24 = (bf16[160,2560]{1,0:T(8,128)(2,1)}, bf16[160,2560]{1,0:T(8,128)(2,1)}, u32[]{:S(2)}, u32[]{:S(2)}) collective-permute-start(bf16[160,2560]{1,0:T(8,128)(2,1)} %add_convert_fusion.9), channel_id=1, source_target_pairs={{1,0},{0,1},{3,2},{2,3},{5,4},{4,5},{7,6},{6,7},{9,8},{8,9},{11,10... | collective-permute-start | bytes 2457608 | tf_op jit(solution)/shard_map/ppermute | solution.py:760
  476.4 52.1 %collective-permute-start.21 = (bf16[4,80,1152]{2,1,0:T(8,128)(2,1)}, bf16[4,80,1152]{2,1,0:T(8,128)(2,1)}, u32[]{:S(2)}, u32[]{:S(2)}) collective-permute-start(bf16[4,80,1152]{2,1,0:T(8,128)(2,1)} %get-tuple-element.208), channel_id=1, source_target_pairs={{0,4},{2,6},{4,0},{6,2},{8,12},{10,14},{12,8},{14,10},{16,20},{18,... | collective-permute-start | bytes 2211848 | tf_op jit(solution)/shard_map/ppermute | solution.py:754
  480.5 50.1 %collective-permute-start.22 = (bf16[2,400,640]{2,1,0:T(8,128)(2,1)}, bf16[2,400,640]{2,1,0:T(8,128)(2,1)}, u32[]{:S(2)}, u32[]{:S(2)}) collective-permute-start(bf16[2,400,640]{2,1,0:T(8,128)(2,1)} %get-tuple-element.204), channel_id=1, source_target_pairs={{0,16},{2,18},{4,20},{6,22},{8,24},{10,26},{12,28},{14,30},{16,0},... | collective-permute-start | bytes 3072008 | tf_op jit(solution)/shard_map/ppermute | solution.py:754
  506.1 26.9 %collective-permute-start.23 = (bf16[2,4,80,768]{3,2,1,0:T(8,128)(2,1)S(1)}, bf16[2,4,80,768]{3,2,1,0:T(8,128)(2,1)S(1)}, u32[]{:S(2)}, u32[]{:S(2)}) collective-permute-start(bf16[2,4,80,768]{3,2,1,0:T(8,128)(2,1)S(1)} %get-tuple-element.159), channel_id=1, source_target_pairs={{1,0},{0,1},{3,2},{2,3},{5,4},{4,5},{7,6},{6,7},{9,8},{8,9},{11,10... | collective-permute-start | bytes 2949128 | tf_op jit(solution)/shard_map/ppermute | solution.py:760
  528.4 45.7 %collective-permute-start.25 = (bf16[1024,1280]{1,0:T(8,128)(2,1)}, bf16[1024,1280]{1,0:T(8,128)(2,1)}, u32[]{:S(2)}, u32[]{:S(2)}) collective-permute-start(bf16[1024,1280]{1,0:T(8,128)(2,1)} %near_norm_theirs.1), channel_id=1, source_target_pairs={{0,2},{2,0},{4,6},{6,4},{8,10},{10,8},{12,14},{14,12},{16,18},{18,... | collective-permute-start | bytes 7864328 | tf_op jit(solution)/shard_map/ppermute | solution.py:754
  534.1 34.8 %collective-permute-start.26 = (bf16[4,80,768]{2,1,0:T(8,128)(2,1)}, bf16[4,80,768]{2,1,0:T(8,128)(2,1)}, u32[]{:S(2)}, u32[]{:S(2)}) collective-permute-start(bf16[4,80,768]{2,1,0:T(8,128)(2,1)} %get-tuple-element.214), channel_id=1, source_target_pairs={{0,4},{2,6},{4,0},{6,2},{8,12},{10,14},{12,8},{14,10},{16,20},{18,... | collective-permute-start | bytes 1474568 | tf_op jit(solution)/shard_map/ppermute | solution.py:754
  537.6 32.6 %collective-permute-start.27 = (bf16[2,80,1152]{2,1,0:T(8,128)(2,1)}, bf16[2,80,1152]{2,1,0:T(8,128)(2,1)S(1)}, u32[]{:S(2)}, u32[]{:S(2)}) collective-permute-start(bf16[2,80,1152]{2,1,0:T(8,128)(2,1)} %get-tuple-element.217), channel_id=1, source_target_pairs={{0,16},{2,18},{4,20},{6,22},{8,24},{10,26},{12,28},{14,30},{16,0},... | collective-permute-start | bytes 1105928 | tf_op jit(solution)/shard_map/ppermute | solution.py:754
  537.6 34.4 %collective-permute-start.28 = (bf16[400,640]{1,0:T(8,128)(2,1)}, bf16[400,640]{1,0:T(8,128)(2,1)S(1)}, u32[]{:S(2)}, u32[]{:S(2)}) collective-permute-start(bf16[400,640]{1,0:T(8,128)(2,1)} %get-tuple-element.211), channel_id=1, source_target_pairs={{0,8},{2,10},{4,12},{6,14},{8,0},{10,2},{12,4},{14,6},{16,24},{18,... | collective-permute-start | bytes 1536008 | tf_op jit(solution)/shard_map/ppermute | solution.py:754
  570.1 12.9 %collective-permute-start.29 = (bf16[2,80,768]{2,1,0:T(8,128)(2,1)S(1)}, bf16[2,80,768]{2,1,0:T(8,128)(2,1)S(1)}, u32[]{:S(2)}, u32[]{:S(2)}) collective-permute-start(bf16[2,80,768]{2,1,0:T(8,128)(2,1)S(1)} %get-tuple-element.221), channel_id=1, source_target_pairs={{0,16},{2,18},{4,20},{6,22},{8,24},{10,26},{12,28},{14,30},{16,0},... | collective-permute-start | bytes 737288 | tf_op jit(solution)/shard_map/ppermute | solution.py:754
  572.1 29.1 %collective-permute-start.37 = (bf16[400,640]{1,0:T(8,128)(2,1)S(1)}, bf16[400,640]{1,0:T(8,128)(2,1)}, u32[]{:S(2)}, u32[]{:S(2)}) collective-permute-start(bf16[400,640]{1,0:T(8,128)(2,1)S(1)} %add_convert_fusion.14), channel_id=1, source_target_pairs={{1,0},{0,1},{3,2},{2,3},{5,4},{4,5},{7,6},{6,7},{9,8},{8,9},{11,10... | collective-permute-start | bytes 1536008 | tf_op jit(solution)/shard_map/ppermute | solution.py:760
  579.1 31.9 %collective-permute-start.40 = (bf16[80,1152]{1,0:T(8,128)(2,1)S(1)}, bf16[80,1152]{1,0:T(8,128)(2,1)}, u32[]{:S(2)}, u32[]{:S(2)}) collective-permute-start(bf16[80,1152]{1,0:T(8,128)(2,1)S(1)} %add_convert_fusion.19), channel_id=1, source_target_pairs={{1,0},{0,1},{3,2},{2,3},{5,4},{4,5},{7,6},{6,7},{9,8},{8,9},{11,10... | collective-permute-start | bytes 552968 | tf_op jit(solution)/shard_map/ppermute | solution.py:760
  583.8 24.7 %collective-permute-start.42 = (bf16[80,768]{1,0:T(8,128)(2,1)}, bf16[80,768]{1,0:T(8,128)(2,1)}, u32[]{:S(2)}, u32[]{:S(2)}) collective-permute-start(bf16[80,768]{1,0:T(8,128)(2,1)} %get-tuple-element.227), channel_id=1, source_target_pairs={{0,8},{2,10},{4,12},{6,14},{8,0},{10,2},{12,4},{14,6},{16,24},{18,... | collective-permute-start | bytes 368648 | tf_op jit(solution)/shard_map/ppermute | solution.py:754
  604.6 14.5 %collective-permute-start.38 = (bf16[400,640]{1,0:T(8,128)(2,1)S(1)}, bf16[400,640]{1,0:T(8,128)(2,1)S(1)}, u32[]{:S(2)}, u32[]{:S(2)}) collective-permute-start(bf16[400,640]{1,0:T(8,128)(2,1)S(1)} %broadcast_select_fusion), channel_id=1, source_target_pairs={{0,2},{2,0},{4,6},{6,4},{8,10},{10,8},{12,14},{14,12},{16,18},{18,... | collective-permute-start | bytes 1536008 | tf_op jit(solution)/shard_map/ppermute | solution.py:754
  604.9 11.2 %collective-permute-start.35 = (bf16[80,2560]{1,0:T(8,128)(2,1)}, bf16[80,2560]{1,0:T(8,128)(2,1)}, u32[]{:S(2)}, u32[]{:S(2)}) collective-permute-start(bf16[80,2560]{1,0:T(8,128)(2,1)} %dynamic-slice_bitcast_fusion), channel_id=1, source_target_pairs={{0,2},{2,0},{4,6},{6,4},{8,10},{10,8},{12,14},{14,12},{16,18},{18,... | collective-permute-start | bytes 1228808 | tf_op jit(solution)/shard_map/ppermute | solution.py:754
  606.8 11.9 %collective-permute-start.34 = (f32[1,2,960]{2,1,0:T(2,128)S(1)}, f32[1,2,960]{2,1,0:T(2,128)S(1)}, u32[]{:S(2)}, u32[]{:S(2)}) collective-permute-start(f32[1,2,960]{2,1,0:T(2,128)S(1)} %dynamic-slice_bitcast_fusion.4), channel_id=1, source_target_pairs={{0,4},{2,6},{4,0},{6,2},{8,12},{10,14},{12,8},{14,10},{16,20},{18,... | collective-permute-start | bytes 23048 | tf_op jit(solution)/shard_map/ppermute | solution.py:754
  (113 other events, 1121.2 us)

commit v7 on v6

--- a/solution.py
+++ b/solution.py
@@ -21,11 +21,6 @@
 NT = (((1,), (1,)), ((), ()))
 TN = (((0,), (0,)), ((), ()))
 VMEM_LIMIT = 56 * 2**20
-
-
-def room(mebibytes, rows):
-    return mebibytes * 2**20 if rows <= 2048 else VMEM_LIMIT
-
 SHARE = 10
 VR = HD + 16
 
@@ -171,7 +166,7 @@
         out_shape=osh,
         grid_spec=pltpu.PrefetchScalarGridSpec(num_scalar_prefetch=1,grid=(nr,S//tq),in_specs=ins,out_specs=outs,
           scratch_shapes=[pltpu.VMEM((heads,tq,128),BF),pltpu.VMEM((heads*VR,Sk),BF),pltpu.VMEM((tk,tq),F32),pltpu.VMEM((W,tq),F32),pltpu.VMEM((hp16,tq),F32),pltpu.VMEM((hp16,tq),F32),pltpu.VMEM((hp16,128),F32)]),
-        compiler_params=pltpu.CompilerParams(dimension_semantics=("arbitrary","arbitrary"),vmem_limit_bytes=room(20, nr * Sk)),
+        compiler_params=pltpu.CompilerParams(dimension_semantics=("arbitrary","arbitrary"),vmem_limit_bytes=VMEM_LIMIT),
         cost_estimate=pl.CostEstimate(flops=fl//SHARE,bytes_accessed=nr*(S*W*2+2*Sk*W*2+S*W*4)//SHARE,transcendentals=0),
         name="attn_fwd_a" if first else "attn_fwd_b",
     )(flags,cq,ck,q,kv,kv,*(state or ()))
@@ -271,7 +266,7 @@
         grid_spec=pltpu.PrefetchScalarGridSpec(num_scalar_prefetch=1,grid=(nr,S//tq),in_specs=ins,out_specs=outs,
           scratch_shapes=[pltpu.VMEM((heads,tq,128),BF),pltpu.VMEM((heads,tq,128),BF),pltpu.VMEM((W,Sk),BF),pltpu.VMEM((tk,tq),F32),pltpu.VMEM((W,tq),F32),
              pltpu.VMEM((Sk,W),F32),pltpu.VMEM((Sk,W),F32),pltpu.VMEM((n16,tq),F32)]),
-        compiler_params=pltpu.CompilerParams(dimension_semantics=("arbitrary","arbitrary"),vmem_limit_bytes=room(28, nr * Sk)),
+        compiler_params=pltpu.CompilerParams(dimension_semantics=("arbitrary","arbitrary"),vmem_limit_bytes=VMEM_LIMIT),
         cost_estimate=pl.CostEstimate(flops=fl//SHARE,bytes_accessed=nr*(3*S*W*2+4*Sk*W*2+S*W*4)//SHARE,transcendentals=0),
         name=name,
     )(flags,cq,ck,q,kv,kv,*do,*o,lse,*extra)
@@ -427,7 +422,7 @@
             num_scalar_prefetch=1, grid=(steps,), in_specs=ins, out_specs=out_specs, scratch_shapes=scratch
         ),
         input_output_aliases={5: 0, 6: 2} if last else {},
-        compiler_params=pltpu.CompilerParams(vmem_limit_bytes=room((52 if last else 22), rows)),
+        compiler_params=pltpu.CompilerParams(vmem_limit_bytes=VMEM_LIMIT),
         cost_estimate=pl.CostEstimate(
             flops=2 * rows * width * ff // SHARE,
             bytes_accessed=(2 * rows * width + width * ff + 3 * rows * ff) // SHARE,
@@ -506,7 +501,7 @@
             scratch_shapes=[pltpu.VMEM((height, tile), F32)],
         ),
         input_output_aliases={1 + len(flat) + i: i for i in range(len(into))},
-        compiler_params=pltpu.CompilerParams(vmem_limit_bytes=room(22, depth)),
+        compiler_params=pltpu.CompilerParams(vmem_limit_bytes=VMEM_LIMIT),
         cost_estimate=pl.CostEstimate(
             flops=2 * depth * height * width // SHARE,
             bytes_accessed=2 * (depth * (height + width) + height * width) // SHARE,
@@ -559,7 +554,7 @@
             out_specs=[pl.BlockSpec(block, index)] * outs + [pl.BlockSpec((1, tile), lambda i, where: (0, i))],
             scratch_shapes=[pltpu.VMEM((height, tile), F32)],
         ),
-        compiler_params=pltpu.CompilerParams(vmem_limit_bytes=room(27, far[0].shape[0])),
+        compiler_params=pltpu.CompilerParams(vmem_limit_bytes=VMEM_LIMIT),
         cost_estimate=pl.CostEstimate(
             flops=2 * (near_a.shape[0] + far_a.shape[0]) * height * width // SHARE,
             bytes_accessed=2 * ((near_a.shape[0] + far_a.shape[0]) * (height + width) + height * width) // SHARE,
@@ -606,7 +601,7 @@
             * 2,
             scratch_shapes=[pltpu.VMEM((rows, width), F32)],
         ),
-        compiler_params=pltpu.CompilerParams(vmem_limit_bytes=room(16, own[0].shape[0])),
+        compiler_params=pltpu.CompilerParams(vmem_limit_bytes=VMEM_LIMIT),
         cost_estimate=pl.CostEstimate(
             flops=4 * tokens * ff * width // SHARE,
             bytes_accessed=2 * (2 * tokens * (ff + width) + ff * width) // SHARE,
@@ -614,6 +609,87 @@
         ),
         name=name,
     )(where, a1, b1, a2, b2)
+
+
+def pack_kernel(where, in_mine, in_row, b_mine, b_row, q_mine, q_row, *outs):
+    core, member = where[1], where[2]
+    half = outs[0].shape[1]
+    rows = in_mine.shape[0] // 2
+    blocks, thirds = in_mine.shape[1] // half, q_mine.shape[1] // half
+    for side, out in enumerate(outs):
+        at = pl.ds(pl.multiple_of(lax.bitwise_xor(core, side) * rows, 16), rows)
+        whole = (in_mine[at, :].astype(F32) + in_row[at, :].astype(F32)).astype(BF)
+        for i in range(blocks):
+            out[i * rows : (i + 1) * rows, :] = whole[:, i * half : (i + 1) * half]
+        mine = lax.bitwise_xor(core, side) == member
+        first = blocks * rows
+        out[first : first + b_mine.shape[0], :] = jnp.where(mine, b_mine[...], b_row[...])
+        first += b_mine.shape[0]
+        q = jnp.where(mine, q_mine[...], q_row[...])
+        for i in range(thirds):
+            out[first + i * rows : first + (i + 1) * rows, :] = q[:, i * half : (i + 1) * half]
+
+
+def pack_call(where, in_pair, b_pair, q_pair):
+    half = b_pair[0].shape[1]
+    rows = in_pair[0].shape[0] // 2
+    height = rows * (in_pair[0].shape[1] + q_pair[0].shape[1]) // half + b_pair[0].shape[0]
+    return pl.pallas_call(
+        pack_kernel,
+        out_shape=[jax.ShapeDtypeStruct((height, half), BF)] * 2,
+        grid_spec=pltpu.PrefetchScalarGridSpec(
+            num_scalar_prefetch=1,
+            grid=(1,),
+            in_specs=[
+                pl.BlockSpec(a.shape, lambda i, where: (0, 0)) for pair in (in_pair, b_pair, q_pair) for a in pair
+            ],
+            out_specs=[pl.BlockSpec((height, half), lambda i, where: (0, 0))] * 2,
+        ),
+        compiler_params=pltpu.CompilerParams(vmem_limit_bytes=20 * 2**20),
+        cost_estimate=pl.CostEstimate(flops=0, bytes_accessed=8 * height * half // SHARE, transcendentals=0),
+        name="pack",
+    )(where, *in_pair, *b_pair, *q_pair)
+
+
+def unpack_kernel(where, kept, other, in_o, back_o, out_o, qkv_o, *, groups):
+    core = where[1]
+    half = kept.shape[1]
+    rows, share = in_o.shape[0], back_o.shape[0]
+    for side in range(2):
+        own = (core == side).astype(F32)
+        whole = jnp.where(own > 0.5, kept[...], other[...]).astype(F32)
+        at = 0
+        for i in range(in_o.shape[1] // 2 // half):
+            first = side * (in_o.shape[1] // 2) + i * half
+            in_o[:, first : first + half] = whole[at : at + rows]
+            at += rows
+        back_o[:, side * half : (side + 1) * half] = whole[at : at + share]
+        at += share
+        out_o[:, side * half : (side + 1) * half] = whole[at : at + rows]
+        at += rows
+        line = jnp.concatenate([whole[at + i * rows : at + (i + 1) * rows] for i in range(3)], axis=1)
+        start, place = 0, 0
+        for n in groups:
+            for part in range(3):
+                to = part * 2 * half + side * half + place
+                qkv_o[:, to : to + n] = line[:, start + part * n : start + (part + 1) * n]
+            start, place = start + 3 * n, place + n
+
+
+def unpack_call(where, kept, other, shapes, groups):
+    return pl.pallas_call(
+        functools.partial(unpack_kernel, groups=groups),
+        out_shape=[jax.ShapeDtypeStruct(shape, F32) for shape in shapes],
+        grid_spec=pltpu.PrefetchScalarGridSpec(
+            num_scalar_prefetch=1,
+            grid=(1,),
+            in_specs=[pl.BlockSpec(kept.shape, lambda i, where: (0, 0))] * 2,
+            out_specs=[pl.BlockSpec(shape, lambda i, where: (0, 0)) for shape in shapes],
+        ),
+        compiler_params=pltpu.CompilerParams(vmem_limit_bytes=24 * 2**20),
+        cost_estimate=pl.CostEstimate(flops=0, bytes_accessed=12 * kept.size // SHARE, transcendentals=0),
+        name="unpack",
+    )(where, kept, other)
 
 
 def own_kernel(where, w, out):
@@ -661,20 +737,26 @@
     place = half or 0
     width = b.shape[0 if turned else 1]
     depth = sum(a.shape[1] for a in parts)
+    out_spec, steps = pl.BlockSpec((rows, tile), lambda i: (0, i)), width // tile
     ins = [
         pl.BlockSpec((rows, a.shape[1]), lambda i: (place, 0), pipeline_mode=pl.Buffered(1)) for a in parts
     ]
-    if turned:
+    if spans:
+        steps = rows // 256
+        ins = [pl.BlockSpec((256, a.shape[1]), lambda i: (place * steps + i, 0)) for a in parts]
+        ins.append(pl.BlockSpec(b.shape, lambda i: (0, 0), pipeline_mode=pl.Buffered(1)))
+        out_spec = pl.BlockSpec((256, width), lambda i: (i, 0))
+    elif turned:
         ins.append(pl.BlockSpec((tile, b.shape[1]), lambda i: (i, 0)))
     else:
         ins.append(pl.BlockSpec((b.shape[0], tile), lambda i: (0, i)))
     return pl.pallas_call(
         functools.partial(product_kernel, dims=dims, spans=spans),
         out_shape=jax.ShapeDtypeStruct((rows, width), BF),
-        grid=(width // tile,),
+        grid=(steps,),
         in_specs=ins + [pl.BlockSpec((t.shape[0], tile), lambda i: (0, i)) for t in terms],
-        out_specs=pl.BlockSpec((rows, tile), lambda i: (0, i)),
-        compiler_params=pltpu.CompilerParams(vmem_limit_bytes=room(22, rows)),
+        out_specs=out_spec,
+        compiler_params=pltpu.CompilerParams(vmem_limit_bytes=VMEM_LIMIT),
         cost_estimate=pl.CostEstimate(
             flops=2 * rows * depth * width // SHARE,
             bytes_accessed=2 * (rows * depth + depth * width + rows * width) // SHARE,
@@ -875,22 +957,20 @@
             return (total.astype(F32) + other.astype(F32)).astype(BF)
         return lax.psum(total, "blk")
 
-    def by_core(total, other, sizes):
-        if halves:
-            kept = jnp.where(member == core, total, other)
-            return kept, jnp.where(member == core, other, total)
+    def by_core(total):
+        split = total.reshape(2, -1, total.shape[-1])
+        return [lax.dynamic_index_in_dim(split, i, 0, keepdims=False) for i in (core, 1 - core)]
+
+    def joined(total, other, sizes):
         total = over_row(total, other)
         parts, at = [], 0
         for size in sizes:
-            parts.append(total[at : at + size].reshape(2, size // 2, total.shape[1]))
+            parts.append(by_core(total[at : at + size]))
             at += size
-        split = jnp.concatenate(parts, axis=1)
-        return (lax.dynamic_index_in_dim(split, i, 0, keepdims=False) for i in (core, 1 - core))
-
-    def swap(split):
-        kept, given = split
-        other = to_mate(given)
-        return jnp.where(core == 0, kept, other).astype(F32), jnp.where(core == 0, other, kept).astype(F32)
+        return [jnp.concatenate(part, axis=0) for part in zip(*parts)]
+
+    def in_blocks(array):
+        return [array[:, at : at + half] for at in range(0, array.shape[1], half)]
 
     d_pre_held = d_pre_mine
     grad_in = grad_call(
@@ -992,84 +1072,97 @@
     for part in far_back:
         d_norm1 = d_norm1 + part.reshape(count, width).astype(F32)
     norm1_sums = (jnp.sum(d_norm1 * xhat1, axis=0), jnp.sum(d_norm1, axis=0))
-    e_total = add_third(e_three, after(e_last, norm1_sums))
-    e_row = ahead(e_total)
-    l_three = add_second(l_two, after(l_more, e_total))
-    l_last = send_third(l_three)
-    xhat1 = after(xhat1, l_three, e_total)
-    grad_tokens = (d_middle + layer_norm_back(d_norm1, norm1_gain, xhat1, rstd1)).reshape(tokens.shape)
-
-    def vectors(parts, *covers):
-        packed = jnp.concatenate([p.reshape(wide, -1) for p in parts], axis=1)
-        total = packed
-        covers = iter(covers)
-        for stride, size in ((2 * first, second), (2, first), (1, 2)):
-            total = total.reshape(-1, size, stride, packed.shape[1])
-            spot = (place // stride) % size
-            kept = lax.dynamic_index_in_dim(total, spot, 1, keepdims=False)
-            given = [
-                across(lax.dynamic_index_in_dim(total, spot ^ by, 1, keepdims=False), by * stride)
-                for by in range(1, size)
-            ]
-            given = after(given, next(covers))
-            for part in given:
-                kept = kept + part
-            total = kept.reshape(stride, packed.shape[1])
-        total = total.reshape(-1)
-        total = total + after(from_ahead(total, 1), next(covers)) if group == 2 else lax.psum(total, "blk")
-        out, at = [], 0
-        for p in parts:
-            size = p.size // wide
-            out.append(total[at : at + size])
-            at += size
-        return out
+    def vector_stage(total, stride, size):
+        total = total.reshape(-1, size, stride, total.shape[-1])
+        spot = (place // stride) % size
+        kept = lax.dynamic_index_in_dim(total, spot, 1, keepdims=False)
+        for by in range(1, size):
+            kept = kept + across(lax.dynamic_index_in_dim(total, spot ^ by, 1, keepdims=False), by * stride)
+        return kept.reshape(stride, -1)
 
     def widened(part):
         n = sum_e.shape[1] // 3, sum_l.shape[1] // 3
         own = jnp.concatenate([s[0, part * m : (part + 1) * m] for s, m in zip((sum_e, sum_l), n)])
         return lax.dynamic_update_slice_in_dim(jnp.zeros((width,), F32), own, core * half, 0)
 
-    in_low, in_high = swap(by_core(after(in_total, grad_tokens), in_row, [width // chips])) if not halves else (None, None)
+    parts = [
+        *norm1_sums,
+        widened(0),
+        widened(2),
+        z_sums[0],
+        z_sums[1],
+        z_sums[2],
+        d_pre_sum,
+        jnp.sum(grad_out, axis=0),
+    ]
+    totals = vector_stage(jnp.concatenate([part.reshape(wide, -1) for part in parts], axis=1), 2 * first, second)
+    e_total = add_third(e_three, after(e_last, norm1_sums))
+    l_three = add_second(l_two, after(l_more, e_total))
+    l_last = send_third(l_three)
+    xhat1 = after(xhat1, l_three, e_total, totals)
+    totals = vector_stage(totals, 2, first)
+    grad_tokens = (d_middle + layer_norm_back(d_norm1, norm1_gain, xhat1, rstd1)).reshape(tokens.shape)
+
+    l_total = add_third(l_three, after(l_last, grad_tokens, totals))
+    totals = vector_stage(totals, 1, 2).reshape(-1)
+    qkv_total = jnp.concatenate([e_total, l_total], axis=1)
+    qkv_row = ahead(qkv_total)
+    in_total, b_total = after((in_total, b_total), grad_tokens, totals)
+    totals = totals + from_ahead(totals, 1) if group == 2 else lax.psum(totals, "blk")
     if halves:
-        in_whole = over_row(after(in_total, grad_tokens), in_row).reshape(2, -1, in_total.shape[1])
-        in_low, in_high = swap([lax.dynamic_index_in_dim(in_whole, i, 0, keepdims=False) for i in (core, 1 - core)])
-    b_low, b_high = swap(by_core(after(b_total, grad_tokens), b_row, [back_rows, out_rows]))
-    e_low, e_high = swap(by_core(after(e_total, grad_tokens), e_row, [out_rows]))
-    l_total = add_third(l_three, after(l_last, grad_tokens))
-    l_low, l_high = swap(by_core(l_total, ahead(l_total), [out_rows]))
-
-    def part_columns(part):
-        return [
-            array[:, part * n : (part + 1) * n]
-            for array, n in ((e_low, n_early), (l_low, n_late), (e_high, n_early), (l_high, n_late))
-        ]
-
+        kept, given = pack_call(where, (in_total, in_row), (b_total, b_row), (qkv_total, qkv_row))
+    else:
+        in_parts = by_core(over_row(in_total, in_row))
+        b_parts = joined(b_total, b_row, [back_rows, out_rows])
+        qkv_parts = joined(qkv_total, qkv_row, [out_rows])
+        kept, given = (
+            jnp.concatenate(in_blocks(i) + [b] + in_blocks(q), axis=0)
+            for i, b, q in zip(in_parts, b_parts, qkv_parts)
+        )
+    other = after(to_mate(given), totals)
     share = ff // wide
-    grad_w_in = jnp.concatenate([in_low, in_high], axis=1)
-    grad_w_back = jnp.concatenate([b_low[:share], b_high[:share]], axis=1)
-    grad_w_out = jnp.concatenate([b_low[share:], b_high[share:]], axis=1)
-    small = vectors(
-        [
-            *norm1_sums,
-            widened(0),
-            widened(2),
-            z_sums[0],
-            z_sums[1],
-            z_sums[2],
-            d_pre_sum,
-            jnp.sum(grad_out, axis=0),
-        ],
-        grad_tokens,
-        grad_w_in,
-        grad_w_back,
-        grad_w_out,
-    )
+    own_rows = width // wide
+    in_count = ff // 2 // half
+
+    def rows_of(array, first_row, size):
+        return array[first_row : first_row + size]
+
+    def blocks_of(array, first_row, count):
+        return [rows_of(array, first_row + i * own_rows, own_rows) for i in range(count)]
+
+    if halves:
+        shapes = [(own_rows, ff), (share, width), (own_rows, width), (own_rows, 3 * width)]
+        grad_w_in, grad_w_back, grad_w_out, grad_w_qkv = unpack_call(where, kept, other, shapes, (n_early, n_late))
+    else:
+        low, high = (jnp.where(core == side, kept, other).astype(F32) for side in range(2))
+        b_at = in_count * own_rows
+        q_at = b_at + share + own_rows
+
+        def part_columns(part):
+            columns = []
+            for side in (low, high):
+                wide_rows = jnp.concatenate(blocks_of(side, q_at, 3), axis=1)
+                for start, n in ((0, n_early), (3 * n_early, n_late)):
+                    columns.append(wide_rows[:, start + part * n : start + (part + 1) * n])
+            return columns
+
+        grad_w_in = jnp.concatenate([b for side in (low, high) for b in blocks_of(side, 0, in_count)], axis=1)
+        grad_w_back = jnp.concatenate([rows_of(side, b_at, share) for side in (low, high)], axis=1)
+        grad_w_out = jnp.concatenate([rows_of(side, b_at + share, own_rows) for side in (low, high)], axis=1)
+        grad_w_qkv = jnp.concatenate([piece for part in range(3) for piece in part_columns(part)], axis=1)
+
+    small, at = [], 0
+    for part in parts:
+        size = part.size // wide
+        small.append(totals[at : at + size])
+        at += size
+
     return (
         mixed,
         grad_tokens,
         small[0],
         small[1],
-        jnp.concatenate([piece for part in range(3) for piece in part_columns(part)], axis=1),
+        grad_w_qkv,
         small[2],
         small[3],
         grad_w_out,

time: 635 us -> 623 us (0.981)
  local copies, waits for them, and re-layouts: 75.1 us -> 22.7 us
  Pallas kernels: 319 us -> 357 us
  starting transfers between devices: 83.6 us -> 62.8 us
  waiting for transfers between devices: 26.7 us -> 43.8 us
    unnamed x211 -> x104, local copies, waits for them, and re-layouts: 64.3 us -> 10.2 us
    ppermute x34 -> x31, starting transfers between devices: 63.7 us -> 45.6 us  [across(): return lax.ppermute(array, 'wide', [(i, i ^ by) for i in range(wide)])]
    pallas_call x5, Pallas kernels: 40.8 us -> 57.5 us  [product(): pl.pallas_call(functools.partial(product_kernel, dims=dims, spans=spans),...]
    ppermute x34 -> x31, waiting for transfers between devices: 14 us -> 24.8 us  [across(): return lax.ppermute(array, 'wide', [(i, i ^ by) for i in range(wide)])]
    pallas_call x2, Pallas kernels: 27.4 us -> 36.7 us  [qkv_call(): pl.pallas_call(functools.partial(qkv_kernel, first=first, second=second,...]
    ppermute x10 -> x9, waiting for transfers between devices: 12.7 us -> 18.9 us  [from_ahead(): lax.ppermute(array, 'blk', [((i + by) % group, i) for i in range(group)])]
    ppermute x10 -> x9, starting transfers between devices: 19.9 us -> 15.4 us  [from_ahead(): lax.ppermute(array, 'blk', [((i + by) % group, i) for i in range(group)])]
  transfers between devices with their start and end apart: 45 -> 41, of which waited for: 11 -> 11; matrix products, arithmetic and copies ran while one was open for 19% -> 20% of each run, Pallas kernels for 44% -> 50%
where the time goes in v7:
time: 623 us; the launch traced here: 611 us
  Pallas kernels  357 us (57%)
  other arithmetic  73.9 us (12%)
  starting transfers between devices  62.8 us (10%)
  matrix products  48.9 us (8%)
  waiting for transfers between devices  43.8 us (7%)
  local copies, waits for them, and re-layouts  22.7 us (4%)
    pallas_call x3, Pallas kernels, attn_bwd(): pl.pallas_call(functools.partial(bwd_kernel, spans=spans, tq=tq, tk=tk),...  94.8 us
    pallas_call x5, Pallas kernels, product(): pl.pallas_call(functools.partial(product_kernel, dims=dims, spans=spans),...  57.5 us
    pallas_call x2, Pallas kernels, attn_fwd(): pl.pallas_call(functools.partial(fwd_kernel, first=first, tq=tq, tk=tk, h...  53.9 us
    pallas_call x2, Pallas kernels, ffn_call(): pl.pallas_call(functools.partial(ffn_kernel, last=last), out_shape=out_sh...  53.9 us
    dot_general x5, matrix products, dot(): return lax.dot_general(a, b, dims, preferred_element_type=F32)  48.9 us
    ppermute x31, starting transfers between devices, across(): return lax.ppermute(array, 'wide', [(i, i ^ by) for i in range(wide)])  45.6 us
    pallas_call x2, Pallas kernels, qkv_call(): pl.pallas_call(functools.partial(qkv_kernel, first=first, second=second,...  36.7 us
    pallas_call x2, Pallas kernels, grad_call(): pl.pallas_call(functools.partial(grad_kernel, groups=[len(g) for g in gro...  30.8 us
  transfers between devices with their start and end apart: 41, of which 11 were waited for; matrix products, arithmetic and copies ran while one was open for 20% of the time, Pallas kernels for 50%

profile of v7, /device:TPU:0, one launch (start us, length us, event | category | flops | bytes accessed | tf_op | source)
XLA Modules:
  0.0 610.7 jit_solution(15425172751776220225)
XLA Ops:
  24.8 13.1 %add_convert_fusion = bf16[2048,1920]{1,0:T(8,128)(2,1)} fusion(f32[1920]{0:T(1024)S(1)} %pad_maximum_fusion.3, bf16[2048,1280]{1,0:T(8,128)(2,1)S(1)} %bitcast.158, bf16[1280,1920]{1,0:T(8,128)(2,1)S(1)} %bitcast.136), kind=kOutput, calls=%fused_computation | convolution fusion | flops 10074193920 | bytes 18030080 | tf_op jit(solution)/shard_map/dot_general | solution.py:29
  39.3 30.1 %attn_fwd_a.1 = (f32[2,640,1024]{2,1,0:T(8,128)}, f32[2,16,1024]{2,1,0:T(8,128)}, f32[2,16,1024]{2,1,0:T(8,128)}) custom-call(s32[2,2,4]{2,1,0:T(2,128)} %get-tuple-element.238.flags, s32[2,1,1024]{2,1,0:T(1,128)} %broadcast_in_dim.40.cq, s32[2,1024,128]{2,1,0:T(8,128)} %broadcast_in_dim.43.ck, bf16[2,1024,1920]{2,1,0:T(8,128)(2,1)} %bitcast.137, ...), custom_call_target="tpu_custom_call" | custom-call | flops 536870912 | bytes 1310720 | tf_op jit(solution)/shard_map/attn_fwd_a/pallas_call | solution.py:165
  69.4 9.3 %collective-permute-done.3 = bf16[1,1024,1280]{2,1,0:T(8,128)(2,1)} collective-permute-done((bf16[1,1024,1280]{2,1,0:T(8,128)(2,1)}, bf16[1,1024,1280]{2,1,0:T(8,128)(2,1)}, u32[]{:S(2)}, u32[]{:S(2)}) %collective-permute-start.3) | collective-permute-done | bytes 2621472 | tf_op jit(solution)/shard_map/ppermute | solution.py:842
  78.7 20.2 %convolution_convert_fusion.d_act = bf16[1024,5120]{1,0:T(8,128)(2,1)} fusion(bf16[1024,1280]{1,0:T(8,128)(2,1)} %bitcast.6.rest_4_.b1, bf16[5120,1280]{1,0:T(8,128)(2,1)} %refs_1_.1), kind=kOutput, calls=%fused_computation.2 | convolution fusion | flops 13427015680 | bytes 26214400 | tf_op jit(solution)/shard_map/dot_general | solution.py:29
  101.9 8.7 %add_convert_fusion.1 = bf16[2048,1280]{1,0:T(8,128)(2,1)} fusion(bf16[2048,1280]{1,0:T(8,128)(2,1)S(1)} %bitcast.161, f32[1280]{0:T(1024)S(1)} %concatenate.50, bf16[1280,1920]{1,0:T(8,128)(2,1)S(1)} %bitcast.136), kind=kOutput, calls=%fused_computation.1 | convolution fusion | flops 6716129280 | bytes 13770752 | tf_op jit(solution)/shard_map/dot_general | solution.py:29
  111.9 23.8 %attn_fwd_b.1 = (bf16[1,1024,640]{2,1,0:T(8,128)(2,1)}, bf16[1,1024,640]{2,1,0:T(8,128)(2,1)}, f32[2,16,1024]{2,1,0:T(8,128)}) custom-call(s32[2,2,4]{2,1,0:T(2,128)} %get-tuple-element.239.flags, s32[2,1,1024]{2,1,0:T(1,128)} %broadcast_in_dim.40.cq, s32[2,1024,128]{2,1,0:T(8,128)} %broadcast_in_dim.41.ck, bf16[2,1024,1920]{2,1,0:T(8,128)(2,1)} %bitcast.140, ...), custom_call_target="tpu_custom_call" | custom-call | flops 536870912 | bytes 1310720 | tf_op jit(solution)/shard_map/attn_fwd_b/pallas_call | solution.py:165
  139.1 4.1 fusion.15
  150.4 23.6 %ffn_theirs.1 = (bf16[1024,5120]{1,0:T(8,128)(2,1)}, bf16[1024,2560]{1,0:T(8,128)(2,1)}, f32[1,5120]{1,0:T(1,128)}, f32[1024,1280]{1,0:T(8,128)}) custom-call(s32[3]{0:T(128)} %copy-done.2, bf16[1024,1280]{1,0:T(8,128)(2,1)} %add_convert_fusion.3.acts.refs_0_, bf16[1280,5120]{1,0:T(8,128)(2,1)} %w.5, f32[1,5120]{1,0:T(1,128)} %bitcast.181, ...), custom_call_target="tpu_custom_call" | custom-call | flops 1342177280 | bytes 2490368 | tf_op jit(solution)/shard_map/ffn_theirs/pallas_call | solution.py:418
  175.2 30.2 %ffn_mine.1 = (bf16[1024,5120]{1,0:T(8,128)(2,1)}, bf16[1024,2560]{1,0:T(8,128)(2,1)}, f32[1,5120]{1,0:T(1,128)}, f32[1024,1280]{1,0:T(8,128)}, bf16[1024,1280]{...) custom-call(s32[3]{0:T(128)} %copy-done.2, ...), custom_call_target="tpu_custom_call", output_to_operand_aliasing={{0}: (5, {}), {2}: (6, {})} | custom-call | flops 1342177280 | bytes 2490368 | tf_op jit(solution)/shard_map/ffn_mine/pallas_call | solution.py:418
  207.7 20.5 %grad_in.1 = (bf16[4,160,2560]{2,1,0:T(8,128)(2,1)}, bf16[4,160,2560]{2,1,0:T(8,128)(2,1)}) custom-call(s32[3]{0:T(128)} %copy-done.2, bf16[1024,1280]{1,0:T(8,128)(2,1)} %add_convert_fusion.3.acts.refs_0_, bf16[1024,2560]{1,0:T(8,128)(2,1)} %get-tuple-element.121.refs_1_, bf16[1024,1280]{1,0:T(8,128)(2,1)} %collective-permute-done.9.refs_2_, ...), custom_call_target="tpu_custom_call" | custom-call | flops 1342177280 | bytes 2228224 | tf_op jit(solution)/shard_map/grad_in/pallas_call | solution.py:491
  228.2 6.0 collective-permute-start.13
  236.0 5.4 collective-permute-done.11.refs_3_.refs_7_
  241.4 23.0 %grad_back.1 = (bf16[2,4,400,640]{3,2,1,0:T(8,128)(2,1)}, bf16[2,4,400,640]{3,2,1,0:T(8,128)(2,1)}) custom-call(s32[3]{0:T(128)} %copy-done.2, bf16[1024,5120]{1,0:T(8,128)(2,1)} %get-tuple-element.166.a1.refs_0_, bf16[1024,1280]{1,0:T(8,128)(2,1)} %bitcast.6.rest_4_.b1, bf16[1024,5120]{1,0:T(8,128)(2,1)} %collective-permute-done.10.a2, ...), custom_call_target="tpu_custom_call" | custom-call | flops 1342177280 | bytes 3014656 | tf_op jit(solution)/shard_map/grad_back/pallas_call | solution.py:584
  264.4 10.3 %grad_out.1 = (bf16[2,4,400,640]{3,2,1,0:T(8,128)(2,1)}, bf16[2,4,400,640]{3,2,1,0:T(8,128)(2,1)}) custom-call(s32[3]{0:T(128)} %add_add_fusion.1.where, bf16[1024,640]{1,0:T(8,128)(2,1)} %bitcast.168, bf16[1024,1280]{1,0:T(8,128)(2,1)} %get-tuple-element.120.refs_1_.refs_5_, ...), custom_call_target="tpu_custom_call", output_to_operand_aliasing={{0}: (9, {}), {1}: (10, {})} | custom-call | flops 335544320 | bytes 950272 | tf_op jit(solution)/shard_map/grad_out/pallas_call | solution.py:491
  279.4 32.6 %attn_bwd_far.1 = (f32[2,640,1024]{2,1,0:T(8,128)}, bf16[2,1024,768]{2,1,0:T(8,128)(2,1)}, bf16[2,1024,512]{2,1,0:T(8,128)(2,1)}) custom-call(s32[2,4,4]{2,1,0:T(4,128)} %get-tuple-element.236.flags, s32[2,1,1024]{2,1,0:T(1,128)} %broadcast_in_dim.40.cq, s32[2,1024,128]{2,1,0:T(8,128)} %broadcast_in_dim.41.ck, bf16[2,1024,1920]{2,1,0:T(8,128)(2,1)} %bitcast.141, ...), custom_call_target="tpu_custom_call" | custom-call | flops 1342177280 | bytes 2359296 | tf_op jit(solution)/shard_map/attn_bwd_far/pallas_call | solution.py:264
  312.0 4.5 add_convert_fusion.6
  316.5 8.4 %far_norm_theirs.1 = bf16[1024,1280]{1,0:T(8,128)(2,1)} custom-call(bf16[2048,768]{1,0:T(8,128)(2,1)} %bitcast.164, bf16[2048,512]{1,0:T(8,128)(2,1)} %bitcast.171, bf16[1280,1920]{1,0:T(8,128)(2,1)} %copy-done), custom_call_target="tpu_custom_call" | custom-call | flops 335544320 | bytes 851968 | tf_op jit(solution)/shard_map/far_norm_theirs/pallas_call | solution.py:753
  325.0 19.0 %collective-permute-start.16 = (bf16[2,160,2560]{2,1,0:T(8,128)(2,1)}, bf16[2,160,2560]{2,1,0:T(8,128)(2,1)}, u32[]{:S(2)}, u32[]{:S(2)}) collective-permute-start(bf16[2,160,2560]{2,1,0:T(8,128)(2,1)} %get-tuple-element.202), channel_id=1, source_target_pairs={{0,16},{2,18},{4,20},{6,22},{8,24},{10,26},{12,28},{14,30},{16,0},... | collective-permute-start | bytes 4915208 | tf_op jit(solution)/shard_map/ppermute | solution.py:836
  344.0 8.1 %far_norm_mine.1 = bf16[1024,1280]{1,0:T(8,128)(2,1)} custom-call(bf16[2048,768]{1,0:T(8,128)(2,1)} %bitcast.165, bf16[2048,512]{1,0:T(8,128)(2,1)} %bitcast.172, bf16[1280,1920]{1,0:T(8,128)(2,1)} %copy-done), custom_call_target="tpu_custom_call" | custom-call | flops 335544320 | bytes 851968 | tf_op jit(solution)/shard_map/far_norm_mine/pallas_call | solution.py:753
  357.8 35.6 %attn_bwd_early.1 = bf16[2,1024,1152]{2,1,0:T(8,128)(2,1)} custom-call(s32[2,4,4]{2,1,0:T(4,128)} %get-tuple-element.237.flags, s32[2,1,1024]{2,1,0:T(1,128)} %broadcast_in_dim.40.cq, s32[2,1024,128]{2,1,0:T(8,128)} %broadcast_in_dim.43.ck, bf16[2,1024,1920]{2,1,0:T(8,128)(2,1)} %bitcast.142, bf16[2,1024,1920]{2,1,0:T(8,128)(2,1)} %bitcast.143, ...), custom_call_target="tpu_custom_call" | custom-call | flops 805306368 | bytes 1415577 | tf_op jit(solution)/shard_map/attn_bwd_early/pallas_call | solution.py:264
  393.4 5.3 fusion.12
  398.7 10.5 %collective-permute-done.16 = bf16[2,160,2560]{2,1,0:T(8,128)(2,1)} collective-permute-done((bf16[2,160,2560]{2,1,0:T(8,128)(2,1)}, bf16[2,160,2560]{2,1,0:T(8,128)(2,1)}, u32[]{:S(2)}, u32[]{:S(2)}) %collective-permute-start.16) | collective-permute-done | bytes 1638432 | tf_op jit(solution)/shard_map/ppermute | solution.py:836
  411.1 22.0 %grad_early.1 = (bf16[2,4,80,1152]{3,2,1,0:T(8,128)(2,1)}, bf16[2,4,80,1152]{3,2,1,0:T(8,128)(2,1)}, f32[1,1152]{1,0:T(1,128)}) custom-call(s32[3]{0:T(128)} %copy-done.2, bf16[2048,1280]{1,0:T(8,128)(2,1)} %bitcast.159, bf16[2048,1152]{1,0:T(8,128)(2,1)} %bitcast.152, bf16[2048,1280]{1,0:T(8,128)(2,1)} %bitcast.162, bf16[2048,768]{1,0:T(8,128)(2,1)} %bitcast.166), custom_call_target="tpu_custom_call" | custom-call | flops 1207959552 | bytes 2287206 | tf_op jit(solution)/shard_map/grad_early/pallas_call | solution.py:542
  435.5 26.7 %attn_bwd_late.1 = bf16[2,1024,768]{2,1,0:T(8,128)(2,1)} custom-call(s32[2,4,4]{2,1,0:T(4,128)} %get-tuple-element.237.flags, s32[2,1,1024]{2,1,0:T(1,128)} %broadcast_in_dim.40.cq, s32[2,1024,128]{2,1,0:T(8,128)} %broadcast_in_dim.43.ck, bf16[2,1024,1920]{2,1,0:T(8,128)(2,1)} %bitcast.145, bf16[2,1024,1920]{2,1,0:T(8,128)(2,1)} %bitcast.146, ...), custom_call_target="tpu_custom_call" | custom-call | flops 536870912 | bytes 943718 | tf_op jit(solution)/shard_map/attn_bwd_late/pallas_call | solution.py:264
  484.5 14.7 %grad_late.1 = (bf16[2,4,80,768]{3,2,1,0:T(8,128)(2,1)}, bf16[2,4,80,768]{3,2,1,0:T(8,128)(2,1)}, f32[1,768]{1,0:T(1,128)}) custom-call(s32[3]{0:T(128)} %copy-done.2, bf16[2048,1280]{1,0:T(8,128)(2,1)} %bitcast.160, bf16[2048,768]{1,0:T(8,128)(2,1)} %bitcast.155, bf16[2048,1280]{1,0:T(8,128)(2,1)} %bitcast.163, bf16[2048,512]{1,0:T(8,128)(2,1)} %bitcast.173), custom_call_target="tpu_custom_call" | custom-call | flops 805306368 | bytes 1874329 | tf_op jit(solution)/shard_map/grad_late/pallas_call | solution.py:542
  499.2 9.9 %near_norm_theirs.1 = bf16[1024,1280]{1,0:T(8,128)(2,1)} custom-call(bf16[2048,1152]{1,0:T(8,128)(2,1)} %bitcast.153, bf16[2048,768]{1,0:T(8,128)(2,1)} %bitcast.156, bf16[1280,1920]{1,0:T(8,128)(2,1)} %copy-done), custom_call_target="tpu_custom_call" | custom-call | flops 503316480 | bytes 1146880 | tf_op jit(solution)/shard_map/near_norm_theirs/pallas_call | solution.py:753
  509.1 10.0 %near_norm_mine.1 = bf16[1024,1280]{1,0:T(8,128)(2,1)} custom-call(bf16[2048,1152]{1,0:T(8,128)(2,1)} %bitcast.154, bf16[2048,768]{1,0:T(8,128)(2,1)} %bitcast.157, bf16[1280,1920]{1,0:T(8,128)(2,1)} %copy-done), custom_call_target="tpu_custom_call" | custom-call | flops 503316480 | bytes 1146880 | tf_op jit(solution)/shard_map/near_norm_mine/pallas_call | solution.py:753
  529.3 21.1 %mixed.1 = bf16[1024,1280]{1,0:T(8,128)(2,1)} custom-call(bf16[1024,5120]{1,0:T(8,128)(2,1)} %get-tuple-element.166.a1.refs_0_, bf16[5120,1280]{1,0:T(8,128)(2,1)} %refs_1_.1, f32[1024,1280]{1,0:T(8,128)} %copy-done.4, f32[1,1280]{1,0:T(1,128)} %reshape.292.refs_3_), custom_call_target="tpu_custom_call" | custom-call | flops 1342177280 | bytes 2621440 | tf_op jit(solution)/shard_map/mixed/pallas_call | solution.py:753
  558.4 5.3 fusion.37
  567.5 6.6 %multiply_reduce_fusion.3 = (f32[1024]{0:T(1024)S(1)}, f32[1024]{0:T(1024)S(1)}) fusion(f32[1280]{0:T(1024)S(1)} %copy-done.30, bf16[1,1024,1280]{2,1,0:T(8,128)(2,1)} %copy-done.12, bf16[1024,1280]{1,0:T(8,128)(2,1)} %collective-permute-done.25, bf16[1024,1280]{1,0:T(8,128)(2,1)} %near_norm_mine.1, f32[1024,1280]{1,0:T(8,128)} %get-tuple-element.176), kind=kLoop, calls=%fused_computation.26 | loop fusion | flops 11794432 | bytes 13120512 | tf_op jit(solution)/shard_map/reduce_sum | solution.py:790
  583.9 9.8 %add_bitcast_fusion = f32[1,1024,1280]{2,1,0:T(8,128)} fusion(f32[1024,1280]{1,0:T(8,128)} %get-tuple-element.167, f32[1024,1280]{1,0:T(8,128)} %get-tuple-element.176, f32[1024]{0:T(1024)S(1)} %get-tuple-element.242, f32[1024]{0:T(1024)S(1)} %get-tuple-element.243, f32[1280]{0:T(1024)S(1)} %copy-done.30, f32[1024]{0:T(1024)S(1)} %copy-done.34, ...), kind=kLoop, calls=%fused_computation.20 | loop fusion | flops 14417920 | bytes 23610368 | tf_op jit(solution)/shard_map/reshape | solution.py:1104
  597.1 4.2 collective-permute-done.39.q_row
  (266 shorter events, 126.5 us)
Async XLA Ops:
  9.6 10.9 %collective-permute-start.2 = (bf16[1,1024,1280]{2,1,0:T(8,128)(2,1)}, bf16[1,1024,1280]{2,1,0:T(8,128)(2,1)}, u32[]{:S(2)}, u32[]{:S(2)}) collective-permute-start(bf16[1,1024,1280]{2,1,0:T(8,128)(2,1)} %fusion.9), channel_id=1, source_target_pairs={{0,2},{2,0},{4,6},{6,4},{8,10},{10,8},{12,14},{14,12},{16,18},{18,... | collective-permute-start | bytes 7864328 | tf_op jit(solution)/shard_map/ppermute | solution.py:836
  19.1 59.6 %collective-permute-start.3 = (bf16[1,1024,1280]{2,1,0:T(8,128)(2,1)}, bf16[1,1024,1280]{2,1,0:T(8,128)(2,1)}, u32[]{:S(2)}, u32[]{:S(2)}) collective-permute-start(bf16[1,1024,1280]{2,1,0:T(8,128)(2,1)} %fusion.9), channel_id=1, source_target_pairs={{1,0},{0,1},{3,2},{2,3},{5,4},{4,5},{7,6},{6,7},{9,8},{8,9},{11,10... | collective-permute-start | bytes 7864328 | tf_op jit(solution)/shard_map/ppermute | solution.py:842
  23.7 55.0 %collective-permute-start.5 = (bf16[1024,1280]{1,0:T(8,128)(2,1)}, bf16[1024,1280]{1,0:T(8,128)(2,1)}, u32[]{:S(2)}, u32[]{:S(2)}) collective-permute-start(bf16[1024,1280]{1,0:T(8,128)(2,1)} %bitcast.6.rest_4_.b1), channel_id=1, source_target_pairs={{0,2},{2,0},{4,6},{6,4},{8,10},{10,8},{12,14},{14,12},{16,18},{18,... | collective-permute-start | bytes 7864328 | tf_op jit(solution)/shard_map/ppermute | solution.py:836
  78.7 20.2 %collective-permute-start.4 = (bf16[1,1024,1280]{2,1,0:T(8,128)(2,1)}, bf16[1,1024,1280]{2,1,0:T(8,128)(2,1)}, u32[]{:S(2)}, u32[]{:S(2)}) collective-permute-start(bf16[1,1024,1280]{2,1,0:T(8,128)(2,1)} %collective-permute-done.3), channel_id=1, source_target_pairs={{0,2},{2,0},{4,6},{6,4},{8,10},{10,8},{12,14},{14,12},{16,18},{18,... | collective-permute-start | bytes 7864328 | tf_op jit(solution)/shard_map/ppermute | solution.py:836
  136.3 13.0 %collective-permute-start.7 = (bf16[1024,640]{1,0:T(8,128)(2,1)}, bf16[1024,640]{1,0:T(8,128)(2,1)S(1)}, u32[]{:S(2)}, u32[]{:S(2)}) collective-permute-start(bf16[1024,640]{1,0:T(8,128)(2,1)} %bitcast.167), channel_id=1, source_target_pairs={{0,2},{2,0},{4,6},{6,4},{8,10},{10,8},{12,14},{14,12},{16,18},{18,... | collective-permute-start | bytes 3932168 | tf_op jit(solution)/shard_map/ppermute | solution.py:836
  174.0 31.4 %collective-permute-start.8 = (bf16[1024,2560]{1,0:T(8,128)(2,1)}, bf16[1024,2560]{1,0:T(8,128)(2,1)S(1)}, u32[]{:S(2)}, u32[]{:S(2)}) collective-permute-start(bf16[1024,2560]{1,0:T(8,128)(2,1)} %get-tuple-element.118), channel_id=1, source_target_pairs={{0,2},{2,0},{4,6},{6,4},{8,10},{10,8},{12,14},{14,12},{16,18},{18,... | collective-permute-start | bytes 15728648 | tf_op jit(solution)/shard_map/ppermute | solution.py:836
  174.5 30.9 %collective-permute-start.9 = (bf16[1024,1280]{1,0:T(8,128)(2,1)S(1)}, bf16[1024,1280]{1,0:T(8,128)(2,1)}, u32[]{:S(2)}, u32[]{:S(2)}) collective-permute-start(bf16[1024,1280]{1,0:T(8,128)(2,1)S(1)} %copy-done.10), channel_id=1, source_target_pairs={{0,2},{2,0},{4,6},{6,4},{8,10},{10,8},{12,14},{14,12},{16,18},{18,... | collective-permute-start | bytes 7864328 | tf_op jit(solution)/shard_map/ppermute | solution.py:836
  205.4 35.9 %collective-permute-start.10 = (bf16[1024,5120]{1,0:T(8,128)(2,1)}, bf16[1024,5120]{1,0:T(8,128)(2,1)}, u32[]{:S(2)}, u32[]{:S(2)}) collective-permute-start(bf16[1024,5120]{1,0:T(8,128)(2,1)} %get-tuple-element.166.a1.refs_0_), channel_id=1, source_target_pairs={{0,2},{2,0},{4,6},{6,4},{8,10},{10,8},{12,14},{14,12},{16,18},{18,... | collective-permute-start | bytes 31457288 | tf_op jit(solution)/shard_map/ppermute | solution.py:836
  228.2 83.8 %collective-permute-start.13 = (bf16[4,160,2560]{2,1,0:T(8,128)(2,1)}, bf16[4,160,2560]{2,1,0:T(8,128)(2,1)}, u32[]{:S(2)}, u32[]{:S(2)}) collective-permute-start(bf16[4,160,2560]{2,1,0:T(8,128)(2,1)} %get-tuple-element.123), channel_id=1, source_target_pairs={{0,4},{2,6},{4,0},{6,2},{8,12},{10,14},{12,8},{14,10},{16,20},{18,... | collective-permute-start | bytes 9830408 | tf_op jit(solution)/shard_map/ppermute | solution.py:836
  234.3 7.1 %collective-permute-start.11 = (bf16[1024,1280]{1,0:T(8,128)(2,1)}, bf16[1024,1280]{1,0:T(8,128)(2,1)}, u32[]{:S(2)}, u32[]{:S(2)}) collective-permute-start(bf16[1024,1280]{1,0:T(8,128)(2,1)} %get-tuple-element.120.refs_1_.refs_5_), channel_id=1, source_target_pairs={{0,2},{2,0},{4,6},{6,4},{8,10},{10,8},{12,14},{14,12},{16,18},{18,... | collective-permute-start | bytes 7864328 | tf_op jit(solution)/shard_map/ppermute | solution.py:836
  234.4 43.9 %collective-permute-start.12 = (bf16[1024,640]{1,0:T(8,128)(2,1)}, bf16[1024,640]{1,0:T(8,128)(2,1)S(1)}, u32[]{:S(2)}, u32[]{:S(2)}) collective-permute-start(bf16[1024,640]{1,0:T(8,128)(2,1)} %get-tuple-element.126), channel_id=1, source_target_pairs={{0,2},{2,0},{4,6},{6,4},{8,10},{10,8},{12,14},{14,12},{16,18},{18,... | collective-permute-start | bytes 3932168 | tf_op jit(solution)/shard_map/ppermute | solution.py:836
  274.7 118.7 %collective-permute-start.15 = (bf16[2,4,400,640]{3,2,1,0:T(8,128)(2,1)}, bf16[2,4,400,640]{3,2,1,0:T(8,128)(2,1)}, u32[]{:S(2)}, u32[]{:S(2)}) collective-permute-start(bf16[2,4,400,640]{3,2,1,0:T(8,128)(2,1)} %get-tuple-element.132), channel_id=1, source_target_pairs={{1,0},{0,1},{3,2},{2,3},{5,4},{4,5},{7,6},{6,7},{9,8},{8,9},{11,10... | collective-permute-start | bytes 12288008 | tf_op jit(solution)/shard_map/ppermute | solution.py:842
  324.9 27.2 %collective-permute-start.14 = (bf16[1024,1280]{1,0:T(8,128)(2,1)}, bf16[1024,1280]{1,0:T(8,128)(2,1)S(1)}, u32[]{:S(2)}, u32[]{:S(2)}) collective-permute-start(bf16[1024,1280]{1,0:T(8,128)(2,1)} %far_norm_theirs.1), channel_id=1, source_target_pairs={{0,2},{2,0},{4,6},{6,4},{8,10},{10,8},{12,14},{14,12},{16,18},{18,... | collective-permute-start | bytes 7864328 | tf_op jit(solution)/shard_map/ppermute | solution.py:836
  325.0 84.1 %collective-permute-start.16 = (bf16[2,160,2560]{2,1,0:T(8,128)(2,1)}, bf16[2,160,2560]{2,1,0:T(8,128)(2,1)}, u32[]{:S(2)}, u32[]{:S(2)}) collective-permute-start(bf16[2,160,2560]{2,1,0:T(8,128)(2,1)} %get-tuple-element.202), channel_id=1, source_target_pairs={{0,16},{2,18},{4,20},{6,22},{8,24},{10,26},{12,28},{14,30},{16,0},... | collective-permute-start | bytes 4915208 | tf_op jit(solution)/shard_map/ppermute | solution.py:836
  356.0 77.4 %collective-permute-start.17 = (bf16[1,1024,1280]{2,1,0:T(8,128)(2,1)}, bf16[1,1024,1280]{2,1,0:T(8,128)(2,1)S(1)}, u32[]{:S(2)}, u32[]{:S(2)}) collective-permute-start(bf16[1,1024,1280]{2,1,0:T(8,128)(2,1)} %fusion.11), channel_id=1, source_target_pairs={{0,1},{1,0},{2,3},{3,2},{4,5},{5,4},{6,7},{7,6},{8,9},{9,8},{10,11... | collective-permute-start | bytes 7864328 | tf_op jit(solution)/shard_map/ppermute | solution.py:845
  411.0 22.2 %collective-permute-start.18 = (bf16[160,2560]{1,0:T(8,128)(2,1)S(1)}, bf16[160,2560]{1,0:T(8,128)(2,1)S(1)}, u32[]{:S(2)}, u32[]{:S(2)}) collective-permute-start(bf16[160,2560]{1,0:T(8,128)(2,1)S(1)} %get-tuple-element.206), channel_id=1, source_target_pairs={{0,8},{2,10},{4,12},{6,14},{8,0},{10,2},{12,4},{14,6},{16,24},{18,... | collective-permute-start | bytes 2457608 | tf_op jit(solution)/shard_map/ppermute | solution.py:836
  411.0 51.1 %collective-permute-start.20 = (bf16[4,400,640]{2,1,0:T(8,128)(2,1)}, bf16[4,400,640]{2,1,0:T(8,128)(2,1)}, u32[]{:S(2)}, u32[]{:S(2)}) collective-permute-start(bf16[4,400,640]{2,1,0:T(8,128)(2,1)} %get-tuple-element.200), channel_id=1, source_target_pairs={{0,4},{2,6},{4,0},{6,2},{8,12},{10,14},{12,8},{14,10},{16,20},{18,... | collective-permute-start | bytes 6144008 | tf_op jit(solution)/shard_map/ppermute | solution.py:836
  433.4 35.5 %collective-permute-start.19 = (bf16[2,4,80,1152]{3,2,1,0:T(8,128)(2,1)}, bf16[2,4,80,1152]{3,2,1,0:T(8,128)(2,1)}, u32[]{:S(2)}, u32[]{:S(2)}) collective-permute-start(bf16[2,4,80,1152]{3,2,1,0:T(8,128)(2,1)} %get-tuple-element.152), channel_id=1, source_target_pairs={{1,0},{0,1},{3,2},{2,3},{5,4},{4,5},{7,6},{6,7},{9,8},{8,9},{11,10... | collective-permute-start | bytes 4423688 | tf_op jit(solution)/shard_map/ppermute | solution.py:842
  434.0 85.1 %collective-permute-start.24 = (bf16[160,2560]{1,0:T(8,128)(2,1)S(1)}, bf16[160,2560]{1,0:T(8,128)(2,1)S(1)}, u32[]{:S(2)}, u32[]{:S(2)}) collective-permute-start(bf16[160,2560]{1,0:T(8,128)(2,1)S(1)} %add_convert_fusion.8.in_mine), channel_id=1, source_target_pairs={{1,0},{0,1},{3,2},{2,3},{5,4},{4,5},{7,6},{6,7},{9,8},{8,9},{11,10... | collective-permute-start | bytes 2457608 | tf_op jit(solution)/shard_map/ppermute | solution.py:842
  471.5 47.7 %collective-permute-start.21 = (bf16[4,80,1152]{2,1,0:T(8,128)(2,1)}, bf16[4,80,1152]{2,1,0:T(8,128)(2,1)}, u32[]{:S(2)}, u32[]{:S(2)}) collective-permute-start(bf16[4,80,1152]{2,1,0:T(8,128)(2,1)} %get-tuple-element.208), channel_id=1, source_target_pairs={{0,4},{2,6},{4,0},{6,2},{8,12},{10,14},{12,8},{14,10},{16,20},{18,... | collective-permute-start | bytes 2211848 | tf_op jit(solution)/shard_map/ppermute | solution.py:836
  474.5 46.9 %collective-permute-start.22 = (bf16[2,400,640]{2,1,0:T(8,128)(2,1)}, bf16[2,400,640]{2,1,0:T(8,128)(2,1)}, u32[]{:S(2)}, u32[]{:S(2)}) collective-permute-start(bf16[2,400,640]{2,1,0:T(8,128)(2,1)} %get-tuple-element.204), channel_id=1, source_target_pairs={{0,16},{2,18},{4,20},{6,22},{8,24},{10,26},{12,28},{14,30},{16,0},... | collective-permute-start | bytes 3072008 | tf_op jit(solution)/shard_map/ppermute | solution.py:836
  499.2 24.5 %collective-permute-start.23 = (bf16[2,4,80,768]{3,2,1,0:T(8,128)(2,1)}, bf16[2,4,80,768]{3,2,1,0:T(8,128)(2,1)S(1)}, u32[]{:S(2)}, u32[]{:S(2)}) collective-permute-start(bf16[2,4,80,768]{3,2,1,0:T(8,128)(2,1)} %get-tuple-element.159), channel_id=1, source_target_pairs={{1,0},{0,1},{3,2},{2,3},{5,4},{4,5},{7,6},{6,7},{9,8},{8,9},{11,10... | collective-permute-start | bytes 2949128 | tf_op jit(solution)/shard_map/ppermute | solution.py:842
  519.1 39.3 %collective-permute-start.25 = (bf16[1024,1280]{1,0:T(8,128)(2,1)}, bf16[1024,1280]{1,0:T(8,128)(2,1)}, u32[]{:S(2)}, u32[]{:S(2)}) collective-permute-start(bf16[1024,1280]{1,0:T(8,128)(2,1)} %near_norm_theirs.1), channel_id=1, source_target_pairs={{0,2},{2,0},{4,6},{6,4},{8,10},{10,8},{12,14},{14,12},{16,18},{18,... | collective-permute-start | bytes 7864328 | tf_op jit(solution)/shard_map/ppermute | solution.py:836
  524.7 25.7 %collective-permute-start.26 = (bf16[4,80,768]{2,1,0:T(8,128)(2,1)}, bf16[4,80,768]{2,1,0:T(8,128)(2,1)}, u32[]{:S(2)}, u32[]{:S(2)}) collective-permute-start(bf16[4,80,768]{2,1,0:T(8,128)(2,1)} %get-tuple-element.214), channel_id=1, source_target_pairs={{0,4},{2,6},{4,0},{6,2},{8,12},{10,14},{12,8},{14,10},{16,20},{18,... | collective-permute-start | bytes 1474568 | tf_op jit(solution)/shard_map/ppermute | solution.py:836
  527.3 26.1 %collective-permute-start.27 = (bf16[2,80,1152]{2,1,0:T(8,128)(2,1)}, bf16[2,80,1152]{2,1,0:T(8,128)(2,1)S(1)}, u32[]{:S(2)}, u32[]{:S(2)}) collective-permute-start(bf16[2,80,1152]{2,1,0:T(8,128)(2,1)} %get-tuple-element.215), channel_id=1, source_target_pairs={{0,16},{2,18},{4,20},{6,22},{8,24},{10,26},{12,28},{14,30},{16,0},... | collective-permute-start | bytes 1105928 | tf_op jit(solution)/shard_map/ppermute | solution.py:836
  527.3 28.9 %collective-permute-start.28 = (bf16[400,640]{1,0:T(8,128)(2,1)}, bf16[400,640]{1,0:T(8,128)(2,1)S(1)}, u32[]{:S(2)}, u32[]{:S(2)}) collective-permute-start(bf16[400,640]{1,0:T(8,128)(2,1)} %get-tuple-element.211), channel_id=1, source_target_pairs={{0,8},{2,10},{4,12},{6,14},{8,0},{10,2},{12,4},{14,6},{16,24},{18,... | collective-permute-start | bytes 1536008 | tf_op jit(solution)/shard_map/ppermute | solution.py:836
  552.4 13.7 %collective-permute-start.29 = (bf16[2,80,768]{2,1,0:T(8,128)(2,1)}, bf16[2,80,768]{2,1,0:T(8,128)(2,1)}, u32[]{:S(2)}, u32[]{:S(2)}) collective-permute-start(bf16[2,80,768]{2,1,0:T(8,128)(2,1)} %get-tuple-element.217), channel_id=1, source_target_pairs={{0,16},{2,18},{4,20},{6,22},{8,24},{10,26},{12,28},{14,30},{16,0},... | collective-permute-start | bytes 737288 | tf_op jit(solution)/shard_map/ppermute | solution.py:836
  554.2 9.7 %collective-permute-start.30 = (bf16[80,1152]{1,0:T(8,128)(2,1)}, bf16[80,1152]{1,0:T(8,128)(2,1)}, u32[]{:S(2)}, u32[]{:S(2)}) collective-permute-start(bf16[80,1152]{1,0:T(8,128)(2,1)} %get-tuple-element.220), channel_id=1, source_target_pairs={{0,8},{2,10},{4,12},{6,14},{8,0},{10,2},{12,4},{14,6},{16,24},{18,... | collective-permute-start | bytes 552968 | tf_op jit(solution)/shard_map/ppermute | solution.py:836
  556.3 40.8 %collective-permute-start.37 = (bf16[400,640]{1,0:T(8,128)(2,1)S(1)}, bf16[400,640]{1,0:T(8,128)(2,1)S(1)}, u32[]{:S(2)}, u32[]{:S(2)}) collective-permute-start(bf16[400,640]{1,0:T(8,128)(2,1)S(1)} %add_convert_fusion.13.b_mine), channel_id=1, source_target_pairs={{1,0},{0,1},{3,2},{2,3},{5,4},{4,5},{7,6},{6,7},{9,8},{8,9},{11,10... | collective-permute-start | bytes 1536008 | tf_op jit(solution)/shard_map/ppermute | solution.py:842
  567.2 26.5 %collective-permute-start.38 = (bf16[80,768]{1,0:T(8,128)(2,1)S(1)}, bf16[80,768]{1,0:T(8,128)(2,1)S(1)}, u32[]{:S(2)}, u32[]{:S(2)}) collective-permute-start(bf16[80,768]{1,0:T(8,128)(2,1)S(1)} %get-tuple-element.221), channel_id=1, source_target_pairs={{0,8},{2,10},{4,12},{6,14},{8,0},{10,2},{12,4},{14,6},{16,24},{18,... | collective-permute-start | bytes 368648 | tf_op jit(solution)/shard_map/ppermute | solution.py:836
  582.7 11.0 %collective-permute-start.34 = (f32[1,2,960]{2,1,0:T(2,128)S(1)}, f32[1,2,960]{2,1,0:T(2,128)S(1)}, u32[]{:S(2)}, u32[]{:S(2)}) collective-permute-start(f32[1,2,960]{2,1,0:T(2,128)S(1)} %dynamic-slice_bitcast_fusion.3), channel_id=1, source_target_pairs={{0,4},{2,6},{4,0},{6,2},{8,12},{10,14},{12,8},{14,10},{16,20},{18,... | collective-permute-start | bytes 23048 | tf_op jit(solution)/shard_map/ppermute | solution.py:836
  593.8 7.5 %collective-permute-start.39 = (bf16[80,1920]{1,0:T(8,128)(2,1)S(1)}, bf16[80,1920]{1,0:T(8,128)(2,1)S(1)}, u32[]{:S(2)}, u32[]{:S(2)}) collective-permute-start(bf16[80,1920]{1,0:T(8,128)(2,1)S(1)} %pad_maximum_fusion.2.q_mine), channel_id=1, source_target_pairs={{1,0},{0,1},{3,2},{2,3},{5,4},{4,5},{7,6},{6,7},{9,8},{8,9},{11,10... | collective-permute-start | bytes 921608 | tf_op jit(solution)/shard_map/ppermute | solution.py:842
  (61 other events, 543.1 us)

commit v8 on v7

--- a/solution.py
+++ b/solution.py
@@ -611,6 +611,41 @@
     )(where, a1, b1, a2, b2)
 
 
+def first_norm_kernel(tokens, d_middle, gain, *rest):
+    parts, (out, sums) = rest[:-2], rest[-2:]
+    d_norm = parts[0][...].astype(F32)
+    for part in parts[1:]:
+        d_norm = d_norm + part[...].astype(F32)
+    xhat, rstd = layer_norm_parts(tokens[...].astype(F32))
+    out[...] = d_middle[...] + layer_norm_back(d_norm, gain[...], xhat, rstd)
+    new = jnp.concatenate(
+        [jnp.sum(d_norm * xhat, axis=0, keepdims=True), jnp.sum(d_norm, axis=0, keepdims=True)], axis=0
+    )
+
+    @pl.when(pl.program_id(0) == 0)
+    def _():
+        sums[...] = jnp.zeros_like(sums)
+
+    sums[0:2, :] += new
+
+
+def first_norm_call(tokens, d_middle, gain, parts):
+    rows, width = tokens.shape
+    block = pl.BlockSpec((128, width), lambda i: (i, 0))
+    return pl.pallas_call(
+        first_norm_kernel,
+        out_shape=[jax.ShapeDtypeStruct((rows, width), F32), jax.ShapeDtypeStruct((8, width), F32)],
+        grid=(rows // 128,),
+        in_specs=[block, block, pl.BlockSpec((1, width), lambda i: (0, 0))] + [block] * len(parts),
+        out_specs=[block, pl.BlockSpec((8, width), lambda i: (0, 0))],
+        compiler_params=pltpu.CompilerParams(vmem_limit_bytes=VMEM_LIMIT),
+        cost_estimate=pl.CostEstimate(
+            flops=20 * rows * width // SHARE, bytes_accessed=20 * rows * width // SHARE, transcendentals=0
+        ),
+        name="first_norm",
+    )(tokens, d_middle, gain, *parts)
+
+
 def pack_kernel(where, in_mine, in_row, b_mine, b_row, q_mine, q_row, *outs):
     core, member = where[1], where[2]
     half = outs[0].shape[1]
@@ -708,7 +743,7 @@
             in_specs=[pl.BlockSpec((depth // 2, tile), lambda j, i, where: (j, 2 * i + where[1]))],
             out_specs=pl.BlockSpec((depth // 2, tile), lambda j, i, where: (j, i)),
         ),
-        compiler_params=pltpu.CompilerParams(vmem_limit_bytes=12 * 2**20),
+        compiler_params=pltpu.CompilerParams(vmem_limit_bytes=VMEM_LIMIT),
         cost_estimate=pl.CostEstimate(flops=0, bytes_accessed=2 * depth * width // SHARE, transcendentals=0),
         name="own_columns",
     )(where, w)
@@ -717,13 +752,21 @@
 def product_kernel(*refs, dims, spans):
     parts = len(spans) if spans else 1
     total = None
+    if spans:
+        cuts, refs = refs[-parts:], refs[:-parts]
+
+        @pl.when(pl.program_id(0) == 0)
+        def _():
+            for i in range(parts):
+                at = 0
+                for low, high in spans[i]:
+                    cuts[i][:, at : at + high - low] = refs[parts][:, low:high]
+                    at += high - low
+
+    else:
+        cuts = [refs[parts]]
     for i in range(parts):
-        b = refs[parts]
-        if spans:
-            b = jnp.concatenate([b[:, low:high] for low, high in spans[i]], axis=1)
-        else:
-            b = b[...]
-        part = dot(refs[i][...], b, dims)
+        part = dot(refs[i][...], cuts[i][...], dims)
         total = part if total is None else total + part
     for term in refs[parts + 1 : -1]:
         total = total + term[...]
@@ -756,6 +799,7 @@
         grid=(steps,),
         in_specs=ins + [pl.BlockSpec((t.shape[0], tile), lambda i: (0, i)) for t in terms],
         out_specs=out_spec,
+        scratch_shapes=[pltpu.VMEM((width, a.shape[1]), BF) for a in parts] if spans else [],
         compiler_params=pltpu.CompilerParams(vmem_limit_bytes=VMEM_LIMIT),
         cost_estimate=pl.CostEstimate(
             flops=2 * rows * depth * width // SHARE,
@@ -1068,10 +1112,12 @@
     b_total = add_third(b_three, after(b_last, e_three))
     b_row = ahead(b_total)
     near_mine, near_given = after((near_mine, near_given), l_two, e_three, b_total)
-    d_norm1 = near_mine.astype(F32) + near_given.astype(F32)
-    for part in far_back:
-        d_norm1 = d_norm1 + part.reshape(count, width).astype(F32)
-    norm1_sums = (jnp.sum(d_norm1 * xhat1, axis=0), jnp.sum(d_norm1, axis=0))
+    grad_tokens, norm1_sums = first_norm_call(
+        tokens.reshape(count, width), d_middle, norm1_gain.reshape(1, width),
+        [near_mine, near_given, *(part.reshape(count, width) for part in far_back)],
+    )
+    grad_tokens = grad_tokens.reshape(tokens.shape)
+
     def vector_stage(total, stride, size):
         total = total.reshape(-1, size, stride, total.shape[-1])
         spot = (place // stride) % size
@@ -1086,7 +1132,8 @@
         return lax.dynamic_update_slice_in_dim(jnp.zeros((width,), F32), own, core * half, 0)
 
     parts = [
-        *norm1_sums,
+        norm1_sums[0],
+        norm1_sums[1],
         widened(0),
         widened(2),
         z_sums[0],
@@ -1099,11 +1146,9 @@
     e_total = add_third(e_three, after(e_last, norm1_sums))
     l_three = add_second(l_two, after(l_more, e_total))
     l_last = send_third(l_three)
-    xhat1 = after(xhat1, l_three, e_total, totals)
     totals = vector_stage(totals, 2, first)
-    grad_tokens = (d_middle + layer_norm_back(d_norm1, norm1_gain, xhat1, rstd1)).reshape(tokens.shape)
-
-    l_total = add_third(l_three, after(l_last, grad_tokens, totals))
+
+    l_total = add_third(l_three, after(l_last, totals))
     totals = vector_stage(totals, 1, 2).reshape(-1)
     qkv_total = jnp.concatenate([e_total, l_total], axis=1)
     qkv_row = ahead(qkv_total)

time: 623 us -> 602 us (0.966); the launches traced: 611 us -> 601 us
  Pallas kernels: 357 us -> 387 us
  other arithmetic: 73.9 us -> 49.9 us
  starting transfers between devices: 62.8 us -> 47.6 us
  local copies, waits for them, and re-layouts: 22.7 us -> 14.6 us
  waiting for transfers between devices: 43.8 us -> 51.6 us
    reduce_sum x2 -> x0, other arithmetic: 11.9 us -> none  [the longest x1 6.58 us: layer_norm_back(): jnp.mean(e, axis=-1, keepdims=True)]
    pallas_call x0 -> x1, Pallas kernels: none -> 11.7 us  [first_norm_call(): pl.pallas_call(first_norm_kernel, out_shape=[jax.ShapeDtypeStruct((rows,...]
    ppermute x31, starting transfers between devices: 45.6 us -> 35.4 us  [across(): return lax.ppermute(array, 'wide', [(i, i ^ by) for i in range(wide)])]
    reshape x1 -> x0, other arithmetic: 9.81 us -> none  [on_device(): (d_middle + layer_norm_back(d_norm1, norm1_gain, xhat1, rstd1)).reshape(t...]
    ppermute x31, waiting for transfers between devices: 24.8 us -> 32.5 us  [across(): return lax.ppermute(array, 'wide', [(i, i ^ by) for i in range(wide)])]
    pallas_call x3, Pallas kernels: 94.8 us -> 102 us  [attn_bwd(): pl.pallas_call(functools.partial(bwd_kernel, spans=spans, tq=tq, tk=tk),...]
  transfers between devices with their start and end apart: 41 -> 41, of which waited for: 11 -> 12; matrix products, arithmetic and copies ran while one was open for 20% -> 16% of each run, Pallas kernels for 50% -> 55%
where the time goes in v8:
time: 602 us; the launch traced here: 601 us
  Pallas kernels  387 us (64%)
  waiting for transfers between devices  51.6 us (9%)
  other arithmetic  49.9 us (8%)
  matrix products  48.2 us (8%)
  starting transfers between devices  47.6 us (8%)
  local copies, waits for them, and re-layouts  14.6 us (2%)
    pallas_call x3, Pallas kernels, attn_bwd(): pl.pallas_call(functools.partial(bwd_kernel, spans=spans, tq=tq, tk=tk),...  102 us
    pallas_call x2, Pallas kernels, attn_fwd(): pl.pallas_call(functools.partial(fwd_kernel, first=first, tq=tq, tk=tk, h...  58.6 us
    pallas_call x5, Pallas kernels, product(): pl.pallas_call(functools.partial(product_kernel, dims=dims, spans=spans),...  58.4 us
    pallas_call x2, Pallas kernels, ffn_call(): pl.pallas_call(functools.partial(ffn_kernel, last=last), out_shape=out_sh...  54.1 us
    dot_general x5, matrix products, dot(): return lax.dot_general(a, b, dims, preferred_element_type=F32)  48.2 us
    pallas_call x2, Pallas kernels, qkv_call(): pl.pallas_call(functools.partial(qkv_kernel, first=first, second=second,...  36.9 us
    ppermute x31, starting transfers between devices, across(): return lax.ppermute(array, 'wide', [(i, i ^ by) for i in range(wide)])  35.4 us
    ppermute x31, waiting for transfers between devices, across(): return lax.ppermute(array, 'wide', [(i, i ^ by) for i in range(wide)])  32.5 us
  transfers between devices with their start and end apart: 41, of which 12 were waited for; matrix products, arithmetic and copies ran while one was open for 16% of the time, Pallas kernels for 55%

profile of v8, /device:TPU:0, one launch (start us, length us, event | category | flops | bytes accessed | tf_op | source)
XLA Modules:
  0.0 600.8 jit_solution(1266869581935746911)
XLA Ops:
  10.4 7.1 %own_columns.1.refs_2_ = bf16[1280,1920]{1,0:T(8,128)(2,1)} custom-call(s32[3]{0:T(128)} %add_add_fusion.where, bf16[1280,3840]{1,0:T(8,128)(2,1)} %w.3), custom_call_target="tpu_custom_call" | custom-call | bytes 983040 | tf_op jit(solution)/shard_map/own_columns/pallas_call | solution.py:737
  24.4 13.1 %add_convert_fusion = bf16[2048,1920]{1,0:T(8,128)(2,1)} fusion(f32[1920]{0:T(1024)S(1)} %pad_maximum_fusion.3, bf16[2048,1280]{1,0:T(8,128)(2,1)S(1)} %bitcast.145, bf16[1280,1920]{1,0:T(8,128)(2,1)S(1)} %bitcast.134), kind=kOutput, calls=%fused_computation | convolution fusion | flops 10074193920 | bytes 18030080 | tf_op jit(solution)/shard_map/dot_general | solution.py:29
  38.8 31.6 %attn_fwd_a.1 = (f32[2,640,1024]{2,1,0:T(8,128)}, f32[2,16,1024]{2,1,0:T(8,128)}, f32[2,16,1024]{2,1,0:T(8,128)}) custom-call(s32[2,2,4]{2,1,0:T(2,128)} %get-tuple-element.233.flags, s32[2,1,1024]{2,1,0:T(1,128)} %broadcast_in_dim.42.cq, s32[2,1024,128]{2,1,0:T(8,128)} %broadcast_in_dim.45.ck, bf16[2,1024,1920]{2,1,0:T(8,128)(2,1)} %bitcast.122, ...), custom_call_target="tpu_custom_call" | custom-call | flops 536870912 | bytes 1310720 | tf_op jit(solution)/shard_map/attn_fwd_a/pallas_call | solution.py:165
  70.4 7.8 %collective-permute-done.3 = bf16[1,1024,1280]{2,1,0:T(8,128)(2,1)} collective-permute-done((bf16[1,1024,1280]{2,1,0:T(8,128)(2,1)}, bf16[1,1024,1280]{2,1,0:T(8,128)(2,1)}, u32[]{:S(2)}, u32[]{:S(2)}) %collective-permute-start.3) | collective-permute-done | bytes 2621472 | tf_op jit(solution)/shard_map/ppermute | solution.py:886
  78.2 20.2 %convolution_convert_fusion.d_act = bf16[1024,5120]{1,0:T(8,128)(2,1)} fusion(bf16[1024,1280]{1,0:T(8,128)(2,1)} %bitcast.6.rest_4_.b1, bf16[5120,1280]{1,0:T(8,128)(2,1)} %refs_1_.1), kind=kOutput, calls=%fused_computation.2 | convolution fusion | flops 13427015680 | bytes 26214400 | tf_op jit(solution)/shard_map/dot_general | solution.py:29
  101.5 8.7 %add_convert_fusion.1 = bf16[2048,1280]{1,0:T(8,128)(2,1)} fusion(bf16[2048,1280]{1,0:T(8,128)(2,1)S(1)} %bitcast.148, f32[1280]{0:T(1024)S(1)} %concatenate.50, bf16[1280,1920]{1,0:T(8,128)(2,1)S(1)} %bitcast.134), kind=kOutput, calls=%fused_computation.1 | convolution fusion | flops 6716129280 | bytes 13770752 | tf_op jit(solution)/shard_map/dot_general | solution.py:29
  111.4 27.0 %attn_fwd_b.1 = (bf16[1,1024,640]{2,1,0:T(8,128)(2,1)}, bf16[1,1024,640]{2,1,0:T(8,128)(2,1)}, f32[2,16,1024]{2,1,0:T(8,128)}) custom-call(s32[2,2,4]{2,1,0:T(2,128)} %get-tuple-element.234.flags, s32[2,1,1024]{2,1,0:T(1,128)} %broadcast_in_dim.42.cq, s32[2,1024,128]{2,1,0:T(8,128)} %broadcast_in_dim.43.ck, bf16[2,1024,1920]{2,1,0:T(8,128)(2,1)} %bitcast.125, ...), custom_call_target="tpu_custom_call" | custom-call | flops 536870912 | bytes 1310720 | tf_op jit(solution)/shard_map/attn_fwd_b/pallas_call | solution.py:165
  153.2 23.8 %ffn_theirs.1 = (bf16[1024,5120]{1,0:T(8,128)(2,1)}, bf16[1024,2560]{1,0:T(8,128)(2,1)}, f32[1,5120]{1,0:T(1,128)}, f32[1024,1280]{1,0:T(8,128)}) custom-call(s32[3]{0:T(128)} %add_add_fusion.where, bf16[1024,1280]{1,0:T(8,128)(2,1)} %add_convert_fusion.3.acts.refs_0_, bf16[1280,5120]{1,0:T(8,128)(2,1)} %w.5, f32[1,5120]{1,0:T(1,128)} %bitcast.169, ...), custom_call_target="tpu_custom_call" | custom-call | flops 1342177280 | bytes 2490368 | tf_op jit(solution)/shard_map/ffn_theirs/pallas_call | solution.py:418
  178.2 30.2 %ffn_mine.1 = (bf16[1024,5120]{1,0:T(8,128)(2,1)}, bf16[1024,2560]{1,0:T(8,128)(2,1)}, f32[1,5120]{1,0:T(1,128)}, f32[1024,1280]{1,0:T(8,128)}, bf16[1024,1280]{...) custom-call(s32[3]{0:T(128)} %add_add_fusion.where, ...), custom_call_target="tpu_custom_call", output_to_operand_aliasing={{0}: (5, {}), {2}: (6, {})} | custom-call | flops 1342177280 | bytes 2490368 | tf_op jit(solution)/shard_map/ffn_mine/pallas_call | solution.py:418
  210.8 20.5 %grad_in.1 = (bf16[4,160,2560]{2,1,0:T(8,128)(2,1)}, bf16[4,160,2560]{2,1,0:T(8,128)(2,1)}) custom-call(s32[3]{0:T(128)} %add_add_fusion.where, bf16[1024,1280]{1,0:T(8,128)(2,1)} %add_convert_fusion.3.acts.refs_0_, bf16[1024,2560]{1,0:T(8,128)(2,1)} %get-tuple-element.121.refs_1_, bf16[1024,1280]{1,0:T(8,128)(2,1)} %collective-permute-done.9.refs_2_, ...), custom_call_target="tpu_custom_call" | custom-call | flops 1342177280 | bytes 2228224 | tf_op jit(solution)/shard_map/grad_in/pallas_call | solution.py:491
  231.3 5.5 collective-permute-start.13
  238.6 5.4 collective-permute-done.11.refs_3_.refs_7_
  244.0 23.0 %grad_back.1 = (bf16[2,4,400,640]{3,2,1,0:T(8,128)(2,1)}, bf16[2,4,400,640]{3,2,1,0:T(8,128)(2,1)}) custom-call(s32[3]{0:T(128)} %add_add_fusion.where, bf16[1024,5120]{1,0:T(8,128)(2,1)} %get-tuple-element.166.a1.refs_0_, bf16[1024,1280]{1,0:T(8,128)(2,1)} %bitcast.6.rest_4_.b1, bf16[1024,5120]{1,0:T(8,128)(2,1)} %collective-permute-done.10.a2, ...), custom_call_target="tpu_custom_call" | custom-call | flops 1342177280 | bytes 3014656 | tf_op jit(solution)/shard_map/grad_back/pallas_call | solution.py:584
  266.9 10.6 %grad_out.1 = (bf16[2,4,400,640]{3,2,1,0:T(8,128)(2,1)}, bf16[2,4,400,640]{3,2,1,0:T(8,128)(2,1)}) custom-call(s32[3]{0:T(128)} %add_add_fusion.1.where, bf16[1024,640]{1,0:T(8,128)(2,1)} %bitcast.156, bf16[1024,1280]{1,0:T(8,128)(2,1)} %get-tuple-element.120.refs_1_.refs_5_, ...), custom_call_target="tpu_custom_call", output_to_operand_aliasing={{0}: (9, {}), {1}: (10, {})} | custom-call | flops 335544320 | bytes 950272 | tf_op jit(solution)/shard_map/grad_out/pallas_call | solution.py:491
  279.7 36.2 %attn_bwd_far.1 = (f32[2,640,1024]{2,1,0:T(8,128)}, bf16[2,1024,768]{2,1,0:T(8,128)(2,1)}, bf16[2,1024,512]{2,1,0:T(8,128)(2,1)}) custom-call(s32[2,4,4]{2,1,0:T(4,128)} %get-tuple-element.231.flags, s32[2,1,1024]{2,1,0:T(1,128)} %broadcast_in_dim.42.cq, s32[2,1024,128]{2,1,0:T(8,128)} %broadcast_in_dim.43.ck, bf16[2,1024,1920]{2,1,0:T(8,128)(2,1)} %bitcast.126, ...), custom_call_target="tpu_custom_call" | custom-call | flops 1342177280 | bytes 2359296 | tf_op jit(solution)/shard_map/attn_bwd_far/pallas_call | solution.py:264
  318.7 8.7 %far_norm_theirs.1 = bf16[1024,1280]{1,0:T(8,128)(2,1)} custom-call(bf16[2048,768]{1,0:T(8,128)(2,1)} %bitcast.152, bf16[2048,512]{1,0:T(8,128)(2,1)} %bitcast.159, bf16[1280,1920]{1,0:T(8,128)(2,1)} %own_columns.1.refs_2_), custom_call_target="tpu_custom_call" | custom-call | flops 335544320 | bytes 851968 | tf_op jit(solution)/shard_map/far_norm_theirs/pallas_call | solution.py:796
  327.4 9.5 %collective-permute-start.16 = (bf16[2,160,2560]{2,1,0:T(8,128)(2,1)S(1)}, bf16[2,160,2560]{2,1,0:T(8,128)(2,1)}, u32[]{:S(2)}, u32[]{:S(2)}) collective-permute-start(bf16[2,160,2560]{2,1,0:T(8,128)(2,1)S(1)} %get-tuple-element.200), channel_id=1, source_target_pairs={{0,16},{2,18},{4,20},{6,22},{8,24},{10,26},{12,28},{14,30},{16,0},... | collective-permute-start | bytes 4915208 | tf_op jit(solution)/shard_map/ppermute | solution.py:880
  336.9 8.3 %far_norm_mine.1 = bf16[1024,1280]{1,0:T(8,128)(2,1)} custom-call(bf16[2048,768]{1,0:T(8,128)(2,1)} %bitcast.153, bf16[2048,512]{1,0:T(8,128)(2,1)} %bitcast.160, bf16[1280,1920]{1,0:T(8,128)(2,1)} %own_columns.1.refs_2_), custom_call_target="tpu_custom_call" | custom-call | flops 335544320 | bytes 851968 | tf_op jit(solution)/shard_map/far_norm_mine/pallas_call | solution.py:796
  345.1 3.9 fusion.10
  350.3 37.7 %attn_bwd_early.1 = bf16[2,1024,1152]{2,1,0:T(8,128)(2,1)} custom-call(s32[2,4,4]{2,1,0:T(4,128)} %get-tuple-element.232.flags, s32[2,1,1024]{2,1,0:T(1,128)} %broadcast_in_dim.42.cq, s32[2,1024,128]{2,1,0:T(8,128)} %broadcast_in_dim.45.ck, bf16[2,1024,1920]{2,1,0:T(8,128)(2,1)} %bitcast.127, bf16[2,1024,1920]{2,1,0:T(8,128)(2,1)} %bitcast.128, ...), custom_call_target="tpu_custom_call" | custom-call | flops 805306368 | bytes 1415577 | tf_op jit(solution)/shard_map/attn_bwd_early/pallas_call | solution.py:264
  388.0 5.2 fusion.11
  393.2 15.4 %collective-permute-done.16 = bf16[2,160,2560]{2,1,0:T(8,128)(2,1)} collective-permute-done((bf16[2,160,2560]{2,1,0:T(8,128)(2,1)S(1)}, bf16[2,160,2560]{2,1,0:T(8,128)(2,1)}, u32[]{:S(2)}, u32[]{:S(2)}) %collective-permute-start.16) | collective-permute-done | bytes 1638432 | tf_op jit(solution)/shard_map/ppermute | solution.py:880
  410.5 22.0 %grad_early.1 = (bf16[2,4,80,1152]{3,2,1,0:T(8,128)(2,1)}, bf16[2,4,80,1152]{3,2,1,0:T(8,128)(2,1)}, f32[1,1152]{1,0:T(1,128)}) custom-call(s32[3]{0:T(128)} %add_add_fusion.where, bf16[2048,1280]{1,0:T(8,128)(2,1)} %bitcast.146, bf16[2048,1152]{1,0:T(8,128)(2,1)} %bitcast.139, bf16[2048,1280]{1,0:T(8,128)(2,1)} %bitcast.149, bf16[2048,768]{1,0:T(8,128)(2,1)} %bitcast.154), custom_call_target="tpu_custom_call" | custom-call | flops 1207959552 | bytes 2287206 | tf_op jit(solution)/shard_map/grad_early/pallas_call | solution.py:542
  434.8 28.2 %attn_bwd_late.1 = bf16[2,1024,768]{2,1,0:T(8,128)(2,1)} custom-call(s32[2,4,4]{2,1,0:T(4,128)} %get-tuple-element.232.flags, s32[2,1,1024]{2,1,0:T(1,128)} %broadcast_in_dim.42.cq, s32[2,1024,128]{2,1,0:T(8,128)} %broadcast_in_dim.45.ck, bf16[2,1024,1920]{2,1,0:T(8,128)(2,1)} %bitcast.130, bf16[2,1024,1920]{2,1,0:T(8,128)(2,1)} %bitcast.131, ...), custom_call_target="tpu_custom_call" | custom-call | flops 536870912 | bytes 943718 | tf_op jit(solution)/shard_map/attn_bwd_late/pallas_call | solution.py:264
  464.6 3.7 collective-permute-done.19
  482.1 14.8 %grad_late.1 = (bf16[2,4,80,768]{3,2,1,0:T(8,128)(2,1)}, bf16[2,4,80,768]{3,2,1,0:T(8,128)(2,1)}, f32[1,768]{1,0:T(1,128)}) custom-call(s32[3]{0:T(128)} %add_add_fusion.where, bf16[2048,1280]{1,0:T(8,128)(2,1)} %bitcast.147, bf16[2048,768]{1,0:T(8,128)(2,1)} %bitcast.142, bf16[2048,1280]{1,0:T(8,128)(2,1)} %bitcast.150, bf16[2048,512]{1,0:T(8,128)(2,1)} %bitcast.161), custom_call_target="tpu_custom_call" | custom-call | flops 805306368 | bytes 1874329 | tf_op jit(solution)/shard_map/grad_late/pallas_call | solution.py:542
  497.0 10.3 %near_norm_theirs.1 = bf16[1024,1280]{1,0:T(8,128)(2,1)} custom-call(bf16[2048,1152]{1,0:T(8,128)(2,1)} %bitcast.140, bf16[2048,768]{1,0:T(8,128)(2,1)} %bitcast.143, bf16[1280,1920]{1,0:T(8,128)(2,1)} %own_columns.1.refs_2_), custom_call_target="tpu_custom_call" | custom-call | flops 503316480 | bytes 1146880 | tf_op jit(solution)/shard_map/near_norm_theirs/pallas_call | solution.py:796
  507.3 10.2 %near_norm_mine.1.rest_0_ = bf16[1024,1280]{1,0:T(8,128)(2,1)} custom-call(bf16[2048,1152]{1,0:T(8,128)(2,1)} %bitcast.141, bf16[2048,768]{1,0:T(8,128)(2,1)} %bitcast.144, bf16[1280,1920]{1,0:T(8,128)(2,1)} %own_columns.1.refs_2_), custom_call_target="tpu_custom_call" | custom-call | flops 503316480 | bytes 1146880 | tf_op jit(solution)/shard_map/near_norm_mine/pallas_call | solution.py:796
  527.1 21.0 %mixed.1 = bf16[1024,1280]{1,0:T(8,128)(2,1)} custom-call(bf16[1024,5120]{1,0:T(8,128)(2,1)} %get-tuple-element.166.a1.refs_0_, bf16[5120,1280]{1,0:T(8,128)(2,1)} %refs_1_.1, f32[1024,1280]{1,0:T(8,128)} %copy-done.1, f32[1,1280]{1,0:T(1,128)} %reshape.287.refs_3_), custom_call_target="tpu_custom_call" | custom-call | flops 1342177280 | bytes 2621440 | tf_op jit(solution)/shard_map/mixed/pallas_call | solution.py:796
  554.7 11.7 %first_norm.1 = (f32[1024,1280]{1,0:T(8,128)}, f32[8,1280]{1,0:T(8,128)}) custom-call(bf16[1024,1280]{1,0:T(8,128)(2,1)} %bitcast.151, f32[1024,1280]{1,0:T(8,128)} %get-tuple-element.167.d_middle, f32[1,1280]{1,0:T(1,128)} %broadcast_in_dim.50.gain, bf16[1024,1280]{1,0:T(8,128)(2,1)} %near_norm_mine.1.rest_0_, ...), custom_call_target="tpu_custom_call" | custom-call | flops 2621440 | bytes 2621440 | tf_op jit(solution)/shard_map/first_norm/pallas_call | solution.py:635
  579.2 4.2 collective-permute-done.38
  586.6 4.8 collective-permute-done.39.q_row
  (229 shorter events, 108.9 us)
Async XLA Ops:
  9.6 10.3 %collective-permute-start.2 = (bf16[1,1024,1280]{2,1,0:T(8,128)(2,1)}, bf16[1,1024,1280]{2,1,0:T(8,128)(2,1)}, u32[]{:S(2)}, u32[]{:S(2)}) collective-permute-start(bf16[1,1024,1280]{2,1,0:T(8,128)(2,1)} %fusion.8), channel_id=1, source_target_pairs={{0,2},{2,0},{4,6},{6,4},{8,10},{10,8},{12,14},{14,12},{16,18},{18,... | collective-permute-start | bytes 7864328 | tf_op jit(solution)/shard_map/ppermute | solution.py:880
  18.5 59.7 %collective-permute-start.3 = (bf16[1,1024,1280]{2,1,0:T(8,128)(2,1)}, bf16[1,1024,1280]{2,1,0:T(8,128)(2,1)}, u32[]{:S(2)}, u32[]{:S(2)}) collective-permute-start(bf16[1,1024,1280]{2,1,0:T(8,128)(2,1)} %fusion.8), channel_id=1, source_target_pairs={{1,0},{0,1},{3,2},{2,3},{5,4},{4,5},{7,6},{6,7},{9,8},{8,9},{11,10... | collective-permute-start | bytes 7864328 | tf_op jit(solution)/shard_map/ppermute | solution.py:886
  23.1 55.1 %collective-permute-start.5 = (bf16[1024,1280]{1,0:T(8,128)(2,1)}, bf16[1024,1280]{1,0:T(8,128)(2,1)}, u32[]{:S(2)}, u32[]{:S(2)}) collective-permute-start(bf16[1024,1280]{1,0:T(8,128)(2,1)} %bitcast.6.rest_4_.b1), channel_id=1, source_target_pairs={{0,2},{2,0},{4,6},{6,4},{8,10},{10,8},{12,14},{14,12},{16,18},{18,... | collective-permute-start | bytes 7864328 | tf_op jit(solution)/shard_map/ppermute | solution.py:880
  78.2 20.2 %collective-permute-start.4 = (bf16[1,1024,1280]{2,1,0:T(8,128)(2,1)}, bf16[1,1024,1280]{2,1,0:T(8,128)(2,1)}, u32[]{:S(2)}, u32[]{:S(2)}) collective-permute-start(bf16[1,1024,1280]{2,1,0:T(8,128)(2,1)} %collective-permute-done.3), channel_id=1, source_target_pairs={{0,2},{2,0},{4,6},{6,4},{8,10},{10,8},{12,14},{14,12},{16,18},{18,... | collective-permute-start | bytes 7864328 | tf_op jit(solution)/shard_map/ppermute | solution.py:880
  139.0 13.2 %collective-permute-start.7 = (bf16[1024,640]{1,0:T(8,128)(2,1)}, bf16[1024,640]{1,0:T(8,128)(2,1)S(1)}, u32[]{:S(2)}, u32[]{:S(2)}) collective-permute-start(bf16[1024,640]{1,0:T(8,128)(2,1)} %bitcast.155), channel_id=1, source_target_pairs={{0,2},{2,0},{4,6},{6,4},{8,10},{10,8},{12,14},{14,12},{16,18},{18,... | collective-permute-start | bytes 3932168 | tf_op jit(solution)/shard_map/ppermute | solution.py:880
  177.1 31.4 %collective-permute-start.8 = (bf16[1024,2560]{1,0:T(8,128)(2,1)}, bf16[1024,2560]{1,0:T(8,128)(2,1)S(1)}, u32[]{:S(2)}, u32[]{:S(2)}) collective-permute-start(bf16[1024,2560]{1,0:T(8,128)(2,1)} %get-tuple-element.118), channel_id=1, source_target_pairs={{0,2},{2,0},{4,6},{6,4},{8,10},{10,8},{12,14},{14,12},{16,18},{18,... | collective-permute-start | bytes 15728648 | tf_op jit(solution)/shard_map/ppermute | solution.py:880
  177.4 31.1 %collective-permute-start.9 = (bf16[1024,1280]{1,0:T(8,128)(2,1)S(1)}, bf16[1024,1280]{1,0:T(8,128)(2,1)}, u32[]{:S(2)}, u32[]{:S(2)}) collective-permute-start(bf16[1024,1280]{1,0:T(8,128)(2,1)S(1)} %copy-done.6), channel_id=1, source_target_pairs={{0,2},{2,0},{4,6},{6,4},{8,10},{10,8},{12,14},{14,12},{16,18},{18,... | collective-permute-start | bytes 7864328 | tf_op jit(solution)/shard_map/ppermute | solution.py:880
  208.5 35.4 %collective-permute-start.10 = (bf16[1024,5120]{1,0:T(8,128)(2,1)}, bf16[1024,5120]{1,0:T(8,128)(2,1)}, u32[]{:S(2)}, u32[]{:S(2)}) collective-permute-start(bf16[1024,5120]{1,0:T(8,128)(2,1)} %get-tuple-element.166.a1.refs_0_), channel_id=1, source_target_pairs={{0,2},{2,0},{4,6},{6,4},{8,10},{10,8},{12,14},{14,12},{16,18},{18,... | collective-permute-start | bytes 31457288 | tf_op jit(solution)/shard_map/ppermute | solution.py:880
  231.3 84.6 %collective-permute-start.13 = (bf16[4,160,2560]{2,1,0:T(8,128)(2,1)}, bf16[4,160,2560]{2,1,0:T(8,128)(2,1)}, u32[]{:S(2)}, u32[]{:S(2)}) collective-permute-start(bf16[4,160,2560]{2,1,0:T(8,128)(2,1)} %get-tuple-element.123), channel_id=1, source_target_pairs={{0,4},{2,6},{4,0},{6,2},{8,12},{10,14},{12,8},{14,10},{16,20},{18,... | collective-permute-start | bytes 9830408 | tf_op jit(solution)/shard_map/ppermute | solution.py:880
  236.8 7.1 %collective-permute-start.11 = (bf16[1024,1280]{1,0:T(8,128)(2,1)}, bf16[1024,1280]{1,0:T(8,128)(2,1)}, u32[]{:S(2)}, u32[]{:S(2)}) collective-permute-start(bf16[1024,1280]{1,0:T(8,128)(2,1)} %get-tuple-element.120.refs_1_.refs_5_), channel_id=1, source_target_pairs={{0,2},{2,0},{4,6},{6,4},{8,10},{10,8},{12,14},{14,12},{16,18},{18,... | collective-permute-start | bytes 7864328 | tf_op jit(solution)/shard_map/ppermute | solution.py:880
  236.8 41.8 %collective-permute-start.12 = (bf16[1024,640]{1,0:T(8,128)(2,1)}, bf16[1024,640]{1,0:T(8,128)(2,1)S(1)}, u32[]{:S(2)}, u32[]{:S(2)}) collective-permute-start(bf16[1024,640]{1,0:T(8,128)(2,1)} %get-tuple-element.126), channel_id=1, source_target_pairs={{0,2},{2,0},{4,6},{6,4},{8,10},{10,8},{12,14},{14,12},{16,18},{18,... | collective-permute-start | bytes 3932168 | tf_op jit(solution)/shard_map/ppermute | solution.py:880
  277.5 110.5 %collective-permute-start.15 = (bf16[2,4,400,640]{3,2,1,0:T(8,128)(2,1)}, bf16[2,4,400,640]{3,2,1,0:T(8,128)(2,1)}, u32[]{:S(2)}, u32[]{:S(2)}) collective-permute-start(bf16[2,4,400,640]{3,2,1,0:T(8,128)(2,1)} %get-tuple-element.132), channel_id=1, source_target_pairs={{1,0},{0,1},{3,2},{2,3},{5,4},{4,5},{7,6},{6,7},{9,8},{8,9},{11,10... | collective-permute-start | bytes 12288008 | tf_op jit(solution)/shard_map/ppermute | solution.py:886
  327.4 17.7 %collective-permute-start.14 = (bf16[1024,1280]{1,0:T(8,128)(2,1)}, bf16[1024,1280]{1,0:T(8,128)(2,1)S(1)}, u32[]{:S(2)}, u32[]{:S(2)}) collective-permute-start(bf16[1024,1280]{1,0:T(8,128)(2,1)} %far_norm_theirs.1), channel_id=1, source_target_pairs={{0,2},{2,0},{4,6},{6,4},{8,10},{10,8},{12,14},{14,12},{16,18},{18,... | collective-permute-start | bytes 7864328 | tf_op jit(solution)/shard_map/ppermute | solution.py:880
  327.4 81.2 %collective-permute-start.16 = (bf16[2,160,2560]{2,1,0:T(8,128)(2,1)S(1)}, bf16[2,160,2560]{2,1,0:T(8,128)(2,1)}, u32[]{:S(2)}, u32[]{:S(2)}) collective-permute-start(bf16[2,160,2560]{2,1,0:T(8,128)(2,1)S(1)} %get-tuple-element.200), channel_id=1, source_target_pairs={{0,16},{2,18},{4,20},{6,22},{8,24},{10,26},{12,28},{14,30},{16,0},... | collective-permute-start | bytes 4915208 | tf_op jit(solution)/shard_map/ppermute | solution.py:880
  349.0 83.8 %collective-permute-start.17 = (bf16[1,1024,1280]{2,1,0:T(8,128)(2,1)}, bf16[1,1024,1280]{2,1,0:T(8,128)(2,1)}, u32[]{:S(2)}, u32[]{:S(2)}) collective-permute-start(bf16[1,1024,1280]{2,1,0:T(8,128)(2,1)} %fusion.10), channel_id=1, source_target_pairs={{0,1},{1,0},{2,3},{3,2},{4,5},{5,4},{6,7},{7,6},{8,9},{9,8},{10,11... | collective-permute-start | bytes 7864328 | tf_op jit(solution)/shard_map/ppermute | solution.py:889
  410.3 22.2 %collective-permute-start.18 = (bf16[160,2560]{1,0:T(8,128)(2,1)S(1)}, bf16[160,2560]{1,0:T(8,128)(2,1)S(1)}, u32[]{:S(2)}, u32[]{:S(2)}) collective-permute-start(bf16[160,2560]{1,0:T(8,128)(2,1)S(1)} %get-tuple-element.204), channel_id=1, source_target_pairs={{0,8},{2,10},{4,12},{6,14},{8,0},{10,2},{12,4},{14,6},{16,24},{18,... | collective-permute-start | bytes 2457608 | tf_op jit(solution)/shard_map/ppermute | solution.py:880
  410.4 52.7 %collective-permute-start.20 = (bf16[4,400,640]{2,1,0:T(8,128)(2,1)}, bf16[4,400,640]{2,1,0:T(8,128)(2,1)S(1)}, u32[]{:S(2)}, u32[]{:S(2)}) collective-permute-start(bf16[4,400,640]{2,1,0:T(8,128)(2,1)} %get-tuple-element.198), channel_id=1, source_target_pairs={{0,4},{2,6},{4,0},{6,2},{8,12},{10,14},{12,8},{14,10},{16,20},{18,... | collective-permute-start | bytes 6144008 | tf_op jit(solution)/shard_map/ppermute | solution.py:880
  432.8 35.5 %collective-permute-start.19 = (bf16[2,4,80,1152]{3,2,1,0:T(8,128)(2,1)}, bf16[2,4,80,1152]{3,2,1,0:T(8,128)(2,1)}, u32[]{:S(2)}, u32[]{:S(2)}) collective-permute-start(bf16[2,4,80,1152]{3,2,1,0:T(8,128)(2,1)} %get-tuple-element.152), channel_id=1, source_target_pairs={{1,0},{0,1},{3,2},{2,3},{5,4},{4,5},{7,6},{6,7},{9,8},{8,9},{11,10... | collective-permute-start | bytes 4423688 | tf_op jit(solution)/shard_map/ppermute | solution.py:886
  433.6 83.9 %collective-permute-start.24 = (bf16[160,2560]{1,0:T(8,128)(2,1)S(1)}, bf16[160,2560]{1,0:T(8,128)(2,1)S(1)}, u32[]{:S(2)}, u32[]{:S(2)}) collective-permute-start(bf16[160,2560]{1,0:T(8,128)(2,1)S(1)} %add_convert_fusion.8.in_mine), channel_id=1, source_target_pairs={{1,0},{0,1},{3,2},{2,3},{5,4},{4,5},{7,6},{6,7},{9,8},{8,9},{11,10... | collective-permute-start | bytes 2457608 | tf_op jit(solution)/shard_map/ppermute | solution.py:886
  470.9 46.7 %collective-permute-start.21 = (bf16[4,80,1152]{2,1,0:T(8,128)(2,1)}, bf16[4,80,1152]{2,1,0:T(8,128)(2,1)}, u32[]{:S(2)}, u32[]{:S(2)}) collective-permute-start(bf16[4,80,1152]{2,1,0:T(8,128)(2,1)} %get-tuple-element.206), channel_id=1, source_target_pairs={{0,4},{2,6},{4,0},{6,2},{8,12},{10,14},{12,8},{14,10},{16,20},{18,... | collective-permute-start | bytes 2211848 | tf_op jit(solution)/shard_map/ppermute | solution.py:880
  473.0 46.9 %collective-permute-start.22 = (bf16[2,400,640]{2,1,0:T(8,128)(2,1)}, bf16[2,400,640]{2,1,0:T(8,128)(2,1)}, u32[]{:S(2)}, u32[]{:S(2)}) collective-permute-start(bf16[2,400,640]{2,1,0:T(8,128)(2,1)} %get-tuple-element.202), channel_id=1, source_target_pairs={{0,16},{2,18},{4,20},{6,22},{8,24},{10,26},{12,28},{14,30},{16,0},... | collective-permute-start | bytes 3072008 | tf_op jit(solution)/shard_map/ppermute | solution.py:880
  496.9 25.2 %collective-permute-start.23 = (bf16[2,4,80,768]{3,2,1,0:T(8,128)(2,1)}, bf16[2,4,80,768]{3,2,1,0:T(8,128)(2,1)S(1)}, u32[]{:S(2)}, u32[]{:S(2)}) collective-permute-start(bf16[2,4,80,768]{3,2,1,0:T(8,128)(2,1)} %get-tuple-element.159), channel_id=1, source_target_pairs={{1,0},{0,1},{3,2},{2,3},{5,4},{4,5},{7,6},{6,7},{9,8},{8,9},{11,10... | collective-permute-start | bytes 2949128 | tf_op jit(solution)/shard_map/ppermute | solution.py:886
  517.5 37.2 %collective-permute-start.25 = (bf16[1024,1280]{1,0:T(8,128)(2,1)}, bf16[1024,1280]{1,0:T(8,128)(2,1)}, u32[]{:S(2)}, u32[]{:S(2)}) collective-permute-start(bf16[1024,1280]{1,0:T(8,128)(2,1)} %near_norm_theirs.1), channel_id=1, source_target_pairs={{0,2},{2,0},{4,6},{6,4},{8,10},{10,8},{12,14},{14,12},{16,18},{18,... | collective-permute-start | bytes 7864328 | tf_op jit(solution)/shard_map/ppermute | solution.py:880
  523.1 24.9 %collective-permute-start.26 = (bf16[4,80,768]{2,1,0:T(8,128)(2,1)}, bf16[4,80,768]{2,1,0:T(8,128)(2,1)}, u32[]{:S(2)}, u32[]{:S(2)}) collective-permute-start(bf16[4,80,768]{2,1,0:T(8,128)(2,1)} %get-tuple-element.211), channel_id=1, source_target_pairs={{0,4},{2,6},{4,0},{6,2},{8,12},{10,14},{12,8},{14,10},{16,20},{18,... | collective-permute-start | bytes 1474568 | tf_op jit(solution)/shard_map/ppermute | solution.py:880
  523.6 28.2 %collective-permute-start.27 = (bf16[2,80,1152]{2,1,0:T(8,128)(2,1)}, bf16[2,80,1152]{2,1,0:T(8,128)(2,1)S(1)}, u32[]{:S(2)}, u32[]{:S(2)}) collective-permute-start(bf16[2,80,1152]{2,1,0:T(8,128)(2,1)} %get-tuple-element.212), channel_id=1, source_target_pairs={{0,16},{2,18},{4,20},{6,22},{8,24},{10,26},{12,28},{14,30},{16,0},... | collective-permute-start | bytes 1105928 | tf_op jit(solution)/shard_map/ppermute | solution.py:880
  526.4 26.1 %collective-permute-start.28 = (bf16[400,640]{1,0:T(8,128)(2,1)}, bf16[400,640]{1,0:T(8,128)(2,1)S(1)}, u32[]{:S(2)}, u32[]{:S(2)}) collective-permute-start(bf16[400,640]{1,0:T(8,128)(2,1)} %get-tuple-element.208), channel_id=1, source_target_pairs={{0,8},{2,10},{4,12},{6,14},{8,0},{10,2},{12,4},{14,6},{16,24},{18,... | collective-permute-start | bytes 1536008 | tf_op jit(solution)/shard_map/ppermute | solution.py:880
  550.0 23.2 %collective-permute-start.37 = (bf16[2,80,768]{2,1,0:T(8,128)(2,1)}, bf16[2,80,768]{2,1,0:T(8,128)(2,1)}, u32[]{:S(2)}, u32[]{:S(2)}) collective-permute-start(bf16[2,80,768]{2,1,0:T(8,128)(2,1)} %get-tuple-element.214), channel_id=1, source_target_pairs={{0,16},{2,18},{4,20},{6,22},{8,24},{10,26},{12,28},{14,30},{16,0},... | collective-permute-start | bytes 737288 | tf_op jit(solution)/shard_map/ppermute | solution.py:880
  552.5 14.8 %collective-permute-start.36 = (bf16[80,1152]{1,0:T(8,128)(2,1)S(1)}, bf16[80,1152]{1,0:T(8,128)(2,1)}, u32[]{:S(2)}, u32[]{:S(2)}) collective-permute-start(bf16[80,1152]{1,0:T(8,128)(2,1)S(1)} %get-tuple-element.216), channel_id=1, source_target_pairs={{0,8},{2,10},{4,12},{6,14},{8,0},{10,2},{12,4},{14,6},{16,24},{18,... | collective-permute-start | bytes 552968 | tf_op jit(solution)/shard_map/ppermute | solution.py:880
  552.6 33.9 %collective-permute-start.35 = (bf16[400,640]{1,0:T(8,128)(2,1)S(1)}, bf16[400,640]{1,0:T(8,128)(2,1)S(1)}, u32[]{:S(2)}, u32[]{:S(2)}) collective-permute-start(bf16[400,640]{1,0:T(8,128)(2,1)S(1)} %add_convert_fusion.13.b_mine), channel_id=1, source_target_pairs={{1,0},{0,1},{3,2},{2,3},{5,4},{4,5},{7,6},{6,7},{9,8},{8,9},{11,10... | collective-permute-start | bytes 1536008 | tf_op jit(solution)/shard_map/ppermute | solution.py:886
  567.7 5.5 collective-permute-start.29
  569.9 5.5 collective-permute-start.31
  584.4 6.9 %collective-permute-start.39 = (bf16[80,1920]{1,0:T(8,128)(2,1)S(1)}, bf16[80,1920]{1,0:T(8,128)(2,1)S(1)}, u32[]{:S(2)}, u32[]{:S(2)}) collective-permute-start(bf16[80,1920]{1,0:T(8,128)(2,1)S(1)} %pad_maximum_fusion.2.q_mine), channel_id=1, source_target_pairs={{1,0},{0,1},{3,2},{2,3},{5,4},{4,5},{7,6},{6,7},{9,8},{8,9},{11,10... | collective-permute-start | bytes 921608 | tf_op jit(solution)/shard_map/ppermute | solution.py:886
  (43 other events, 431.5 us)

commit v9 on v8

--- a/solution.py
+++ b/solution.py
@@ -727,21 +727,33 @@
     )(where, kept, other)
 
 
-def own_kernel(where, w, out):
-    out[...] = w[...]
+def own_kernel(where, w, out, sems):
+    width = w.shape[1] // 6
+    copies = []
+    for part in range(3):
+        first = pl.multiple_of((2 * part + where[1]) * width, 128)
+        copies.append(
+            pltpu.make_async_copy(
+                w.at[:, pl.ds(first, width)], out.at[:, pl.ds(part * width, width)], sems.at[part]
+            )
+        )
+    for copy in copies:
+        copy.start()
+    for copy in copies:
+        copy.wait()
 
 
 def own_columns_call(where, w):
     depth, width = w.shape
-    tile = width // 6
     return pl.pallas_call(
         own_kernel,
         out_shape=jax.ShapeDtypeStruct((depth, width // 2), w.dtype),
         grid_spec=pltpu.PrefetchScalarGridSpec(
             num_scalar_prefetch=1,
-            grid=(2, 3),
-            in_specs=[pl.BlockSpec((depth // 2, tile), lambda j, i, where: (j, 2 * i + where[1]))],
-            out_specs=pl.BlockSpec((depth // 2, tile), lambda j, i, where: (j, i)),
+            grid=(1,),
+            in_specs=[pl.BlockSpec(memory_space=pl.ANY)],
+            out_specs=pl.BlockSpec(memory_space=pl.ANY),
+            scratch_shapes=[pltpu.SemaphoreType.DMA((3,))],
         ),
         compiler_params=pltpu.CompilerParams(vmem_limit_bytes=VMEM_LIMIT),
         cost_estimate=pl.CostEstimate(flops=0, bytes_accessed=2 * depth * width // SHARE, transcendentals=0),

time: 602 us -> 746 us (1.24)
  Pallas kernels: 387 us -> 532 us
    pallas_call x1, Pallas kernels: 7.14 us -> 151 us  [own_columns_call(): pl.pallas_call(own_kernel, out_shape=jax.ShapeDtypeStruct((depth, width /...]
    ppermute x31, starting transfers between devices: 35.4 us -> 27.7 us  [across(): return lax.ppermute(array, 'wide', [(i, i ^ by) for i in range(wide)])]
  transfers between devices with their start and end apart: 41 -> 41, of which waited for: 12 -> 12; matrix products, arithmetic and copies ran while one was open for 16% -> 13% of each run, Pallas kernels for 55% -> 64%
where the time goes in v9:
time: 746 us; the launch traced here: 740 us
  Pallas kernels  532 us (71%)
  waiting for transfers between devices  50.8 us (7%)
  other arithmetic  49.9 us (7%)
  matrix products  48.4 us (6%)
  starting transfers between devices  42.2 us (6%)
  local copies, waits for them, and re-layouts  14.7 us (2%)
    pallas_call x1, Pallas kernels, own_columns_call(): pl.pallas_call(own_kernel, out_shape=jax.ShapeDtypeStruct((depth, width /...  151 us
    pallas_call x3, Pallas kernels, attn_bwd(): pl.pallas_call(functools.partial(bwd_kernel, spans=spans, tq=tq, tk=tk),...  104 us
    pallas_call x5, Pallas kernels, product(): pl.pallas_call(functools.partial(product_kernel, dims=dims, spans=spans),...  58.5 us
    pallas_call x2, Pallas kernels, attn_fwd(): pl.pallas_call(functools.partial(fwd_kernel, first=first, tq=tq, tk=tk, h...  58.3 us
    pallas_call x2, Pallas kernels, ffn_call(): pl.pallas_call(functools.partial(ffn_kernel, last=last), out_shape=out_sh...  54.1 us
    dot_general x5, matrix products, dot(): return lax.dot_general(a, b, dims, preferred_element_type=F32)  48.4 us
    pallas_call x2, Pallas kernels, qkv_call(): pl.pallas_call(functools.partial(qkv_kernel, first=first, second=second,...  36.9 us
    ppermute x31, waiting for transfers between devices, across(): return lax.ppermute(array, 'wide', [(i, i ^ by) for i in range(wide)])  33.8 us
  transfers between devices with their start and end apart: 41, of which 12 were waited for; matrix products, arithmetic and copies ran while one was open for 13% of the time, Pallas kernels for 64%

profile of v9, /device:TPU:0, one launch (start us, length us, event | category | flops | bytes accessed | tf_op | source)
XLA Modules:
  0.0 739.8 jit_solution(18150763023549948084)
XLA Ops:
  10.4 150.7 %own_columns.1.refs_2_ = bf16[1280,1920]{1,0:T(8,128)(2,1)} custom-call(s32[3]{0:T(128)} %add_add_fusion.where, bf16[1280,3840]{1,0:T(8,128)(2,1)} %w.3), custom_call_target="tpu_custom_call" | custom-call | bytes 983040 | tf_op jit(solution)/shard_map/own_columns/pallas_call | solution.py:748
  168.0 13.2 %add_convert_fusion = bf16[2048,1920]{1,0:T(8,128)(2,1)} fusion(f32[1920]{0:T(1024)S(1)} %pad_maximum_fusion.3, bf16[2048,1280]{1,0:T(8,128)(2,1)S(1)} %bitcast.145, bf16[1280,1920]{1,0:T(8,128)(2,1)S(1)} %bitcast.134), kind=kOutput, calls=%fused_computation | convolution fusion | flops 10074193920 | bytes 18030080 | tf_op jit(solution)/shard_map/dot_general | solution.py:29
  182.5 31.3 %attn_fwd_a.1 = (f32[2,640,1024]{2,1,0:T(8,128)}, f32[2,16,1024]{2,1,0:T(8,128)}, f32[2,16,1024]{2,1,0:T(8,128)}) custom-call(s32[2,2,4]{2,1,0:T(2,128)} %get-tuple-element.233.flags, s32[2,1,1024]{2,1,0:T(1,128)} %broadcast_in_dim.42.cq, s32[2,1024,128]{2,1,0:T(8,128)} %broadcast_in_dim.45.ck, bf16[2,1024,1920]{2,1,0:T(8,128)(2,1)} %bitcast.122, ...), custom_call_target="tpu_custom_call" | custom-call | flops 536870912 | bytes 1310720 | tf_op jit(solution)/shard_map/attn_fwd_a/pallas_call | solution.py:165
  213.9 7.9 %collective-permute-done.3 = bf16[1,1024,1280]{2,1,0:T(8,128)(2,1)} collective-permute-done((bf16[1,1024,1280]{2,1,0:T(8,128)(2,1)}, bf16[1,1024,1280]{2,1,0:T(8,128)(2,1)}, u32[]{:S(2)}, u32[]{:S(2)}) %collective-permute-start.3) | collective-permute-done | bytes 2621472 | tf_op jit(solution)/shard_map/ppermute | solution.py:898
  221.8 20.0 %convolution_convert_fusion.d_act = bf16[1024,5120]{1,0:T(8,128)(2,1)} fusion(bf16[1024,1280]{1,0:T(8,128)(2,1)} %bitcast.6.rest_4_.b1, bf16[5120,1280]{1,0:T(8,128)(2,1)} %refs_1_.1), kind=kOutput, calls=%fused_computation.2 | convolution fusion | flops 13427015680 | bytes 26214400 | tf_op jit(solution)/shard_map/dot_general | solution.py:29
  244.8 8.9 %add_convert_fusion.1 = bf16[2048,1280]{1,0:T(8,128)(2,1)} fusion(bf16[2048,1280]{1,0:T(8,128)(2,1)S(1)} %bitcast.148, f32[1280]{0:T(1024)S(1)} %concatenate.50, bf16[1280,1920]{1,0:T(8,128)(2,1)S(1)} %bitcast.134), kind=kOutput, calls=%fused_computation.1 | convolution fusion | flops 6716129280 | bytes 13770752 | tf_op jit(solution)/shard_map/dot_general | solution.py:29
  255.0 27.0 %attn_fwd_b.1 = (bf16[1,1024,640]{2,1,0:T(8,128)(2,1)}, bf16[1,1024,640]{2,1,0:T(8,128)(2,1)}, f32[2,16,1024]{2,1,0:T(8,128)}) custom-call(s32[2,2,4]{2,1,0:T(2,128)} %get-tuple-element.234.flags, s32[2,1,1024]{2,1,0:T(1,128)} %broadcast_in_dim.42.cq, s32[2,1024,128]{2,1,0:T(8,128)} %broadcast_in_dim.43.ck, bf16[2,1024,1920]{2,1,0:T(8,128)(2,1)} %bitcast.125, ...), custom_call_target="tpu_custom_call" | custom-call | flops 536870912 | bytes 1310720 | tf_op jit(solution)/shard_map/attn_fwd_b/pallas_call | solution.py:165
  282.7 3.5 collective-permute-done.6.refs_4_
  296.9 23.8 %ffn_theirs.1 = (bf16[1024,5120]{1,0:T(8,128)(2,1)}, bf16[1024,2560]{1,0:T(8,128)(2,1)}, f32[1,5120]{1,0:T(1,128)}, f32[1024,1280]{1,0:T(8,128)}) custom-call(s32[3]{0:T(128)} %add_add_fusion.where, bf16[1024,1280]{1,0:T(8,128)(2,1)} %add_convert_fusion.3.acts.refs_0_, bf16[1280,5120]{1,0:T(8,128)(2,1)} %w.5, f32[1,5120]{1,0:T(1,128)} %bitcast.169, ...), custom_call_target="tpu_custom_call" | custom-call | flops 1342177280 | bytes 2490368 | tf_op jit(solution)/shard_map/ffn_theirs/pallas_call | solution.py:418
  321.9 30.2 %ffn_mine.1 = (bf16[1024,5120]{1,0:T(8,128)(2,1)}, bf16[1024,2560]{1,0:T(8,128)(2,1)}, f32[1,5120]{1,0:T(1,128)}, f32[1024,1280]{1,0:T(8,128)}, bf16[1024,1280]{...) custom-call(s32[3]{0:T(128)} %add_add_fusion.where, ...), custom_call_target="tpu_custom_call", output_to_operand_aliasing={{0}: (5, {}), {2}: (6, {})} | custom-call | flops 1342177280 | bytes 2490368 | tf_op jit(solution)/shard_map/ffn_mine/pallas_call | solution.py:418
  354.4 20.5 %grad_in.1 = (bf16[4,160,2560]{2,1,0:T(8,128)(2,1)}, bf16[4,160,2560]{2,1,0:T(8,128)(2,1)}) custom-call(s32[3]{0:T(128)} %add_add_fusion.where, bf16[1024,1280]{1,0:T(8,128)(2,1)} %add_convert_fusion.3.acts.refs_0_, bf16[1024,2560]{1,0:T(8,128)(2,1)} %get-tuple-element.121.refs_1_, bf16[1024,1280]{1,0:T(8,128)(2,1)} %collective-permute-done.9.refs_2_, ...), custom_call_target="tpu_custom_call" | custom-call | flops 1342177280 | bytes 2228224 | tf_op jit(solution)/shard_map/grad_in/pallas_call | solution.py:491
  374.9 4.6 collective-permute-start.13
  381.3 5.4 collective-permute-done.11.refs_3_.refs_7_
  386.7 23.0 %grad_back.1 = (bf16[2,4,400,640]{3,2,1,0:T(8,128)(2,1)}, bf16[2,4,400,640]{3,2,1,0:T(8,128)(2,1)}) custom-call(s32[3]{0:T(128)} %add_add_fusion.where, bf16[1024,5120]{1,0:T(8,128)(2,1)} %get-tuple-element.166.a1.refs_0_, bf16[1024,1280]{1,0:T(8,128)(2,1)} %bitcast.6.rest_4_.b1, bf16[1024,5120]{1,0:T(8,128)(2,1)} %collective-permute-done.10.a2, ...), custom_call_target="tpu_custom_call" | custom-call | flops 1342177280 | bytes 3014656 | tf_op jit(solution)/shard_map/grad_back/pallas_call | solution.py:584
  409.7 10.6 %grad_out.1 = (bf16[2,4,400,640]{3,2,1,0:T(8,128)(2,1)}, bf16[2,4,400,640]{3,2,1,0:T(8,128)(2,1)}) custom-call(s32[3]{0:T(128)} %add_add_fusion.1.where, bf16[1024,640]{1,0:T(8,128)(2,1)} %bitcast.156, bf16[1024,1280]{1,0:T(8,128)(2,1)} %get-tuple-element.120.refs_1_.refs_5_, ...), custom_call_target="tpu_custom_call", output_to_operand_aliasing={{0}: (9, {}), {1}: (10, {})} | custom-call | flops 335544320 | bytes 950272 | tf_op jit(solution)/shard_map/grad_out/pallas_call | solution.py:491
  421.3 37.9 %attn_bwd_far.1 = (f32[2,640,1024]{2,1,0:T(8,128)}, bf16[2,1024,768]{2,1,0:T(8,128)(2,1)}, bf16[2,1024,512]{2,1,0:T(8,128)(2,1)}) custom-call(s32[2,4,4]{2,1,0:T(4,128)} %get-tuple-element.231.flags, s32[2,1,1024]{2,1,0:T(1,128)} %broadcast_in_dim.42.cq, s32[2,1024,128]{2,1,0:T(8,128)} %broadcast_in_dim.43.ck, bf16[2,1024,1920]{2,1,0:T(8,128)(2,1)} %bitcast.126, ...), custom_call_target="tpu_custom_call" | custom-call | flops 1342177280 | bytes 2359296 | tf_op jit(solution)/shard_map/attn_bwd_far/pallas_call | solution.py:264
  462.0 8.7 %far_norm_theirs.1 = bf16[1024,1280]{1,0:T(8,128)(2,1)} custom-call(bf16[2048,768]{1,0:T(8,128)(2,1)} %bitcast.152, bf16[2048,512]{1,0:T(8,128)(2,1)} %bitcast.159, bf16[1280,1920]{1,0:T(8,128)(2,1)} %own_columns.1.refs_2_), custom_call_target="tpu_custom_call" | custom-call | flops 335544320 | bytes 851968 | tf_op jit(solution)/shard_map/far_norm_theirs/pallas_call | solution.py:808
  470.7 8.3 %far_norm_mine.1 = bf16[1024,1280]{1,0:T(8,128)(2,1)} custom-call(bf16[2048,768]{1,0:T(8,128)(2,1)} %bitcast.153, bf16[2048,512]{1,0:T(8,128)(2,1)} %bitcast.160, bf16[1280,1920]{1,0:T(8,128)(2,1)} %own_columns.1.refs_2_), custom_call_target="tpu_custom_call" | custom-call | flops 335544320 | bytes 851968 | tf_op jit(solution)/shard_map/far_norm_mine/pallas_call | solution.py:808
  479.0 3.9 fusion.10
  485.8 37.7 %attn_bwd_early.1 = bf16[2,1024,1152]{2,1,0:T(8,128)(2,1)} custom-call(s32[2,4,4]{2,1,0:T(4,128)} %get-tuple-element.232.flags, s32[2,1,1024]{2,1,0:T(1,128)} %broadcast_in_dim.42.cq, s32[2,1024,128]{2,1,0:T(8,128)} %broadcast_in_dim.45.ck, bf16[2,1024,1920]{2,1,0:T(8,128)(2,1)} %bitcast.127, bf16[2,1024,1920]{2,1,0:T(8,128)(2,1)} %bitcast.128, ...), custom_call_target="tpu_custom_call" | custom-call | flops 805306368 | bytes 1415577 | tf_op jit(solution)/shard_map/attn_bwd_early/pallas_call | solution.py:264
  523.5 5.2 fusion.11
  528.7 16.3 %collective-permute-done.16 = bf16[2,160,2560]{2,1,0:T(8,128)(2,1)} collective-permute-done((bf16[2,160,2560]{2,1,0:T(8,128)(2,1)S(1)}, bf16[2,160,2560]{2,1,0:T(8,128)(2,1)}, u32[]{:S(2)}, u32[]{:S(2)}) %collective-permute-start.16) | collective-permute-done | bytes 1638432 | tf_op jit(solution)/shard_map/ppermute | solution.py:892
  546.9 4.4 collective-permute-start.20
  551.2 22.0 %grad_early.1 = (bf16[2,4,80,1152]{3,2,1,0:T(8,128)(2,1)}, bf16[2,4,80,1152]{3,2,1,0:T(8,128)(2,1)}, f32[1,1152]{1,0:T(1,128)}) custom-call(s32[3]{0:T(128)} %add_add_fusion.where, bf16[2048,1280]{1,0:T(8,128)(2,1)} %bitcast.146, bf16[2048,1152]{1,0:T(8,128)(2,1)} %bitcast.139, bf16[2048,1280]{1,0:T(8,128)(2,1)} %bitcast.149, bf16[2048,768]{1,0:T(8,128)(2,1)} %bitcast.154), custom_call_target="tpu_custom_call" | custom-call | flops 1207959552 | bytes 2287206 | tf_op jit(solution)/shard_map/grad_early/pallas_call | solution.py:542
  575.6 28.2 %attn_bwd_late.1 = bf16[2,1024,768]{2,1,0:T(8,128)(2,1)} custom-call(s32[2,4,4]{2,1,0:T(4,128)} %get-tuple-element.232.flags, s32[2,1,1024]{2,1,0:T(1,128)} %broadcast_in_dim.42.cq, s32[2,1024,128]{2,1,0:T(8,128)} %broadcast_in_dim.45.ck, bf16[2,1024,1920]{2,1,0:T(8,128)(2,1)} %bitcast.130, bf16[2,1024,1920]{2,1,0:T(8,128)(2,1)} %bitcast.131, ...), custom_call_target="tpu_custom_call" | custom-call | flops 536870912 | bytes 943718 | tf_op jit(solution)/shard_map/attn_bwd_late/pallas_call | solution.py:264
  605.3 3.8 collective-permute-done.19
  621.2 14.8 %grad_late.1 = (bf16[2,4,80,768]{3,2,1,0:T(8,128)(2,1)}, bf16[2,4,80,768]{3,2,1,0:T(8,128)(2,1)}, f32[1,768]{1,0:T(1,128)}) custom-call(s32[3]{0:T(128)} %add_add_fusion.where, bf16[2048,1280]{1,0:T(8,128)(2,1)} %bitcast.147, bf16[2048,768]{1,0:T(8,128)(2,1)} %bitcast.142, bf16[2048,1280]{1,0:T(8,128)(2,1)} %bitcast.150, bf16[2048,512]{1,0:T(8,128)(2,1)} %bitcast.161), custom_call_target="tpu_custom_call" | custom-call | flops 805306368 | bytes 1874329 | tf_op jit(solution)/shard_map/grad_late/pallas_call | solution.py:542
  637.1 10.3 %near_norm_theirs.1 = bf16[1024,1280]{1,0:T(8,128)(2,1)} custom-call(bf16[2048,1152]{1,0:T(8,128)(2,1)} %bitcast.140, bf16[2048,768]{1,0:T(8,128)(2,1)} %bitcast.143, bf16[1280,1920]{1,0:T(8,128)(2,1)} %own_columns.1.refs_2_), custom_call_target="tpu_custom_call" | custom-call | flops 503316480 | bytes 1146880 | tf_op jit(solution)/shard_map/near_norm_theirs/pallas_call | solution.py:808
  647.4 10.2 %near_norm_mine.1.rest_0_ = bf16[1024,1280]{1,0:T(8,128)(2,1)} custom-call(bf16[2048,1152]{1,0:T(8,128)(2,1)} %bitcast.141, bf16[2048,768]{1,0:T(8,128)(2,1)} %bitcast.144, bf16[1280,1920]{1,0:T(8,128)(2,1)} %own_columns.1.refs_2_), custom_call_target="tpu_custom_call" | custom-call | flops 503316480 | bytes 1146880 | tf_op jit(solution)/shard_map/near_norm_mine/pallas_call | solution.py:808
  668.9 21.0 %mixed.1 = bf16[1024,1280]{1,0:T(8,128)(2,1)} custom-call(bf16[1024,5120]{1,0:T(8,128)(2,1)} %get-tuple-element.166.a1.refs_0_, bf16[5120,1280]{1,0:T(8,128)(2,1)} %refs_1_.1, f32[1024,1280]{1,0:T(8,128)} %copy-done.1, f32[1,1280]{1,0:T(1,128)} %reshape.287.refs_3_), custom_call_target="tpu_custom_call" | custom-call | flops 1342177280 | bytes 2621440 | tf_op jit(solution)/shard_map/mixed/pallas_call | solution.py:808
  695.4 11.7 %first_norm.1 = (f32[1024,1280]{1,0:T(8,128)}, f32[8,1280]{1,0:T(8,128)}) custom-call(bf16[1024,1280]{1,0:T(8,128)(2,1)} %bitcast.151, f32[1024,1280]{1,0:T(8,128)} %get-tuple-element.167.d_middle, f32[1,1280]{1,0:T(1,128)} %broadcast_in_dim.50.gain, bf16[1024,1280]{1,0:T(8,128)(2,1)} %near_norm_mine.1.rest_0_, ...), custom_call_target="tpu_custom_call" | custom-call | flops 2621440 | bytes 2621440 | tf_op jit(solution)/shard_map/first_norm/pallas_call | solution.py:635
  726.7 3.6 collective-permute-done.39.q_row
  (229 shorter events, 109.4 us)
Async XLA Ops:
  9.6 153.9 %collective-permute-start.2 = (bf16[1,1024,1280]{2,1,0:T(8,128)(2,1)}, bf16[1,1024,1280]{2,1,0:T(8,128)(2,1)}, u32[]{:S(2)}, u32[]{:S(2)}) collective-permute-start(bf16[1,1024,1280]{2,1,0:T(8,128)(2,1)} %fusion.8), channel_id=1, source_target_pairs={{0,2},{2,0},{4,6},{6,4},{8,10},{10,8},{12,14},{14,12},{16,18},{18,... | collective-permute-start | bytes 7864328 | tf_op jit(solution)/shard_map/ppermute | solution.py:892
  162.1 59.7 %collective-permute-start.3 = (bf16[1,1024,1280]{2,1,0:T(8,128)(2,1)}, bf16[1,1024,1280]{2,1,0:T(8,128)(2,1)}, u32[]{:S(2)}, u32[]{:S(2)}) collective-permute-start(bf16[1,1024,1280]{2,1,0:T(8,128)(2,1)} %fusion.8), channel_id=1, source_target_pairs={{1,0},{0,1},{3,2},{2,3},{5,4},{4,5},{7,6},{6,7},{9,8},{8,9},{11,10... | collective-permute-start | bytes 7864328 | tf_op jit(solution)/shard_map/ppermute | solution.py:898
  166.7 55.1 %collective-permute-start.5 = (bf16[1024,1280]{1,0:T(8,128)(2,1)}, bf16[1024,1280]{1,0:T(8,128)(2,1)}, u32[]{:S(2)}, u32[]{:S(2)}) collective-permute-start(bf16[1024,1280]{1,0:T(8,128)(2,1)} %bitcast.6.rest_4_.b1), channel_id=1, source_target_pairs={{0,2},{2,0},{4,6},{6,4},{8,10},{10,8},{12,14},{14,12},{16,18},{18,... | collective-permute-start | bytes 7864328 | tf_op jit(solution)/shard_map/ppermute | solution.py:892
  221.8 20.0 %collective-permute-start.4 = (bf16[1,1024,1280]{2,1,0:T(8,128)(2,1)}, bf16[1,1024,1280]{2,1,0:T(8,128)(2,1)}, u32[]{:S(2)}, u32[]{:S(2)}) collective-permute-start(bf16[1,1024,1280]{2,1,0:T(8,128)(2,1)} %collective-permute-done.3), channel_id=1, source_target_pairs={{0,2},{2,0},{4,6},{6,4},{8,10},{10,8},{12,14},{14,12},{16,18},{18,... | collective-permute-start | bytes 7864328 | tf_op jit(solution)/shard_map/ppermute | solution.py:892
  282.6 13.2 %collective-permute-start.7 = (bf16[1024,640]{1,0:T(8,128)(2,1)}, bf16[1024,640]{1,0:T(8,128)(2,1)S(1)}, u32[]{:S(2)}, u32[]{:S(2)}) collective-permute-start(bf16[1024,640]{1,0:T(8,128)(2,1)} %bitcast.155), channel_id=1, source_target_pairs={{0,2},{2,0},{4,6},{6,4},{8,10},{10,8},{12,14},{14,12},{16,18},{18,... | collective-permute-start | bytes 3932168 | tf_op jit(solution)/shard_map/ppermute | solution.py:892
  320.7 31.4 %collective-permute-start.8 = (bf16[1024,2560]{1,0:T(8,128)(2,1)}, bf16[1024,2560]{1,0:T(8,128)(2,1)S(1)}, u32[]{:S(2)}, u32[]{:S(2)}) collective-permute-start(bf16[1024,2560]{1,0:T(8,128)(2,1)} %get-tuple-element.118), channel_id=1, source_target_pairs={{0,2},{2,0},{4,6},{6,4},{8,10},{10,8},{12,14},{14,12},{16,18},{18,... | collective-permute-start | bytes 15728648 | tf_op jit(solution)/shard_map/ppermute | solution.py:892
  321.0 31.1 %collective-permute-start.9 = (bf16[1024,1280]{1,0:T(8,128)(2,1)S(1)}, bf16[1024,1280]{1,0:T(8,128)(2,1)}, u32[]{:S(2)}, u32[]{:S(2)}) collective-permute-start(bf16[1024,1280]{1,0:T(8,128)(2,1)S(1)} %copy-done.6), channel_id=1, source_target_pairs={{0,2},{2,0},{4,6},{6,4},{8,10},{10,8},{12,14},{14,12},{16,18},{18,... | collective-permute-start | bytes 7864328 | tf_op jit(solution)/shard_map/ppermute | solution.py:892
  352.1 34.5 %collective-permute-start.10 = (bf16[1024,5120]{1,0:T(8,128)(2,1)}, bf16[1024,5120]{1,0:T(8,128)(2,1)}, u32[]{:S(2)}, u32[]{:S(2)}) collective-permute-start(bf16[1024,5120]{1,0:T(8,128)(2,1)} %get-tuple-element.166.a1.refs_0_), channel_id=1, source_target_pairs={{0,2},{2,0},{4,6},{6,4},{8,10},{10,8},{12,14},{14,12},{16,18},{18,... | collective-permute-start | bytes 31457288 | tf_op jit(solution)/shard_map/ppermute | solution.py:892
  374.9 84.3 %collective-permute-start.13 = (bf16[4,160,2560]{2,1,0:T(8,128)(2,1)}, bf16[4,160,2560]{2,1,0:T(8,128)(2,1)}, u32[]{:S(2)}, u32[]{:S(2)}) collective-permute-start(bf16[4,160,2560]{2,1,0:T(8,128)(2,1)} %get-tuple-element.123), channel_id=1, source_target_pairs={{0,4},{2,6},{4,0},{6,2},{8,12},{10,14},{12,8},{14,10},{16,20},{18,... | collective-permute-start | bytes 9830408 | tf_op jit(solution)/shard_map/ppermute | solution.py:892
  379.5 7.1 collective-permute-start.11
  379.5 40.7 %collective-permute-start.12 = (bf16[1024,640]{1,0:T(8,128)(2,1)}, bf16[1024,640]{1,0:T(8,128)(2,1)S(1)}, u32[]{:S(2)}, u32[]{:S(2)}) collective-permute-start(bf16[1024,640]{1,0:T(8,128)(2,1)} %get-tuple-element.126), channel_id=1, source_target_pairs={{0,2},{2,0},{4,6},{6,4},{8,10},{10,8},{12,14},{14,12},{16,18},{18,... | collective-permute-start | bytes 3932168 | tf_op jit(solution)/shard_map/ppermute | solution.py:892
  420.2 103.3 %collective-permute-start.15 = (bf16[2,4,400,640]{3,2,1,0:T(8,128)(2,1)}, bf16[2,4,400,640]{3,2,1,0:T(8,128)(2,1)}, u32[]{:S(2)}, u32[]{:S(2)}) collective-permute-start(bf16[2,4,400,640]{3,2,1,0:T(8,128)(2,1)} %get-tuple-element.132), channel_id=1, source_target_pairs={{1,0},{0,1},{3,2},{2,3},{5,4},{4,5},{7,6},{6,7},{9,8},{8,9},{11,10... | collective-permute-start | bytes 12288008 | tf_op jit(solution)/shard_map/ppermute | solution.py:898
  470.7 8.3 %collective-permute-start.14 = (bf16[1024,1280]{1,0:T(8,128)(2,1)}, bf16[1024,1280]{1,0:T(8,128)(2,1)S(1)}, u32[]{:S(2)}, u32[]{:S(2)}) collective-permute-start(bf16[1024,1280]{1,0:T(8,128)(2,1)} %far_norm_theirs.1), channel_id=1, source_target_pairs={{0,2},{2,0},{4,6},{6,4},{8,10},{10,8},{12,14},{14,12},{16,18},{18,... | collective-permute-start | bytes 7864328 | tf_op jit(solution)/shard_map/ppermute | solution.py:892
  470.7 74.3 %collective-permute-start.16 = (bf16[2,160,2560]{2,1,0:T(8,128)(2,1)S(1)}, bf16[2,160,2560]{2,1,0:T(8,128)(2,1)}, u32[]{:S(2)}, u32[]{:S(2)}) collective-permute-start(bf16[2,160,2560]{2,1,0:T(8,128)(2,1)S(1)} %get-tuple-element.200), channel_id=1, source_target_pairs={{0,16},{2,18},{4,20},{6,22},{8,24},{10,26},{12,28},{14,30},{16,0},... | collective-permute-start | bytes 4915208 | tf_op jit(solution)/shard_map/ppermute | solution.py:892
  482.9 90.6 %collective-permute-start.17 = (bf16[1,1024,1280]{2,1,0:T(8,128)(2,1)}, bf16[1,1024,1280]{2,1,0:T(8,128)(2,1)}, u32[]{:S(2)}, u32[]{:S(2)}) collective-permute-start(bf16[1,1024,1280]{2,1,0:T(8,128)(2,1)} %fusion.10), channel_id=1, source_target_pairs={{0,1},{1,0},{2,3},{3,2},{4,5},{5,4},{6,7},{7,6},{8,9},{9,8},{10,11... | collective-permute-start | bytes 7864328 | tf_op jit(solution)/shard_map/ppermute | solution.py:901
  546.8 26.5 %collective-permute-start.18 = (bf16[160,2560]{1,0:T(8,128)(2,1)S(1)}, bf16[160,2560]{1,0:T(8,128)(2,1)S(1)}, u32[]{:S(2)}, u32[]{:S(2)}) collective-permute-start(bf16[160,2560]{1,0:T(8,128)(2,1)S(1)} %get-tuple-element.204), channel_id=1, source_target_pairs={{0,8},{2,10},{4,12},{6,14},{8,0},{10,2},{12,4},{14,6},{16,24},{18,... | collective-permute-start | bytes 2457608 | tf_op jit(solution)/shard_map/ppermute | solution.py:892
  546.9 56.9 %collective-permute-start.20 = (bf16[4,400,640]{2,1,0:T(8,128)(2,1)}, bf16[4,400,640]{2,1,0:T(8,128)(2,1)S(1)}, u32[]{:S(2)}, u32[]{:S(2)}) collective-permute-start(bf16[4,400,640]{2,1,0:T(8,128)(2,1)} %get-tuple-element.198), channel_id=1, source_target_pairs={{0,4},{2,6},{4,0},{6,2},{8,12},{10,14},{12,8},{14,10},{16,20},{18,... | collective-permute-start | bytes 6144008 | tf_op jit(solution)/shard_map/ppermute | solution.py:892
  573.5 35.6 %collective-permute-start.19 = (bf16[2,4,80,1152]{3,2,1,0:T(8,128)(2,1)}, bf16[2,4,80,1152]{3,2,1,0:T(8,128)(2,1)}, u32[]{:S(2)}, u32[]{:S(2)}) collective-permute-start(bf16[2,4,80,1152]{3,2,1,0:T(8,128)(2,1)} %get-tuple-element.152), channel_id=1, source_target_pairs={{1,0},{0,1},{3,2},{2,3},{5,4},{4,5},{7,6},{6,7},{9,8},{8,9},{11,10... | collective-permute-start | bytes 4423688 | tf_op jit(solution)/shard_map/ppermute | solution.py:898
  574.7 82.9 %collective-permute-start.24 = (bf16[160,2560]{1,0:T(8,128)(2,1)S(1)}, bf16[160,2560]{1,0:T(8,128)(2,1)S(1)}, u32[]{:S(2)}, u32[]{:S(2)}) collective-permute-start(bf16[160,2560]{1,0:T(8,128)(2,1)S(1)} %add_convert_fusion.8.in_mine), channel_id=1, source_target_pairs={{1,0},{0,1},{3,2},{2,3},{5,4},{4,5},{7,6},{6,7},{9,8},{8,9},{11,10... | collective-permute-start | bytes 2457608 | tf_op jit(solution)/shard_map/ppermute | solution.py:898
  611.8 46.0 %collective-permute-start.21 = (bf16[4,80,1152]{2,1,0:T(8,128)(2,1)}, bf16[4,80,1152]{2,1,0:T(8,128)(2,1)}, u32[]{:S(2)}, u32[]{:S(2)}) collective-permute-start(bf16[4,80,1152]{2,1,0:T(8,128)(2,1)} %get-tuple-element.206), channel_id=1, source_target_pairs={{0,4},{2,6},{4,0},{6,2},{8,12},{10,14},{12,8},{14,10},{16,20},{18,... | collective-permute-start | bytes 2211848 | tf_op jit(solution)/shard_map/ppermute | solution.py:892
  611.8 48.2 %collective-permute-start.22 = (bf16[2,400,640]{2,1,0:T(8,128)(2,1)}, bf16[2,400,640]{2,1,0:T(8,128)(2,1)}, u32[]{:S(2)}, u32[]{:S(2)}) collective-permute-start(bf16[2,400,640]{2,1,0:T(8,128)(2,1)} %get-tuple-element.202), channel_id=1, source_target_pairs={{0,16},{2,18},{4,20},{6,22},{8,24},{10,26},{12,28},{14,30},{16,0},... | collective-permute-start | bytes 3072008 | tf_op jit(solution)/shard_map/ppermute | solution.py:892
  636.0 26.2 %collective-permute-start.23 = (bf16[2,4,80,768]{3,2,1,0:T(8,128)(2,1)}, bf16[2,4,80,768]{3,2,1,0:T(8,128)(2,1)S(1)}, u32[]{:S(2)}, u32[]{:S(2)}) collective-permute-start(bf16[2,4,80,768]{3,2,1,0:T(8,128)(2,1)} %get-tuple-element.159), channel_id=1, source_target_pairs={{1,0},{0,1},{3,2},{2,3},{5,4},{4,5},{7,6},{6,7},{9,8},{8,9},{11,10... | collective-permute-start | bytes 2949128 | tf_op jit(solution)/shard_map/ppermute | solution.py:898
  657.6 37.8 %collective-permute-start.25 = (bf16[1024,1280]{1,0:T(8,128)(2,1)}, bf16[1024,1280]{1,0:T(8,128)(2,1)}, u32[]{:S(2)}, u32[]{:S(2)}) collective-permute-start(bf16[1024,1280]{1,0:T(8,128)(2,1)} %near_norm_theirs.1), channel_id=1, source_target_pairs={{0,2},{2,0},{4,6},{6,4},{8,10},{10,8},{12,14},{14,12},{16,18},{18,... | collective-permute-start | bytes 7864328 | tf_op jit(solution)/shard_map/ppermute | solution.py:892
  663.2 26.7 %collective-permute-start.26 = (bf16[4,80,768]{2,1,0:T(8,128)(2,1)}, bf16[4,80,768]{2,1,0:T(8,128)(2,1)}, u32[]{:S(2)}, u32[]{:S(2)}) collective-permute-start(bf16[4,80,768]{2,1,0:T(8,128)(2,1)} %get-tuple-element.211), channel_id=1, source_target_pairs={{0,4},{2,6},{4,0},{6,2},{8,12},{10,14},{12,8},{14,10},{16,20},{18,... | collective-permute-start | bytes 1474568 | tf_op jit(solution)/shard_map/ppermute | solution.py:892
  665.7 28.3 %collective-permute-start.27 = (bf16[2,80,1152]{2,1,0:T(8,128)(2,1)}, bf16[2,80,1152]{2,1,0:T(8,128)(2,1)S(1)}, u32[]{:S(2)}, u32[]{:S(2)}) collective-permute-start(bf16[2,80,1152]{2,1,0:T(8,128)(2,1)} %get-tuple-element.212), channel_id=1, source_target_pairs={{0,16},{2,18},{4,20},{6,22},{8,24},{10,26},{12,28},{14,30},{16,0},... | collective-permute-start | bytes 1105928 | tf_op jit(solution)/shard_map/ppermute | solution.py:892
  665.8 29.0 %collective-permute-start.28 = (bf16[400,640]{1,0:T(8,128)(2,1)}, bf16[400,640]{1,0:T(8,128)(2,1)S(1)}, u32[]{:S(2)}, u32[]{:S(2)}) collective-permute-start(bf16[400,640]{1,0:T(8,128)(2,1)} %get-tuple-element.208), channel_id=1, source_target_pairs={{0,8},{2,10},{4,12},{6,14},{8,0},{10,2},{12,4},{14,6},{16,24},{18,... | collective-permute-start | bytes 1536008 | tf_op jit(solution)/shard_map/ppermute | solution.py:892
  691.8 22.0 %collective-permute-start.37 = (bf16[2,80,768]{2,1,0:T(8,128)(2,1)}, bf16[2,80,768]{2,1,0:T(8,128)(2,1)}, u32[]{:S(2)}, u32[]{:S(2)}) collective-permute-start(bf16[2,80,768]{2,1,0:T(8,128)(2,1)} %get-tuple-element.214), channel_id=1, source_target_pairs={{0,16},{2,18},{4,20},{6,22},{8,24},{10,26},{12,28},{14,30},{16,0},... | collective-permute-start | bytes 737288 | tf_op jit(solution)/shard_map/ppermute | solution.py:892
  694.7 13.3 %collective-permute-start.36 = (bf16[80,1152]{1,0:T(8,128)(2,1)S(1)}, bf16[80,1152]{1,0:T(8,128)(2,1)}, u32[]{:S(2)}, u32[]{:S(2)}) collective-permute-start(bf16[80,1152]{1,0:T(8,128)(2,1)S(1)} %get-tuple-element.216), channel_id=1, source_target_pairs={{0,8},{2,10},{4,12},{6,14},{8,0},{10,2},{12,4},{14,6},{16,24},{18,... | collective-permute-start | bytes 552968 | tf_op jit(solution)/shard_map/ppermute | solution.py:892
  694.9 31.8 %collective-permute-start.35 = (bf16[400,640]{1,0:T(8,128)(2,1)S(1)}, bf16[400,640]{1,0:T(8,128)(2,1)S(1)}, u32[]{:S(2)}, u32[]{:S(2)}) collective-permute-start(bf16[400,640]{1,0:T(8,128)(2,1)S(1)} %add_convert_fusion.13.b_mine), channel_id=1, source_target_pairs={{1,0},{0,1},{3,2},{2,3},{5,4},{4,5},{7,6},{6,7},{9,8},{8,9},{11,10... | collective-permute-start | bytes 1536008 | tf_op jit(solution)/shard_map/ppermute | solution.py:898
  708.4 5.4 collective-permute-start.29
  710.8 5.5 collective-permute-start.31
  723.4 6.9 collective-permute-start.39
  (43 other events, 429.9 us)
